TPU v7x, 256 devices: a whole 4x4x8 slice. The times are simulated.
256 devices in a mesh: shards: 16 (over x, y), tensor: 4 (over z_hi, core), replica: 4 (over z_lo).
Axes of the slice: x: 4, y: 4, z: 8 (z_hi: 2, z_lo: 4; z = z_hi * 4 + z_lo), core: 2. Of those that a mesh axis runs over, the one named last changes fastest.
Arguments:
- activations: bfloat16 [262144, 1024], P(('shards', 'tensor', 'replica')), may hold values from -24 to 24
- grads_out: bfloat16 [262144, 1024], P(('shards', 'tensor', 'replica')), may hold values from -24 to 24
- grad_parts: float32 [64, 1024, 1024], P(('shards', 'replica'), None, 'tensor'), may hold values from -80 to 80
- old_factors: float32 [16, 128, 128], replicated, may hold values from -16 to 16, as said below
- block_owner: int32 [16], replicated, may hold values from 0 to 15, as said below
- weights: float32 [1024, 1024], P(('shards', 'replica'), 'tensor'), may hold values from -0.1875 to 0.1875
- momentum: float32 [1024, 1024], P(('shards', 'replica'), 'tensor'), may hold values from -4 to 4
Outputs:
- weights_next: float32 [1024, 1024], P(None, 'tensor')
- momentum_next: float32 [1024, 1024], P(('shards', 'replica'), 'tensor')
- next_factor_blocks: float32 [32, 128, 128], P('shards')
Inputs may be any that keep to these rules, and one draw needn't show every extreme that they name: `block_owner`: each shard index owns at most 2 of the 16 blocks, and some index owns exactly 2. `old_factors`: each block is symmetric and positive definite.
All inputs are finite; a program needn't handle non-finite values. Where the computation divides by a largest or mean magnitude, that divisor is 1e-20 or more.
Results may differ from a plain program's by a relative error of at most 0.0003.
Values sent between devices are 32-bit elements; how exact they have to be, the bound alone decides.
No kernel may reach another device: no remote copies, remote signals or barrier semaphores. Data moves between devices by JAX's collectives and lax.ppermute only.
A program may use at most 64 MiB of HBM per device.

v0:
```python
import jax
import jax.numpy as jnp
from jax import lax
from jax.sharding import PartitionSpec as P

NS_STEPS = 4


exact_mode = lax.Precision.HIGHEST
decay_rate = 0.75
damping = 0.1
damp_shift = 0.001
clip_norm = 256.0
momentum_rate = 0.9
step_rate = 0.05


def sample_stats(samples, block_size):
    sample_rows, width = samples.shape
    blocks = samples.reshape(sample_rows, width // block_size, block_size)
    return jnp.einsum("tnb,tnc->nbc", blocks, blocks, preferred_element_type=jnp.float32)


def build_slots(block_owner, capacity, slot_count):
    block_count = block_owner.shape[0]
    positions = jnp.arange(block_count, dtype=jnp.int32)
    earlier = (block_owner[:, None] == block_owner[None, :]) & (
        positions[None, :] < positions[:, None]
    )
    owner_slot_list = block_owner * capacity + jnp.sum(earlier.astype(jnp.int32), axis=1)
    return (owner_slot_list[None, :] == jnp.arange(slot_count, dtype=jnp.int32)[:, None]).astype(
        jnp.float32
    )


def newton_inverse(mixed_factor_blocks):
    block_size = mixed_factor_blocks.shape[-1]
    identity = jnp.eye(block_size, dtype=jnp.float32)
    traces = jnp.trace(mixed_factor_blocks, axis1=1, axis2=2)
    damped = (
        mixed_factor_blocks + (damping * traces / block_size + damp_shift)[:, None, None] * identity
    )
    bounds = jnp.max(jnp.sum(jnp.abs(damped), axis=2), axis=1)
    approx = identity[None, :, :] / bounds[:, None, None]
    for iteration in range(NS_STEPS):
        left_part = jnp.einsum("nab,nbc->nac", approx, damped, precision=exact_mode)
        approx = 2.0 * approx - jnp.einsum("nab,nbc->nac", left_part, approx, precision=exact_mode)
    return approx


def apply_right(left_part, right_inv, block_size):
    row_count, col_count = left_part.shape
    right_count = col_count // block_size
    return jnp.einsum(
        "rnb,nbc->rnc",
        left_part.reshape(row_count, right_count, block_size),
        right_inv,
        precision=exact_mode,
    ).reshape(row_count, col_count)


def body(activations, grads_out, grad_parts, old_factors, block_owner, weights, momentum):
    shard_count = lax.axis_size("shards")
    block_count = old_factors.shape[0]
    block_size = old_factors.shape[1]
    capacity = (block_count + shard_count - 1) // shard_count + 1
    slot_count = capacity * shard_count
    slot_table = build_slots(block_owner, capacity, slot_count)
    local_stats = jnp.concatenate(
        [sample_stats(activations, block_size), sample_stats(grads_out, block_size)], axis=0
    )
    packed = jnp.dot(
        slot_table, local_stats.reshape(block_count, block_size * block_size), precision=exact_mode
    )
    first_slot = lax.axis_index("shards") * capacity
    summed = lax.psum(packed, ("shards", "tensor", "replica"))
    owned = lax.dynamic_slice_in_dim(summed, first_slot, capacity, 0)
    sample_count = (
        activations.shape[0] * shard_count * lax.axis_size("tensor") * lax.axis_size("replica")
    )
    owned_table = lax.dynamic_slice_in_dim(slot_table, first_slot, capacity, 0)
    old_owned = jnp.dot(
        owned_table, old_factors.reshape(block_count, block_size * block_size), precision=exact_mode
    )
    mixed_factor_blocks = (
        decay_rate * old_owned + (1.0 - decay_rate) * (owned / sample_count)
    ).reshape(capacity, block_size, block_size)
    inverse_owned = newton_inverse(mixed_factor_blocks)
    start_blocks = jnp.zeros((block_count, block_size * block_size), jnp.float32)
    shard_piece = lax.all_gather(inverse_owned, "shards", axis=0, tiled=True)
    piece_rows = shard_piece.shape[0]
    rows_table = lax.slice_in_dim(slot_table, 0, piece_rows, axis=0)
    flat_piece = shard_piece.reshape(piece_rows, block_size * block_size)
    inverse_flat = start_blocks + jnp.einsum(
        "sb,sk->bk", rows_table, flat_piece, precision=exact_mode
    )
    inverse_blocks = inverse_flat.reshape(block_count, block_size, block_size)
    partial_grad = grad_parts[0]
    row_count, col_count = partial_grad.shape
    left_count = row_count // block_size
    right_count = col_count // block_size
    right_first = left_count + lax.axis_index("tensor") * right_count
    right_inv = lax.dynamic_slice_in_dim(inverse_blocks, right_first, right_count, 0)
    left_part = jnp.einsum(
        "nab,nbc->nac",
        inverse_blocks[:left_count],
        partial_grad.reshape(left_count, block_size, col_count),
        precision=exact_mode,
    ).reshape(row_count, col_count)
    precond = apply_right(left_part, right_inv, block_size)
    total_precond, total_grad = (
        lax.psum_scatter(precond, ("shards", "replica"), scatter_dimension=0, tiled=True),
        lax.psum_scatter(partial_grad, ("shards", "replica"), scatter_dimension=0, tiled=True),
    )
    alignment_sum = lax.psum(jnp.sum(total_precond * total_grad), ("shards", "tensor", "replica"))
    clip_scale = jnp.minimum(1.0, clip_norm / jnp.sqrt(alignment_sum))
    momentum_next = momentum_rate * momentum + clip_scale * total_precond
    weights_next = weights - step_rate * momentum_next
    gathered = lax.all_gather(weights_next, ("shards", "replica"), axis=0, tiled=True)
    return (gathered, momentum_next, mixed_factor_blocks)


def solution(mesh):
    placed = (
        P(("shards", "tensor", "replica"), None),
        P(("shards", "tensor", "replica"), None),
        P(("shards", "replica"), None, "tensor"),
        P(),
        P(),
        P(("shards", "replica"), "tensor"),
        P(("shards", "replica"), "tensor"),
    )
    return jax.shard_map(
        body,
        mesh=mesh,
        in_specs=placed,
        out_specs=(P(None, "tensor"), P(("shards", "replica"), "tensor"), P("shards", None, None)),
        check_vma=False,
    )
```

profile of v0, /device:TPU:94, one launch (start us, length us, event | category | flops | bytes accessed | tf_op | source)
XLA Modules:
  0.0 1458.4 jit_solution(3931337511195937440)
XLA Ops:
  8.0 0.0 copy-start
  8.0 0.0 all-reduce.2.cloned.1.call-start
  8.1 1.0 convert_reduce_fusion
  9.1 0.9 multiply_add_fusion.7
  10.0 1.1 fusion.4
  11.0 1.1 fusion.7
  12.2 0.1 pad_maximum_fusion
  12.2 0.0 copy-start.4
  12.3 2.8 fusion.10
  15.1 0.0 all-reduce.2.cloned.1.call-update
  15.1 0.0 all-gather.3.cloned.1.call-start
  15.2 259.1 %all-reduce.2.cloned.1.call-done = f32[32,16384]{1,0:T(8,128)} async-done(((f32[32,16384]{1,0:T(8,128)}), f32[32,16384]{1,0:T(8,128)}) %all-reduce.2.cloned.1.call-update) | async-done | bytes 2097168 | tf_op jit(solution)/shard_map/psum | solution.py:76
  274.3 2.3 select_reduce_fusion
  276.6 0.2 abs_reduce_fusion
  276.8 0.0 copy-start.3
  276.8 0.1 reduce_max.9
  276.9 0.3 fusion.20
  277.3 0.3 convolution_subtract_fusion.3
  277.6 0.3 fusion.25
  278.0 0.3 convolution_subtract_fusion.2
  278.3 0.3 fusion.24
  278.6 0.3 convolution_subtract_fusion.1
  278.9 0.3 fusion.23
  279.2 0.9 convolution_subtract_fusion
  280.1 0.0 all-gather.3.cloned.1.call-update
  280.2 0.0 reduce-scatter.5.cloned.1.call-start
  280.2 0.5 reduce-scatter.5.cloned.1.call-update
  280.8 0.2 reduce-scatter.3.cloned.1.call-start
  281.0 49.9 %all-gather.3.cloned.1.call-done = f32[32,128,128]{2,1,0:T(8,128)} async-done(((f32[2,128,128]{2,1,0:T(8,128)}), f32[32,128,128]{2,1,0:T(8,128)}) %all-gather.3.cloned.1.call-update) | async-done | bytes 2097168 | tf_op jit(solution)/shard_map/all_gather | solution.py:90
  330.9 3.6 fusion.1
  334.6 2.0 fusion.17
  336.7 2.7 reshape_reshape.3
  339.4 0.2 copy.41
  339.6 1.0 copy-done.1
  340.6 1.1 fusion.15
  341.7 0.0 copy-start.5
  341.7 0.0 copy-start.6
  341.7 1.3 copy.33
  343.0 0.0 reduce-scatter.3.cloned.1.call-update
  343.0 0.0 all-gather.5.cloned.1.call-start
  343.1 310.3 %reduce-scatter.5.cloned.1.call-done = f32[16,256]{1,0:T(8,128)} async-done(((f32[1024,256]{1,0:T(8,128)}), f32[16,256]{1,0:T(8,128)}) %reduce-scatter.5.cloned.1.call-update) | async-done | bytes 16400 | tf_op jit(solution)/shard_map/reduce_scatter | solution.py:113
  653.4 370.3 %reduce-scatter.3.cloned.1.call-done = f32[16,256]{1,0:T(8,128)} async-done(((f32[1024,256]{1,0:T(8,128)}), f32[16,256]{1,0:T(8,128)}) %reduce-scatter.3.cloned.1.call-update) | async-done | bytes 16400 | tf_op jit(solution)/shard_map/reduce_scatter | solution.py:112
  1023.7 1.3 multiply_reduce_fusion
  1025.0 72.1 %psum.15 = f32[]{:T(128)} all-reduce(f32[]{:T(128)} %multiply_reduce_fusion), channel_id=1, replica_groups=mesh['shards'=16,'tensor'=4,'replica'=4] {'shards','tensor','replica'}, use_global_device_ids=true, to_apply=%region_8.9 | all-reduce | flops 1 | bytes 8 | tf_op jit(solution)/shard_map/psum | solution.py:115
  1097.9 1.3 multiply_subtract_fusion
  1099.2 0.0 all-gather.5.cloned.1.call-update
  1099.2 349.3 %all-gather.5.cloned.1.call-done = f32[1024,256]{1,0:T(8,128)} async-done(((f32[16,256]{1,0:T(8,128)}), f32[1024,256]{1,0:T(8,128)}) %all-gather.5.cloned.1.call-update) | async-done | bytes 1048592 | tf_op jit(solution)/shard_map/all_gather | solution.py:119
  1448.5 2.3 copy.72
  (15 shorter events, 0.1 us)
Async XLA Ops:
  8.0 2.0 copy-start
  8.0 266.3 %all-reduce.2.cloned.1.call-start = ((), (), s32[]{:S(2)}) async-start(), calls=%async_computation.2 | async-start | bytes 4194304 | tf_op jit(solution)/shard_map/psum | solution.py:76
  8.1 3.0 copy-start.7
  12.2 262.0 %copy-start.4 = (f32[16,128,128]{2,1,0:T(8,128)S(1)}, f32[16,128,128]{2,1,0:T(8,128)}, u32[]{:S(2)}) copy-start(f32[16,128,128]{2,1,0:T(8,128)} %param.10) | copy-start | bytes 3145732
  15.1 315.9 %all-gather.3.cloned.1.call-start = ((), (), s32[]{:S(2)}) async-start(), calls=%async_computation.3 | async-start | bytes 2228224 | tf_op jit(solution)/shard_map/all_gather | solution.py:90
  276.8 3.9 copy-start.3
  280.2 373.2 %reduce-scatter.5.cloned.1.call-start = ((), (), s32[]{:S(2)}) async-start(), calls=%async_computation.5 | async-start | bytes 1064960 | tf_op jit(solution)/shard_map/reduce_scatter | solution.py:113
  280.8 742.9 %reduce-scatter.3.cloned.1.call-start = ((), (), s32[]{:S(2)}) async-start(), calls=%async_computation.4 | async-start | bytes 1064960 | tf_op jit(solution)/shard_map/reduce_scatter | solution.py:112
  330.9 3.7 copy-start.2
  339.4 1.2 copy-start.1
  341.7 756.2 %copy-start.5 = (f32[16,256]{1,0:T(8,128)S(1)}, f32[16,256]{1,0:T(8,128)}, u32[]{:S(2)}) copy-start(f32[16,256]{1,0:T(8,128)} %param.12) | copy-start | bytes 49156
  341.7 756.2 %copy-start.6 = (f32[16,256]{1,0:T(8,128)S(1)}, f32[16,256]{1,0:T(8,128)}, u32[]{:S(2)}) copy-start(f32[16,256]{1,0:T(8,128)} %param.13) | copy-start | bytes 49156
  343.0 1105.5 %all-gather.5.cloned.1.call-start = ((), (), s32[]{:S(2)}) async-start(), calls=%async_computation.6 | async-start | bytes 1064960 | tf_op jit(solution)/shard_map/all_gather | solution.py:119
Sparse Core Ops, SparseCore 0:
  15.2 259.0 all-reduce.1
  280.3 50.6 all-gather.2
Sparse Core Ops, SparseCore 1:
  283.1 370.2 reduce-scatter.4
  656.5 367.1 reduce-scatter.2
  1099.3 349.2 all-gather.4
where the time goes:
time: 1460 us
  waiting for transfers between devices  1340 us (92%)
  blocking collectives  72.1 us (5%)
  matrix products  17.2 us (1%)
  between operations  16.6 us (1%)
    reduce_scatter x1, waiting for transfers between devices, body(): lax.psum_scatter(precond, ('shards', 'replica'), scatter_dimension=0, til...  370 us
    all_gather x1, waiting for transfers between devices, body(): lax.all_gather(weights_next, ('shards', 'replica'), axis=0, tiled=True)  349 us
    reduce_scatter x1, waiting for transfers between devices, body(): lax.psum_scatter(partial_grad, ('shards', 'replica'), scatter_dimension=0...  310 us
    psum x1, waiting for transfers between devices, body(): summed = lax.psum(packed, ('shards', 'tensor', 'replica'))  259 us
    psum x1, blocking collectives, body(): lax.psum(jnp.sum(total_precond * total_grad), ('shards', 'tensor', 'repli...  72.1 us
    all_gather x1, waiting for transfers between devices, body(): shard_piece = lax.all_gather(inverse_owned, 'shards', axis=0, tiled=True)  49.9 us
  transfers between devices with their start and end apart: 5, of which 5 were waited for; matrix products, arithmetic and copies ran while one was open for 1% of the time, Pallas kernels for 0%

commit v1 on v0

v1 whole, which is shorter than its diff:
```python
import jax
import jax.numpy as jnp
from jax import lax
from jax.sharding import PartitionSpec as P

NS_STEPS = 4


exact_mode = lax.Precision.HIGHEST
decay_rate = 0.75
damping = 0.1
damp_shift = 0.001
clip_norm = 256.0
momentum_rate = 0.9
step_rate = 0.05


def sample_stats(samples, block_size):
    sample_rows, width = samples.shape
    blocks = samples.reshape(sample_rows, width // block_size, block_size)
    return jnp.einsum("tnb,tnc->nbc", blocks, blocks, preferred_element_type=jnp.float32)


def newton_inverse(mixed_factor_blocks):
    block_size = mixed_factor_blocks.shape[-1]
    identity = jnp.eye(block_size, dtype=jnp.float32)
    traces = jnp.trace(mixed_factor_blocks, axis1=1, axis2=2)
    damped = (
        mixed_factor_blocks + (damping * traces / block_size + damp_shift)[:, None, None] * identity
    )
    bounds = jnp.max(jnp.sum(jnp.abs(damped), axis=2), axis=1)
    approx = identity[None, :, :] / bounds[:, None, None]
    for iteration in range(NS_STEPS):
        left_part = jnp.einsum("nab,nbc->nac", approx, damped, precision=exact_mode)
        approx = 2.0 * approx - jnp.einsum("nab,nbc->nac", left_part, approx, precision=exact_mode)
    return approx


def swap(value, axis, flip):
    size = lax.axis_size(axis)
    return lax.ppermute(value, axis, [(i, i ^ flip) for i in range(size)])


def exchange_sum(value, axis):
    parts = [swap(value, axis, flip) for flip in range(1, lax.axis_size(axis))]
    for part in parts:
        value = value + part
    return value


def body(activations, grads_out, grad_parts, old_factors, block_owner, weights, momentum):
    shard_count = lax.axis_size("shards")
    block_count = old_factors.shape[0]
    block_size = old_factors.shape[1]
    capacity = (block_count + shard_count - 1) // shard_count + 1
    sample_count = (
        activations.shape[0] * shard_count * lax.axis_size("tensor") * lax.axis_size("replica")
    )
    partial_grad = grad_parts[0]
    row_count, col_count = partial_grad.shape
    left_count = row_count // block_size
    right_count = col_count // block_size

    base = weights - (step_rate * momentum_rate) * momentum
    base = lax.all_gather(base, "replica", axis=0, tiled=True)
    base = lax.all_gather(base, "shards", axis=0, tiled=True)

    stats = jnp.concatenate(
        [sample_stats(activations, block_size), sample_stats(grads_out, block_size)], axis=0
    )
    piece_rows = row_count // shard_count
    grad_pieces = [
        partial_grad[:, n * block_size : (n + 1) * block_size].reshape(
            shard_count, piece_rows, block_size
        )
        for n in range(right_count)
    ]
    outgoing = jnp.concatenate([stats] + grad_pieces, axis=1)
    incoming = lax.all_to_all(outgoing, "shards", 0, 0)
    summed = exchange_sum(jnp.sum(incoming, axis=0), "replica")
    own_stats = summed[:block_size]
    own_stats = own_stats + swap(own_stats, "tensor", 1)
    own_stats = own_stats + swap(own_stats, "tensor", 2)
    own = jnp.concatenate([own_stats, summed[block_size:]], axis=0)
    own, base = lax.optimization_barrier((own, base))
    gathered = lax.all_to_all(
        jnp.broadcast_to(own[None], (shard_count,) + own.shape), "shards", 0, 0
    )
    blended = decay_rate * old_factors + (1.0 - decay_rate) * (
        gathered[:, :block_size] / sample_count
    )
    grad_columns = [
        gathered[
            :, block_size + n * piece_rows : block_size + (n + 1) * piece_rows
        ].reshape(left_count, block_size, block_size)
        for n in range(right_count)
    ]

    positions = jnp.arange(block_count, dtype=jnp.int32)
    earlier = (block_owner[:, None] == block_owner[None, :]) & (
        positions[None, :] < positions[:, None]
    )
    slots = block_owner * capacity + jnp.sum(earlier.astype(jnp.int32), axis=1)
    owned = []
    for place in range(capacity):
        match = slots == lax.axis_index("shards") * capacity + place
        which = jnp.sum(jnp.where(match, positions, 0))
        block = lax.dynamic_index_in_dim(blended, which, 0, keepdims=False)
        owned.append(jnp.where(jnp.any(match), block, 0.0))
    owned_blocks = jnp.stack(owned)

    right_first = left_count + lax.axis_index("tensor") * right_count
    needed = jnp.concatenate(
        [
            blended[:left_count],
            lax.dynamic_slice_in_dim(blended, right_first, right_count, 0),
        ],
        axis=0,
    )
    inverses = newton_inverse(needed)
    precond_columns = []
    for n in range(right_count):
        left_part = jnp.einsum(
            "nab,nbc->nac", inverses[:left_count], grad_columns[n], precision=exact_mode
        )
        precond_columns.append(
            jnp.einsum("nab,bc->nac", left_part, inverses[left_count + n], precision=exact_mode)
        )
    local_sum = sum(jnp.sum(p * g) for p, g in zip(precond_columns, grad_columns))
    precond = jnp.concatenate(
        [p.reshape(row_count, block_size) for p in precond_columns], axis=1
    )
    alignment_sum = lax.psum(local_sum, "tensor")
    clip_scale = jnp.minimum(1.0, clip_norm / jnp.sqrt(alignment_sum))
    own_rows = weights.shape[0]
    first_row = lax.axis_index(("shards", "replica")) * own_rows
    own_precond = lax.dynamic_slice_in_dim(precond, first_row, own_rows, 0)
    momentum_next = momentum_rate * momentum + clip_scale * own_precond
    weights_next = base - (step_rate * clip_scale) * precond
    return (weights_next, momentum_next, owned_blocks)


def solution(mesh):
    placed = (
        P(("shards", "tensor", "replica"), None),
        P(("shards", "tensor", "replica"), None),
        P(("shards", "replica"), None, "tensor"),
        P(),
        P(),
        P(("shards", "replica"), "tensor"),
        P(("shards", "replica"), "tensor"),
    )
    return jax.shard_map(
        body,
        mesh=mesh,
        in_specs=placed,
        out_specs=(P(None, "tensor"), P(("shards", "replica"), "tensor"), P("shards", None, None)),
        check_vma=False,
    )
```

time: 1460 us -> 161 us (0.11)
  the two profiles are of different devices: /device:TPU:94 before, /device:TPU:1 now
where the time goes in v1:
time: 161 us
  waiting for transfers between devices  56.6 us (35%)
  blocking collectives  27.7 us (17%)
  starting transfers between devices  26 us (16%)
  between operations  20.3 us (13%)
  other arithmetic  13.5 us (8%)
  matrix products  11.2 us (7%)
  local copies, waits for them, and re-layouts  5.53 us (3%)
    all_to_all x1, waiting for transfers between devices, body(): lax.all_to_all(jnp.broadcast_to(own[None], (shard_count,) + own.shape), '...  20.6 us
    all_to_all x1, waiting for transfers between devices, body(): incoming = lax.all_to_all(outgoing, 'shards', 0, 0)  14.8 us
    psum x1, blocking collectives, body(): alignment_sum = lax.psum(local_sum, 'tensor')  14.8 us
    ppermute x5, starting transfers between devices, swap(): return lax.ppermute(value, axis, [(i, i ^ flip) for i in range(size)])  13 us
    all_gather x1, blocking collectives, body(): base = lax.all_gather(base, 'replica', axis=0, tiled=True)  13 us
    ppermute x5, waiting for transfers between devices, swap(): return lax.ppermute(value, axis, [(i, i ^ flip) for i in range(size)])  12.1 us
    all_gather x1, waiting for transfers between devices, body(): base = lax.all_gather(base, 'shards', axis=0, tiled=True)  8.98 us
    all_to_all x1, starting transfers between devices, body(): incoming = lax.all_to_all(outgoing, 'shards', 0, 0)  7.77 us
  transfers between devices with their start and end apart: 8, of which 7 were waited for; matrix products, arithmetic and copies ran while one was open for 2% of the time, Pallas kernels for 0%

profile of v1, /device:TPU:1, one launch (start us, length us, event | category | flops | bytes accessed | tf_op | source)
XLA Modules:
  0.0 160.8 jit_solution(14424945549130774064)
XLA Ops:
  7.2 1.6 copy-done
  8.8 1.1 fusion.3
  9.8 1.1 fusion
  11.0 0.1 copy-done.3
  11.1 1.5 pad_maximum_fusion
  12.6 7.8 %all-to-all-start = ((f32[16,256,128]{2,1,0:T(8,128)}), f32[16,256,128]{2,1,0:T(8,128)}, u32[]{:S(2)}, u32[]{:S(2)}) async-start(f32[16,256,128]{2,1,0:T(8,128)} %pad_maximum_fusion), calls=%async_computation | async-start | bytes 4194304 | tf_op jit(solution)/shard_map/all_to_all | solution.py:79
  20.5 13.0 %all_gather.6 = f32[64,256]{1,0:T(8,128)} all-gather(f32[16,256]{1,0:T(8,128)S(1)} %multiply_subtract_fusion), channel_id=1, replica_groups=mesh['shards'=16,'tensor'=4,'replica'=4] {'replica'}, dimensions={0}, use_global_device_ids=true | all-gather | bytes 81920 | tf_op jit(solution)/shard_map/all_gather | solution.py:65
  33.4 14.8 %all-to-all-done = f32[16,256,128]{2,1,0:T(8,128)} async-done(((f32[16,256,128]{2,1,0:T(8,128)}), f32[16,256,128]{2,1,0:T(8,128)}, u32[]{:S(2)}, u32[]{:S(2)}) %all-to-all-start) | async-done | bytes 2097184 | tf_op jit(solution)/shard_map/all_to_all | solution.py:79
  48.3 1.7 %reduce_sum.73 = f32[256,128]{1,0:T(8,128)S(1)} reduce(f32[16,256,128]{2,1,0:T(8,128)} %all-to-all-done, f32[]{:T(128)} %constant.25.clone.1), dimensions={0}, to_apply=%region_0.0 | reduce | flops 491520 | bytes 2228228 | tf_op jit(solution)/shard_map/reduce_sum | solution.py:80
  50.0 4.5 %collective-permute-start.2 = (f32[256,128]{1,0:T(8,128)S(1)}, f32[256,128]{1,0:T(8,128)S(1)}, u32[]{:S(2)}, u32[]{:S(2)}) collective-permute-start(f32[256,128]{1,0:T(8,128)S(1)} %reduce_sum.73), channel_id=1, source_target_pairs={{0,3},{1,2},{2,1},{3,0},{4,7},{5,6},{6,5},{7,4},{8,11},{9,10},{10,... | collective-permute-start | bytes 393224 | tf_op jit(solution)/shard_map/ppermute | solution.py:41
  54.5 0.4 collective-permute-start
  54.8 2.0 %collective-permute-done.2 = f32[256,128]{1,0:T(8,128)S(1)} collective-permute-done((f32[256,128]{1,0:T(8,128)S(1)}, f32[256,128]{1,0:T(8,128)S(1)}, u32[]{:S(2)}, u32[]{:S(2)}) %collective-permute-start.2) | collective-permute-done | bytes 131104 | tf_op jit(solution)/shard_map/ppermute | solution.py:41
  56.9 7.0 %collective-permute-done.1 = f32[256,128]{1,0:T(8,128)S(1)} collective-permute-done((f32[256,128]{1,0:T(8,128)S(1)}, f32[256,128]{1,0:T(8,128)S(1)}, u32[]{:S(2)}, u32[]{:S(2)}) %collective-permute-start.1) | collective-permute-done | bytes 131104 | tf_op jit(solution)/shard_map/ppermute | solution.py:41
  64.0 2.2 %collective-permute-start.3 = (f32[128,128]{1,0:T(8,128)S(1)}, f32[128,128]{1,0:T(8,128)S(1)}, u32[]{:S(2)}, u32[]{:S(2)}) collective-permute-start(f32[128,128]{1,0:T(8,128)S(1)} %slice.47), channel_id=1, source_target_pairs={{0,4},{4,0},{8,12},{12,8},{1,5},{5,1},{9,13},{13,9},{2,6},{6,2},{1... | collective-permute-start | bytes 196616 | tf_op jit(solution)/shard_map/ppermute | solution.py:41
  66.1 0.9 collective-permute-done.3
  67.1 5.9 %collective-permute-start.4 = (f32[128,128]{1,0:T(8,128)S(1)}, f32[128,128]{1,0:T(8,128)S(1)}, u32[]{:S(2)}, u32[]{:S(2)}) collective-permute-start(f32[128,128]{1,0:T(8,128)S(1)} %get-tuple-element.18), channel_id=1, source_target_pairs={{0,8},{4,12},{8,0},{12,4},{1,9},{5,13},{9,1},{13,5},{2,10},{6,14},... | collective-permute-start | bytes 196616 | tf_op jit(solution)/shard_map/ppermute | solution.py:41
  73.0 2.2 %collective-permute-done.4 = f32[128,128]{1,0:T(8,128)S(1)} collective-permute-done((f32[128,128]{1,0:T(8,128)S(1)}, f32[128,128]{1,0:T(8,128)S(1)}, u32[]{:S(2)}, u32[]{:S(2)}) %collective-permute-start.4) | collective-permute-done | bytes 65568 | tf_op jit(solution)/shard_map/ppermute | solution.py:41
  75.2 9.0 %all-gather.2.cloned.1.call-done = f32[1024,256]{1,0:T(8,128)} async-done(((f32[64,256]{1,0:T(8,128)}), f32[1024,256]{1,0:T(8,128)}) %all-gather.2.cloned.1.call-update) | async-done | bytes 1048592 | tf_op jit(solution)/shard_map/all_gather | solution.py:66
  84.2 1.5 broadcast_in_dim.33
  85.7 5.2 %all-to-all-start.1 = ((f32[16,256,128]{2,1,0:T(8,128)}), f32[16,256,128]{2,1,0:T(8,128)}, u32[]{:S(2)}, u32[]{:S(2)}) async-start(f32[16,256,128]{2,1,0:T(8,128)} %broadcast_in_dim.33), calls=%async_computation.1 | async-start | bytes 4194304 | tf_op jit(solution)/shard_map/all_to_all | solution.py:86
  90.9 0.2 convert_reduce_fusion
  91.0 0.7 compare_reduce_fusion.1
  91.8 0.7 fusion.21
  95.8 20.6 %all-to-all-done.1 = f32[16,256,128]{2,1,0:T(8,128)} async-done(((f32[16,256,128]{2,1,0:T(8,128)}), f32[16,256,128]{2,1,0:T(8,128)}, u32[]{:S(2)}, u32[]{:S(2)}) %all-to-all-start.1) | async-done | bytes 2097184 | tf_op jit(solution)/shard_map/all_to_all | solution.py:86
  116.5 1.4 fusion.8
  117.9 0.9 copy-done.1
  118.8 0.2 select_reduce_fusion
  119.0 0.3 abs_reduce_fusion
  119.3 0.1 reduce_max.9
  119.4 0.9 fusion.9
  120.3 0.8 convolution_subtract_fusion.3
  121.2 0.8 fusion.25
  122.0 0.8 convolution_subtract_fusion.2
  122.8 0.8 fusion.24
  123.6 0.8 convolution_subtract_fusion.1
  124.4 0.8 fusion.23
  125.3 0.8 convolution_subtract_fusion
  126.1 1.3 fusion.26
  127.4 0.6 fusion.28
  128.0 0.6 fusion.17
  128.6 0.6 fusion.29
  129.3 0.6 fusion.16
  129.9 0.8 multiply_reduce_fusion
  132.7 14.8 %psum.7 = f32[]{:T(128)} all-reduce(f32[]{:T(128)S(6)} %add.69), channel_id=1, replica_groups=mesh['shards'=16,'tensor'=4,'replica'=4] {'tensor'}, use_global_device_ids=true, to_apply=%region_6.7 | all-reduce | flops 1 | bytes 8 | tf_op jit(solution)/shard_map/psum | solution.py:133
  148.1 2.2 %dynamic-slice_select_fusion.1 = (f32[1,128,128]{2,1,0:T(8,128)S(1)}, f32[1,128,128]{2,1,0:T(8,128)S(1)}) fusion(f32[16,128,128]{2,1,0:T(8,128)} %copy-done.1, s32[]{:T(128)S(6)} %select_n.46, pred[]{:T(512)} %get-tuple-element.7, s32[]{:T(128)S(6)} %select_n.50, pred[]{:T(512)} %get-tuple-element.8), kind=kLoop, calls=%fused_computation.39 | loop fusion | flops 32768 | bytes 262154 | tf_op jit(solution)/shard_map/jit(_where)/select_n | solution.py:109
  150.3 0.7 pad_maximum_fusion.4
  151.0 0.6 multiply_add_fusion.1
  151.6 2.3 %fusion.7 = f32[1024,256]{1,0:T(8,128)} fusion(f32[1024,256]{1,0:T(8,128)} %all-gather.2.cloned.1.call-done, f32[1024,128]{1,0:T(8,128)S(1)} %bitcast.51, f32[1024,128]{1,0:T(8,128)S(1)} %bitcast.49, f32[]{:T(128)S(6)} %mul_shard_map.3), kind=kLoop, calls=%fused_computation.15 | loop fusion | flops 786432 | bytes 3145732 | tf_op jit(solution)/shard_map/sub | solution.py:139
  (29 shorter events, 0.3 us)
Async XLA Ops:
  7.2 1.6 copy-start
  7.2 2.6 %copy-start.7 = (bf16[1024,1024]{1,0:T(8,128)(2,1)S(1)}, bf16[1024,1024]{1,0:T(8,128)(2,1)}, u32[]{:S(2)}) copy-start(bf16[1024,1024]{1,0:T(8,128)(2,1)} %param.8) | copy-start | bytes 6291460
  9.8 1.2 copy-start.3
  12.6 7.8 %copy-start.4 = (f32[16,256]{1,0:T(8,128)S(1)}, f32[16,256]{1,0:T(8,128)}, u32[]{:S(2)}) copy-start(f32[16,256]{1,0:T(8,128)} %param.13) | copy-start | bytes 49156
  12.6 7.8 %copy-start.5 = (f32[16,256]{1,0:T(8,128)S(1)}, f32[16,256]{1,0:T(8,128)}, u32[]{:S(2)}) copy-start(f32[16,256]{1,0:T(8,128)} %param.12) | copy-start | bytes 49156
  12.6 35.7 %all-to-all-start = ((f32[16,256,128]{2,1,0:T(8,128)}), f32[16,256,128]{2,1,0:T(8,128)}, u32[]{:S(2)}, u32[]{:S(2)}) async-start(f32[16,256,128]{2,1,0:T(8,128)} %pad_maximum_fusion), calls=%async_computation | async-start | bytes 4194304 | tf_op jit(solution)/shard_map/all_to_all | solution.py:79
  20.4 63.8 %all-gather.2.cloned.1.call-start = ((), (), s32[]{:S(2)}) async-start(), calls=%async_computation.2 | async-start | bytes 1114112 | tf_op jit(solution)/shard_map/all_gather | solution.py:66
  50.0 6.9 %collective-permute-start.2 = (f32[256,128]{1,0:T(8,128)S(1)}, f32[256,128]{1,0:T(8,128)S(1)}, u32[]{:S(2)}, u32[]{:S(2)}) collective-permute-start(f32[256,128]{1,0:T(8,128)S(1)} %reduce_sum.73), channel_id=1, source_target_pairs={{0,3},{1,2},{2,1},{3,0},{4,7},{5,6},{6,5},{7,4},{8,11},{9,10},{10,... | collective-permute-start | bytes 393224 | tf_op jit(solution)/shard_map/ppermute | solution.py:41
  54.5 9.4 %collective-permute-start.1 = (f32[256,128]{1,0:T(8,128)S(1)}, f32[256,128]{1,0:T(8,128)S(1)}, u32[]{:S(2)}, u32[]{:S(2)}) collective-permute-start(f32[256,128]{1,0:T(8,128)S(1)} %reduce_sum.73), channel_id=1, source_target_pairs={{0,2},{1,3},{2,0},{3,1},{4,6},{5,7},{6,4},{7,5},{8,10},{9,11},{10,... | collective-permute-start | bytes 393224 | tf_op jit(solution)/shard_map/ppermute | solution.py:41
  54.5 9.4 %collective-permute-start = (f32[256,128]{1,0:T(8,128)S(1)}, f32[256,128]{1,0:T(8,128)S(1)}, u32[]{:S(2)}, u32[]{:S(2)}) collective-permute-start(f32[256,128]{1,0:T(8,128)S(1)} %reduce_sum.73), channel_id=1, source_target_pairs={{0,1},{1,0},{2,3},{3,2},{4,5},{5,4},{6,7},{7,6},{8,9},{9,8},{10,11... | collective-permute-start | bytes 393224 | tf_op jit(solution)/shard_map/ppermute | solution.py:41
  64.0 3.1 %collective-permute-start.3 = (f32[128,128]{1,0:T(8,128)S(1)}, f32[128,128]{1,0:T(8,128)S(1)}, u32[]{:S(2)}, u32[]{:S(2)}) collective-permute-start(f32[128,128]{1,0:T(8,128)S(1)} %slice.47), channel_id=1, source_target_pairs={{0,4},{4,0},{8,12},{12,8},{1,5},{5,1},{9,13},{13,9},{2,6},{6,2},{1... | collective-permute-start | bytes 196616 | tf_op jit(solution)/shard_map/ppermute | solution.py:41
  67.1 8.1 %collective-permute-start.4 = (f32[128,128]{1,0:T(8,128)S(1)}, f32[128,128]{1,0:T(8,128)S(1)}, u32[]{:S(2)}, u32[]{:S(2)}) collective-permute-start(f32[128,128]{1,0:T(8,128)S(1)} %get-tuple-element.18), channel_id=1, source_target_pairs={{0,8},{4,12},{8,0},{12,4},{1,9},{5,13},{9,1},{13,5},{2,10},{6,14},... | collective-permute-start | bytes 196616 | tf_op jit(solution)/shard_map/ppermute | solution.py:41
  85.7 5.2 %copy-start.6 = (s32[16]{0:T(128)S(1)}, s32[16]{0:T(128)}, u32[]{:S(2)}) copy-start(s32[16]{0:T(128)} %param.11) | copy-start | bytes 196
  85.7 30.8 %copy-start.2 = (f32[16,128,128]{2,1,0:T(8,128)S(1)}, f32[16,128,128]{2,1,0:T(8,128)}, u32[]{:S(2)}) copy-start(f32[16,128,128]{2,1,0:T(8,128)} %param.10) | copy-start | bytes 3145732
  85.7 30.8 %all-to-all-start.1 = ((f32[16,256,128]{2,1,0:T(8,128)}), f32[16,256,128]{2,1,0:T(8,128)}, u32[]{:S(2)}, u32[]{:S(2)}) async-start(f32[16,256,128]{2,1,0:T(8,128)} %broadcast_in_dim.33), calls=%async_computation.1 | async-start | bytes 4194304 | tf_op jit(solution)/shard_map/all_to_all | solution.py:86
  117.8 1.0 copy-start.1
Sparse Core Ops, SparseCore 0:
  33.6 50.5 all-gather.1

commit v2 on v1

v2 whole, which is shorter than its diff:
```python
import jax
import jax.numpy as jnp
from jax import lax
from jax.experimental import pallas as pl
from jax.experimental.pallas import tpu as pltpu
from jax.sharding import PartitionSpec as P

NS_STEPS = 4


exact_mode = lax.Precision.HIGHEST
decay_rate = 0.75
damping = 0.1
damp_shift = 0.001
clip_norm = 256.0
momentum_rate = 0.9
step_rate = 0.05


def sample_stats(samples, block_size):
    sample_rows, width = samples.shape
    blocks = samples.reshape(sample_rows, width // block_size, block_size)
    return jnp.einsum("tnb,tnc->nbc", blocks, blocks, preferred_element_type=jnp.float32)


def pack_kernel(left_ref, right_ref, grad_ref, packed_ref):
    left_count, size, _ = left_ref.shape
    half = size // 2
    chunks = packed_ref.shape[0]
    piece_rows = grad_ref.shape[0] // chunks
    row = lax.broadcasted_iota(jnp.int32, (half, size), 0)
    col = lax.broadcasted_iota(jnp.int32, (half, size), 1)
    for n in range(chunks):
        stats_ref, at = (left_ref, n) if n < left_count else (right_ref, n - left_count)
        top = stats_ref[at, :half, :]
        bottom = stats_ref[at, half:, :]
        packed_ref[n, :half, :] = jnp.where(col >= row, top, pltpu.roll(bottom, half, 1))
        diagonal = jnp.sum(jnp.where(col == row + half, bottom, 0.0), axis=0, keepdims=True)
        packed_ref[n, half : half + 8, :] = jnp.broadcast_to(diagonal, (8, size))
        for c in range(grad_ref.shape[1] // size):
            first = half + 8 + c * piece_rows
            packed_ref[n, first : first + piece_rows, :] = grad_ref[
                n * piece_rows : (n + 1) * piece_rows, c * size : (c + 1) * size
            ]


def pack(left_stats, right_stats, grad):
    left_count, size, _ = left_stats.shape
    chunks = left_count + right_stats.shape[0]
    rows = size // 2 + 8 + grad.size // (chunks * size)
    return pl.pallas_call(
        pack_kernel,
        out_shape=jax.ShapeDtypeStruct((chunks, rows, size), jnp.float32),
        name="pack",
    )(left_stats, right_stats, grad)


def dot(a, b):
    return jnp.dot(a, b, precision=exact_mode, preferred_element_type=jnp.float32)


def damp(mixed, on_diagonal):
    size = mixed.shape[0]
    trace = jnp.sum(jnp.where(on_diagonal, mixed, 0.0), keepdims=True)
    damped = mixed + jnp.where(on_diagonal, damping * trace / size + damp_shift, 0.0)
    bound = jnp.max(jnp.sum(jnp.abs(damped), axis=1, keepdims=True), keepdims=True)
    return jnp.where(on_diagonal, 1.0, 0.0) - damped / bound, bound


def update_kernel(
    sample_count,
    place_ref,
    packed_ref,
    old_ref,
    precond_ref,
    owned_ref,
    align_ref,
    blended_ref,
):
    blocks, size, _ = old_ref.shape
    half = size // 2
    right_count = precond_ref.shape[1] // size
    left_count = precond_ref.shape[0] // size
    piece_rows = precond_ref.shape[0] // blocks
    row = lax.broadcasted_iota(jnp.int32, (half, size), 0)
    col = lax.broadcasted_iota(jnp.int32, (half, size), 1)
    for n in range(blocks):
        part = packed_ref[n, :half, :]
        diagonal = packed_ref[n, half : half + 1, :]
        turned = jnp.concatenate([part, jnp.zeros_like(part)], axis=0).T
        top = jnp.where(col >= row, part, turned[:half])
        corner = jnp.where(
            col < row + half, pltpu.roll(part, half, 1), pltpu.roll(turned[:half], half, 1)
        )
        corner = jnp.where(col == row + half, diagonal, corner)
        bottom = jnp.where(col < half, turned[half:], corner)
        for first, stats in ((0, top), (half, bottom)):
            blended_ref[n, first : first + half, :] = decay_rate * old_ref[
                n, first : first + half, :
            ] + (1.0 - decay_rate) * (stats / sample_count)

    for place in range(owned_ref.shape[0]):
        block = place_ref[1 + place]
        used = block >= 0
        value = blended_ref[jnp.maximum(block, 0)]
        owned_ref[place] = jnp.where(used, value, jnp.zeros_like(value))

    on_diagonal = lax.broadcasted_iota(jnp.int32, (size, size), 0) == lax.broadcasted_iota(
        jnp.int32, (size, size), 1
    )
    needed = [blended_ref[n] for n in range(left_count)]
    needed += [blended_ref[place_ref[0] + n] for n in range(right_count)]
    powers, bounds, inverses = [], [], []
    for mixed in needed:
        power, bound = damp(mixed, on_diagonal)
        powers.append(power)
        bounds.append(bound)
        inverses.append(jnp.where(on_diagonal, 1.0, 0.0) + power)
    for step in range(NS_STEPS - 1):
        powers = [dot(power, power) for power in powers]
        inverses = [x + dot(x, power) for x, power in zip(inverses, powers)]
    inverses = [x / bound for x, bound in zip(inverses, bounds)]

    total = jnp.zeros((size, size), jnp.float32)
    for a in range(left_count):
        for c in range(right_count):
            first = half + 8 + c * piece_rows
            pieces = size // piece_rows
            grad = jnp.concatenate(
                [
                    packed_ref[pieces * a + k, first : first + piece_rows, :]
                    for k in range(pieces)
                ],
                axis=0,
            )
            value = dot(dot(inverses[a], grad), inverses[left_count + c])
            precond_ref[a * size : (a + 1) * size, c * size : (c + 1) * size] = value
            total = total + value * grad
    align_ref[...] = jnp.broadcast_to(jnp.sum(total, keepdims=True), align_ref.shape)


def update(places, packed, old_factors, capacity, rows, cols, sample_count):
    size = old_factors.shape[1]
    return pl.pallas_call(
        lambda *refs: update_kernel(sample_count, *refs),
        in_specs=[
            pl.BlockSpec(memory_space=pltpu.SMEM),
            pl.BlockSpec(memory_space=pltpu.VMEM),
            pl.BlockSpec(memory_space=pltpu.VMEM),
        ],
        out_shape=(
            jax.ShapeDtypeStruct((rows, cols), jnp.float32),
            jax.ShapeDtypeStruct((capacity, size, size), jnp.float32),
            jax.ShapeDtypeStruct((8, 128), jnp.float32),
        ),
        scratch_shapes=[pltpu.VMEM(old_factors.shape, jnp.float32)],
        compiler_params=pltpu.CompilerParams(vmem_limit_bytes=40 * 1024 * 1024),
        name="update",
    )(places, packed, old_factors)


def swap(value, axis, flip):
    size = lax.axis_size(axis)
    return lax.ppermute(value, axis, [(i, i ^ flip) for i in range(size)])


def exchange(value, axis):
    return [value] + [swap(value, axis, flip) for flip in range(1, lax.axis_size(axis))]


def spread(value, axis):
    copies = jnp.broadcast_to(value[None], (lax.axis_size(axis),) + value.shape)
    return lax.all_to_all(copies, axis, 0, 0)


def body(activations, grads_out, grad_parts, old_factors, block_owner, weights, momentum):
    shard_count = lax.axis_size("shards")
    replica_count = lax.axis_size("replica")
    block_count = old_factors.shape[0]
    block_size = old_factors.shape[1]
    capacity = (block_count + shard_count - 1) // shard_count + 1
    sample_count = activations.shape[0] * shard_count * lax.axis_size("tensor") * replica_count
    partial_grad = grad_parts[0]
    row_count, col_count = partial_grad.shape
    left_count = row_count // block_size
    right_count = col_count // block_size
    piece_rows = row_count // shard_count

    outgoing = pack(
        sample_stats(activations, block_size), sample_stats(grads_out, block_size), partial_grad
    )
    incoming = lax.all_to_all(outgoing, "shards", 0, 0)

    base = weights - (step_rate * momentum_rate) * momentum
    base_parts = exchange(base, "replica")
    replica = lax.axis_index("replica")
    base_rows = []
    for place in range(replica_count):
        rows = base_parts[0]
        for flip in range(1, replica_count):
            rows = jnp.where(replica ^ flip == place, base_parts[flip], rows)
        base_rows.append(rows)
    base = lax.all_gather(jnp.concatenate(base_rows, axis=0), "shards", axis=0, tiled=True)

    own = sum(exchange(jnp.sum(incoming, axis=0), "replica"))
    fold_rows = block_size // 2 + 8
    own_stats = own[:fold_rows]
    own_stats = own_stats + swap(own_stats, "tensor", 1)
    own_stats = own_stats + swap(own_stats, "tensor", 2)
    packed = spread(jnp.concatenate([own_stats, own[fold_rows:]], axis=0), "shards")

    positions = jnp.arange(block_count, dtype=jnp.int32)
    earlier = (block_owner[:, None] == block_owner[None, :]) & (
        positions[None, :] < positions[:, None]
    )
    slots = block_owner * capacity + jnp.sum(earlier.astype(jnp.int32), axis=1)
    own_slots = lax.axis_index("shards") * capacity + jnp.arange(capacity, dtype=jnp.int32)
    holds = jnp.max(jnp.where(slots[None, :] == own_slots[:, None], positions[None, :], -1), axis=1)
    right_first = left_count + lax.axis_index("tensor") * right_count
    places = jnp.concatenate([right_first.reshape(1).astype(jnp.int32), holds])

    precond, owned_blocks, align = update(
        places, packed, old_factors, capacity, row_count, col_count, sample_count
    )
    align, base = lax.optimization_barrier((align, base))
    align = align[:1]
    align = align + swap(align, "tensor", 1)
    align = align + swap(align, "tensor", 2)
    clip_scale = jnp.minimum(1.0, clip_norm / jnp.sqrt(align[0, 0]))
    own_rows = weights.shape[0]
    first_row = lax.axis_index(("shards", "replica")) * own_rows
    own_precond = lax.dynamic_slice_in_dim(precond, first_row, own_rows, 0)
    momentum_next = momentum_rate * momentum + clip_scale * own_precond
    weights_next = base - (step_rate * clip_scale) * precond
    return (weights_next, momentum_next, owned_blocks)


def solution(mesh):
    placed = (
        P(("shards", "tensor", "replica"), None),
        P(("shards", "tensor", "replica"), None),
        P(("shards", "replica"), None, "tensor"),
        P(),
        P(),
        P(("shards", "replica"), "tensor"),
        P(("shards", "replica"), "tensor"),
    )
    return jax.shard_map(
        body,
        mesh=mesh,
        in_specs=placed,
        out_specs=(P(None, "tensor"), P(("shards", "replica"), "tensor"), P("shards", None, None)),
        check_vma=False,
    )
```

time: 161 us -> 129 us (0.80)
  blocking collectives: 27.7 us -> 0 us
  starting transfers between devices: 26 us -> 40.6 us
  Pallas kernels: 0 us -> 11.2 us
  other arithmetic: 13.5 us -> 5.64 us
  waiting for transfers between devices: 56.6 us -> 48.8 us
  matrix products: 11.2 us -> 3.8 us
  between operations: 20.3 us -> 14.2 us
    ppermute x5 -> x10, starting transfers between devices: 13 us -> 27.8 us  [swap(): return lax.ppermute(value, axis, [(i, i ^ flip) for i in range(size)])]
    psum x1 -> x0, blocking collectives: 14.8 us -> none  [body(): alignment_sum = lax.psum(local_sum, 'tensor')]
    all_gather x1 -> x0, blocking collectives: 13 us -> none  [body(): base = lax.all_gather(base, 'replica', axis=0, tiled=True)]
    pallas_call x0 -> x2, Pallas kernels: none -> 11.2 us  [the longest x1 8.23 us: update(): pl.pallas_call(lambda *refs: update_kernel(sample_count, *refs), in_specs...]
    dot_general x12 -> x0, matrix products: 9 us -> none  [the longest x4 3.38 us: newton_inverse(): left_part = jnp.einsum('nab,nbc->nac', approx, damped, precision=exact_mode)]
    all_gather x1, waiting for transfers between devices: 8.98 us -> 3.23 us  [body(): lax.all_gather(jnp.concatenate(base_rows, axis=0), 'shards', axis=0, tile...]
    reduce_sum x5 -> x1, other arithmetic: 3.74 us -> 1.52 us  [body(): own = sum(exchange(jnp.sum(incoming, axis=0), 'replica'))]
    select_n x1, other arithmetic: 2.19 us -> 0.01 us  [body(): rows = jnp.where(replica ^ flip == place, base_parts[flip], rows)]
  transfers between devices with their start and end apart: 8 -> 13, of which waited for: 7 -> 11; matrix products, arithmetic and copies ran while one was open for 2% -> 2% of each run, Pallas kernels for 0% -> 6%
where the time goes in v2:
time: 129 us; the launch traced here: 128 us
  waiting for transfers between devices  48.8 us (38%)
  starting transfers between devices  40.6 us (31%)
  between operations  14.2 us (11%)
  Pallas kernels  11.2 us (9%)
  other arithmetic  5.64 us (4%)
  local copies, waits for them, and re-layouts  4.11 us (3%)
  matrix products  3.8 us (3%)
    ppermute x10, starting transfers between devices, swap(): return lax.ppermute(value, axis, [(i, i ^ flip) for i in range(size)])  27.8 us
    all_to_all x1, waiting for transfers between devices, spread(): return lax.all_to_all(copies, axis, 0, 0)  21.1 us
    all_to_all x1, waiting for transfers between devices, body(): incoming = lax.all_to_all(outgoing, 'shards', 0, 0)  13 us
    ppermute x10, waiting for transfers between devices, swap(): return lax.ppermute(value, axis, [(i, i ^ flip) for i in range(size)])  11.4 us
    pallas_call x1, Pallas kernels, update(): pl.pallas_call(lambda *refs: update_kernel(sample_count, *refs), in_specs...  8.23 us
    all_to_all x1, starting transfers between devices, body(): incoming = lax.all_to_all(outgoing, 'shards', 0, 0)  7.76 us
    all_to_all x1, starting transfers between devices, spread(): return lax.all_to_all(copies, axis, 0, 0)  5 us
    dot_general x2, matrix products, sample_stats(): jnp.einsum('tnb,tnc->nbc', blocks, blocks, preferred_element_type=jnp.flo...  3.8 us
  transfers between devices with their start and end apart: 13, of which 11 were waited for; matrix products, arithmetic and copies ran while one was open for 2% of the time, Pallas kernels for 6%

profile of v2, /device:TPU:1, one launch (start us, length us, event | category | flops | bytes accessed | tf_op | source)
XLA Modules:
  0.0 128.4 jit_solution(1875959094298948247)
XLA Ops:
  7.2 0.0 copy-start
  7.2 0.0 copy-start.4
  7.2 1.6 %copy-done = bf16[1024,1024]{1,0:T(8,128)(2,1)S(1)} copy-done((bf16[1024,1024]{1,0:T(8,128)(2,1)S(1)}, bf16[1024,1024]{1,0:T(8,128)(2,1)}, u32[]{:S(2)}) %copy-start) | copy-done | bytes 2097176
  8.8 1.8 %fusion.3.left_ref = f32[8,128,128]{2,1,0:T(8,128)} fusion(bf16[1024,1024]{1,0:T(8,128)(2,1)S(1)} %copy-done), kind=kOutput, calls=%fused_computation.3 | convolution fusion | flops 268435456 | bytes 2621440 | tf_op jit(solution)/shard_map/tnb,tnc->nbc/dot_general | solution.py:23
  10.6 0.0 copy-done.4
  10.6 2.0 %fusion.right_ref = f32[8,128,128]{2,1,0:T(8,128)} fusion(bf16[1024,1024]{1,0:T(8,128)(2,1)S(1)} %copy-done.4), kind=kOutput, calls=%fused_computation | convolution fusion | flops 268435456 | bytes 2621440 | tf_op jit(solution)/shard_map/tnb,tnc->nbc/dot_general | solution.py:23
  12.6 3.0 %pack.1 = f32[16,200,128]{2,1,0:T(8,128)} custom-call(f32[8,128,128]{2,1,0:T(8,128)} %fusion.3.left_ref, f32[8,128,128]{2,1,0:T(8,128)} %fusion.right_ref, f32[1024,256]{1,0:T(8,128)} %bitcast.18), custom_call_target="tpu_custom_call" | custom-call | tf_op jit(solution)/shard_map/pack/pallas_call | solution.py:51
  15.5 7.8 %all-to-all-start = ((f32[16,200,128]{2,1,0:T(8,128)}), f32[16,200,128]{2,1,0:T(8,128)}, u32[]{:S(2)}, u32[]{:S(2)}) async-start(f32[16,200,128]{2,1,0:T(8,128)} %pack.1), calls=%async_computation | async-start | bytes 3276800 | tf_op jit(solution)/shard_map/all_to_all | solution.py:192
  23.3 0.0 all-gather.2.cloned.1.call-start
  23.3 0.0 copy-done.2
  23.4 0.0 copy-done.3
  23.4 4.4 %collective-permute-start.5 = (f32[16,256]{1,0:T(8,128)S(1)}, f32[16,256]{1,0:T(8,128)S(1)}, u32[]{:S(2)}, u32[]{:S(2)}) collective-permute-start(f32[16,256]{1,0:T(8,128)S(1)} %multiply_subtract_fusion.1), channel_id=1, source_target_pairs={{0,3},{1,2},{2,1},{3,0},{4,7},{5,6},{6,5},{7,4},{8,11},{9,10},{10,... | collective-permute-start | bytes 49160 | tf_op jit(solution)/shard_map/ppermute | solution.py:164
  27.8 0.0 collective-permute-start.6
  27.8 0.4 collective-permute-start.7
  28.2 1.1 collective-permute-done.5
  29.3 2.4 %collective-permute-done.6 = f32[16,256]{1,0:T(8,128)S(1)} collective-permute-done((f32[16,256]{1,0:T(8,128)S(1)}, f32[16,256]{1,0:T(8,128)S(1)}, u32[]{:S(2)}, u32[]{:S(2)}) %collective-permute-start.6) | collective-permute-done | bytes 16416 | tf_op jit(solution)/shard_map/ppermute | solution.py:164
  31.7 0.0 collective-permute-done.7
  31.7 13.0 %all-to-all-done = f32[16,200,128]{2,1,0:T(8,128)} async-done(((f32[16,200,128]{2,1,0:T(8,128)}), f32[16,200,128]{2,1,0:T(8,128)}, u32[]{:S(2)}, u32[]{:S(2)}) %all-to-all-start) | async-done | bytes 1638432 | tf_op jit(solution)/shard_map/all_to_all | solution.py:192
  44.7 1.5 %reduce_sum.19 = f32[200,128]{1,0:T(8,128)S(1)} reduce(f32[16,200,128]{2,1,0:T(8,128)} %all-to-all-done, f32[]{:T(128)} %constant.16.clone.1), dimensions={0}, to_apply=%region_2.3 | reduce | flops 384000 | bytes 1740804 | tf_op jit(solution)/shard_map/reduce_sum | solution.py:205
  46.2 4.4 %collective-permute-start.2 = (f32[200,128]{1,0:T(8,128)S(1)}, f32[200,128]{1,0:T(8,128)S(1)}, u32[]{:S(2)}, u32[]{:S(2)}) collective-permute-start(f32[200,128]{1,0:T(8,128)S(1)} %reduce_sum.19), channel_id=1, source_target_pairs={{0,3},{1,2},{2,1},{3,0},{4,7},{5,6},{6,5},{7,4},{8,11},{9,10},{10,... | collective-permute-start | bytes 307208 | tf_op jit(solution)/shard_map/ppermute | solution.py:164
  50.7 0.0 collective-permute-start.1
  50.7 0.4 collective-permute-start
  51.0 0.6 pad_maximum_fusion.1
  51.7 0.0 all-gather.2.cloned.1.call-update
  51.7 1.0 collective-permute-done.2
  52.7 2.8 %collective-permute-done.1 = f32[200,128]{1,0:T(8,128)S(1)} collective-permute-done((f32[200,128]{1,0:T(8,128)S(1)}, f32[200,128]{1,0:T(8,128)S(1)}, u32[]{:S(2)}, u32[]{:S(2)}) %collective-permute-start.1) | collective-permute-done | bytes 102432 | tf_op jit(solution)/shard_map/ppermute | solution.py:164
  55.5 0.0 collective-permute-done
  55.5 5.5 %collective-permute-start.3 = (f32[72,128]{1,0:T(8,128)S(1)}, f32[72,128]{1,0:T(8,128)S(1)}, u32[]{:S(2)}, u32[]{:S(2)}) collective-permute-start(f32[72,128]{1,0:T(8,128)S(1)} %slice.16), channel_id=1, source_target_pairs={{0,4},{4,0},{8,12},{12,8},{1,5},{5,1},{9,13},{13,9},{2,6},{6,2},{1... | collective-permute-start | bytes 110600 | tf_op jit(solution)/shard_map/ppermute | solution.py:164
  61.0 0.9 collective-permute-done.3
  61.9 5.2 %collective-permute-start.4 = (f32[72,128]{1,0:T(8,128)S(1)}, f32[72,128]{1,0:T(8,128)S(1)}, u32[]{:S(2)}, u32[]{:S(2)}) collective-permute-start(f32[72,128]{1,0:T(8,128)S(1)} %slice_add_fusion.1), channel_id=1, source_target_pairs={{0,8},{4,12},{8,0},{12,4},{1,9},{5,13},{9,1},{13,5},{2,10},{6,14},... | collective-permute-start | bytes 110600 | tf_op jit(solution)/shard_map/ppermute | solution.py:164
  67.0 1.5 %collective-permute-done.4 = f32[72,128]{1,0:T(8,128)S(1)} collective-permute-done((f32[72,128]{1,0:T(8,128)S(1)}, f32[72,128]{1,0:T(8,128)S(1)}, u32[]{:S(2)}, u32[]{:S(2)}) %collective-permute-start.4) | collective-permute-done | bytes 36896 | tf_op jit(solution)/shard_map/ppermute | solution.py:164
  68.6 0.0 copy-start.5
  68.6 1.3 broadcast_in_dim.12
  69.9 5.0 %all-to-all-start.1 = ((f32[16,200,128]{2,1,0:T(8,128)}), f32[16,200,128]{2,1,0:T(8,128)}, u32[]{:S(2)}, u32[]{:S(2)}) async-start(f32[16,200,128]{2,1,0:T(8,128)} %broadcast_in_dim.12), calls=%async_computation.1 | async-start | bytes 3276800 | tf_op jit(solution)/shard_map/all_to_all | solution.py:173
  74.9 0.0 copy-done.5
  74.9 0.2 convert_reduce_fusion
  75.1 0.2 fusion.7
  75.3 0.1 pad_add_fusion.refs_0_
  75.4 21.1 %all-to-all-done.1.refs_1_ = f32[16,200,128]{2,1,0:T(8,128)} async-done(((f32[16,200,128]{2,1,0:T(8,128)}), f32[16,200,128]{2,1,0:T(8,128)}, u32[]{:S(2)}, u32[]{:S(2)}) %all-to-all-start.1) | async-done | bytes 1638432 | tf_op jit(solution)/shard_map/all_to_all | solution.py:173
  96.5 1.2 copy-done.1
  97.7 8.2 %update.1 = (f32[1024,256]{1,0:T(8,128)S(1)}, f32[2,128,128]{2,1,0:T(8,128)}, f32[8,128]{1,0:T(8,128)S(1)}) custom-call(s32[3]{0:T(128)S(1)} %pad_add_fusion.refs_0_, f32[16,200,128]{2,1,0:T(8,128)} %all-to-all-done.1.refs_1_, f32[16,128,128]{2,1,0:T(8,128)S(1)} %copy-done.1), custom_call_target="tpu_custom_call" | custom-call | tf_op jit(solution)/shard_map/update/pallas_call | solution.py:144
  106.0 3.2 %all-gather.2.cloned.1.call-done = f32[1024,256]{1,0:T(8,128)} async-done(((f32[64,256]{1,0:T(8,128)}), f32[1024,256]{1,0:T(8,128)}) %all-gather.2.cloned.1.call-update) | async-done | bytes 1048592 | tf_op jit(solution)/shard_map/all_gather | solution.py:203
  109.2 2.1 %collective-permute-start.8 = (f32[1,128]{1,0:T(1,128)S(1)}, f32[1,128]{1,0:T(1,128)S(1)}, u32[]{:S(2)}, u32[]{:S(2)}) collective-permute-start(f32[1,128]{1,0:T(1,128)S(1)} %slice.14), channel_id=1, source_target_pairs={{0,4},{4,0},{8,12},{12,8},{1,5},{5,1},{9,13},{13,9},{2,6},{6,2},{1... | collective-permute-start | bytes 1544 | tf_op jit(solution)/shard_map/ppermute | solution.py:164
  111.3 0.8 collective-permute-done.8
  112.1 5.5 %collective-permute-start.9 = (f32[1,128]{1,0:T(1,128)S(1)}, f32[1,128]{1,0:T(1,128)S(1)}, u32[]{:S(2)}, u32[]{:S(2)}) collective-permute-start(f32[1,128]{1,0:T(1,128)S(1)} %slice_add_fusion), channel_id=1, source_target_pairs={{0,8},{4,12},{8,0},{12,4},{1,9},{5,13},{9,1},{13,5},{2,10},{6,14},... | collective-permute-start | bytes 1544 | tf_op jit(solution)/shard_map/ppermute | solution.py:164
  117.6 0.9 collective-permute-done.9
  118.6 0.6 multiply_add_fusion
  119.2 2.3 %multiply_subtract_fusion = f32[1024,256]{1,0:T(8,128)} fusion(f32[1024,256]{1,0:T(8,128)} %all-gather.2.cloned.1.call-done, f32[1024,256]{1,0:T(8,128)S(1)} %get-tuple-element.11, f32[]{:T(128)S(6)} %mul_shard_map.3), kind=kLoop, calls=%fused_computation.6 | loop fusion | flops 524288 | bytes 3145732 | tf_op jit(solution)/shard_map/sub | solution.py:234
  (16 shorter events, 0.1 us)
Async XLA Ops:
  7.2 1.6 %copy-start = (bf16[1024,1024]{1,0:T(8,128)(2,1)S(1)}, bf16[1024,1024]{1,0:T(8,128)(2,1)}, u32[]{:S(2)}) copy-start(bf16[1024,1024]{1,0:T(8,128)(2,1)} %param.7) | copy-start | bytes 6291460
  7.2 3.4 %copy-start.4 = (bf16[1024,1024]{1,0:T(8,128)(2,1)S(1)}, bf16[1024,1024]{1,0:T(8,128)(2,1)}, u32[]{:S(2)}) copy-start(bf16[1024,1024]{1,0:T(8,128)(2,1)} %param.8) | copy-start | bytes 6291460
  15.5 7.8 %copy-start.2 = (f32[16,256]{1,0:T(8,128)S(1)}, f32[16,256]{1,0:T(8,128)}, u32[]{:S(2)}) copy-start(f32[16,256]{1,0:T(8,128)} %param.13) | copy-start | bytes 49156
  15.5 7.8 %copy-start.3 = (f32[16,256]{1,0:T(8,128)S(1)}, f32[16,256]{1,0:T(8,128)}, u32[]{:S(2)}) copy-start(f32[16,256]{1,0:T(8,128)} %param.12) | copy-start | bytes 49156
  15.5 29.2 %all-to-all-start = ((f32[16,200,128]{2,1,0:T(8,128)}), f32[16,200,128]{2,1,0:T(8,128)}, u32[]{:S(2)}, u32[]{:S(2)}) async-start(f32[16,200,128]{2,1,0:T(8,128)} %pack.1), calls=%async_computation | async-start | bytes 3276800 | tf_op jit(solution)/shard_map/all_to_all | solution.py:192
  23.3 85.9 %all-gather.2.cloned.1.call-start = ((), (), s32[]{:S(2)}) async-start(), calls=%async_computation.2 | async-start | bytes 1114112 | tf_op jit(solution)/shard_map/all_gather | solution.py:203
  23.4 6.0 %collective-permute-start.5 = (f32[16,256]{1,0:T(8,128)S(1)}, f32[16,256]{1,0:T(8,128)S(1)}, u32[]{:S(2)}, u32[]{:S(2)}) collective-permute-start(f32[16,256]{1,0:T(8,128)S(1)} %multiply_subtract_fusion.1), channel_id=1, source_target_pairs={{0,3},{1,2},{2,1},{3,0},{4,7},{5,6},{6,5},{7,4},{8,11},{9,10},{10,... | collective-permute-start | bytes 49160 | tf_op jit(solution)/shard_map/ppermute | solution.py:164
  27.8 3.9 %collective-permute-start.6 = (f32[16,256]{1,0:T(8,128)S(1)}, f32[16,256]{1,0:T(8,128)S(1)}, u32[]{:S(2)}, u32[]{:S(2)}) collective-permute-start(f32[16,256]{1,0:T(8,128)S(1)} %multiply_subtract_fusion.1), channel_id=1, source_target_pairs={{0,2},{1,3},{2,0},{3,1},{4,6},{5,7},{6,4},{7,5},{8,10},{9,11},{10,... | collective-permute-start | bytes 49160 | tf_op jit(solution)/shard_map/ppermute | solution.py:164
  27.8 3.9 %collective-permute-start.7 = (f32[16,256]{1,0:T(8,128)S(1)}, f32[16,256]{1,0:T(8,128)S(1)}, u32[]{:S(2)}, u32[]{:S(2)}) collective-permute-start(f32[16,256]{1,0:T(8,128)S(1)} %multiply_subtract_fusion.1), channel_id=1, source_target_pairs={{0,1},{1,0},{2,3},{3,2},{4,5},{5,4},{6,7},{7,6},{8,9},{9,8},{10,11... | collective-permute-start | bytes 49160 | tf_op jit(solution)/shard_map/ppermute | solution.py:164
  46.2 6.5 %collective-permute-start.2 = (f32[200,128]{1,0:T(8,128)S(1)}, f32[200,128]{1,0:T(8,128)S(1)}, u32[]{:S(2)}, u32[]{:S(2)}) collective-permute-start(f32[200,128]{1,0:T(8,128)S(1)} %reduce_sum.19), channel_id=1, source_target_pairs={{0,3},{1,2},{2,1},{3,0},{4,7},{5,6},{6,5},{7,4},{8,11},{9,10},{10,... | collective-permute-start | bytes 307208 | tf_op jit(solution)/shard_map/ppermute | solution.py:164
  50.7 4.8 %collective-permute-start.1 = (f32[200,128]{1,0:T(8,128)S(1)}, f32[200,128]{1,0:T(8,128)S(1)}, u32[]{:S(2)}, u32[]{:S(2)}) collective-permute-start(f32[200,128]{1,0:T(8,128)S(1)} %reduce_sum.19), channel_id=1, source_target_pairs={{0,2},{1,3},{2,0},{3,1},{4,6},{5,7},{6,4},{7,5},{8,10},{9,11},{10,... | collective-permute-start | bytes 307208 | tf_op jit(solution)/shard_map/ppermute | solution.py:164
  50.7 4.8 %collective-permute-start = (f32[200,128]{1,0:T(8,128)S(1)}, f32[200,128]{1,0:T(8,128)S(1)}, u32[]{:S(2)}, u32[]{:S(2)}) collective-permute-start(f32[200,128]{1,0:T(8,128)S(1)} %reduce_sum.19), channel_id=1, source_target_pairs={{0,1},{1,0},{2,3},{3,2},{4,5},{5,4},{6,7},{7,6},{8,9},{9,8},{10,11... | collective-permute-start | bytes 307208 | tf_op jit(solution)/shard_map/ppermute | solution.py:164
  55.5 6.3 %collective-permute-start.3 = (f32[72,128]{1,0:T(8,128)S(1)}, f32[72,128]{1,0:T(8,128)S(1)}, u32[]{:S(2)}, u32[]{:S(2)}) collective-permute-start(f32[72,128]{1,0:T(8,128)S(1)} %slice.16), channel_id=1, source_target_pairs={{0,4},{4,0},{8,12},{12,8},{1,5},{5,1},{9,13},{13,9},{2,6},{6,2},{1... | collective-permute-start | bytes 110600 | tf_op jit(solution)/shard_map/ppermute | solution.py:164
  61.9 6.7 %collective-permute-start.4 = (f32[72,128]{1,0:T(8,128)S(1)}, f32[72,128]{1,0:T(8,128)S(1)}, u32[]{:S(2)}, u32[]{:S(2)}) collective-permute-start(f32[72,128]{1,0:T(8,128)S(1)} %slice_add_fusion.1), channel_id=1, source_target_pairs={{0,8},{4,12},{8,0},{12,4},{1,9},{5,13},{9,1},{13,5},{2,10},{6,14},... | collective-permute-start | bytes 110600 | tf_op jit(solution)/shard_map/ppermute | solution.py:164
  68.6 6.3 %copy-start.5 = (s32[16]{0:T(128)S(1)}, s32[16]{0:T(128)}, u32[]{:S(2)}) copy-start(s32[16]{0:T(128)} %param.11) | copy-start | bytes 196
  69.9 26.6 %all-to-all-start.1 = ((f32[16,200,128]{2,1,0:T(8,128)}), f32[16,200,128]{2,1,0:T(8,128)}, u32[]{:S(2)}, u32[]{:S(2)}) async-start(f32[16,200,128]{2,1,0:T(8,128)} %broadcast_in_dim.12), calls=%async_computation.1 | async-start | bytes 3276800 | tf_op jit(solution)/shard_map/all_to_all | solution.py:173
  96.5 1.2 copy-start.1
  109.2 2.9 %collective-permute-start.8 = (f32[1,128]{1,0:T(1,128)S(1)}, f32[1,128]{1,0:T(1,128)S(1)}, u32[]{:S(2)}, u32[]{:S(2)}) collective-permute-start(f32[1,128]{1,0:T(1,128)S(1)} %slice.14), channel_id=1, source_target_pairs={{0,4},{4,0},{8,12},{12,8},{1,5},{5,1},{9,13},{13,9},{2,6},{6,2},{1... | collective-permute-start | bytes 1544 | tf_op jit(solution)/shard_map/ppermute | solution.py:164
  112.1 6.4 %collective-permute-start.9 = (f32[1,128]{1,0:T(1,128)S(1)}, f32[1,128]{1,0:T(1,128)S(1)}, u32[]{:S(2)}, u32[]{:S(2)}) collective-permute-start(f32[1,128]{1,0:T(1,128)S(1)} %slice_add_fusion), channel_id=1, source_target_pairs={{0,8},{4,12},{8,0},{12,4},{1,9},{5,13},{9,1},{13,5},{2,10},{6,14},... | collective-permute-start | bytes 1544 | tf_op jit(solution)/shard_map/ppermute | solution.py:164
Sparse Core Ops, SparseCore 0:
  51.8 57.3 all-gather.1

commit v3 on v2

v3 whole, which is shorter than its diff:
```python
import jax
import jax.numpy as jnp
from jax import lax
from jax.experimental import pallas as pl
from jax.experimental.pallas import tpu as pltpu
from jax.sharding import PartitionSpec as P

NS_STEPS = 4


exact_mode = lax.Precision.HIGHEST
decay_rate = 0.75
damping = 0.1
damp_shift = 0.001
clip_norm = 256.0
momentum_rate = 0.9
step_rate = 0.05


def sample_stats(samples, block_size):
    sample_rows, width = samples.shape
    blocks = samples.reshape(sample_rows, width // block_size, block_size)
    return jnp.einsum("tnb,tnc->nbc", blocks, blocks, preferred_element_type=jnp.float32)


def fold_kernel(place_ref, left_ref, right_ref, *folded_refs):
    left_count, size, _ = left_ref.shape
    half = size // 2
    side = len(folded_refs)
    row = lax.broadcasted_iota(jnp.int32, (half, size), 0)
    col = lax.broadcasted_iota(jnp.int32, (half, size), 1)
    for k in range(side):
        for j in range(side):
            n = (place_ref[0] ^ k) * side + (place_ref[1] ^ j)
            at = n % left_count
            stats = jnp.where(n < left_count, left_ref[at], right_ref[at])
            top, bottom = stats[:half], stats[half:]
            folded_refs[k][j, :half, :] = jnp.where(col >= row, top, pltpu.roll(bottom, half, 1))
            diagonal = jnp.sum(jnp.where(col == row + half, bottom, 0.0), axis=0, keepdims=True)
            folded_refs[k][j, half:, :] = jnp.broadcast_to(diagonal, (8, size))


def fold(places, left_stats, right_stats, side):
    size = left_stats.shape[1]
    return pl.pallas_call(
        fold_kernel,
        in_specs=[
            pl.BlockSpec(memory_space=pltpu.SMEM),
            pl.BlockSpec(memory_space=pltpu.VMEM),
            pl.BlockSpec(memory_space=pltpu.VMEM),
        ],
        out_shape=[jax.ShapeDtypeStruct((side, size // 2 + 8, size), jnp.float32)] * side,
        name="fold",
    )(places, left_stats, right_stats)


def dot(a, b):
    return jnp.dot(a, b, precision=exact_mode, preferred_element_type=jnp.float32)


def damp(mixed, on_diagonal):
    size = mixed.shape[0]
    trace = jnp.sum(jnp.where(on_diagonal, mixed, 0.0), keepdims=True)
    damped = mixed + jnp.where(on_diagonal, damping * trace / size + damp_shift, 0.0)
    bound = jnp.max(jnp.sum(jnp.abs(damped), axis=1, keepdims=True), keepdims=True)
    return jnp.where(on_diagonal, 1.0, 0.0) - damped / bound, bound


def update_kernel(side, sample_count, place_ref, *refs):
    folded_refs = refs[:side]
    grad_ref, old_ref, precond_ref, owned_ref, align_ref, blended_ref = refs[side:]
    size = old_ref.shape[1]
    half = size // 2
    right_count = precond_ref.shape[1] // size
    left_count = precond_ref.shape[0] // size
    row = lax.broadcasted_iota(jnp.int32, (half, size), 0)
    col = lax.broadcasted_iota(jnp.int32, (half, size), 1)
    for k in range(side):
        for j in range(side):
            n = (place_ref[0] ^ k) * side + (place_ref[1] ^ j)
            part = folded_refs[k][j, :half, :]
            diagonal = folded_refs[k][j, half : half + 1, :]
            turned = jnp.concatenate([part, jnp.zeros_like(part)], axis=0).T
            top = jnp.where(col >= row, part, turned[:half])
            corner = jnp.where(
                col < row + half, pltpu.roll(part, half, 1), pltpu.roll(turned[:half], half, 1)
            )
            corner = jnp.where(col == row + half, diagonal, corner)
            bottom = jnp.where(col < half, turned[half:], corner)
            for first, stats in ((0, top), (half, bottom)):
                blended_ref[n, first : first + half, :] = decay_rate * old_ref[
                    n, first : first + half, :
                ] + (1.0 - decay_rate) * (stats / sample_count)

    for place in range(owned_ref.shape[0]):
        block = place_ref[3 + place]
        used = block >= 0
        value = blended_ref[jnp.maximum(block, 0)]
        owned_ref[place] = jnp.where(used, value, jnp.zeros_like(value))

    on_diagonal = lax.broadcasted_iota(jnp.int32, (size, size), 0) == lax.broadcasted_iota(
        jnp.int32, (size, size), 1
    )
    needed = [blended_ref[n] for n in range(left_count)]
    needed += [blended_ref[place_ref[2] + n] for n in range(right_count)]
    powers, bounds, inverses = [], [], []
    for mixed in needed:
        power, bound = damp(mixed, on_diagonal)
        powers.append(power)
        bounds.append(bound)
        inverses.append(jnp.where(on_diagonal, 1.0, 0.0) + power)
    for step in range(NS_STEPS - 1):
        powers = [dot(power, power) for power in powers]
        inverses = [x + dot(x, power) for x, power in zip(inverses, powers)]
    inverses = [x / bound for x, bound in zip(inverses, bounds)]

    total = jnp.zeros((size, size), jnp.float32)
    for a in range(left_count):
        for c in range(right_count):
            grad = grad_ref[a * size : (a + 1) * size, c * size : (c + 1) * size]
            value = dot(dot(inverses[a], grad), inverses[left_count + c])
            precond_ref[a * size : (a + 1) * size, c * size : (c + 1) * size] = value
            total = total + value * grad
    align_ref[...] = jnp.broadcast_to(jnp.sum(total, keepdims=True), align_ref.shape)


def update(places, folded, gradient, old_factors, capacity, sample_count):
    size = old_factors.shape[1]
    side = len(folded)
    return pl.pallas_call(
        lambda *refs: update_kernel(side, sample_count, *refs),
        in_specs=[pl.BlockSpec(memory_space=pltpu.SMEM)]
        + [pl.BlockSpec(memory_space=pltpu.VMEM)] * (side + 2),
        out_shape=(
            jax.ShapeDtypeStruct(gradient.shape, jnp.float32),
            jax.ShapeDtypeStruct((capacity, size, size), jnp.float32),
            jax.ShapeDtypeStruct((8, 128), jnp.float32),
        ),
        scratch_shapes=[pltpu.VMEM(old_factors.shape, jnp.float32)],
        compiler_params=pltpu.CompilerParams(vmem_limit_bytes=40 * 1024 * 1024),
        name="update",
    )(places, *folded, gradient, old_factors)


def swap(value, axis, flip):
    size = lax.axis_size(axis)
    return lax.ppermute(value, axis, [(i, i ^ flip) for i in range(size)])


def exchange(value, axis):
    return [value] + [swap(value, axis, flip) for flip in range(1, lax.axis_size(axis))]


def spread(value, axis):
    copies = jnp.broadcast_to(value[None], (lax.axis_size(axis),) + value.shape)
    return lax.all_to_all(copies, axis, 0, 0)


def body(activations, grads_out, grad_parts, old_factors, block_owner, weights, momentum):
    shard_count = lax.axis_size("shards")
    replica_count = lax.axis_size("replica")
    block_count = old_factors.shape[0]
    block_size = old_factors.shape[1]
    capacity = (block_count + shard_count - 1) // shard_count + 1
    sample_count = activations.shape[0] * shard_count * lax.axis_size("tensor") * replica_count
    partial_grad = grad_parts[0]
    row_count, col_count = partial_grad.shape
    left_count = row_count // block_size
    right_count = col_count // block_size
    piece_rows = row_count // shard_count

    side = 4
    shard = lax.axis_index("shards")

    grad_in = lax.all_to_all(partial_grad.reshape(shard_count, piece_rows, col_count), "shards", 0, 0)

    coords = jnp.stack([shard // side, shard % side]).astype(jnp.int32)
    along_x = fold(
        coords,
        sample_stats(activations, block_size),
        sample_stats(grads_out, block_size),
        side,
    )
    parts = [along_x[0]] + [swap(along_x[k], "shards", k * side) for k in range(1, side)]
    along_y = [sum(part[j] for part in parts) for j in range(side)]
    own_stats = along_y[0] + sum(swap(along_y[j], "shards", j) for j in range(1, side))

    base = weights - (step_rate * momentum_rate) * momentum
    base_parts = exchange(base, "replica")
    replica = lax.axis_index("replica")
    base_rows = []
    for place in range(replica_count):
        rows = base_parts[0]
        for flip in range(1, replica_count):
            rows = jnp.where(replica ^ flip == place, base_parts[flip], rows)
        base_rows.append(rows)
    base = lax.all_gather(jnp.concatenate(base_rows, axis=0), "shards", axis=0, tiled=True)

    own_grad = sum(exchange(jnp.sum(grad_in, axis=0), "replica"))
    gradient = spread(own_grad, "shards").reshape(row_count, col_count)

    own_stats = own_stats + swap(own_stats, "tensor", 1)
    own_stats = own_stats + swap(own_stats, "replica", 1)
    own_stats = own_stats + swap(own_stats, "replica", 2)
    own_stats = own_stats + swap(own_stats, "tensor", 2)
    row_of_y = jnp.stack([own_stats] + [swap(own_stats, "shards", j) for j in range(1, side)])
    folded = [row_of_y] + [swap(row_of_y, "shards", k * side) for k in range(1, side)]
    gradient, base = lax.optimization_barrier((gradient, base))

    positions = jnp.arange(block_count, dtype=jnp.int32)
    earlier = (block_owner[:, None] == block_owner[None, :]) & (
        positions[None, :] < positions[:, None]
    )
    slots = block_owner * capacity + jnp.sum(earlier.astype(jnp.int32), axis=1)
    own_slots = lax.axis_index("shards") * capacity + jnp.arange(capacity, dtype=jnp.int32)
    holds = jnp.max(jnp.where(slots[None, :] == own_slots[:, None], positions[None, :], -1), axis=1)
    right_first = left_count + lax.axis_index("tensor") * right_count
    places = jnp.concatenate([coords, right_first.reshape(1).astype(jnp.int32), holds])

    precond, owned_blocks, align = update(
        places, folded, gradient, old_factors, capacity, sample_count
    )
    align = align[:1]
    align = align + swap(align, "tensor", 1)
    align = align + swap(align, "tensor", 2)
    clip_scale = jnp.minimum(1.0, clip_norm / jnp.sqrt(align[0, 0]))
    own_rows = weights.shape[0]
    first_row = lax.axis_index(("shards", "replica")) * own_rows
    own_precond = lax.dynamic_slice_in_dim(precond, first_row, own_rows, 0)
    momentum_next = momentum_rate * momentum + clip_scale * own_precond
    weights_next = base - (step_rate * clip_scale) * precond
    return (weights_next, momentum_next, owned_blocks)


def solution(mesh):
    placed = (
        P(("shards", "tensor", "replica"), None),
        P(("shards", "tensor", "replica"), None),
        P(("shards", "replica"), None, "tensor"),
        P(),
        P(),
        P(("shards", "replica"), "tensor"),
        P(("shards", "replica"), "tensor"),
    )
    return jax.shard_map(
        body,
        mesh=mesh,
        in_specs=placed,
        out_specs=(P(None, "tensor"), P(("shards", "replica"), "tensor"), P("shards", None, None)),
        check_vma=False,
    )
```

time: 129 us -> 123 us (0.953)
  waiting for transfers between devices: 48.8 us -> 21.7 us
  starting transfers between devices: 40.6 us -> 58.1 us
  other arithmetic: 5.64 us -> 9.05 us
  matrix products: 3.8 us -> 5.94 us
    all_to_all x1, waiting for transfers between devices: 21.1 us -> 0.01 us  [spread(): return lax.all_to_all(copies, axis, 0, 0)]
    ppermute x10 -> x24, starting transfers between devices: 27.8 us -> 47.6 us  [swap(): return lax.ppermute(value, axis, [(i, i ^ flip) for i in range(size)])]
    all_to_all x1, waiting for transfers between devices: 13 us -> 1.81 us  [body(): lax.all_to_all(partial_grad.reshape(shard_count, piece_rows, col_count),...]
    ppermute x10 -> x24, waiting for transfers between devices: 11.4 us -> 19.8 us  [swap(): return lax.ppermute(value, axis, [(i, i ^ flip) for i in range(size)])]
    all_gather x1, waiting for transfers between devices: 3.23 us -> 0.01 us  [body(): lax.all_gather(jnp.concatenate(base_rows, axis=0), 'shards', axis=0, tile...]
    add x1 -> x5, other arithmetic: 0.03 us -> 2.4 us  [the longest x1 1.51 us: body(): along_y = [sum((part[j] for part in parts)) for j in range(side)]]
    dot_general x2, matrix products: 3.8 us -> 5.94 us  [sample_stats(): jnp.einsum('tnb,tnc->nbc', blocks, blocks, preferred_element_type=jnp.flo...]
    reduce_sum x1, other arithmetic: 1.52 us -> 0.06 us  [body(): own_grad = sum(exchange(jnp.sum(grad_in, axis=0), 'replica'))]
  transfers between devices with their start and end apart: 13 -> 27, of which waited for: 11 -> 13; matrix products, arithmetic and copies ran while one was open for 2% -> 9% of each run, Pallas kernels for 6% -> 2%
where the time goes in v3:
time: 123 us; the launch traced here: 122 us
  starting transfers between devices  58.1 us (47%)
  waiting for transfers between devices  21.7 us (18%)
  between operations  14.3 us (12%)
  Pallas kernels  10.2 us (8%)
  other arithmetic  9.05 us (7%)
  matrix products  5.94 us (5%)
  local copies, waits for them, and re-layouts  3.28 us (3%)
    ppermute x24, starting transfers between devices, swap(): return lax.ppermute(value, axis, [(i, i ^ flip) for i in range(size)])  47.6 us
    ppermute x24, waiting for transfers between devices, swap(): return lax.ppermute(value, axis, [(i, i ^ flip) for i in range(size)])  19.8 us
    pallas_call x1, Pallas kernels, update(): pl.pallas_call(lambda *refs: update_kernel(side, sample_count, *refs), in...  8.01 us
    all_to_all x1, starting transfers between devices, body(): lax.all_to_all(partial_grad.reshape(shard_count, piece_rows, col_count),...  6.76 us
    dot_general x2, matrix products, sample_stats(): jnp.einsum('tnb,tnc->nbc', blocks, blocks, preferred_element_type=jnp.flo...  5.94 us
    all_to_all x1, starting transfers between devices, spread(): return lax.all_to_all(copies, axis, 0, 0)  3.66 us
    sub x1, other arithmetic, body(): weights_next = base - step_rate * clip_scale * precond  2.64 us
  transfers between devices with their start and end apart: 27, of which 13 were waited for; matrix products, arithmetic and copies ran while one was open for 9% of the time, Pallas kernels for 2%

profile of v3, /device:TPU:1, one launch (start us, length us, event | category | flops | bytes accessed | tf_op | source)
XLA Modules:
  0.0 122.5 jit_solution(3158502107964722428)
XLA Ops:
  7.2 0.9 multiply_subtract_fusion.1
  8.1 2.5 %collective-permute-start.5 = (f32[16,256]{1,0:T(8,128)S(1)}, f32[16,256]{1,0:T(8,128)S(1)}, u32[]{:S(2)}, u32[]{:S(2)}) collective-permute-start(f32[16,256]{1,0:T(8,128)S(1)} %multiply_subtract_fusion.1), channel_id=1, source_target_pairs={{0,1},{1,0},{2,3},{3,2},{4,5},{5,4},{6,7},{7,6},{8,9},{9,8},{10,11... | collective-permute-start | bytes 49160 | tf_op jit(solution)/shard_map/ppermute | solution.py:147
  10.5 3.0 %collective-permute-start.4 = (f32[16,256]{1,0:T(8,128)S(1)}, f32[16,256]{1,0:T(8,128)S(1)}, u32[]{:S(2)}, u32[]{:S(2)}) collective-permute-start(f32[16,256]{1,0:T(8,128)S(1)} %multiply_subtract_fusion.1), channel_id=1, source_target_pairs={{0,2},{1,3},{2,0},{3,1},{4,6},{5,7},{6,4},{7,5},{8,10},{9,11},{10,... | collective-permute-start | bytes 49160 | tf_op jit(solution)/shard_map/ppermute | solution.py:147
  13.5 6.8 %all-to-all-start = ((f32[16,64,256]{2,1,0:T(8,128)}), f32[16,64,256]{2,1,0:T(8,128)S(1)}, u32[]{:S(2)}, u32[]{:S(2)}) async-start(f32[16,64,256]{2,1,0:T(8,128)} %bitcast.36), calls=%async_computation | async-start | bytes 2097152 | tf_op jit(solution)/shard_map/all_to_all | solution.py:175
  20.4 1.8 %fusion.3.left_ref = f32[8,128,128]{2,1,0:T(8,128)} fusion(bf16[1024,1024]{1,0:T(8,128)(2,1)S(1)} %copy-done), kind=kOutput, calls=%fused_computation.3 | convolution fusion | flops 268435456 | bytes 2621440 | tf_op jit(solution)/shard_map/tnb,tnc->nbc/dot_general | solution.py:23
  22.2 0.6 pad_add_fusion.1.place_ref
  22.8 0.6 pad_maximum_fusion.1
  23.5 4.1 %fusion.right_ref = f32[8,128,128]{2,1,0:T(8,128)} fusion(bf16[1024,1024]{1,0:T(8,128)(2,1)} %param.8), kind=kOutput, calls=%fused_computation | convolution fusion | flops 268435456 | bytes 2621440 | tf_op jit(solution)/shard_map/tnb,tnc->nbc/dot_general | solution.py:23
  27.6 2.2 %fold.1 = (f32[4,72,128]{2,1,0:T(8,128)}, f32[4,72,128]{2,1,0:T(8,128)}, f32[4,72,128]{2,1,0:T(8,128)}, f32[4,72,128]{2,1,0:T(8,128)}) custom-call(s32[2]{0:T(128)} %pad_add_fusion.1.place_ref, f32[8,128,128]{2,1,0:T(8,128)} %fusion.3.left_ref, f32[8,128,128]{2,1,0:T(8,128)} %fusion.right_ref), custom_call_target="tpu_custom_call" | custom-call | tf_op jit(solution)/shard_map/fold/pallas_call | solution.py:45
  29.7 1.4 %collective-permute-start.6 = (f32[4,72,128]{2,1,0:T(8,128)}, f32[4,72,128]{2,1,0:T(8,128)S(1)}, u32[]{:S(2)}, u32[]{:S(2)}) collective-permute-start(f32[4,72,128]{2,1,0:T(8,128)} %get-tuple-element.14), channel_id=1, source_target_pairs={{0,64},{16,80},{32,96},{48,112},{64,0},{80,16},{96,32},{112,48},{1... | collective-permute-start | bytes 442376 | tf_op jit(solution)/shard_map/ppermute | solution.py:147
  31.1 2.4 %collective-permute-start.7 = (f32[4,72,128]{2,1,0:T(8,128)}, f32[4,72,128]{2,1,0:T(8,128)S(1)}, u32[]{:S(2)}, u32[]{:S(2)}) collective-permute-start(f32[4,72,128]{2,1,0:T(8,128)} %get-tuple-element.15), channel_id=1, source_target_pairs={{0,128},{16,144},{32,160},{48,176},{64,192},{80,208},{96,224},{112... | collective-permute-start | bytes 442376 | tf_op jit(solution)/shard_map/ppermute | solution.py:147
  33.6 1.8 %all-to-all-done = f32[16,64,256]{2,1,0:T(8,128)S(1)} async-done(((f32[16,64,256]{2,1,0:T(8,128)}), f32[16,64,256]{2,1,0:T(8,128)S(1)}, u32[]{:S(2)}, u32[]{:S(2)}) %all-to-all-start) | async-done | bytes 1048608 | tf_op jit(solution)/shard_map/all_to_all | solution.py:175
  35.5 3.1 %collective-permute-start.2 = (f32[64,256]{1,0:T(8,128)S(1)}, f32[64,256]{1,0:T(8,128)S(1)}, u32[]{:S(2)}, u32[]{:S(2)}) collective-permute-start(f32[64,256]{1,0:T(8,128)S(1)} %reduce_sum.18), channel_id=1, source_target_pairs={{0,3},{1,2},{2,1},{3,0},{4,7},{5,6},{6,5},{7,4},{8,11},{9,10},{10,... | collective-permute-start | bytes 196616 | tf_op jit(solution)/shard_map/ppermute | solution.py:147
  38.6 0.5 collective-permute-start
  39.1 1.8 %collective-permute-done.7 = f32[4,72,128]{2,1,0:T(8,128)S(1)} collective-permute-done((f32[4,72,128]{2,1,0:T(8,128)}, f32[4,72,128]{2,1,0:T(8,128)S(1)}, u32[]{:S(2)}, u32[]{:S(2)}) %collective-permute-start.7) | collective-permute-done | bytes 147488 | tf_op jit(solution)/shard_map/ppermute | solution.py:147
  40.9 1.6 %collective-permute-done.8 = f32[4,72,128]{2,1,0:T(8,128)} collective-permute-done((f32[4,72,128]{2,1,0:T(8,128)}, f32[4,72,128]{2,1,0:T(8,128)}, u32[]{:S(2)}, u32[]{:S(2)}) %collective-permute-start.8) | collective-permute-done | bytes 147488 | tf_op jit(solution)/shard_map/ppermute | solution.py:147
  42.5 1.5 %fusion.7 = (f32[72,128]{1,0:T(8,128)}, f32[72,128]{1,0:T(8,128)}, f32[72,128]{1,0:T(8,128)}) fusion(f32[4,72,128]{2,1,0:T(8,128)} %collective-permute-done.8, f32[4,72,128]{2,1,0:T(8,128)S(1)} %collective-permute-done.7, f32[4,72,128]{2,1,0:T(8,128)S(1)} %collective-permute-done.6, f32[4,72,128]{2,1,0:T(8,128)} %get-tuple-element.13), kind=kLoop, calls=%fused_computation.15 | loop fusion | flops 82944 | bytes 552960 | tf_op jit(solution)/shard_map/add | solution.py:185
  44.0 1.3 %collective-permute-start.10 = (f32[72,128]{1,0:T(8,128)}, f32[72,128]{1,0:T(8,128)}, u32[]{:S(2)}, u32[]{:S(2)}) collective-permute-start(f32[72,128]{1,0:T(8,128)} %get-tuple-element.21), channel_id=1, source_target_pairs={{0,32},{16,48},{32,0},{48,16},{64,96},{80,112},{96,64},{112,80},{1... | collective-permute-start | bytes 110600 | tf_op jit(solution)/shard_map/ppermute | solution.py:147
  45.3 2.3 %collective-permute-start.11 = (f32[72,128]{1,0:T(8,128)}, f32[72,128]{1,0:T(8,128)}, u32[]{:S(2)}, u32[]{:S(2)}) collective-permute-start(f32[72,128]{1,0:T(8,128)} %get-tuple-element.22), channel_id=1, source_target_pairs={{0,48},{16,32},{32,16},{48,0},{64,112},{80,96},{96,80},{112,64},{1... | collective-permute-start | bytes 110600 | tf_op jit(solution)/shard_map/ppermute | solution.py:147
  47.7 1.1 broadcast_in_dim.10
  48.7 3.7 %all-to-all-start.1 = ((f32[16,64,256]{2,1,0:T(8,128)}), f32[16,64,256]{2,1,0:T(8,128)S(1)}, u32[]{:S(2)}, u32[]{:S(2)}) async-start(f32[16,64,256]{2,1,0:T(8,128)} %broadcast_in_dim.10), calls=%async_computation.1 | async-start | bytes 2097152 | tf_op jit(solution)/shard_map/all_to_all | solution.py:156
  52.4 0.9 fusion.10
  53.3 4.0 %collective-permute-start.12 = (f32[72,128]{1,0:T(8,128)S(1)}, f32[72,128]{1,0:T(8,128)S(1)}, u32[]{:S(2)}, u32[]{:S(2)}) collective-permute-start(f32[72,128]{1,0:T(8,128)S(1)} %fusion.10), channel_id=1, source_target_pairs={{0,4},{4,0},{8,12},{12,8},{1,5},{5,1},{9,13},{13,9},{2,6},{6,2},{1... | collective-permute-start | bytes 110600 | tf_op jit(solution)/shard_map/ppermute | solution.py:147
  57.3 0.9 collective-permute-done.12
  58.1 0.2 collective-permute-start.13
  58.4 2.9 %collective-permute-done.13 = f32[72,128]{1,0:T(8,128)S(1)} collective-permute-done((f32[72,128]{1,0:T(8,128)S(1)}, f32[72,128]{1,0:T(8,128)S(1)}, u32[]{:S(2)}, u32[]{:S(2)}) %collective-permute-start.13) | collective-permute-done | bytes 36896 | tf_op jit(solution)/shard_map/ppermute | solution.py:147
  61.2 2.4 %collective-permute-start.14 = (f32[72,128]{1,0:T(8,128)S(1)}, f32[72,128]{1,0:T(8,128)S(1)}, u32[]{:S(2)}, u32[]{:S(2)}) collective-permute-start(f32[72,128]{1,0:T(8,128)S(1)} %add.146), channel_id=1, source_target_pairs={{0,2},{1,3},{2,0},{3,1},{4,6},{5,7},{6,4},{7,5},{8,10},{9,11},{10,... | collective-permute-start | bytes 110600 | tf_op jit(solution)/shard_map/ppermute | solution.py:147
  63.8 1.5 %collective-permute-done.14 = f32[72,128]{1,0:T(8,128)S(1)} collective-permute-done((f32[72,128]{1,0:T(8,128)S(1)}, f32[72,128]{1,0:T(8,128)S(1)}, u32[]{:S(2)}, u32[]{:S(2)}) %collective-permute-start.14) | collective-permute-done | bytes 36896 | tf_op jit(solution)/shard_map/ppermute | solution.py:147
  65.3 6.5 %collective-permute-start.15 = (f32[72,128]{1,0:T(8,128)S(1)}, f32[72,128]{1,0:T(8,128)S(1)}, u32[]{:S(2)}, u32[]{:S(2)}) collective-permute-start(f32[72,128]{1,0:T(8,128)S(1)} %add.147), channel_id=1, source_target_pairs={{0,8},{4,12},{8,0},{12,4},{1,9},{5,13},{9,1},{13,5},{2,10},{6,14},... | collective-permute-start | bytes 110600 | tf_op jit(solution)/shard_map/ppermute | solution.py:147
  71.7 1.3 %collective-permute-done.15 = f32[72,128]{1,0:T(8,128)S(1)} collective-permute-done((f32[72,128]{1,0:T(8,128)S(1)}, f32[72,128]{1,0:T(8,128)S(1)}, u32[]{:S(2)}, u32[]{:S(2)}) %collective-permute-start.15) | collective-permute-done | bytes 36896 | tf_op jit(solution)/shard_map/ppermute | solution.py:147
  73.1 2.9 %collective-permute-start.18 = (f32[72,128]{1,0:T(8,128)S(1)}, f32[72,128]{1,0:T(8,128)S(1)}, u32[]{:S(2)}, u32[]{:S(2)}) collective-permute-start(f32[72,128]{1,0:T(8,128)S(1)} %add.148), channel_id=1, source_target_pairs={{0,48},{16,32},{32,16},{48,0},{64,112},{80,96},{96,80},{112,64},{1... | collective-permute-start | bytes 110600 | tf_op jit(solution)/shard_map/ppermute | solution.py:147
  75.9 0.6 collective-permute-start.17
  76.6 1.2 %collective-permute-done.18 = f32[72,128]{1,0:T(8,128)S(1)} collective-permute-done((f32[72,128]{1,0:T(8,128)S(1)}, f32[72,128]{1,0:T(8,128)S(1)}, u32[]{:S(2)}, u32[]{:S(2)}) %collective-permute-start.18) | collective-permute-done | bytes 36896 | tf_op jit(solution)/shard_map/ppermute | solution.py:147
  77.9 2.4 %collective-permute-done.17 = f32[72,128]{1,0:T(8,128)S(1)} collective-permute-done((f32[72,128]{1,0:T(8,128)S(1)}, f32[72,128]{1,0:T(8,128)S(1)}, u32[]{:S(2)}, u32[]{:S(2)}) %collective-permute-start.17) | collective-permute-done | bytes 36896 | tf_op jit(solution)/shard_map/ppermute | solution.py:147
  80.3 2.4 %collective-permute-start.21 = (f32[4,72,128]{2,1,0:T(8,128)S(1)}, f32[4,72,128]{2,1,0:T(8,128)S(1)}, u32[]{:S(2)}, u32[]{:S(2)}) collective-permute-start(f32[4,72,128]{2,1,0:T(8,128)S(1)} %pad_maximum_fusion.refs_1_), channel_id=1, source_target_pairs={{0,192},{16,208},{32,224},{48,240},{64,128},{80,144},{96,160},{112... | collective-permute-start | bytes 442376 | tf_op jit(solution)/shard_map/ppermute | solution.py:147
  82.8 0.6 collective-permute-start.20
  83.3 0.3 collective-permute-start.19
  83.9 2.5 %collective-permute-done.21.refs_4_ = f32[4,72,128]{2,1,0:T(8,128)S(1)} collective-permute-done((f32[4,72,128]{2,1,0:T(8,128)S(1)}, f32[4,72,128]{2,1,0:T(8,128)S(1)}, u32[]{:S(2)}, u32[]{:S(2)}) %collective-permute-start.21) | collective-permute-done | bytes 147488 | tf_op jit(solution)/shard_map/ppermute | solution.py:147
  86.4 1.9 %collective-permute-done.20.refs_3_ = f32[4,72,128]{2,1,0:T(8,128)} collective-permute-done((f32[4,72,128]{2,1,0:T(8,128)S(1)}, f32[4,72,128]{2,1,0:T(8,128)}, u32[]{:S(2)}, u32[]{:S(2)}) %collective-permute-start.20) | collective-permute-done | bytes 147488 | tf_op jit(solution)/shard_map/ppermute | solution.py:147
  88.4 1.2 copy-done.2
  89.6 8.0 %update.1 = (f32[1024,256]{1,0:T(8,128)S(1)}, f32[2,128,128]{2,1,0:T(8,128)}, f32[8,128]{1,0:T(8,128)S(1)}) custom-call(s32[5]{0:T(128)S(1)} %pad_add_fusion.refs_0_, f32[4,72,128]{2,1,0:T(8,128)S(1)} %pad_maximum_fusion.refs_1_, f32[4,72,128]{2,1,0:T(8,128)} %collective-permute-done.19.refs_2_, f32[4,72,128]{2,1,0:T(8,128)} %collective-permute-done.20.refs_3_, ...), custom_call_target="tpu_custom_call" | custom-call | tf_op jit(solution)/shard_map/update/pallas_call | solution.py:130
  97.6 1.0 copy-done.1
  98.6 5.6 %collective-permute-start.22 = (f32[1,128]{1,0:T(1,128)S(1)}, f32[1,128]{1,0:T(1,128)S(1)}, u32[]{:S(2)}, u32[]{:S(2)}) collective-permute-start(f32[1,128]{1,0:T(1,128)S(1)} %slice.70), channel_id=1, source_target_pairs={{0,4},{4,0},{8,12},{12,8},{1,5},{5,1},{9,13},{13,9},{2,6},{6,2},{1... | collective-permute-start | bytes 1544 | tf_op jit(solution)/shard_map/ppermute | solution.py:147
  104.1 0.8 collective-permute-done.22
  105.0 5.7 %collective-permute-start.23 = (f32[1,128]{1,0:T(1,128)S(1)}, f32[1,128]{1,0:T(1,128)S(1)}, u32[]{:S(2)}, u32[]{:S(2)}) collective-permute-start(f32[1,128]{1,0:T(1,128)S(1)} %slice_add_fusion.12), channel_id=1, source_target_pairs={{0,8},{4,12},{8,0},{12,4},{1,9},{5,13},{9,1},{13,5},{2,10},{6,14},... | collective-permute-start | bytes 1544 | tf_op jit(solution)/shard_map/ppermute | solution.py:147
  110.6 0.9 collective-permute-done.23
  111.7 1.3 %multiply_add_fusion = f32[16,256]{1,0:T(8,128)} fusion(f32[1024,256]{1,0:T(8,128)} %copy-done.1, s32[]{:T(128)S(6)} %select_n.119, f32[16,256]{1,0:T(8,128)S(1)} %copy-done.3, f32[]{:T(128)} %bitcast.13), kind=kLoop, calls=%fused_computation.27 | loop fusion | flops 12288 | bytes 49160 | tf_op jit(solution)/shard_map/add | solution.py:230
  113.0 2.6 %multiply_subtract_fusion = f32[1024,256]{1,0:T(8,128)} fusion(f32[1024,256]{1,0:T(8,128)} %all-gather.2.cloned.1.call-done, f32[1024,256]{1,0:T(8,128)} %copy-done.1, f32[]{:T(128)S(6)} %mul_shard_map.3), kind=kLoop, calls=%fused_computation.6 | loop fusion | flops 524288 | bytes 3145732 | tf_op jit(solution)/shard_map/sub | solution.py:231
  (45 shorter events, 0.9 us)
Async XLA Ops:
  7.2 13.2 %copy-start = (bf16[1024,1024]{1,0:T(8,128)(2,1)S(1)}, bf16[1024,1024]{1,0:T(8,128)(2,1)}, u32[]{:S(2)}) copy-start(bf16[1024,1024]{1,0:T(8,128)(2,1)} %param.7) | copy-start | bytes 6291460
  8.1 14.7 %collective-permute-start.5 = (f32[16,256]{1,0:T(8,128)S(1)}, f32[16,256]{1,0:T(8,128)S(1)}, u32[]{:S(2)}, u32[]{:S(2)}) collective-permute-start(f32[16,256]{1,0:T(8,128)S(1)} %multiply_subtract_fusion.1), channel_id=1, source_target_pairs={{0,1},{1,0},{2,3},{3,2},{4,5},{5,4},{6,7},{7,6},{8,9},{9,8},{10,11... | collective-permute-start | bytes 49160 | tf_op jit(solution)/shard_map/ppermute | solution.py:147
  10.5 12.2 %collective-permute-start.4 = (f32[16,256]{1,0:T(8,128)S(1)}, f32[16,256]{1,0:T(8,128)S(1)}, u32[]{:S(2)}, u32[]{:S(2)}) collective-permute-start(f32[16,256]{1,0:T(8,128)S(1)} %multiply_subtract_fusion.1), channel_id=1, source_target_pairs={{0,2},{1,3},{2,0},{3,1},{4,6},{5,7},{6,4},{7,5},{8,10},{9,11},{10,... | collective-permute-start | bytes 49160 | tf_op jit(solution)/shard_map/ppermute | solution.py:147
  13.5 9.3 %collective-permute-start.3 = (f32[16,256]{1,0:T(8,128)S(1)}, f32[16,256]{1,0:T(8,128)S(1)}, u32[]{:S(2)}, u32[]{:S(2)}) collective-permute-start(f32[16,256]{1,0:T(8,128)S(1)} %multiply_subtract_fusion.1), channel_id=1, source_target_pairs={{0,3},{1,2},{2,1},{3,0},{4,7},{5,6},{6,5},{7,4},{8,11},{9,10},{10,... | collective-permute-start | bytes 49160 | tf_op jit(solution)/shard_map/ppermute | solution.py:147
  13.5 21.9 %all-to-all-start = ((f32[16,64,256]{2,1,0:T(8,128)}), f32[16,64,256]{2,1,0:T(8,128)S(1)}, u32[]{:S(2)}, u32[]{:S(2)}) async-start(f32[16,64,256]{2,1,0:T(8,128)} %bitcast.36), calls=%async_computation | async-start | bytes 2097152 | tf_op jit(solution)/shard_map/all_to_all | solution.py:175
  20.3 63.6 %all-gather.2.cloned.1.call-start = ((), (), s32[]{:S(2)}) async-start(), calls=%async_computation.2 | async-start | bytes 1114112 | tf_op jit(solution)/shard_map/all_gather | solution.py:197
  29.7 8.9 %collective-permute-start.6 = (f32[4,72,128]{2,1,0:T(8,128)}, f32[4,72,128]{2,1,0:T(8,128)S(1)}, u32[]{:S(2)}, u32[]{:S(2)}) collective-permute-start(f32[4,72,128]{2,1,0:T(8,128)} %get-tuple-element.14), channel_id=1, source_target_pairs={{0,64},{16,80},{32,96},{48,112},{64,0},{80,16},{96,32},{112,48},{1... | collective-permute-start | bytes 442376 | tf_op jit(solution)/shard_map/ppermute | solution.py:147
  31.1 9.8 %collective-permute-start.7 = (f32[4,72,128]{2,1,0:T(8,128)}, f32[4,72,128]{2,1,0:T(8,128)S(1)}, u32[]{:S(2)}, u32[]{:S(2)}) collective-permute-start(f32[4,72,128]{2,1,0:T(8,128)} %get-tuple-element.15), channel_id=1, source_target_pairs={{0,128},{16,144},{32,160},{48,176},{64,192},{80,208},{96,224},{112... | collective-permute-start | bytes 442376 | tf_op jit(solution)/shard_map/ppermute | solution.py:147
  33.5 9.0 %collective-permute-start.8 = (f32[4,72,128]{2,1,0:T(8,128)}, f32[4,72,128]{2,1,0:T(8,128)}, u32[]{:S(2)}, u32[]{:S(2)}) collective-permute-start(f32[4,72,128]{2,1,0:T(8,128)} %get-tuple-element.16), channel_id=1, source_target_pairs={{0,192},{16,208},{32,224},{48,240},{64,128},{80,144},{96,160},{112... | collective-permute-start | bytes 442376 | tf_op jit(solution)/shard_map/ppermute | solution.py:147
  35.5 12.1 %collective-permute-start.2 = (f32[64,256]{1,0:T(8,128)S(1)}, f32[64,256]{1,0:T(8,128)S(1)}, u32[]{:S(2)}, u32[]{:S(2)}) collective-permute-start(f32[64,256]{1,0:T(8,128)S(1)} %reduce_sum.18), channel_id=1, source_target_pairs={{0,3},{1,2},{2,1},{3,0},{4,7},{5,6},{6,5},{7,4},{8,11},{9,10},{10,... | collective-permute-start | bytes 196616 | tf_op jit(solution)/shard_map/ppermute | solution.py:147
  38.6 9.0 %collective-permute-start.1 = (f32[64,256]{1,0:T(8,128)S(1)}, f32[64,256]{1,0:T(8,128)S(1)}, u32[]{:S(2)}, u32[]{:S(2)}) collective-permute-start(f32[64,256]{1,0:T(8,128)S(1)} %reduce_sum.18), channel_id=1, source_target_pairs={{0,2},{1,3},{2,0},{3,1},{4,6},{5,7},{6,4},{7,5},{8,10},{9,11},{10,... | collective-permute-start | bytes 196616 | tf_op jit(solution)/shard_map/ppermute | solution.py:147
  38.6 9.0 %collective-permute-start = (f32[64,256]{1,0:T(8,128)S(1)}, f32[64,256]{1,0:T(8,128)S(1)}, u32[]{:S(2)}, u32[]{:S(2)}) collective-permute-start(f32[64,256]{1,0:T(8,128)S(1)} %reduce_sum.18), channel_id=1, source_target_pairs={{0,1},{1,0},{2,3},{3,2},{4,5},{5,4},{6,7},{7,6},{8,9},{9,8},{10,11... | collective-permute-start | bytes 196616 | tf_op jit(solution)/shard_map/ppermute | solution.py:147
  44.0 19.6 %copy-start.4 = (s32[16]{0:T(128)S(1)}, s32[16]{0:T(128)}, u32[]{:S(2)}) copy-start(s32[16]{0:T(128)} %param.11) | copy-start | bytes 196
  44.0 8.4 %collective-permute-start.10 = (f32[72,128]{1,0:T(8,128)}, f32[72,128]{1,0:T(8,128)}, u32[]{:S(2)}, u32[]{:S(2)}) collective-permute-start(f32[72,128]{1,0:T(8,128)} %get-tuple-element.21), channel_id=1, source_target_pairs={{0,32},{16,48},{32,0},{48,16},{64,96},{80,112},{96,64},{112,80},{1... | collective-permute-start | bytes 110600 | tf_op jit(solution)/shard_map/ppermute | solution.py:147
  45.3 7.1 %collective-permute-start.11 = (f32[72,128]{1,0:T(8,128)}, f32[72,128]{1,0:T(8,128)}, u32[]{:S(2)}, u32[]{:S(2)}) collective-permute-start(f32[72,128]{1,0:T(8,128)} %get-tuple-element.22), channel_id=1, source_target_pairs={{0,48},{16,32},{32,16},{48,0},{64,112},{80,96},{96,80},{112,64},{1... | collective-permute-start | bytes 110600 | tf_op jit(solution)/shard_map/ppermute | solution.py:147
  47.6 4.8 %collective-permute-start.9 = (f32[72,128]{1,0:T(8,128)}, f32[72,128]{1,0:T(8,128)}, u32[]{:S(2)}, u32[]{:S(2)}) collective-permute-start(f32[72,128]{1,0:T(8,128)} %get-tuple-element.23), channel_id=1, source_target_pairs={{0,16},{16,0},{32,48},{48,32},{64,80},{80,64},{96,112},{112,96},{1... | collective-permute-start | bytes 110600 | tf_op jit(solution)/shard_map/ppermute | solution.py:147
  48.7 35.2 %all-to-all-start.1 = ((f32[16,64,256]{2,1,0:T(8,128)}), f32[16,64,256]{2,1,0:T(8,128)S(1)}, u32[]{:S(2)}, u32[]{:S(2)}) async-start(f32[16,64,256]{2,1,0:T(8,128)} %broadcast_in_dim.10), calls=%async_computation.1 | async-start | bytes 2097152 | tf_op jit(solution)/shard_map/all_to_all | solution.py:156
  52.4 59.3 %copy-start.3 = (f32[16,256]{1,0:T(8,128)S(1)}, f32[16,256]{1,0:T(8,128)}, u32[]{:S(2)}) copy-start(f32[16,256]{1,0:T(8,128)} %param.13) | copy-start | bytes 49156
  53.3 4.8 %collective-permute-start.12 = (f32[72,128]{1,0:T(8,128)S(1)}, f32[72,128]{1,0:T(8,128)S(1)}, u32[]{:S(2)}, u32[]{:S(2)}) collective-permute-start(f32[72,128]{1,0:T(8,128)S(1)} %fusion.10), channel_id=1, source_target_pairs={{0,4},{4,0},{8,12},{12,8},{1,5},{5,1},{9,13},{13,9},{2,6},{6,2},{1... | collective-permute-start | bytes 110600 | tf_op jit(solution)/shard_map/ppermute | solution.py:147
  58.1 3.1 %collective-permute-start.13 = (f32[72,128]{1,0:T(8,128)S(1)}, f32[72,128]{1,0:T(8,128)S(1)}, u32[]{:S(2)}, u32[]{:S(2)}) collective-permute-start(f32[72,128]{1,0:T(8,128)S(1)} %add.145), channel_id=1, source_target_pairs={{0,1},{1,0},{2,3},{3,2},{4,5},{5,4},{6,7},{7,6},{8,9},{9,8},{10,11... | collective-permute-start | bytes 110600 | tf_op jit(solution)/shard_map/ppermute | solution.py:147
  61.2 4.0 %collective-permute-start.14 = (f32[72,128]{1,0:T(8,128)S(1)}, f32[72,128]{1,0:T(8,128)S(1)}, u32[]{:S(2)}, u32[]{:S(2)}) collective-permute-start(f32[72,128]{1,0:T(8,128)S(1)} %add.146), channel_id=1, source_target_pairs={{0,2},{1,3},{2,0},{3,1},{4,6},{5,7},{6,4},{7,5},{8,10},{9,11},{10,... | collective-permute-start | bytes 110600 | tf_op jit(solution)/shard_map/ppermute | solution.py:147
  65.3 7.8 %collective-permute-start.15 = (f32[72,128]{1,0:T(8,128)S(1)}, f32[72,128]{1,0:T(8,128)S(1)}, u32[]{:S(2)}, u32[]{:S(2)}) collective-permute-start(f32[72,128]{1,0:T(8,128)S(1)} %add.147), channel_id=1, source_target_pairs={{0,8},{4,12},{8,0},{12,4},{1,9},{5,13},{9,1},{13,5},{2,10},{6,14},... | collective-permute-start | bytes 110600 | tf_op jit(solution)/shard_map/ppermute | solution.py:147
  73.1 4.8 %collective-permute-start.18 = (f32[72,128]{1,0:T(8,128)S(1)}, f32[72,128]{1,0:T(8,128)S(1)}, u32[]{:S(2)}, u32[]{:S(2)}) collective-permute-start(f32[72,128]{1,0:T(8,128)S(1)} %add.148), channel_id=1, source_target_pairs={{0,48},{16,32},{32,16},{48,0},{64,112},{80,96},{96,80},{112,64},{1... | collective-permute-start | bytes 110600 | tf_op jit(solution)/shard_map/ppermute | solution.py:147
  75.9 4.4 %collective-permute-start.17 = (f32[72,128]{1,0:T(8,128)S(1)}, f32[72,128]{1,0:T(8,128)S(1)}, u32[]{:S(2)}, u32[]{:S(2)}) collective-permute-start(f32[72,128]{1,0:T(8,128)S(1)} %add.148), channel_id=1, source_target_pairs={{0,32},{16,48},{32,0},{48,16},{64,96},{80,112},{96,64},{112,80},{1... | collective-permute-start | bytes 110600 | tf_op jit(solution)/shard_map/ppermute | solution.py:147
  76.5 3.8 %collective-permute-start.16 = (f32[72,128]{1,0:T(8,128)S(1)}, f32[72,128]{1,0:T(8,128)S(1)}, u32[]{:S(2)}, u32[]{:S(2)}) collective-permute-start(f32[72,128]{1,0:T(8,128)S(1)} %add.148), channel_id=1, source_target_pairs={{0,16},{16,0},{32,48},{48,32},{64,80},{80,64},{96,112},{112,96},{1... | collective-permute-start | bytes 110600 | tf_op jit(solution)/shard_map/ppermute | solution.py:147
  80.3 6.1 %collective-permute-start.21 = (f32[4,72,128]{2,1,0:T(8,128)S(1)}, f32[4,72,128]{2,1,0:T(8,128)S(1)}, u32[]{:S(2)}, u32[]{:S(2)}) collective-permute-start(f32[4,72,128]{2,1,0:T(8,128)S(1)} %pad_maximum_fusion.refs_1_), channel_id=1, source_target_pairs={{0,192},{16,208},{32,224},{48,240},{64,128},{80,144},{96,160},{112... | collective-permute-start | bytes 442376 | tf_op jit(solution)/shard_map/ppermute | solution.py:147
  82.8 5.6 %collective-permute-start.20 = (f32[4,72,128]{2,1,0:T(8,128)S(1)}, f32[4,72,128]{2,1,0:T(8,128)}, u32[]{:S(2)}, u32[]{:S(2)}) collective-permute-start(f32[4,72,128]{2,1,0:T(8,128)S(1)} %pad_maximum_fusion.refs_1_), channel_id=1, source_target_pairs={{0,128},{16,144},{32,160},{48,176},{64,192},{80,208},{96,224},{112... | collective-permute-start | bytes 442376 | tf_op jit(solution)/shard_map/ppermute | solution.py:147
  83.3 5.0 %collective-permute-start.19 = (f32[4,72,128]{2,1,0:T(8,128)S(1)}, f32[4,72,128]{2,1,0:T(8,128)}, u32[]{:S(2)}, u32[]{:S(2)}) collective-permute-start(f32[4,72,128]{2,1,0:T(8,128)S(1)} %pad_maximum_fusion.refs_1_), channel_id=1, source_target_pairs={{0,64},{16,80},{32,96},{48,112},{64,0},{80,16},{96,32},{112,48},{1... | collective-permute-start | bytes 442376 | tf_op jit(solution)/shard_map/ppermute | solution.py:147
  88.4 1.2 %copy-start.2 = (f32[16,128,128]{2,1,0:T(8,128)S(1)}, f32[16,128,128]{2,1,0:T(8,128)}, u32[]{:S(2)}) copy-start(f32[16,128,128]{2,1,0:T(8,128)} %refs_6_.1) | copy-start | bytes 3145732
  97.6 1.0 copy-start.1
  98.6 6.4 %collective-permute-start.22 = (f32[1,128]{1,0:T(1,128)S(1)}, f32[1,128]{1,0:T(1,128)S(1)}, u32[]{:S(2)}, u32[]{:S(2)}) collective-permute-start(f32[1,128]{1,0:T(1,128)S(1)} %slice.70), channel_id=1, source_target_pairs={{0,4},{4,0},{8,12},{12,8},{1,5},{5,1},{9,13},{13,9},{2,6},{6,2},{1... | collective-permute-start | bytes 1544 | tf_op jit(solution)/shard_map/ppermute | solution.py:147
  105.0 6.6 %collective-permute-start.23 = (f32[1,128]{1,0:T(1,128)S(1)}, f32[1,128]{1,0:T(1,128)S(1)}, u32[]{:S(2)}, u32[]{:S(2)}) collective-permute-start(f32[1,128]{1,0:T(1,128)S(1)} %slice_add_fusion.12), channel_id=1, source_target_pairs={{0,8},{4,12},{8,0},{12,4},{1,9},{5,13},{9,1},{13,5},{2,10},{6,14},... | collective-permute-start | bytes 1544 | tf_op jit(solution)/shard_map/ppermute | solution.py:147
Sparse Core Ops, SparseCore 0:
  24.1 52.8 all-gather.1

commit v4 on v3

v4 whole, which is shorter than its diff:
```python
import jax
import jax.numpy as jnp
from jax import lax
from jax.experimental import pallas as pl
from jax.experimental.pallas import tpu as pltpu
from jax.sharding import PartitionSpec as P

NS_STEPS = 4


exact_mode = lax.Precision.HIGHEST
decay_rate = 0.75
damping = 0.1
damp_shift = 0.001
clip_norm = 256.0
momentum_rate = 0.9
step_rate = 0.05


def sample_stats(samples, block_size):
    sample_rows, width = samples.shape
    blocks = samples.reshape(sample_rows, width // block_size, block_size)
    return jnp.einsum("tnb,tnc->nbc", blocks, blocks, preferred_element_type=jnp.float32)


def fold_kernel(left_ref, right_ref, old_ref, folded_ref, old_folded_ref):
    left_count, size, _ = left_ref.shape
    half = size // 2
    row = lax.broadcasted_iota(jnp.int32, (half, size), 0)
    col = lax.broadcasted_iota(jnp.int32, (half, size), 1)

    def fold_block(from_ref, at, to_ref, to):
        top = from_ref[at, :half, :]
        bottom = from_ref[at, half:, :]
        to_ref[to, :half, :] = jnp.where(col >= row, top, pltpu.roll(bottom, half, 1))
        diagonal = jnp.sum(jnp.where(col == row + half, bottom, 0.0), axis=0, keepdims=True)
        to_ref[to, half:, :] = jnp.broadcast_to(diagonal, (to_ref.shape[1] - half, size))

    def step(n, carry):
        fold_block(left_ref, n, folded_ref, n)
        fold_block(right_ref, n, folded_ref, n + left_count)
        return carry

    lax.fori_loop(0, left_count, step, 0)
    fold_block(old_ref, 0, old_folded_ref, 0)


def fold(left_stats, right_stats, old_block):
    count, size, _ = left_stats.shape
    rows = size // 2 + 8
    return pl.pallas_call(
        fold_kernel,
        out_shape=(
            jax.ShapeDtypeStruct((2 * count, rows, size), jnp.float32),
            jax.ShapeDtypeStruct((1, rows, size), jnp.float32),
        ),
        name="fold",
    )(left_stats, right_stats, old_block)


def dot(a, b):
    return jnp.dot(a, b, precision=exact_mode, preferred_element_type=jnp.float32)


def unfold(part, diagonal):
    half, size = part.shape
    row = lax.broadcasted_iota(jnp.int32, (half, size), 0)
    col = lax.broadcasted_iota(jnp.int32, (half, size), 1)
    turned = jnp.concatenate([part, jnp.zeros_like(part)], axis=0).T
    top = jnp.where(col >= row, part, turned[:half])
    corner = jnp.where(
        col < row + half, pltpu.roll(part, half, 1), pltpu.roll(turned[:half], half, 1)
    )
    corner = jnp.where(col == row + half, diagonal, corner)
    bottom = jnp.where(col < half, turned[half:], corner)
    return jnp.concatenate([top, bottom], axis=0)


def inverse_kernel(group, place_ref, folded_ref, inverse_ref, owned_ref):
    size = inverse_ref.shape[1]
    half = size // 2
    left_count = inverse_ref.shape[0] - place_ref[1]
    on_diagonal = lax.broadcasted_iota(jnp.int32, (size, size), 0) == lax.broadcasted_iota(
        jnp.int32, (size, size), 1
    )
    unit = jnp.where(on_diagonal, 1.0, 0.0)

    def load(block):
        return unfold(folded_ref[block, :half, :], folded_ref[block, half : half + 1, :])

    def invert(step, carry):
        powers, bounds, inverses = [], [], []
        for k in range(group):
            at = step * group + k
            mixed = load(jnp.where(at < left_count, at, place_ref[0] + at - left_count))
            trace = jnp.sum(jnp.where(on_diagonal, mixed, 0.0), keepdims=True)
            damped = mixed + jnp.where(on_diagonal, damping * trace / size + damp_shift, 0.0)
            bound = jnp.max(jnp.sum(jnp.abs(damped), axis=1, keepdims=True), keepdims=True)
            power = unit - damped / bound
            powers.append(power)
            bounds.append(bound)
            inverses.append(unit + power)
        for iteration in range(NS_STEPS - 1):
            powers = [dot(power, power) for power in powers]
            inverses = [x + dot(x, power) for x, power in zip(inverses, powers)]
        for k in range(group):
            inverse_ref[step * group + k] = inverses[k] / bounds[k]
        return carry

    lax.fori_loop(0, inverse_ref.shape[0] // group, invert, 0)

    def place_block(place, carry):
        block = place_ref[2 + place]
        value = load(jnp.maximum(block, 0))
        owned_ref[place] = jnp.where(block >= 0, value, jnp.zeros_like(value))
        return carry

    lax.fori_loop(0, owned_ref.shape[0], place_block, 0)


def invert_needed(places, folded, needed, capacity):
    size = folded.shape[2]
    group = 5
    return pl.pallas_call(
        lambda *refs: inverse_kernel(group, *refs),
        in_specs=[
            pl.BlockSpec(memory_space=pltpu.SMEM),
            pl.BlockSpec(memory_space=pltpu.VMEM),
        ],
        out_shape=(
            jax.ShapeDtypeStruct((needed, size, size), jnp.float32),
            jax.ShapeDtypeStruct((capacity, size, size), jnp.float32),
        ),
        name="inverse",
    )(places, folded)


def precondition_kernel(inverse_ref, grad_ref, precond_ref, align_ref):
    size = inverse_ref.shape[1]
    left_count = grad_ref.shape[0] // size
    right_count = grad_ref.shape[1] // size

    def step(a, total):
        first = pl.multiple_of(a * size, size)
        grad = grad_ref[pl.ds(first, size), :]
        left_part = dot(inverse_ref[a], grad)
        for c in range(right_count):
            cols = slice(c * size, (c + 1) * size)
            value = dot(left_part[:, cols], inverse_ref[left_count + c])
            precond_ref[pl.ds(first, size), cols] = value
            total = total + value * grad[:, cols]
        return total

    total = lax.fori_loop(0, left_count, step, jnp.zeros((size, size), jnp.float32), unroll=2)
    align_ref[...] = jnp.broadcast_to(jnp.sum(total, keepdims=True), align_ref.shape)


def precondition(inverses, gradient):
    return pl.pallas_call(
        precondition_kernel,
        out_shape=(
            jax.ShapeDtypeStruct(gradient.shape, jnp.float32),
            jax.ShapeDtypeStruct((8, 128), jnp.float32),
        ),
        name="precondition",
    )(inverses, gradient)


def swap(value, axis, flip):
    size = lax.axis_size(axis)
    return lax.ppermute(value, axis, [(i, i ^ flip) for i in range(size)])


def exchange(value, axis):
    return [value] + [swap(value, axis, flip) for flip in range(1, lax.axis_size(axis))]


def spread(value, axis):
    copies = jnp.broadcast_to(value[None], (lax.axis_size(axis),) + value.shape)
    return lax.all_to_all(copies, axis, 0, 0)


def body(activations, grads_out, grad_parts, old_factors, block_owner, weights, momentum):
    shard_count = lax.axis_size("shards")
    replica_count = lax.axis_size("replica")
    block_count = old_factors.shape[0]
    block_size = old_factors.shape[1]
    capacity = (block_count + shard_count - 1) // shard_count + 1
    sample_count = activations.shape[0] * shard_count * lax.axis_size("tensor") * replica_count
    partial_grad = grad_parts[0]
    row_count, col_count = partial_grad.shape
    left_count = row_count // block_size
    right_count = col_count // block_size
    piece_rows = row_count // shard_count
    own_rows = weights.shape[0]
    shard = lax.axis_index("shards")
    replica = lax.axis_index("replica")

    grad_in = lax.all_to_all(partial_grad.reshape(shard_count, piece_rows, col_count), "shards", 0, 0)

    old_block = lax.dynamic_slice_in_dim(old_factors, shard, 1, 0)
    folded, old_folded = fold(
        sample_stats(activations, block_size), sample_stats(grads_out, block_size), old_block
    )
    folded, grad_in = lax.optimization_barrier((folded, grad_in))
    stats_in = lax.all_to_all(folded, "shards", 0, 0)

    base = weights - (step_rate * momentum_rate) * momentum
    base_rows = lax.dynamic_update_slice_in_dim(
        jnp.zeros((piece_rows, col_count), jnp.float32), base, replica * own_rows, 0
    )
    own = sum(
        exchange(jnp.concatenate([jnp.sum(grad_in, axis=0), base_rows], axis=0), "replica")
    )
    own_grad = own[:piece_rows]
    base = lax.all_gather(own[piece_rows:], "shards", axis=0, tiled=True)

    own_stats = jnp.sum(stats_in, axis=0)
    own_stats, own_grad = lax.optimization_barrier((own_stats, own_grad))
    gradient = spread(own_grad, "shards").reshape(row_count, col_count)
    own_stats = own_stats + swap(own_stats, "tensor", 1)
    own_stats = sum(exchange(own_stats, "replica"))
    own_stats = own_stats + swap(own_stats, "tensor", 2)
    blended = decay_rate * old_folded[0] + ((1.0 - decay_rate) / sample_count) * own_stats
    blended, gradient = lax.optimization_barrier((blended, gradient))
    folded = spread(blended, "shards")

    positions = jnp.arange(block_count, dtype=jnp.int32)
    earlier = (block_owner[:, None] == block_owner[None, :]) & (
        positions[None, :] < positions[:, None]
    )
    slots = block_owner * capacity + jnp.sum(earlier.astype(jnp.int32), axis=1)
    own_slots = shard * capacity + jnp.arange(capacity, dtype=jnp.int32)
    holds = jnp.max(jnp.where(slots[None, :] == own_slots[:, None], positions[None, :], -1), axis=1)
    right_first = left_count + lax.axis_index("tensor") * right_count
    places = jnp.concatenate(
        [jnp.stack([right_first, jnp.asarray(right_count)]).astype(jnp.int32), holds]
    )
    inverses, owned_blocks = invert_needed(places, folded, left_count + right_count, capacity)
    precond, align = precondition(inverses, gradient)
    align, base = lax.optimization_barrier((align, base))
    align = align[:1]
    align = align + swap(align, "tensor", 1)
    align = align + swap(align, "tensor", 2)
    clip_scale = jnp.minimum(1.0, clip_norm / jnp.sqrt(align[0, 0]))
    first_row = (shard * replica_count + replica) * own_rows
    own_precond = lax.dynamic_slice_in_dim(precond, first_row, own_rows, 0)
    momentum_next = momentum_rate * momentum + clip_scale * own_precond
    weights_next = base - (step_rate * clip_scale) * precond
    return (weights_next, momentum_next, owned_blocks)


def solution(mesh):
    placed = (
        P(("shards", "tensor", "replica"), None),
        P(("shards", "tensor", "replica"), None),
        P(("shards", "replica"), None, "tensor"),
        P(),
        P(),
        P(("shards", "replica"), "tensor"),
        P(("shards", "replica"), "tensor"),
    )
    return jax.shard_map(
        body,
        mesh=mesh,
        in_specs=placed,
        out_specs=(P(None, "tensor"), P(("shards", "replica"), "tensor"), P("shards", None, None)),
        check_vma=False,
    )
```

time: 123 us -> 129 us (1.049)
  waiting for transfers between devices: 21.7 us -> 33 us
  starting transfers between devices: 58.1 us -> 50.2 us
  Pallas kernels: 10.2 us -> 16.3 us
  other arithmetic: 9.05 us -> 5.79 us
  matrix products: 5.94 us -> 3.77 us
  local copies, waits for them, and re-layouts: 3.28 us -> 4.97 us
    ppermute x24 -> x10, starting transfers between devices: 47.6 us -> 28 us  [swap(): return lax.ppermute(value, axis, [(i, i ^ flip) for i in range(size)])]
    all_to_all x1 -> x2, waiting for transfers between devices: 0.01 us -> 8.86 us  [spread(): return lax.all_to_all(copies, axis, 0, 0)]
    all_to_all x1 -> x2, starting transfers between devices: 3.66 us -> 10.5 us  [spread(): return lax.all_to_all(copies, axis, 0, 0)]
    ppermute x24 -> x10, waiting for transfers between devices: 19.8 us -> 13.5 us  [swap(): return lax.ppermute(value, axis, [(i, i ^ flip) for i in range(size)])]
    pallas_call x2 -> x3, Pallas kernels: 10.2 us -> 16.3 us  [the longest x1 7.77 us: invert_needed(): pl.pallas_call(lambda *refs: inverse_kernel(group, *refs), in_specs=[pl.B...]
    all_to_all x1, waiting for transfers between devices: 1.81 us -> 7.34 us  [body(): lax.all_to_all(partial_grad.reshape(shard_count, piece_rows, col_count),...]
    all_to_all x0 -> x1, starting transfers between devices: none -> 3.97 us  [body(): stats_in = lax.all_to_all(folded, 'shards', 0, 0)]
    all_to_all x0 -> x1, waiting for transfers between devices: none -> 3.28 us  [body(): stats_in = lax.all_to_all(folded, 'shards', 0, 0)]
  transfers between devices with their start and end apart: 27 -> 15, of which waited for: 13 -> 10; matrix products, arithmetic and copies ran while one was open for 9% -> 7% of each run, Pallas kernels for 2% -> 13%
where the time goes in v4:
time: 129 us; the launch traced here: 128 us
  starting transfers between devices  50.2 us (39%)
  waiting for transfers between devices  33 us (26%)
  Pallas kernels  16.3 us (13%)
  between operations  14.3 us (11%)
  other arithmetic  5.79 us (4%)
  local copies, waits for them, and re-layouts  4.97 us (4%)
  matrix products  3.77 us (3%)
    ppermute x10, starting transfers between devices, swap(): return lax.ppermute(value, axis, [(i, i ^ flip) for i in range(size)])  28 us
    ppermute x10, waiting for transfers between devices, swap(): return lax.ppermute(value, axis, [(i, i ^ flip) for i in range(size)])  13.5 us
    all_to_all x2, starting transfers between devices, spread(): return lax.all_to_all(copies, axis, 0, 0)  10.5 us
    all_to_all x2, waiting for transfers between devices, spread(): return lax.all_to_all(copies, axis, 0, 0)  8.86 us
    pallas_call x1, Pallas kernels, invert_needed(): pl.pallas_call(lambda *refs: inverse_kernel(group, *refs), in_specs=[pl.B...  7.77 us
    all_to_all x1, starting transfers between devices, body(): lax.all_to_all(partial_grad.reshape(shard_count, piece_rows, col_count),...  7.73 us
    all_to_all x1, waiting for transfers between devices, body(): lax.all_to_all(partial_grad.reshape(shard_count, piece_rows, col_count),...  7.34 us
    pallas_call x1, Pallas kernels, precondition(): pl.pallas_call(precondition_kernel, out_shape=(jax.ShapeDtypeStruct(gradi...  5.79 us
  transfers between devices with their start and end apart: 15, of which 10 were waited for; matrix products, arithmetic and copies ran while one was open for 7% of the time, Pallas kernels for 13%

profile of v4, /device:TPU:1, one launch (start us, length us, event | category | flops | bytes accessed | tf_op | source)
XLA Modules:
  0.0 128.3 jit_solution(4573443471195022097)
XLA Ops:
  7.2 0.0 copy-start
  7.2 7.7 %all-to-all-start = ((f32[16,64,256]{2,1,0:T(8,128)}), f32[16,64,256]{2,1,0:T(8,128)S(1)}, u32[]{:S(2)}, u32[]{:S(2)}) async-start(f32[16,64,256]{2,1,0:T(8,128)} %bitcast.22), calls=%async_computation | async-start | bytes 2097152 | tf_op jit(solution)/shard_map/all_to_all | solution.py:199
  14.9 0.0 copy-start.5
  14.9 1.6 %constant_dynamic-slice_fusion.old_ref = f32[1,128,128]{2,1,0:T(8,128)} fusion(f32[16,128,128]{2,1,0:T(8,128)} %param.10, s32[]{:T(128)S(6)} %select_n.14), kind=kLoop, calls=%fused_computation.18 | loop fusion | bytes 131076 | tf_op jit(solution)/shard_map/dynamic_slice | solution.py:201
  16.6 1.8 %fusion.3.left_ref = f32[8,128,128]{2,1,0:T(8,128)} fusion(bf16[1024,1024]{1,0:T(8,128)(2,1)S(1)} %copy-done), kind=kOutput, calls=%fused_computation.3 | convolution fusion | flops 268435456 | bytes 2621440 | tf_op jit(solution)/shard_map/tnb,tnc->nbc/dot_general | solution.py:23
  18.4 1.9 %fusion.right_ref = f32[8,128,128]{2,1,0:T(8,128)} fusion(bf16[1024,1024]{1,0:T(8,128)(2,1)S(1)} %copy-done.5), kind=kOutput, calls=%fused_computation | convolution fusion | flops 268435456 | bytes 2621440 | tf_op jit(solution)/shard_map/tnb,tnc->nbc/dot_general | solution.py:23
  20.3 2.7 %fold.1 = (f32[16,72,128]{2,1,0:T(8,128)}, f32[1,72,128]{2,1,0:T(8,128)}) custom-call(f32[8,128,128]{2,1,0:T(8,128)} %fusion.3.left_ref, f32[8,128,128]{2,1,0:T(8,128)} %fusion.right_ref, f32[1,128,128]{2,1,0:T(8,128)} %constant_dynamic-slice_fusion.old_ref), custom_call_target="tpu_custom_call" | custom-call | tf_op jit(solution)/shard_map/fold/pallas_call | solution.py:51
  23.1 7.3 %all-to-all-done = f32[16,64,256]{2,1,0:T(8,128)S(1)} async-done(((f32[16,64,256]{2,1,0:T(8,128)}), f32[16,64,256]{2,1,0:T(8,128)S(1)}, u32[]{:S(2)}, u32[]{:S(2)}) %all-to-all-start) | async-done | bytes 1048608 | tf_op jit(solution)/shard_map/all_to_all | solution.py:199
  30.4 0.1 reduce_sum.29
  30.5 4.4 %collective-permute-start.2 = (f32[128,256]{1,0:T(8,128)S(1)}, f32[128,256]{1,0:T(8,128)S(1)}, u32[]{:S(2)}, u32[]{:S(2)}) collective-permute-start(f32[128,256]{1,0:T(8,128)S(1)} %pad_maximum_fusion), channel_id=1, source_target_pairs={{0,3},{1,2},{2,1},{3,0},{4,7},{5,6},{6,5},{7,4},{8,11},{9,10},{10,... | collective-permute-start | bytes 393224 | tf_op jit(solution)/shard_map/ppermute | solution.py:171
  34.9 0.0 collective-permute-start.1
  34.9 0.4 collective-permute-start
  35.3 4.0 %all-to-all-start.1 = ((f32[16,72,128]{2,1,0:T(8,128)}), f32[16,72,128]{2,1,0:T(8,128)S(1)}, u32[]{:S(2)}, u32[]{:S(2)}) async-start(f32[16,72,128]{2,1,0:T(8,128)} %get-tuple-element.19), calls=%async_computation.1 | async-start | bytes 1179648 | tf_op jit(solution)/shard_map/all_to_all | solution.py:206
  39.3 0.0 all-gather.2.cloned.1.call-start
  39.3 0.0 collective-permute-done.2
  39.4 5.3 %collective-permute-done.1 = f32[128,256]{1,0:T(8,128)S(1)} collective-permute-done((f32[128,256]{1,0:T(8,128)S(1)}, f32[128,256]{1,0:T(8,128)S(1)}, u32[]{:S(2)}, u32[]{:S(2)}) %collective-permute-start.1) | collective-permute-done | bytes 131104 | tf_op jit(solution)/shard_map/ppermute | solution.py:171
  44.7 0.0 collective-permute-done
  44.7 0.6 fusion.8
  45.4 0.0 all-gather.2.cloned.1.call-update
  45.4 3.3 %all-to-all-done.1 = f32[16,72,128]{2,1,0:T(8,128)S(1)} async-done(((f32[16,72,128]{2,1,0:T(8,128)}), f32[16,72,128]{2,1,0:T(8,128)S(1)}, u32[]{:S(2)}, u32[]{:S(2)}) %all-to-all-start.1) | async-done | bytes 589856 | tf_op jit(solution)/shard_map/all_to_all | solution.py:206
  48.7 1.1 broadcast_in_dim.17
  49.8 3.7 %all-to-all-start.2 = ((f32[16,64,256]{2,1,0:T(8,128)}), f32[16,64,256]{2,1,0:T(8,128)S(1)}, u32[]{:S(2)}, u32[]{:S(2)}) async-start(f32[16,64,256]{2,1,0:T(8,128)} %broadcast_in_dim.17), calls=%async_computation.2 | async-start | bytes 2097152 | tf_op jit(solution)/shard_map/all_to_all | solution.py:180
  53.4 4.4 %collective-permute-start.3 = (f32[72,128]{1,0:T(8,128)S(1)}, f32[72,128]{1,0:T(8,128)S(1)}, u32[]{:S(2)}, u32[]{:S(2)}) collective-permute-start(f32[72,128]{1,0:T(8,128)S(1)} %reduce_sum.28), channel_id=1, source_target_pairs={{0,4},{4,0},{8,12},{12,8},{1,5},{5,1},{9,13},{13,9},{2,6},{6,2},{1... | collective-permute-start | bytes 110600 | tf_op jit(solution)/shard_map/ppermute | solution.py:171
  57.9 0.9 collective-permute-done.3
  58.8 3.4 %collective-permute-start.6 = (f32[72,128]{1,0:T(8,128)S(1)}, f32[72,128]{1,0:T(8,128)S(1)}, u32[]{:S(2)}, u32[]{:S(2)}) collective-permute-start(f32[72,128]{1,0:T(8,128)S(1)} %add.69), channel_id=1, source_target_pairs={{0,3},{1,2},{2,1},{3,0},{4,7},{5,6},{6,5},{7,4},{8,11},{9,10},{10,... | collective-permute-start | bytes 110600 | tf_op jit(solution)/shard_map/ppermute | solution.py:171
  62.2 0.4 collective-permute-start.4
  62.6 1.3 collective-permute-done.6
  63.8 2.4 %collective-permute-done.5 = f32[72,128]{1,0:T(8,128)S(1)} collective-permute-done((f32[72,128]{1,0:T(8,128)S(1)}, f32[72,128]{1,0:T(8,128)S(1)}, u32[]{:S(2)}, u32[]{:S(2)}) %collective-permute-start.5) | collective-permute-done | bytes 36896 | tf_op jit(solution)/shard_map/ppermute | solution.py:171
  66.2 0.0 collective-permute-done.4
  66.2 5.2 %collective-permute-start.7 = (f32[72,128]{1,0:T(8,128)S(1)}, f32[72,128]{1,0:T(8,128)S(1)}, u32[]{:S(2)}, u32[]{:S(2)}) collective-permute-start(f32[72,128]{1,0:T(8,128)S(1)} %add_add_fusion.1), channel_id=1, source_target_pairs={{0,8},{4,12},{8,0},{12,4},{1,9},{5,13},{9,1},{13,5},{2,10},{6,14},... | collective-permute-start | bytes 110600 | tf_op jit(solution)/shard_map/ppermute | solution.py:171
  71.5 0.2 convert_reduce_fusion
  71.7 1.4 %collective-permute-done.7 = f32[72,128]{1,0:T(8,128)S(1)} collective-permute-done((f32[72,128]{1,0:T(8,128)S(1)}, f32[72,128]{1,0:T(8,128)S(1)}, u32[]{:S(2)}, u32[]{:S(2)}) %collective-permute-start.7) | collective-permute-done | bytes 36896 | tf_op jit(solution)/shard_map/ppermute | solution.py:171
  73.1 0.0 copy-start.1
  73.1 0.9 broadcast_in_dim.18
  74.0 6.8 %all-to-all-start.3 = ((f32[16,72,128]{2,1,0:T(8,128)}), f32[16,72,128]{2,1,0:T(8,128)}, u32[]{:S(2)}, u32[]{:S(2)}) async-start(f32[16,72,128]{2,1,0:T(8,128)} %broadcast_in_dim.18), calls=%async_computation.3 | async-start | bytes 1179648 | tf_op jit(solution)/shard_map/all_to_all | solution.py:180
  80.9 0.2 fusion.7
  81.1 0.6 pad_add_fusion.refs_0_
  81.6 8.9 %all-to-all-done.3.refs_1_ = f32[16,72,128]{2,1,0:T(8,128)} async-done(((f32[16,72,128]{2,1,0:T(8,128)}), f32[16,72,128]{2,1,0:T(8,128)}, u32[]{:S(2)}, u32[]{:S(2)}) %all-to-all-start.3) | async-done | bytes 589856 | tf_op jit(solution)/shard_map/all_to_all | solution.py:180
  90.5 7.8 %inverse.1 = (f32[10,128,128]{2,1,0:T(8,128)}, f32[2,128,128]{2,1,0:T(8,128)}) custom-call(s32[4]{0:T(128)} %pad_add_fusion.refs_0_, f32[16,72,128]{2,1,0:T(8,128)} %all-to-all-done.3.refs_1_), custom_call_target="tpu_custom_call" | custom-call | tf_op jit(solution)/shard_map/inverse/pallas_call | solution.py:124
  98.2 5.8 %precondition.1 = (f32[1024,256]{1,0:T(8,128)}, f32[8,128]{1,0:T(8,128)}) custom-call(f32[10,128,128]{2,1,0:T(8,128)} %get-tuple-element.24.inverse_ref, f32[1024,256]{1,0:T(8,128)} %bitcast.21), custom_call_target="tpu_custom_call" | custom-call | tf_op jit(solution)/shard_map/precondition/pallas_call | solution.py:159
  104.0 0.7 slice.14
  104.7 4.8 %collective-permute-start.8 = (f32[1,128]{1,0:T(1,128)S(1)}, f32[1,128]{1,0:T(1,128)S(1)}, u32[]{:S(2)}, u32[]{:S(2)}) collective-permute-start(f32[1,128]{1,0:T(1,128)S(1)} %slice.14), channel_id=1, source_target_pairs={{0,4},{4,0},{8,12},{12,8},{1,5},{5,1},{9,13},{13,9},{2,6},{6,2},{1... | collective-permute-start | bytes 1544 | tf_op jit(solution)/shard_map/ppermute | solution.py:171
  109.6 0.8 collective-permute-done.8
  110.4 0.7 slice_add_fusion
  111.1 4.9 %collective-permute-start.9 = (f32[1,128]{1,0:T(1,128)S(1)}, f32[1,128]{1,0:T(1,128)S(1)}, u32[]{:S(2)}, u32[]{:S(2)}) collective-permute-start(f32[1,128]{1,0:T(1,128)S(1)} %slice_add_fusion), channel_id=1, source_target_pairs={{0,8},{4,12},{8,0},{12,4},{1,9},{5,13},{9,1},{13,5},{2,10},{6,14},... | collective-permute-start | bytes 1544 | tf_op jit(solution)/shard_map/ppermute | solution.py:171
  115.9 1.4 %collective-permute-done.9 = f32[1,128]{1,0:T(1,128)S(1)} collective-permute-done((f32[1,128]{1,0:T(1,128)S(1)}, f32[1,128]{1,0:T(1,128)S(1)}, u32[]{:S(2)}, u32[]{:S(2)}) %collective-permute-start.9) | collective-permute-done | bytes 544 | tf_op jit(solution)/shard_map/ppermute | solution.py:171
  117.5 1.3 %multiply_add_fusion = f32[16,256]{1,0:T(8,128)} fusion(f32[1024,256]{1,0:T(8,128)} %get-tuple-element.29, s32[]{:T(128)S(6)} %select_n.16, f32[16,256]{1,0:T(8,128)S(1)} %copy-done.2, f32[]{:T(128)} %bitcast.4), kind=kLoop, calls=%fused_computation.11 | loop fusion | flops 12288 | bytes 49160 | tf_op jit(solution)/shard_map/add | solution.py:248
  118.8 2.6 %multiply_subtract_fusion = f32[1024,256]{1,0:T(8,128)} fusion(f32[1024,256]{1,0:T(8,128)} %all-gather.2.cloned.1.call-done, f32[1024,256]{1,0:T(8,128)} %get-tuple-element.29, f32[]{:T(128)S(6)} %mul_shard_map.3), kind=kLoop, calls=%fused_computation.6 | loop fusion | flops 524288 | bytes 3145732 | tf_op jit(solution)/shard_map/sub | solution.py:249
  (25 shorter events, 0.2 us)
Async XLA Ops:
  7.2 9.4 %copy-start = (bf16[1024,1024]{1,0:T(8,128)(2,1)S(1)}, bf16[1024,1024]{1,0:T(8,128)(2,1)}, u32[]{:S(2)}) copy-start(bf16[1024,1024]{1,0:T(8,128)(2,1)} %param.7) | copy-start | bytes 6291460
  7.2 23.2 %all-to-all-start = ((f32[16,64,256]{2,1,0:T(8,128)}), f32[16,64,256]{2,1,0:T(8,128)S(1)}, u32[]{:S(2)}, u32[]{:S(2)}) async-start(f32[16,64,256]{2,1,0:T(8,128)} %bitcast.22), calls=%async_computation | async-start | bytes 2097152 | tf_op jit(solution)/shard_map/all_to_all | solution.py:199
  14.9 3.5 %copy-start.5 = (bf16[1024,1024]{1,0:T(8,128)(2,1)S(1)}, bf16[1024,1024]{1,0:T(8,128)(2,1)}, u32[]{:S(2)}) copy-start(bf16[1024,1024]{1,0:T(8,128)(2,1)} %param.8) | copy-start | bytes 6291460
  18.4 4.6 %copy-start.2 = (f32[16,256]{1,0:T(8,128)S(1)}, f32[16,256]{1,0:T(8,128)}, u32[]{:S(2)}) copy-start(f32[16,256]{1,0:T(8,128)} %param.13) | copy-start | bytes 49156
  18.4 4.7 %copy-start.4 = (f32[16,256]{1,0:T(8,128)S(1)}, f32[16,256]{1,0:T(8,128)}, u32[]{:S(2)}) copy-start(f32[16,256]{1,0:T(8,128)} %param.12) | copy-start | bytes 49156
  30.5 8.8 %collective-permute-start.2 = (f32[128,256]{1,0:T(8,128)S(1)}, f32[128,256]{1,0:T(8,128)S(1)}, u32[]{:S(2)}, u32[]{:S(2)}) collective-permute-start(f32[128,256]{1,0:T(8,128)S(1)} %pad_maximum_fusion), channel_id=1, source_target_pairs={{0,3},{1,2},{2,1},{3,0},{4,7},{5,6},{6,5},{7,4},{8,11},{9,10},{10,... | collective-permute-start | bytes 393224 | tf_op jit(solution)/shard_map/ppermute | solution.py:171
  34.9 9.7 %collective-permute-start.1 = (f32[128,256]{1,0:T(8,128)S(1)}, f32[128,256]{1,0:T(8,128)S(1)}, u32[]{:S(2)}, u32[]{:S(2)}) collective-permute-start(f32[128,256]{1,0:T(8,128)S(1)} %pad_maximum_fusion), channel_id=1, source_target_pairs={{0,2},{1,3},{2,0},{3,1},{4,6},{5,7},{6,4},{7,5},{8,10},{9,11},{10,... | collective-permute-start | bytes 393224 | tf_op jit(solution)/shard_map/ppermute | solution.py:171
  34.9 9.7 %collective-permute-start = (f32[128,256]{1,0:T(8,128)S(1)}, f32[128,256]{1,0:T(8,128)S(1)}, u32[]{:S(2)}, u32[]{:S(2)}) collective-permute-start(f32[128,256]{1,0:T(8,128)S(1)} %pad_maximum_fusion), channel_id=1, source_target_pairs={{0,1},{1,0},{2,3},{3,2},{4,5},{5,4},{6,7},{7,6},{8,9},{9,8},{10,11... | collective-permute-start | bytes 393224 | tf_op jit(solution)/shard_map/ppermute | solution.py:171
  35.3 13.3 %all-to-all-start.1 = ((f32[16,72,128]{2,1,0:T(8,128)}), f32[16,72,128]{2,1,0:T(8,128)S(1)}, u32[]{:S(2)}, u32[]{:S(2)}) async-start(f32[16,72,128]{2,1,0:T(8,128)} %get-tuple-element.19), calls=%async_computation.1 | async-start | bytes 1179648 | tf_op jit(solution)/shard_map/all_to_all | solution.py:206
  39.3 64.7 %all-gather.2.cloned.1.call-start = ((), (), s32[]{:S(2)}) async-start(), calls=%async_computation.4 | async-start | bytes 1114112 | tf_op jit(solution)/shard_map/all_gather | solution.py:216
  45.4 26.1 %copy-start.6 = (s32[16]{0:T(128)S(1)}, s32[16]{0:T(128)}, u32[]{:S(2)}) copy-start(s32[16]{0:T(128)} %param.11) | copy-start | bytes 196
  45.4 27.7 %copy-start.3 = (f32[1,72,128]{2,1,0:T(8,128)S(1)}, f32[1,72,128]{2,1,0:T(8,128)}, u32[]{:S(2)}) copy-start(f32[1,72,128]{2,1,0:T(8,128)} %get-tuple-element.17) | copy-start | bytes 110596
  49.8 23.3 %all-to-all-start.2 = ((f32[16,64,256]{2,1,0:T(8,128)}), f32[16,64,256]{2,1,0:T(8,128)S(1)}, u32[]{:S(2)}, u32[]{:S(2)}) async-start(f32[16,64,256]{2,1,0:T(8,128)} %broadcast_in_dim.17), calls=%async_computation.2 | async-start | bytes 2097152 | tf_op jit(solution)/shard_map/all_to_all | solution.py:180
  53.4 5.3 %collective-permute-start.3 = (f32[72,128]{1,0:T(8,128)S(1)}, f32[72,128]{1,0:T(8,128)S(1)}, u32[]{:S(2)}, u32[]{:S(2)}) collective-permute-start(f32[72,128]{1,0:T(8,128)S(1)} %reduce_sum.28), channel_id=1, source_target_pairs={{0,4},{4,0},{8,12},{12,8},{1,5},{5,1},{9,13},{13,9},{2,6},{6,2},{1... | collective-permute-start | bytes 110600 | tf_op jit(solution)/shard_map/ppermute | solution.py:171
  58.8 5.1 %collective-permute-start.6 = (f32[72,128]{1,0:T(8,128)S(1)}, f32[72,128]{1,0:T(8,128)S(1)}, u32[]{:S(2)}, u32[]{:S(2)}) collective-permute-start(f32[72,128]{1,0:T(8,128)S(1)} %add.69), channel_id=1, source_target_pairs={{0,3},{1,2},{2,1},{3,0},{4,7},{5,6},{6,5},{7,4},{8,11},{9,10},{10,... | collective-permute-start | bytes 110600 | tf_op jit(solution)/shard_map/ppermute | solution.py:171
  62.2 4.0 %collective-permute-start.5 = (f32[72,128]{1,0:T(8,128)S(1)}, f32[72,128]{1,0:T(8,128)S(1)}, u32[]{:S(2)}, u32[]{:S(2)}) collective-permute-start(f32[72,128]{1,0:T(8,128)S(1)} %add.69), channel_id=1, source_target_pairs={{0,2},{1,3},{2,0},{3,1},{4,6},{5,7},{6,4},{7,5},{8,10},{9,11},{10,... | collective-permute-start | bytes 110600 | tf_op jit(solution)/shard_map/ppermute | solution.py:171
  62.2 4.0 %collective-permute-start.4 = (f32[72,128]{1,0:T(8,128)S(1)}, f32[72,128]{1,0:T(8,128)S(1)}, u32[]{:S(2)}, u32[]{:S(2)}) collective-permute-start(f32[72,128]{1,0:T(8,128)S(1)} %add.69), channel_id=1, source_target_pairs={{0,1},{1,0},{2,3},{3,2},{4,5},{5,4},{6,7},{7,6},{8,9},{9,8},{10,11... | collective-permute-start | bytes 110600 | tf_op jit(solution)/shard_map/ppermute | solution.py:171
  66.2 6.8 %collective-permute-start.7 = (f32[72,128]{1,0:T(8,128)S(1)}, f32[72,128]{1,0:T(8,128)S(1)}, u32[]{:S(2)}, u32[]{:S(2)}) collective-permute-start(f32[72,128]{1,0:T(8,128)S(1)} %add_add_fusion.1), channel_id=1, source_target_pairs={{0,8},{4,12},{8,0},{12,4},{1,9},{5,13},{9,1},{13,5},{2,10},{6,14},... | collective-permute-start | bytes 110600 | tf_op jit(solution)/shard_map/ppermute | solution.py:171
  73.1 25.2 %copy-start.1 = (f32[16,64,256]{2,1,0:T(8,128)}, f32[16,64,256]{2,1,0:T(8,128)S(1)}, u32[]{:S(2)}) copy-start(f32[16,64,256]{2,1,0:T(8,128)S(1)} %all-to-all-done.2) | copy-start | bytes 3145732
  74.0 16.5 %all-to-all-start.3 = ((f32[16,72,128]{2,1,0:T(8,128)}), f32[16,72,128]{2,1,0:T(8,128)}, u32[]{:S(2)}, u32[]{:S(2)}) async-start(f32[16,72,128]{2,1,0:T(8,128)} %broadcast_in_dim.18), calls=%async_computation.3 | async-start | bytes 1179648 | tf_op jit(solution)/shard_map/all_to_all | solution.py:180
  104.7 5.7 %collective-permute-start.8 = (f32[1,128]{1,0:T(1,128)S(1)}, f32[1,128]{1,0:T(1,128)S(1)}, u32[]{:S(2)}, u32[]{:S(2)}) collective-permute-start(f32[1,128]{1,0:T(1,128)S(1)} %slice.14), channel_id=1, source_target_pairs={{0,4},{4,0},{8,12},{12,8},{1,5},{5,1},{9,13},{13,9},{2,6},{6,2},{1... | collective-permute-start | bytes 1544 | tf_op jit(solution)/shard_map/ppermute | solution.py:171
  111.1 6.3 %collective-permute-start.9 = (f32[1,128]{1,0:T(1,128)S(1)}, f32[1,128]{1,0:T(1,128)S(1)}, u32[]{:S(2)}, u32[]{:S(2)}) collective-permute-start(f32[1,128]{1,0:T(1,128)S(1)} %slice_add_fusion), channel_id=1, source_target_pairs={{0,8},{4,12},{8,0},{12,4},{1,9},{5,13},{9,1},{13,5},{2,10},{6,14},... | collective-permute-start | bytes 1544 | tf_op jit(solution)/shard_map/ppermute | solution.py:171
Sparse Core Ops, SparseCore 0:
  45.5 54.1 all-gather.1

commit v5 on v3

v5 whole, which is shorter than its diff:
```python
import jax
import jax.numpy as jnp
from jax import lax
from jax.experimental import pallas as pl
from jax.experimental.pallas import tpu as pltpu
from jax.sharding import PartitionSpec as P

NS_STEPS = 4


exact_mode = lax.Precision.HIGHEST
decay_rate = 0.75
damping = 0.1
damp_shift = 0.001
clip_norm = 256.0
momentum_rate = 0.9
step_rate = 0.05


def sample_stats(samples, block_size):
    sample_rows, width = samples.shape
    blocks = samples.reshape(sample_rows, width // block_size, block_size)
    return jnp.einsum("tnb,tnc->nbc", blocks, blocks, preferred_element_type=jnp.float32)


def fold_block(block, rows):
    size = block.shape[1]
    half = size // 2
    row = lax.broadcasted_iota(jnp.int32, (half, size), 0)
    col = lax.broadcasted_iota(jnp.int32, (half, size), 1)
    top, bottom = block[:half], block[half:]
    triangle = jnp.where(col >= row, top, pltpu.roll(bottom, half, 1))
    diagonal = jnp.sum(jnp.where(col == row + half, bottom, 0.0), axis=0, keepdims=True)
    return triangle, jnp.broadcast_to(diagonal, (rows - half, size))


def fold_kernel(place_ref, left_ref, right_ref, *folded_refs):
    left_count, size, _ = left_ref.shape
    side = len(folded_refs)
    rows = folded_refs[0].shape[1]
    for k in range(side):
        for j in range(side):
            n = (place_ref[0] ^ k) * side + (place_ref[1] ^ j)
            at = n % left_count
            triangle, diagonal = fold_block(
                jnp.where(n < left_count, left_ref[at], right_ref[at]), rows
            )
            folded_refs[k][j, : size // 2, :] = triangle
            folded_refs[k][j, size // 2 :, :] = diagonal


def fold(places, left_stats, right_stats, side):
    size = left_stats.shape[1]
    return pl.pallas_call(
        fold_kernel,
        in_specs=[
            pl.BlockSpec(memory_space=pltpu.SMEM),
            pl.BlockSpec(memory_space=pltpu.VMEM),
            pl.BlockSpec(memory_space=pltpu.VMEM),
        ],
        out_shape=[jax.ShapeDtypeStruct((side, size // 2 + 8, size), jnp.float32)] * side,
        name="fold",
    )(places, left_stats, right_stats)


def fold_one_kernel(block_ref, folded_ref):
    half = block_ref.shape[1] // 2
    triangle, diagonal = fold_block(block_ref[0], folded_ref.shape[0])
    folded_ref[:half, :] = triangle
    folded_ref[half:, :] = diagonal


def fold_one(block):
    size = block.shape[2]
    return pl.pallas_call(
        fold_one_kernel,
        out_shape=jax.ShapeDtypeStruct((size // 2 + 8, size), jnp.float32),
        name="fold_one",
    )(block)


def dot(a, b):
    return jnp.dot(a, b, precision=exact_mode, preferred_element_type=jnp.float32)


def unfold(part, diagonal):
    half, size = part.shape
    row = lax.broadcasted_iota(jnp.int32, (half, size), 0)
    col = lax.broadcasted_iota(jnp.int32, (half, size), 1)
    turned = jnp.concatenate([part, jnp.zeros_like(part)], axis=0).T
    top = jnp.where(col >= row, part, turned[:half])
    corner = jnp.where(
        col < row + half, pltpu.roll(part, half, 1), pltpu.roll(turned[:half], half, 1)
    )
    corner = jnp.where(col == row + half, diagonal, corner)
    bottom = jnp.where(col < half, turned[half:], corner)
    return jnp.concatenate([top, bottom], axis=0)


def update_kernel(side, place_ref, *refs):
    folded_refs = refs[:side]
    grad_ref, precond_ref, owned_ref, align_ref, blended_ref = refs[side:]
    size = blended_ref.shape[2]
    half = blended_ref.shape[1] - 8
    right_count = grad_ref.shape[1] // size
    left_count = grad_ref.shape[0] // size
    for k in range(side):
        for j in range(side):
            n = (place_ref[0] ^ k) * side + (place_ref[1] ^ j)
            blended_ref[n] = folded_refs[k][j]

    def load(block):
        return unfold(blended_ref[block, :half, :], blended_ref[block, half : half + 1, :])

    on_diagonal = lax.broadcasted_iota(jnp.int32, (size, size), 0) == lax.broadcasted_iota(
        jnp.int32, (size, size), 1
    )
    unit = jnp.where(on_diagonal, 1.0, 0.0)
    powers, bounds, inverses = [], [], []
    for block in list(range(left_count)) + [place_ref[2] + n for n in range(right_count)]:
        mixed = load(block)
        trace = jnp.sum(jnp.where(on_diagonal, mixed, 0.0), keepdims=True)
        damped = mixed + jnp.where(on_diagonal, damping * trace / size + damp_shift, 0.0)
        bound = jnp.max(jnp.sum(jnp.abs(damped), axis=1, keepdims=True), keepdims=True)
        power = unit - damped / bound
        powers.append(power)
        bounds.append(bound)
        inverses.append(unit + power)
    for step in range(NS_STEPS - 1):
        powers = [dot(power, power) for power in powers]
        inverses = [x + dot(x, power) for x, power in zip(inverses, powers)]
    inverses = [x / bound for x, bound in zip(inverses, bounds)]

    total = jnp.zeros((size, size), jnp.float32)
    for a in range(left_count):
        rows = slice(a * size, (a + 1) * size)
        left_part = dot(inverses[a], grad_ref[rows, :])
        for c in range(right_count):
            cols = slice(c * size, (c + 1) * size)
            value = dot(left_part[:, cols], inverses[left_count + c])
            precond_ref[rows, cols] = value
            total = total + value * grad_ref[rows, cols]
    align_ref[...] = jnp.broadcast_to(jnp.sum(total, keepdims=True), align_ref.shape)

    for place in range(owned_ref.shape[0]):
        block = place_ref[3 + place]
        value = load(jnp.maximum(block, 0))
        owned_ref[place] = jnp.where(block >= 0, value, jnp.zeros_like(value))


def update(places, folded, gradient, capacity):
    side, rows, size = folded[0].shape
    return pl.pallas_call(
        lambda *refs: update_kernel(side, *refs),
        in_specs=[pl.BlockSpec(memory_space=pltpu.SMEM)]
        + [pl.BlockSpec(memory_space=pltpu.VMEM)] * (side + 1),
        out_shape=(
            jax.ShapeDtypeStruct(gradient.shape, jnp.float32),
            jax.ShapeDtypeStruct((capacity, size, size), jnp.float32),
            jax.ShapeDtypeStruct((1, size), jnp.float32),
        ),
        scratch_shapes=[pltpu.VMEM((side * side, rows, size), jnp.float32)],
        compiler_params=pltpu.CompilerParams(vmem_limit_bytes=40 * 1024 * 1024),
        name="update",
    )(places, *folded, gradient)


def swap(value, axis, flip):
    size = lax.axis_size(axis)
    return lax.ppermute(value, axis, [(i, i ^ flip) for i in range(size)])


def exchange(value, axis):
    return [value] + [swap(value, axis, flip) for flip in range(1, lax.axis_size(axis))]


def spread(value, axis):
    copies = jnp.broadcast_to(value[None], (lax.axis_size(axis),) + value.shape)
    return lax.all_to_all(copies, axis, 0, 0)


def body(activations, grads_out, grad_parts, old_factors, block_owner, weights, momentum):
    shard_count = lax.axis_size("shards")
    replica_count = lax.axis_size("replica")
    block_count = old_factors.shape[0]
    block_size = old_factors.shape[1]
    capacity = (block_count + shard_count - 1) // shard_count + 1
    sample_count = activations.shape[0] * shard_count * lax.axis_size("tensor") * replica_count
    partial_grad = grad_parts[0]
    row_count, col_count = partial_grad.shape
    left_count = row_count // block_size
    right_count = col_count // block_size
    piece_rows = row_count // shard_count
    own_rows = weights.shape[0]
    shard = lax.axis_index("shards")
    replica = lax.axis_index("replica")

    grad_in = lax.all_to_all(partial_grad.reshape(shard_count, piece_rows, col_count), "shards", 0, 0)

    side = 4
    coords = jnp.stack([shard // side, shard % side]).astype(jnp.int32)
    along_x = fold(
        coords,
        sample_stats(activations, block_size),
        sample_stats(grads_out, block_size),
        side,
    )
    parts = [along_x[0]] + [swap(along_x[k], "shards", k * side) for k in range(1, side)]
    along_y = [sum(part[j] for part in parts) for j in range(side)]
    along_y, grad_in = lax.optimization_barrier((along_y, grad_in))
    own_stats = along_y[0] + sum(swap(along_y[j], "shards", j) for j in range(1, side))

    base = weights - (step_rate * momentum_rate) * momentum
    base_rows = lax.dynamic_update_slice_in_dim(
        jnp.zeros((piece_rows, col_count), jnp.float32), base, replica * own_rows, 0
    )
    own_parts = exchange(jnp.concatenate([jnp.sum(grad_in, axis=0), base_rows], axis=0), "replica")
    own_stats = own_stats + swap(own_stats, "tensor", 1)
    own_stats, own_parts = lax.optimization_barrier((own_stats, own_parts))
    own = sum(own_parts)
    own_grad = own[:piece_rows]
    base = lax.all_gather(own[piece_rows:], "shards", axis=0, tiled=True)
    gradient = spread(own_grad, "shards").reshape(row_count, col_count)

    old_factors, own = lax.optimization_barrier((old_factors, own))
    old_block = fold_one(lax.dynamic_slice_in_dim(old_factors, shard, 1, 0))
    own_stats = sum(exchange(own_stats, "replica"))
    own_stats = own_stats + swap(own_stats, "tensor", 2)
    blended = decay_rate * old_block + ((1.0 - decay_rate) / sample_count) * own_stats
    row_of_y = jnp.stack([blended] + [swap(blended, "shards", j) for j in range(1, side)])
    folded = [row_of_y] + [swap(row_of_y, "shards", k * side) for k in range(1, side)]

    positions = jnp.arange(block_count, dtype=jnp.int32)
    earlier = (block_owner[:, None] == block_owner[None, :]) & (
        positions[None, :] < positions[:, None]
    )
    slots = block_owner * capacity + jnp.sum(earlier.astype(jnp.int32), axis=1)
    own_slots = shard * capacity + jnp.arange(capacity, dtype=jnp.int32)
    holds = jnp.max(jnp.where(slots[None, :] == own_slots[:, None], positions[None, :], -1), axis=1)
    right_first = left_count + lax.axis_index("tensor") * right_count
    places = jnp.concatenate([coords, right_first.reshape(1).astype(jnp.int32), holds])
    precond, owned_blocks, align = update(places, folded, gradient, capacity)
    align, base = lax.optimization_barrier((align, base))
    align = align + swap(align, "tensor", 1)
    align = align + swap(align, "tensor", 2)
    clip_scale = jnp.minimum(1.0, clip_norm / jnp.sqrt(align[0, 0]))
    first_row = (shard * replica_count + replica) * own_rows
    own_precond = lax.dynamic_slice_in_dim(precond, first_row, own_rows, 0)
    momentum_next = momentum_rate * momentum + clip_scale * own_precond
    weights_next = base - (step_rate * clip_scale) * precond
    return (weights_next, momentum_next, owned_blocks)


def solution(mesh):
    placed = (
        P(("shards", "tensor", "replica"), None),
        P(("shards", "tensor", "replica"), None),
        P(("shards", "replica"), None, "tensor"),
        P(),
        P(),
        P(("shards", "replica"), "tensor"),
        P(("shards", "replica"), "tensor"),
    )
    return jax.shard_map(
        body,
        mesh=mesh,
        in_specs=placed,
        out_specs=(P(None, "tensor"), P(("shards", "replica"), "tensor"), P("shards", None, None)),
        check_vma=False,
    )
```

time: 123 us -> 129 us (1.049)
  waiting for transfers between devices: 21.7 us -> 31.6 us
  starting transfers between devices: 58.1 us -> 54.2 us
  Pallas kernels: 10.2 us -> 12.5 us
  matrix products: 5.94 us -> 3.81 us
  other arithmetic: 9.05 us -> 7.58 us
    all_gather x1, waiting for transfers between devices: 0.01 us -> 6.98 us  [body(): base = lax.all_gather(own[piece_rows:], 'shards', axis=0, tiled=True)]
    ppermute x24 -> x22, starting transfers between devices: 47.6 us -> 41.9 us  [swap(): return lax.ppermute(value, axis, [(i, i ^ flip) for i in range(size)])]
    ppermute x24 -> x22, waiting for transfers between devices: 19.8 us -> 24.6 us  [swap(): return lax.ppermute(value, axis, [(i, i ^ flip) for i in range(size)])]
    pallas_call x1 -> x2, Pallas kernels: 8.01 us -> 10.4 us  [the longest x1 8.85 us: update(): pl.pallas_call(lambda *refs: update_kernel(side, *refs), in_specs=[pl.Blo...]
    dot_general x2, matrix products: 5.94 us -> 3.81 us  [sample_stats(): jnp.einsum('tnb,tnc->nbc', blocks, blocks, preferred_element_type=jnp.flo...]
    all_to_all x1, waiting for transfers between devices: 1.81 us -> 0.01 us  [body(): lax.all_to_all(partial_grad.reshape(shard_count, piece_rows, col_count),...]
    dynamic_slice x0 -> x1, local copies, waits for them, and re-layouts: none -> 1.47 us  [body(): old_block = fold_one(lax.dynamic_slice_in_dim(old_factors, shard, 1, 0))]
  transfers between devices with their start and end apart: 27 -> 25, of which waited for: 13 -> 10; matrix products, arithmetic and copies ran while one was open for 9% -> 8% of each run, Pallas kernels for 2% -> 10%
where the time goes in v5:
time: 129 us; the launch traced here: 128 us
  starting transfers between devices  54.2 us (42%)
  waiting for transfers between devices  31.6 us (24%)
  between operations  14.3 us (11%)
  Pallas kernels  12.5 us (10%)
  other arithmetic  7.58 us (6%)
  local copies, waits for them, and re-layouts  4.17 us (3%)
  matrix products  3.81 us (3%)
    ppermute x22, starting transfers between devices, swap(): return lax.ppermute(value, axis, [(i, i ^ flip) for i in range(size)])  41.9 us
    ppermute x22, waiting for transfers between devices, swap(): return lax.ppermute(value, axis, [(i, i ^ flip) for i in range(size)])  24.6 us
    pallas_call x1, Pallas kernels, update(): pl.pallas_call(lambda *refs: update_kernel(side, *refs), in_specs=[pl.Blo...  8.85 us
    all_to_all x1, starting transfers between devices, body(): lax.all_to_all(partial_grad.reshape(shard_count, piece_rows, col_count),...  7.73 us
    all_gather x1, waiting for transfers between devices, body(): base = lax.all_gather(own[piece_rows:], 'shards', axis=0, tiled=True)  6.98 us
    all_to_all x1, starting transfers between devices, spread(): return lax.all_to_all(copies, axis, 0, 0)  4.54 us
    dot_general x2, matrix products, sample_stats(): jnp.einsum('tnb,tnc->nbc', blocks, blocks, preferred_element_type=jnp.flo...  3.81 us
    sub x1, other arithmetic, body(): weights_next = base - step_rate * clip_scale * precond  2.64 us
  transfers between devices with their start and end apart: 25, of which 10 were waited for; matrix products, arithmetic and copies ran while one was open for 8% of the time, Pallas kernels for 10%

profile of v5, /device:TPU:1, one launch (start us, length us, event | category | flops | bytes accessed | tf_op | source)
XLA Modules:
  0.0 128.2 jit_solution(15050824570608757358)
XLA Ops:
  7.2 7.7 %all-to-all-start = ((f32[16,64,256]{2,1,0:T(8,128)}), f32[16,64,256]{2,1,0:T(8,128)S(1)}, u32[]{:S(2)}, u32[]{:S(2)}) async-start(f32[16,64,256]{2,1,0:T(8,128)} %bitcast.34), calls=%async_computation | async-start | bytes 2097152 | tf_op jit(solution)/shard_map/all_to_all | solution.py:198
  15.0 0.6 pad_add_fusion.1.place_ref
  15.6 1.8 %fusion.3.left_ref = f32[8,128,128]{2,1,0:T(8,128)} fusion(bf16[1024,1024]{1,0:T(8,128)(2,1)S(1)} %copy-done), kind=kOutput, calls=%fused_computation.3 | convolution fusion | flops 268435456 | bytes 2621440 | tf_op jit(solution)/shard_map/tnb,tnc->nbc/dot_general | solution.py:23
  17.4 2.0 %fusion.right_ref = f32[8,128,128]{2,1,0:T(8,128)} fusion(bf16[1024,1024]{1,0:T(8,128)(2,1)S(1)} %copy-done.4), kind=kOutput, calls=%fused_computation | convolution fusion | flops 268435456 | bytes 2621440 | tf_op jit(solution)/shard_map/tnb,tnc->nbc/dot_general | solution.py:23
  19.4 2.2 %fold.1 = (f32[4,72,128]{2,1,0:T(8,128)}, f32[4,72,128]{2,1,0:T(8,128)}, f32[4,72,128]{2,1,0:T(8,128)}, f32[4,72,128]{2,1,0:T(8,128)}) custom-call(s32[2]{0:T(128)} %pad_add_fusion.1.place_ref, f32[8,128,128]{2,1,0:T(8,128)} %fusion.3.left_ref, f32[8,128,128]{2,1,0:T(8,128)} %fusion.right_ref), custom_call_target="tpu_custom_call" | custom-call | tf_op jit(solution)/shard_map/fold/pallas_call | solution.py:54
  21.6 2.6 %collective-permute-start.2 = (f32[4,72,128]{2,1,0:T(8,128)}, f32[4,72,128]{2,1,0:T(8,128)S(1)}, u32[]{:S(2)}, u32[]{:S(2)}) collective-permute-start(f32[4,72,128]{2,1,0:T(8,128)} %get-tuple-element.26), channel_id=1, source_target_pairs={{0,192},{16,208},{32,224},{48,240},{64,128},{80,144},{96,160},{112... | collective-permute-start | bytes 442376 | tf_op jit(solution)/shard_map/ppermute | solution.py:170
  24.2 0.6 collective-permute-start.1
  24.7 0.1 collective-permute-start
  24.9 10.3 %collective-permute-done.2 = f32[4,72,128]{2,1,0:T(8,128)S(1)} collective-permute-done((f32[4,72,128]{2,1,0:T(8,128)}, f32[4,72,128]{2,1,0:T(8,128)S(1)}, u32[]{:S(2)}, u32[]{:S(2)}) %collective-permute-start.2) | collective-permute-done | bytes 147488 | tf_op jit(solution)/shard_map/ppermute | solution.py:170
  35.2 1.6 %fusion.6 = (f32[72,128]{1,0:T(8,128)}, f32[72,128]{1,0:T(8,128)S(1)}, f32[72,128]{1,0:T(8,128)S(1)}, f32[72,128]{1,0:T(8,128)S(1)}) fusion(f32[4,72,128]{2,1,0:T(8,128)S(1)} %collective-permute-done.2, f32[4,72,128]{2,1,0:T(8,128)} %collective-permute-done.1, f32[4,72,128]{2,1,0:T(8,128)} %collective-permute-done, f32[4,72,128]{2,1,0:T(8,128)} %get-tuple-element.23), kind=kLoop, calls=%fused_computation.11 | loop fusion | flops 110592 | bytes 737280 | tf_op jit(solution)/shard_map/add | solution.py:209
  36.8 2.5 %collective-permute-start.5 = (f32[72,128]{1,0:T(8,128)}, f32[72,128]{1,0:T(8,128)S(1)}, u32[]{:S(2)}, u32[]{:S(2)}) collective-permute-start(f32[72,128]{1,0:T(8,128)} %get-tuple-element.30), channel_id=1, source_target_pairs={{0,48},{16,32},{32,16},{48,0},{64,112},{80,96},{96,80},{112,64},{1... | collective-permute-start | bytes 110600 | tf_op jit(solution)/shard_map/ppermute | solution.py:170
  39.4 1.3 %collective-permute-start.4 = (f32[72,128]{1,0:T(8,128)S(1)}, f32[72,128]{1,0:T(8,128)S(1)}, u32[]{:S(2)}, u32[]{:S(2)}) collective-permute-start(f32[72,128]{1,0:T(8,128)S(1)} %get-tuple-element.29), channel_id=1, source_target_pairs={{0,32},{16,48},{32,0},{48,16},{64,96},{80,112},{96,64},{112,80},{1... | collective-permute-start | bytes 110600 | tf_op jit(solution)/shard_map/ppermute | solution.py:170
  40.8 1.7 %collective-permute-start.7 = (f32[128,256]{1,0:T(8,128)S(1)}, f32[128,256]{1,0:T(8,128)S(1)}, u32[]{:S(2)}, u32[]{:S(2)}) collective-permute-start(f32[128,256]{1,0:T(8,128)S(1)} %pad_maximum_fusion.1), channel_id=1, source_target_pairs={{0,1},{1,0},{2,3},{3,2},{4,5},{5,4},{6,7},{7,6},{8,9},{9,8},{10,11... | collective-permute-start | bytes 393224 | tf_op jit(solution)/shard_map/ppermute | solution.py:170
  42.5 3.0 %collective-permute-start.8 = (f32[128,256]{1,0:T(8,128)S(1)}, f32[128,256]{1,0:T(8,128)S(1)}, u32[]{:S(2)}, u32[]{:S(2)}) collective-permute-start(f32[128,256]{1,0:T(8,128)S(1)} %pad_maximum_fusion.1), channel_id=1, source_target_pairs={{0,2},{1,3},{2,0},{3,1},{4,6},{5,7},{6,4},{7,5},{8,10},{9,11},{10,... | collective-permute-start | bytes 393224 | tf_op jit(solution)/shard_map/ppermute | solution.py:170
  45.5 3.2 %collective-permute-start.6 = (f32[72,128]{1,0:T(8,128)S(1)}, f32[72,128]{1,0:T(8,128)S(1)}, u32[]{:S(2)}, u32[]{:S(2)}) collective-permute-start(f32[72,128]{1,0:T(8,128)S(1)} %add_add_fusion.2), channel_id=1, source_target_pairs={{0,4},{4,0},{8,12},{12,8},{1,5},{5,1},{9,13},{13,9},{2,6},{6,2},{1... | collective-permute-start | bytes 110600 | tf_op jit(solution)/shard_map/ppermute | solution.py:170
  48.7 0.9 collective-permute-done.6
  49.6 2.9 %collective-permute-done.9 = f32[128,256]{1,0:T(8,128)S(1)} collective-permute-done((f32[128,256]{1,0:T(8,128)S(1)}, f32[128,256]{1,0:T(8,128)S(1)}, u32[]{:S(2)}, u32[]{:S(2)}) %collective-permute-start.9) | collective-permute-done | bytes 131104 | tf_op jit(solution)/shard_map/ppermute | solution.py:170
  52.5 0.6 fusion.12
  53.2 0.2 convert_reduce_fusion
  53.4 2.5 %collective-permute-start.12 = (f32[72,128]{1,0:T(8,128)S(1)}, f32[72,128]{1,0:T(8,128)S(1)}, u32[]{:S(2)}, u32[]{:S(2)}) collective-permute-start(f32[72,128]{1,0:T(8,128)S(1)} %add.154), channel_id=1, source_target_pairs={{0,3},{1,2},{2,1},{3,0},{4,7},{5,6},{6,5},{7,4},{8,11},{9,10},{10,... | collective-permute-start | bytes 110600 | tf_op jit(solution)/shard_map/ppermute | solution.py:170
  55.9 2.7 %collective-permute-start.11 = (f32[72,128]{1,0:T(8,128)S(1)}, f32[72,128]{1,0:T(8,128)S(1)}, u32[]{:S(2)}, u32[]{:S(2)}) collective-permute-start(f32[72,128]{1,0:T(8,128)S(1)} %add.154), channel_id=1, source_target_pairs={{0,2},{1,3},{2,0},{3,1},{4,6},{5,7},{6,4},{7,5},{8,10},{9,11},{10,... | collective-permute-start | bytes 110600 | tf_op jit(solution)/shard_map/ppermute | solution.py:170
  58.6 1.1 broadcast_in_dim.15
  59.6 4.5 %all-to-all-start.1 = ((f32[16,64,256]{2,1,0:T(8,128)}), f32[16,64,256]{2,1,0:T(8,128)S(1)}, u32[]{:S(2)}, u32[]{:S(2)}) async-start(f32[16,64,256]{2,1,0:T(8,128)} %broadcast_in_dim.15), calls=%async_computation.1 | async-start | bytes 2097152 | tf_op jit(solution)/shard_map/all_to_all | solution.py:179
  64.2 6.7 %collective-permute-start.13 = (f32[72,128]{1,0:T(8,128)S(1)}, f32[72,128]{1,0:T(8,128)S(1)}, u32[]{:S(2)}, u32[]{:S(2)}) collective-permute-start(f32[72,128]{1,0:T(8,128)S(1)} %add_add_fusion.1), channel_id=1, source_target_pairs={{0,8},{4,12},{8,0},{12,4},{1,9},{5,13},{9,1},{13,5},{2,10},{6,14},... | collective-permute-start | bytes 110600 | tf_op jit(solution)/shard_map/ppermute | solution.py:170
  70.9 1.5 %constant_dynamic-slice_fusion.block_ref = f32[1,128,128]{2,1,0:T(8,128)} fusion(f32[16,128,128]{2,1,0:T(8,128)} %param.10, s32[]{:T(128)S(6)} %select_n.28), kind=kLoop, calls=%fused_computation.36 | loop fusion | bytes 131076 | tf_op jit(solution)/shard_map/dynamic_slice | solution.py:226
  72.4 1.5 %fold_one.1 = f32[72,128]{1,0:T(8,128)} custom-call(f32[1,128,128]{2,1,0:T(8,128)} %constant_dynamic-slice_fusion.block_ref), custom_call_target="tpu_custom_call" | custom-call | tf_op jit(solution)/shard_map/fold_one/pallas_call | solution.py:75
  73.9 0.8 multiply_add_fusion
  74.7 2.7 %collective-permute-start.16 = (f32[72,128]{1,0:T(8,128)S(1)}, f32[72,128]{1,0:T(8,128)S(1)}, u32[]{:S(2)}, u32[]{:S(2)}) collective-permute-start(f32[72,128]{1,0:T(8,128)S(1)} %multiply_add_fusion), channel_id=1, source_target_pairs={{0,48},{16,32},{32,16},{48,0},{64,112},{80,96},{96,80},{112,64},{1... | collective-permute-start | bytes 110600 | tf_op jit(solution)/shard_map/ppermute | solution.py:170
  77.4 0.6 collective-permute-start.15
  77.9 0.3 collective-permute-start.14
  78.2 3.9 %collective-permute-done.16 = f32[72,128]{1,0:T(8,128)S(1)} collective-permute-done((f32[72,128]{1,0:T(8,128)S(1)}, f32[72,128]{1,0:T(8,128)S(1)}, u32[]{:S(2)}, u32[]{:S(2)}) %collective-permute-start.16) | collective-permute-done | bytes 36896 | tf_op jit(solution)/shard_map/ppermute | solution.py:170
  82.1 0.5 collective-permute-done.15
  82.6 1.0 collective-permute-start.17
  83.6 1.7 %collective-permute-start.18 = (f32[4,72,128]{2,1,0:T(8,128)S(1)}, f32[4,72,128]{2,1,0:T(8,128)}, u32[]{:S(2)}, u32[]{:S(2)}) collective-permute-start(f32[4,72,128]{2,1,0:T(8,128)S(1)} %pad_maximum_fusion.refs_1_), channel_id=1, source_target_pairs={{0,128},{16,144},{32,160},{48,176},{64,192},{80,208},{96,224},{112... | collective-permute-start | bytes 442376 | tf_op jit(solution)/shard_map/ppermute | solution.py:170
  85.4 1.2 collective-permute-start.19
  86.6 0.2 fusion.11
  86.7 0.1 pad_add_fusion.refs_0_
  86.8 2.8 %collective-permute-done.18.refs_3_ = f32[4,72,128]{2,1,0:T(8,128)} collective-permute-done((f32[4,72,128]{2,1,0:T(8,128)S(1)}, f32[4,72,128]{2,1,0:T(8,128)}, u32[]{:S(2)}, u32[]{:S(2)}) %collective-permute-start.18) | collective-permute-done | bytes 147488 | tf_op jit(solution)/shard_map/ppermute | solution.py:170
  89.6 1.5 %collective-permute-done.19.refs_4_ = f32[4,72,128]{2,1,0:T(8,128)} collective-permute-done((f32[4,72,128]{2,1,0:T(8,128)S(1)}, f32[4,72,128]{2,1,0:T(8,128)}, u32[]{:S(2)}, u32[]{:S(2)}) %collective-permute-start.19) | collective-permute-done | bytes 147488 | tf_op jit(solution)/shard_map/ppermute | solution.py:170
  91.2 8.8 %update.1 = (f32[1024,256]{1,0:T(8,128)S(1)}, f32[2,128,128]{2,1,0:T(8,128)}, f32[1,128]{1,0:T(1,128)S(1)}) custom-call(s32[5]{0:T(128)S(1)} %pad_add_fusion.refs_0_, f32[4,72,128]{2,1,0:T(8,128)S(1)} %pad_maximum_fusion.refs_1_, f32[4,72,128]{2,1,0:T(8,128)S(1)} %collective-permute-done.17.refs_2_, f32[4,72,128]{2,1,0:T(8,128)} %collective-permute-done.18.refs_3_, ...), custom_call_target="tpu_custom_call" | custom-call | tf_op jit(solution)/shard_map/update/pallas_call | solution.py:153
  100.0 1.0 copy-done.1
  101.0 7.0 %all-gather.2.cloned.1.call-done = f32[1024,256]{1,0:T(8,128)} async-done(((f32[64,256]{1,0:T(8,128)}), f32[1024,256]{1,0:T(8,128)}) %all-gather.2.cloned.1.call-update) | async-done | bytes 1048592 | tf_op jit(solution)/shard_map/all_gather | solution.py:222
  108.0 2.1 %collective-permute-start.20 = (f32[1,128]{1,0:T(1,128)S(1)}, f32[1,128]{1,0:T(1,128)S(1)}, u32[]{:S(2)}, u32[]{:S(2)}) collective-permute-start(f32[1,128]{1,0:T(1,128)S(1)} %get-tuple-element.40), channel_id=1, source_target_pairs={{0,4},{4,0},{8,12},{12,8},{1,5},{5,1},{9,13},{13,9},{2,6},{6,2},{1... | collective-permute-start | bytes 1544 | tf_op jit(solution)/shard_map/ppermute | solution.py:170
  110.0 0.8 collective-permute-done.20
  110.9 5.5 %collective-permute-start.21 = (f32[1,128]{1,0:T(1,128)S(1)}, f32[1,128]{1,0:T(1,128)S(1)}, u32[]{:S(2)}, u32[]{:S(2)}) collective-permute-start(f32[1,128]{1,0:T(1,128)S(1)} %add.165), channel_id=1, source_target_pairs={{0,8},{4,12},{8,0},{12,4},{1,9},{5,13},{9,1},{13,5},{2,10},{6,14},... | collective-permute-start | bytes 1544 | tf_op jit(solution)/shard_map/ppermute | solution.py:170
  116.3 0.9 collective-permute-done.21
  117.3 1.3 %multiply_add_fusion.1 = f32[16,256]{1,0:T(8,128)} fusion(f32[1024,256]{1,0:T(8,128)} %copy-done.1, s32[]{:T(128)S(6)} %select_n.29, f32[16,256]{1,0:T(8,128)S(1)} %copy-done.2, f32[]{:T(128)} %bitcast.13), kind=kLoop, calls=%fused_computation.29 | loop fusion | flops 12288 | bytes 49160 | tf_op jit(solution)/shard_map/add | solution.py:249
  118.7 2.6 %multiply_subtract_fusion = f32[1024,256]{1,0:T(8,128)} fusion(f32[1024,256]{1,0:T(8,128)} %all-gather.2.cloned.1.call-done, f32[1024,256]{1,0:T(8,128)} %copy-done.1, f32[]{:T(128)S(6)} %mul_shard_map.3), kind=kLoop, calls=%fused_computation.6 | loop fusion | flops 524288 | bytes 3145732 | tf_op jit(solution)/shard_map/sub | solution.py:250
  (44 shorter events, 0.3 us)
Async XLA Ops:
  7.2 8.4 %copy-start = (bf16[1024,1024]{1,0:T(8,128)(2,1)S(1)}, bf16[1024,1024]{1,0:T(8,128)(2,1)}, u32[]{:S(2)}) copy-start(bf16[1024,1024]{1,0:T(8,128)(2,1)} %param.7) | copy-start | bytes 6291460
  7.2 29.7 %all-to-all-start = ((f32[16,64,256]{2,1,0:T(8,128)}), f32[16,64,256]{2,1,0:T(8,128)S(1)}, u32[]{:S(2)}, u32[]{:S(2)}) async-start(f32[16,64,256]{2,1,0:T(8,128)} %bitcast.34), calls=%async_computation | async-start | bytes 2097152 | tf_op jit(solution)/shard_map/all_to_all | solution.py:198
  14.9 93.0 %all-gather.2.cloned.1.call-start = ((), (), s32[]{:S(2)}) async-start(), calls=%async_computation.2 | async-start | bytes 1114112 | tf_op jit(solution)/shard_map/all_gather | solution.py:222
  15.0 2.5 %copy-start.4 = (bf16[1024,1024]{1,0:T(8,128)(2,1)S(1)}, bf16[1024,1024]{1,0:T(8,128)(2,1)}, u32[]{:S(2)}) copy-start(bf16[1024,1024]{1,0:T(8,128)(2,1)} %param.8) | copy-start | bytes 6291460
  17.4 7.4 %copy-start.2 = (f32[16,256]{1,0:T(8,128)S(1)}, f32[16,256]{1,0:T(8,128)}, u32[]{:S(2)}) copy-start(f32[16,256]{1,0:T(8,128)} %param.13) | copy-start | bytes 49156
  17.4 7.4 %copy-start.3 = (f32[16,256]{1,0:T(8,128)S(1)}, f32[16,256]{1,0:T(8,128)}, u32[]{:S(2)}) copy-start(f32[16,256]{1,0:T(8,128)} %param.12) | copy-start | bytes 49156
  19.4 33.8 %copy-start.5 = (s32[16]{0:T(128)S(1)}, s32[16]{0:T(128)}, u32[]{:S(2)}) copy-start(s32[16]{0:T(128)} %param.11) | copy-start | bytes 196
  21.6 13.6 %collective-permute-start.2 = (f32[4,72,128]{2,1,0:T(8,128)}, f32[4,72,128]{2,1,0:T(8,128)S(1)}, u32[]{:S(2)}, u32[]{:S(2)}) collective-permute-start(f32[4,72,128]{2,1,0:T(8,128)} %get-tuple-element.26), channel_id=1, source_target_pairs={{0,192},{16,208},{32,224},{48,240},{64,128},{80,144},{96,160},{112... | collective-permute-start | bytes 442376 | tf_op jit(solution)/shard_map/ppermute | solution.py:170
  24.2 11.1 %collective-permute-start.1 = (f32[4,72,128]{2,1,0:T(8,128)}, f32[4,72,128]{2,1,0:T(8,128)}, u32[]{:S(2)}, u32[]{:S(2)}) collective-permute-start(f32[4,72,128]{2,1,0:T(8,128)} %get-tuple-element.25), channel_id=1, source_target_pairs={{0,128},{16,144},{32,160},{48,176},{64,192},{80,208},{96,224},{112... | collective-permute-start | bytes 442376 | tf_op jit(solution)/shard_map/ppermute | solution.py:170
  24.7 10.5 %collective-permute-start = (f32[4,72,128]{2,1,0:T(8,128)}, f32[4,72,128]{2,1,0:T(8,128)}, u32[]{:S(2)}, u32[]{:S(2)}) collective-permute-start(f32[4,72,128]{2,1,0:T(8,128)} %get-tuple-element.24), channel_id=1, source_target_pairs={{0,64},{16,80},{32,96},{48,112},{64,0},{80,16},{96,32},{112,48},{1... | collective-permute-start | bytes 442376 | tf_op jit(solution)/shard_map/ppermute | solution.py:170
  36.8 8.7 %collective-permute-start.5 = (f32[72,128]{1,0:T(8,128)}, f32[72,128]{1,0:T(8,128)S(1)}, u32[]{:S(2)}, u32[]{:S(2)}) collective-permute-start(f32[72,128]{1,0:T(8,128)} %get-tuple-element.30), channel_id=1, source_target_pairs={{0,48},{16,32},{32,16},{48,0},{64,112},{80,96},{96,80},{112,64},{1... | collective-permute-start | bytes 110600 | tf_op jit(solution)/shard_map/ppermute | solution.py:170
  39.4 6.1 %collective-permute-start.3 = (f32[72,128]{1,0:T(8,128)S(1)}, f32[72,128]{1,0:T(8,128)S(1)}, u32[]{:S(2)}, u32[]{:S(2)}) collective-permute-start(f32[72,128]{1,0:T(8,128)S(1)} %get-tuple-element.28), channel_id=1, source_target_pairs={{0,16},{16,0},{32,48},{48,32},{64,80},{80,64},{96,112},{112,96},{1... | collective-permute-start | bytes 110600 | tf_op jit(solution)/shard_map/ppermute | solution.py:170
  39.4 6.1 %collective-permute-start.4 = (f32[72,128]{1,0:T(8,128)S(1)}, f32[72,128]{1,0:T(8,128)S(1)}, u32[]{:S(2)}, u32[]{:S(2)}) collective-permute-start(f32[72,128]{1,0:T(8,128)S(1)} %get-tuple-element.29), channel_id=1, source_target_pairs={{0,32},{16,48},{32,0},{48,16},{64,96},{80,112},{96,64},{112,80},{1... | collective-permute-start | bytes 110600 | tf_op jit(solution)/shard_map/ppermute | solution.py:170
  40.8 8.8 %collective-permute-start.7 = (f32[128,256]{1,0:T(8,128)S(1)}, f32[128,256]{1,0:T(8,128)S(1)}, u32[]{:S(2)}, u32[]{:S(2)}) collective-permute-start(f32[128,256]{1,0:T(8,128)S(1)} %pad_maximum_fusion.1), channel_id=1, source_target_pairs={{0,1},{1,0},{2,3},{3,2},{4,5},{5,4},{6,7},{7,6},{8,9},{9,8},{10,11... | collective-permute-start | bytes 393224 | tf_op jit(solution)/shard_map/ppermute | solution.py:170
  42.5 7.1 %collective-permute-start.8 = (f32[128,256]{1,0:T(8,128)S(1)}, f32[128,256]{1,0:T(8,128)S(1)}, u32[]{:S(2)}, u32[]{:S(2)}) collective-permute-start(f32[128,256]{1,0:T(8,128)S(1)} %pad_maximum_fusion.1), channel_id=1, source_target_pairs={{0,2},{1,3},{2,0},{3,1},{4,6},{5,7},{6,4},{7,5},{8,10},{9,11},{10,... | collective-permute-start | bytes 393224 | tf_op jit(solution)/shard_map/ppermute | solution.py:170
  45.5 7.0 %collective-permute-start.9 = (f32[128,256]{1,0:T(8,128)S(1)}, f32[128,256]{1,0:T(8,128)S(1)}, u32[]{:S(2)}, u32[]{:S(2)}) collective-permute-start(f32[128,256]{1,0:T(8,128)S(1)} %pad_maximum_fusion.1), channel_id=1, source_target_pairs={{0,3},{1,2},{2,1},{3,0},{4,7},{5,6},{6,5},{7,4},{8,11},{9,10},{10,... | collective-permute-start | bytes 393224 | tf_op jit(solution)/shard_map/ppermute | solution.py:170
  45.5 4.0 %collective-permute-start.6 = (f32[72,128]{1,0:T(8,128)S(1)}, f32[72,128]{1,0:T(8,128)S(1)}, u32[]{:S(2)}, u32[]{:S(2)}) collective-permute-start(f32[72,128]{1,0:T(8,128)S(1)} %add_add_fusion.2), channel_id=1, source_target_pairs={{0,4},{4,0},{8,12},{12,8},{1,5},{5,1},{9,13},{13,9},{2,6},{6,2},{1... | collective-permute-start | bytes 110600 | tf_op jit(solution)/shard_map/ppermute | solution.py:170
  53.4 10.8 %collective-permute-start.12 = (f32[72,128]{1,0:T(8,128)S(1)}, f32[72,128]{1,0:T(8,128)S(1)}, u32[]{:S(2)}, u32[]{:S(2)}) collective-permute-start(f32[72,128]{1,0:T(8,128)S(1)} %add.154), channel_id=1, source_target_pairs={{0,3},{1,2},{2,1},{3,0},{4,7},{5,6},{6,5},{7,4},{8,11},{9,10},{10,... | collective-permute-start | bytes 110600 | tf_op jit(solution)/shard_map/ppermute | solution.py:170
  55.9 8.3 %collective-permute-start.11 = (f32[72,128]{1,0:T(8,128)S(1)}, f32[72,128]{1,0:T(8,128)S(1)}, u32[]{:S(2)}, u32[]{:S(2)}) collective-permute-start(f32[72,128]{1,0:T(8,128)S(1)} %add.154), channel_id=1, source_target_pairs={{0,2},{1,3},{2,0},{3,1},{4,6},{5,7},{6,4},{7,5},{8,10},{9,11},{10,... | collective-permute-start | bytes 110600 | tf_op jit(solution)/shard_map/ppermute | solution.py:170
  58.5 5.7 %collective-permute-start.10 = (f32[72,128]{1,0:T(8,128)S(1)}, f32[72,128]{1,0:T(8,128)S(1)}, u32[]{:S(2)}, u32[]{:S(2)}) collective-permute-start(f32[72,128]{1,0:T(8,128)S(1)} %add.154), channel_id=1, source_target_pairs={{0,1},{1,0},{2,3},{3,2},{4,5},{5,4},{6,7},{7,6},{8,9},{9,8},{10,11... | collective-permute-start | bytes 110600 | tf_op jit(solution)/shard_map/ppermute | solution.py:170
  59.6 31.5 %all-to-all-start.1 = ((f32[16,64,256]{2,1,0:T(8,128)}), f32[16,64,256]{2,1,0:T(8,128)S(1)}, u32[]{:S(2)}, u32[]{:S(2)}) async-start(f32[16,64,256]{2,1,0:T(8,128)} %broadcast_in_dim.15), calls=%async_computation.1 | async-start | bytes 2097152 | tf_op jit(solution)/shard_map/all_to_all | solution.py:179
  64.2 9.7 %collective-permute-start.13 = (f32[72,128]{1,0:T(8,128)S(1)}, f32[72,128]{1,0:T(8,128)S(1)}, u32[]{:S(2)}, u32[]{:S(2)}) collective-permute-start(f32[72,128]{1,0:T(8,128)S(1)} %add_add_fusion.1), channel_id=1, source_target_pairs={{0,8},{4,12},{8,0},{12,4},{1,9},{5,13},{9,1},{13,5},{2,10},{6,14},... | collective-permute-start | bytes 110600 | tf_op jit(solution)/shard_map/ppermute | solution.py:170
  74.7 7.4 %collective-permute-start.16 = (f32[72,128]{1,0:T(8,128)S(1)}, f32[72,128]{1,0:T(8,128)S(1)}, u32[]{:S(2)}, u32[]{:S(2)}) collective-permute-start(f32[72,128]{1,0:T(8,128)S(1)} %multiply_add_fusion), channel_id=1, source_target_pairs={{0,48},{16,32},{32,16},{48,0},{64,112},{80,96},{96,80},{112,64},{1... | collective-permute-start | bytes 110600 | tf_op jit(solution)/shard_map/ppermute | solution.py:170
  77.4 5.2 %collective-permute-start.15 = (f32[72,128]{1,0:T(8,128)S(1)}, f32[72,128]{1,0:T(8,128)S(1)}, u32[]{:S(2)}, u32[]{:S(2)}) collective-permute-start(f32[72,128]{1,0:T(8,128)S(1)} %multiply_add_fusion), channel_id=1, source_target_pairs={{0,32},{16,48},{32,0},{48,16},{64,96},{80,112},{96,64},{112,80},{1... | collective-permute-start | bytes 110600 | tf_op jit(solution)/shard_map/ppermute | solution.py:170
  77.9 4.7 %collective-permute-start.14 = (f32[72,128]{1,0:T(8,128)S(1)}, f32[72,128]{1,0:T(8,128)S(1)}, u32[]{:S(2)}, u32[]{:S(2)}) collective-permute-start(f32[72,128]{1,0:T(8,128)S(1)} %multiply_add_fusion), channel_id=1, source_target_pairs={{0,16},{16,0},{32,48},{48,32},{64,80},{80,64},{96,112},{112,96},{1... | collective-permute-start | bytes 110600 | tf_op jit(solution)/shard_map/ppermute | solution.py:170
  82.6 4.2 %collective-permute-start.17 = (f32[4,72,128]{2,1,0:T(8,128)S(1)}, f32[4,72,128]{2,1,0:T(8,128)S(1)}, u32[]{:S(2)}, u32[]{:S(2)}) collective-permute-start(f32[4,72,128]{2,1,0:T(8,128)S(1)} %pad_maximum_fusion.refs_1_), channel_id=1, source_target_pairs={{0,64},{16,80},{32,96},{48,112},{64,0},{80,16},{96,32},{112,48},{1... | collective-permute-start | bytes 442376 | tf_op jit(solution)/shard_map/ppermute | solution.py:170
  83.6 6.0 %collective-permute-start.18 = (f32[4,72,128]{2,1,0:T(8,128)S(1)}, f32[4,72,128]{2,1,0:T(8,128)}, u32[]{:S(2)}, u32[]{:S(2)}) collective-permute-start(f32[4,72,128]{2,1,0:T(8,128)S(1)} %pad_maximum_fusion.refs_1_), channel_id=1, source_target_pairs={{0,128},{16,144},{32,160},{48,176},{64,192},{80,208},{96,224},{112... | collective-permute-start | bytes 442376 | tf_op jit(solution)/shard_map/ppermute | solution.py:170
  85.4 5.8 %collective-permute-start.19 = (f32[4,72,128]{2,1,0:T(8,128)S(1)}, f32[4,72,128]{2,1,0:T(8,128)}, u32[]{:S(2)}, u32[]{:S(2)}) collective-permute-start(f32[4,72,128]{2,1,0:T(8,128)S(1)} %pad_maximum_fusion.refs_1_), channel_id=1, source_target_pairs={{0,192},{16,208},{32,224},{48,240},{64,128},{80,144},{96,160},{112... | collective-permute-start | bytes 442376 | tf_op jit(solution)/shard_map/ppermute | solution.py:170
  100.0 1.0 copy-start.1
  108.0 2.9 %collective-permute-start.20 = (f32[1,128]{1,0:T(1,128)S(1)}, f32[1,128]{1,0:T(1,128)S(1)}, u32[]{:S(2)}, u32[]{:S(2)}) collective-permute-start(f32[1,128]{1,0:T(1,128)S(1)} %get-tuple-element.40), channel_id=1, source_target_pairs={{0,4},{4,0},{8,12},{12,8},{1,5},{5,1},{9,13},{13,9},{2,6},{6,2},{1... | collective-permute-start | bytes 1544 | tf_op jit(solution)/shard_map/ppermute | solution.py:170
  110.9 6.4 %collective-permute-start.21 = (f32[1,128]{1,0:T(1,128)S(1)}, f32[1,128]{1,0:T(1,128)S(1)}, u32[]{:S(2)}, u32[]{:S(2)}) collective-permute-start(f32[1,128]{1,0:T(1,128)S(1)} %add.165), channel_id=1, source_target_pairs={{0,8},{4,12},{8,0},{12,4},{1,9},{5,13},{9,1},{13,5},{2,10},{6,14},... | collective-permute-start | bytes 1544 | tf_op jit(solution)/shard_map/ppermute | solution.py:170
Sparse Core Ops, SparseCore 0:
  53.3 54.6 all-gather.1

commit v6 on v5

--- a/solution.py
+++ b/solution.py
@@ -165,6 +165,31 @@
     )(places, *folded, gradient)
 
 
+def finish_kernel(row_ref, align_ref, momentum_ref, precond_ref, base_ref, weights_ref, next_ref):
+    scale = jnp.minimum(1.0, clip_norm / jnp.sqrt(align_ref[0:1, 0:1]))
+    rows = next_ref.shape[0]
+    own = precond_ref[pl.ds(pl.multiple_of(row_ref[0], rows), rows), :]
+    next_ref[...] = momentum_rate * momentum_ref[...] + scale * own
+    weights_ref[...] = base_ref[...] - (step_rate * scale) * precond_ref[...]
+
+
+def finish(first_row, align, momentum, precond, base):
+    return pl.pallas_call(
+        finish_kernel,
+        in_specs=[pl.BlockSpec(memory_space=pltpu.SMEM)]
+        + [pl.BlockSpec(memory_space=pltpu.VMEM)] * 4,
+        out_shape=(
+            jax.ShapeDtypeStruct(base.shape, jnp.float32),
+            jax.ShapeDtypeStruct(momentum.shape, jnp.float32),
+        ),
+        name="finish",
+    )(first_row.reshape(1).astype(jnp.int32), align, momentum, precond, base)
+
+
+def after(value, first):
+    return lax.optimization_barrier((value, first))[0]
+
+
 def swap(value, axis, flip):
     size = lax.axis_size(axis)
     return lax.ppermute(value, axis, [(i, i ^ flip) for i in range(size)])
@@ -207,24 +232,25 @@
     )
     parts = [along_x[0]] + [swap(along_x[k], "shards", k * side) for k in range(1, side)]
     along_y = [sum(part[j] for part in parts) for j in range(side)]
-    along_y, grad_in = lax.optimization_barrier((along_y, grad_in))
     own_stats = along_y[0] + sum(swap(along_y[j], "shards", j) for j in range(1, side))
-
-    base = weights - (step_rate * momentum_rate) * momentum
-    base_rows = lax.dynamic_update_slice_in_dim(
-        jnp.zeros((piece_rows, col_count), jnp.float32), base, replica * own_rows, 0
-    )
-    own_parts = exchange(jnp.concatenate([jnp.sum(grad_in, axis=0), base_rows], axis=0), "replica")
     own_stats = own_stats + swap(own_stats, "tensor", 1)
-    own_stats, own_parts = lax.optimization_barrier((own_stats, own_parts))
-    own = sum(own_parts)
-    own_grad = own[:piece_rows]
-    base = lax.all_gather(own[piece_rows:], "shards", axis=0, tiled=True)
+
+    weights, momentum_then, old_then = after((weights, momentum, old_factors), along_x[0])
+    base_parts = exchange(weights - (step_rate * momentum_rate) * momentum_then, "replica")
+    base_rows = []
+    for place in range(replica_count):
+        rows = base_parts[0]
+        for flip in range(1, replica_count):
+            rows = jnp.where(replica ^ flip == place, base_parts[flip], rows)
+        base_rows.append(rows)
+    base = lax.all_gather(jnp.concatenate(base_rows, axis=0), "shards", axis=0, tiled=True)
+    old_block = fold_one(lax.dynamic_slice_in_dim(old_then, shard, 1, 0))
+
+    grad_parts_in = exchange(jnp.sum(after(grad_in, along_x[0]), axis=0), "replica")
+    own_grad = sum(after(grad_parts_in, own_stats))
     gradient = spread(own_grad, "shards").reshape(row_count, col_count)
 
-    old_factors, own = lax.optimization_barrier((old_factors, own))
-    old_block = fold_one(lax.dynamic_slice_in_dim(old_factors, shard, 1, 0))
-    own_stats = sum(exchange(own_stats, "replica"))
+    own_stats = sum(exchange(after(own_stats, old_block), "replica"))
     own_stats = own_stats + swap(own_stats, "tensor", 2)
     blended = decay_rate * old_block + ((1.0 - decay_rate) / sample_count) * own_stats
     row_of_y = jnp.stack([blended] + [swap(blended, "shards", j) for j in range(1, side)])
@@ -243,11 +269,8 @@
     align, base = lax.optimization_barrier((align, base))
     align = align + swap(align, "tensor", 1)
     align = align + swap(align, "tensor", 2)
-    clip_scale = jnp.minimum(1.0, clip_norm / jnp.sqrt(align[0, 0]))
     first_row = (shard * replica_count + replica) * own_rows
-    own_precond = lax.dynamic_slice_in_dim(precond, first_row, own_rows, 0)
-    momentum_next = momentum_rate * momentum + clip_scale * own_precond
-    weights_next = base - (step_rate * clip_scale) * precond
+    weights_next, momentum_next = finish(first_row, align, momentum, precond, base)
     return (weights_next, momentum_next, owned_blocks)
 
 

time: 129 us -> 124 us (0.961)
  waiting for transfers between devices: 31.6 us -> 22.5 us
  starting transfers between devices: 54.2 us -> 59.7 us
  other arithmetic: 7.58 us -> 4.09 us
  Pallas kernels: 12.5 us -> 15.3 us
    all_gather x1, waiting for transfers between devices: 6.98 us -> 0.01 us  [body(): lax.all_gather(jnp.concatenate(base_rows, axis=0), 'shards', axis=0, tile...]
    ppermute x22 -> x25, starting transfers between devices: 41.9 us -> 47.1 us  [swap(): return lax.ppermute(value, axis, [(i, i ^ flip) for i in range(size)])]
    pallas_call x0 -> x1, Pallas kernels: none -> 2.78 us  [finish(): pl.pallas_call(finish_kernel, in_specs=[pl.BlockSpec(memory_space=pltpu.S...]
    sub x1, other arithmetic: 2.64 us -> 0.01 us  [body(): weights - step_rate * momentum_rate * momentum_then]
    ppermute x22 -> x25, waiting for transfers between devices: 24.6 us -> 22.5 us  [swap(): return lax.ppermute(value, axis, [(i, i ^ flip) for i in range(size)])]
    add x3 -> x2, other arithmetic: 1.38 us -> 0.03 us  [the longest x1 0.02 us: body(): own_grad = sum(after(grad_parts_in, own_stats))]
  transfers between devices with their start and end apart: 25 -> 28, of which waited for: 10 -> 13; matrix products, arithmetic and copies ran while one was open for 8% -> 8% of each run, Pallas kernels for 10% -> 10%
where the time goes in v6:
time: 124 us; the launch traced here: 123 us
  starting transfers between devices  59.7 us (48%)
  waiting for transfers between devices  22.5 us (18%)
  Pallas kernels  15.3 us (12%)
  between operations  14.2 us (11%)
  other arithmetic  4.09 us (3%)
  matrix products  3.79 us (3%)
  local copies, waits for them, and re-layouts  3.54 us (3%)
    ppermute x25, starting transfers between devices, swap(): return lax.ppermute(value, axis, [(i, i ^ flip) for i in range(size)])  47.1 us
    ppermute x25, waiting for transfers between devices, swap(): return lax.ppermute(value, axis, [(i, i ^ flip) for i in range(size)])  22.5 us
    pallas_call x1, Pallas kernels, update(): pl.pallas_call(lambda *refs: update_kernel(side, *refs), in_specs=[pl.Blo...  8.85 us
    all_to_all x1, starting transfers between devices, body(): lax.all_to_all(partial_grad.reshape(shard_count, piece_rows, col_count),...  7.73 us
    all_to_all x1, starting transfers between devices, spread(): return lax.all_to_all(copies, axis, 0, 0)  4.84 us
    dot_general x2, matrix products, sample_stats(): jnp.einsum('tnb,tnc->nbc', blocks, blocks, preferred_element_type=jnp.flo...  3.79 us
    pallas_call x1, Pallas kernels, finish(): pl.pallas_call(finish_kernel, in_specs=[pl.BlockSpec(memory_space=pltpu.S...  2.78 us
  transfers between devices with their start and end apart: 28, of which 13 were waited for; matrix products, arithmetic and copies ran while one was open for 8% of the time, Pallas kernels for 10%

profile of v6, /device:TPU:1, one launch (start us, length us, event | category | flops | bytes accessed | tf_op | source)
XLA Modules:
  0.0 123.2 jit_solution(13051421094269299136)
XLA Ops:
  7.2 7.7 %all-to-all-start = ((f32[16,64,256]{2,1,0:T(8,128)}), f32[16,64,256]{2,1,0:T(8,128)S(1)}, u32[]{:S(2)}, u32[]{:S(2)}) async-start(f32[16,64,256]{2,1,0:T(8,128)} %bitcast.35), calls=%async_computation | async-start | bytes 2097152 | tf_op jit(solution)/shard_map/all_to_all | solution.py:223
  15.0 1.9 %fusion.3.left_ref = f32[8,128,128]{2,1,0:T(8,128)} fusion(bf16[1024,1024]{1,0:T(8,128)(2,1)S(1)} %copy-done), kind=kOutput, calls=%fused_computation.3 | convolution fusion | flops 268435456 | bytes 2621440 | tf_op jit(solution)/shard_map/tnb,tnc->nbc/dot_general | solution.py:23
  16.9 1.9 %fusion.right_ref = f32[8,128,128]{2,1,0:T(8,128)} fusion(bf16[1024,1024]{1,0:T(8,128)(2,1)S(1)} %copy-done.5), kind=kOutput, calls=%fused_computation | convolution fusion | flops 268435456 | bytes 2621440 | tf_op jit(solution)/shard_map/tnb,tnc->nbc/dot_general | solution.py:23
  18.8 0.6 pad_add_fusion.1.place_ref
  19.4 2.2 %fold.1 = (f32[4,72,128]{2,1,0:T(8,128)}, f32[4,72,128]{2,1,0:T(8,128)}, f32[4,72,128]{2,1,0:T(8,128)}, f32[4,72,128]{2,1,0:T(8,128)}) custom-call(s32[2]{0:T(128)} %pad_add_fusion.1.place_ref, f32[8,128,128]{2,1,0:T(8,128)} %fusion.3.left_ref, f32[8,128,128]{2,1,0:T(8,128)} %fusion.right_ref), custom_call_target="tpu_custom_call" | custom-call | tf_op jit(solution)/shard_map/fold/pallas_call | solution.py:54
  21.6 4.4 %collective-permute-start.20 = (f32[16,256]{1,0:T(8,128)S(1)}, f32[16,256]{1,0:T(8,128)S(1)}, u32[]{:S(2)}, u32[]{:S(2)}) collective-permute-start(f32[16,256]{1,0:T(8,128)S(1)} %multiply_subtract_fusion), channel_id=1, source_target_pairs={{0,3},{1,2},{2,1},{3,0},{4,7},{5,6},{6,5},{7,4},{8,11},{9,10},{10,... | collective-permute-start | bytes 49160 | tf_op jit(solution)/shard_map/ppermute | solution.py:195
  26.0 0.4 collective-permute-start.22
  26.4 2.6 %collective-permute-start.2 = (f32[4,72,128]{2,1,0:T(8,128)}, f32[4,72,128]{2,1,0:T(8,128)S(1)}, u32[]{:S(2)}, u32[]{:S(2)}) collective-permute-start(f32[4,72,128]{2,1,0:T(8,128)} %get-tuple-element.27), channel_id=1, source_target_pairs={{0,192},{16,208},{32,224},{48,240},{64,128},{80,144},{96,160},{112... | collective-permute-start | bytes 442376 | tf_op jit(solution)/shard_map/ppermute | solution.py:195
  29.0 0.6 collective-permute-start.1
  29.8 0.6 pad_maximum_fusion.1
  30.4 4.5 %collective-permute-done.2 = f32[4,72,128]{2,1,0:T(8,128)S(1)} collective-permute-done((f32[4,72,128]{2,1,0:T(8,128)}, f32[4,72,128]{2,1,0:T(8,128)S(1)}, u32[]{:S(2)}, u32[]{:S(2)}) %collective-permute-start.2) | collective-permute-done | bytes 147488 | tf_op jit(solution)/shard_map/ppermute | solution.py:195
  34.9 0.3 collective-permute-done
  35.2 0.9 fusion.7
  36.1 2.4 %collective-permute-start.5 = (f32[72,128]{1,0:T(8,128)S(1)}, f32[72,128]{1,0:T(8,128)S(1)}, u32[]{:S(2)}, u32[]{:S(2)}) collective-permute-start(f32[72,128]{1,0:T(8,128)S(1)} %get-tuple-element.44), channel_id=1, source_target_pairs={{0,48},{16,32},{32,16},{48,0},{64,112},{80,96},{96,80},{112,64},{1... | collective-permute-start | bytes 110600 | tf_op jit(solution)/shard_map/ppermute | solution.py:195
  38.4 1.6 %collective-permute-start.4 = (f32[72,128]{1,0:T(8,128)S(1)}, f32[72,128]{1,0:T(8,128)S(1)}, u32[]{:S(2)}, u32[]{:S(2)}) collective-permute-start(f32[72,128]{1,0:T(8,128)S(1)} %get-tuple-element.43), channel_id=1, source_target_pairs={{0,32},{16,48},{32,0},{48,16},{64,96},{80,112},{96,64},{112,80},{1... | collective-permute-start | bytes 110600 | tf_op jit(solution)/shard_map/ppermute | solution.py:195
  40.0 1.5 %constant_dynamic-slice_fusion.block_ref = f32[1,128,128]{2,1,0:T(8,128)} fusion(f32[16,128,128]{2,1,0:T(8,128)} %param.10, s32[]{:T(128)S(6)} %select_n.95), kind=kLoop, calls=%fused_computation.42 | loop fusion | bytes 131076 | tf_op jit(solution)/shard_map/dynamic_slice | solution.py:247
  41.5 1.3 %collective-permute-done.4 = f32[72,128]{1,0:T(8,128)S(1)} collective-permute-done((f32[72,128]{1,0:T(8,128)S(1)}, f32[72,128]{1,0:T(8,128)S(1)}, u32[]{:S(2)}, u32[]{:S(2)}) %collective-permute-start.4) | collective-permute-done | bytes 36896 | tf_op jit(solution)/shard_map/ppermute | solution.py:195
  42.8 0.8 fusion.10
  43.6 5.3 %collective-permute-start.6 = (f32[72,128]{1,0:T(8,128)S(1)}, f32[72,128]{1,0:T(8,128)S(1)}, u32[]{:S(2)}, u32[]{:S(2)}) collective-permute-start(f32[72,128]{1,0:T(8,128)S(1)} %fusion.10), channel_id=1, source_target_pairs={{0,4},{4,0},{8,12},{12,8},{1,5},{5,1},{9,13},{13,9},{2,6},{6,2},{1... | collective-permute-start | bytes 110600 | tf_op jit(solution)/shard_map/ppermute | solution.py:195
  48.9 1.2 collective-permute-start.17
  50.1 2.4 %collective-permute-start.18 = (f32[64,256]{1,0:T(8,128)S(1)}, f32[64,256]{1,0:T(8,128)S(1)}, u32[]{:S(2)}, u32[]{:S(2)}) collective-permute-start(f32[64,256]{1,0:T(8,128)S(1)} %reduce_sum.19), channel_id=1, source_target_pairs={{0,2},{1,3},{2,0},{3,1},{4,6},{5,7},{6,4},{7,5},{8,10},{9,11},{10,... | collective-permute-start | bytes 196616 | tf_op jit(solution)/shard_map/ppermute | solution.py:195
  52.5 0.2 convert_reduce_fusion
  52.7 1.5 %fold_one.1 = f32[72,128]{1,0:T(8,128)} custom-call(f32[1,128,128]{2,1,0:T(8,128)} %constant_dynamic-slice_fusion.block_ref), custom_call_target="tpu_custom_call" | custom-call | tf_op jit(solution)/shard_map/fold_one/pallas_call | solution.py:75
  54.2 3.2 %collective-permute-start.9 = (f32[72,128]{1,0:T(8,128)S(1)}, f32[72,128]{1,0:T(8,128)S(1)}, u32[]{:S(2)}, u32[]{:S(2)}) collective-permute-start(f32[72,128]{1,0:T(8,128)S(1)} %add.147), channel_id=1, source_target_pairs={{0,3},{1,2},{2,1},{3,0},{4,7},{5,6},{6,5},{7,4},{8,11},{9,10},{10,... | collective-permute-start | bytes 110600 | tf_op jit(solution)/shard_map/ppermute | solution.py:195
  57.5 0.4 collective-permute-start.7
  57.9 1.1 broadcast_in_dim.12
  59.0 4.8 %all-to-all-start.1 = ((f32[16,64,256]{2,1,0:T(8,128)}), f32[16,64,256]{2,1,0:T(8,128)S(1)}, u32[]{:S(2)}, u32[]{:S(2)}) async-start(f32[16,64,256]{2,1,0:T(8,128)} %broadcast_in_dim.12), calls=%async_computation.1 | async-start | bytes 2097152 | tf_op jit(solution)/shard_map/all_to_all | solution.py:204
  63.9 5.8 %collective-permute-start.10 = (f32[72,128]{1,0:T(8,128)S(1)}, f32[72,128]{1,0:T(8,128)S(1)}, u32[]{:S(2)}, u32[]{:S(2)}) collective-permute-start(f32[72,128]{1,0:T(8,128)S(1)} %add_add_fusion.1), channel_id=1, source_target_pairs={{0,8},{4,12},{8,0},{12,4},{1,9},{5,13},{9,1},{13,5},{2,10},{6,14},... | collective-permute-start | bytes 110600 | tf_op jit(solution)/shard_map/ppermute | solution.py:195
  69.7 1.3 %collective-permute-done.10 = f32[72,128]{1,0:T(8,128)S(1)} collective-permute-done((f32[72,128]{1,0:T(8,128)S(1)}, f32[72,128]{1,0:T(8,128)S(1)}, u32[]{:S(2)}, u32[]{:S(2)}) %collective-permute-start.10) | collective-permute-done | bytes 36896 | tf_op jit(solution)/shard_map/ppermute | solution.py:195
  71.1 2.7 %collective-permute-start.13 = (f32[72,128]{1,0:T(8,128)S(1)}, f32[72,128]{1,0:T(8,128)S(1)}, u32[]{:S(2)}, u32[]{:S(2)}) collective-permute-start(f32[72,128]{1,0:T(8,128)S(1)} %multiply_add_fusion), channel_id=1, source_target_pairs={{0,48},{16,32},{32,16},{48,0},{64,112},{80,96},{96,80},{112,64},{1... | collective-permute-start | bytes 110600 | tf_op jit(solution)/shard_map/ppermute | solution.py:195
  73.7 0.6 collective-permute-start.12
  74.4 6.0 %collective-permute-done.13 = f32[72,128]{1,0:T(8,128)S(1)} collective-permute-done((f32[72,128]{1,0:T(8,128)S(1)}, f32[72,128]{1,0:T(8,128)S(1)}, u32[]{:S(2)}, u32[]{:S(2)}) %collective-permute-start.13) | collective-permute-done | bytes 36896 | tf_op jit(solution)/shard_map/ppermute | solution.py:195
  80.4 2.4 %collective-permute-done.12 = f32[72,128]{1,0:T(8,128)S(1)} collective-permute-done((f32[72,128]{1,0:T(8,128)S(1)}, f32[72,128]{1,0:T(8,128)S(1)}, u32[]{:S(2)}, u32[]{:S(2)}) %collective-permute-start.12) | collective-permute-done | bytes 36896 | tf_op jit(solution)/shard_map/ppermute | solution.py:195
  82.8 0.6 collective-permute-done.11
  83.5 1.5 %collective-permute-start.15 = (f32[4,72,128]{2,1,0:T(8,128)S(1)}, f32[4,72,128]{2,1,0:T(8,128)}, u32[]{:S(2)}, u32[]{:S(2)}) collective-permute-start(f32[4,72,128]{2,1,0:T(8,128)S(1)} %pad_maximum_fusion.refs_1_), channel_id=1, source_target_pairs={{0,128},{16,144},{32,160},{48,176},{64,192},{80,208},{96,224},{112... | collective-permute-start | bytes 442376 | tf_op jit(solution)/shard_map/ppermute | solution.py:195
  85.1 2.3 %collective-permute-start.16 = (f32[4,72,128]{2,1,0:T(8,128)S(1)}, f32[4,72,128]{2,1,0:T(8,128)}, u32[]{:S(2)}, u32[]{:S(2)}) collective-permute-start(f32[4,72,128]{2,1,0:T(8,128)S(1)} %pad_maximum_fusion.refs_1_), channel_id=1, source_target_pairs={{0,192},{16,208},{32,224},{48,240},{64,128},{80,144},{96,160},{112... | collective-permute-start | bytes 442376 | tf_op jit(solution)/shard_map/ppermute | solution.py:195
  87.4 0.2 fusion.12
  87.6 0.7 collective-permute-done.14.refs_2_
  88.3 2.9 %collective-permute-done.15.refs_3_ = f32[4,72,128]{2,1,0:T(8,128)} collective-permute-done((f32[4,72,128]{2,1,0:T(8,128)S(1)}, f32[4,72,128]{2,1,0:T(8,128)}, u32[]{:S(2)}, u32[]{:S(2)}) %collective-permute-start.15) | collective-permute-done | bytes 147488 | tf_op jit(solution)/shard_map/ppermute | solution.py:195
  91.2 0.7 collective-permute-done.16.refs_4_
  91.9 8.8 %update.1 = (f32[1024,256]{1,0:T(8,128)S(1)}, f32[2,128,128]{2,1,0:T(8,128)}, f32[1,128]{1,0:T(1,128)S(1)}) custom-call(s32[5]{0:T(128)S(1)} %pad_add_fusion.refs_0_, f32[4,72,128]{2,1,0:T(8,128)S(1)} %pad_maximum_fusion.refs_1_, f32[4,72,128]{2,1,0:T(8,128)S(1)} %collective-permute-done.14.refs_2_, f32[4,72,128]{2,1,0:T(8,128)} %collective-permute-done.15.refs_3_, ...), custom_call_target="tpu_custom_call" | custom-call | tf_op jit(solution)/shard_map/update/pallas_call | solution.py:153
  100.8 1.0 copy-done.1
  101.7 3.8 %collective-permute-start.23 = (f32[1,128]{1,0:T(1,128)S(1)}, f32[1,128]{1,0:T(1,128)S(1)}, u32[]{:S(2)}, u32[]{:S(2)}) collective-permute-start(f32[1,128]{1,0:T(1,128)S(1)} %get-tuple-element.37), channel_id=1, source_target_pairs={{0,4},{4,0},{8,12},{12,8},{1,5},{5,1},{9,13},{13,9},{2,6},{6,2},{1... | collective-permute-start | bytes 1544 | tf_op jit(solution)/shard_map/ppermute | solution.py:195
  105.6 0.8 collective-permute-done.23
  106.4 5.6 %collective-permute-start.24 = (f32[1,128]{1,0:T(1,128)S(1)}, f32[1,128]{1,0:T(1,128)S(1)}, u32[]{:S(2)}, u32[]{:S(2)}) collective-permute-start(f32[1,128]{1,0:T(1,128)S(1)} %add.156), channel_id=1, source_target_pairs={{0,8},{4,12},{8,0},{12,4},{1,9},{5,13},{9,1},{13,5},{2,10},{6,14},... | collective-permute-start | bytes 1544 | tf_op jit(solution)/shard_map/ppermute | solution.py:195
  112.0 0.9 collective-permute-done.24
  112.9 0.6 add.157.align_ref
  113.5 2.8 %finish.1 = (f32[1024,256]{1,0:T(8,128)}, f32[16,256]{1,0:T(8,128)}) custom-call(s32[1]{0:T(128)} %bitcast.row_ref, f32[1,128]{1,0:T(1,128)} %add.157.align_ref, f32[16,256]{1,0:T(8,128)} %momentum_ref.1, f32[1024,256]{1,0:T(8,128)} %copy-done.1, f32[1024,256]{1,0:T(8,128)} %all-gather.2.cloned.1.call-done.base_ref), custom_call_target="tpu_custom_call" | custom-call | tf_op jit(solution)/shard_map/finish/pallas_call | solution.py:177
  (50 shorter events, 0.9 us)
Async XLA Ops:
  7.2 7.8 %copy-start = (bf16[1024,1024]{1,0:T(8,128)(2,1)S(1)}, bf16[1024,1024]{1,0:T(8,128)(2,1)}, u32[]{:S(2)}) copy-start(bf16[1024,1024]{1,0:T(8,128)(2,1)} %param.7) | copy-start | bytes 6291460
  7.2 41.6 %all-to-all-start = ((f32[16,64,256]{2,1,0:T(8,128)}), f32[16,64,256]{2,1,0:T(8,128)S(1)}, u32[]{:S(2)}, u32[]{:S(2)}) async-start(f32[16,64,256]{2,1,0:T(8,128)} %bitcast.35), calls=%async_computation | async-start | bytes 2097152 | tf_op jit(solution)/shard_map/all_to_all | solution.py:223
  14.9 86.8 %all-gather.2.cloned.1.call-start = ((), (), s32[]{:S(2)}) async-start(), calls=%async_computation.2 | async-start | bytes 1114112 | tf_op jit(solution)/shard_map/all_gather | solution.py:246
  15.0 1.9 %copy-start.5 = (bf16[1024,1024]{1,0:T(8,128)(2,1)S(1)}, bf16[1024,1024]{1,0:T(8,128)(2,1)}, u32[]{:S(2)}) copy-start(bf16[1024,1024]{1,0:T(8,128)(2,1)} %param.8) | copy-start | bytes 6291460
  16.9 4.7 %copy-start.3 = (f32[16,256]{1,0:T(8,128)S(1)}, f32[16,256]{1,0:T(8,128)}, u32[]{:S(2)}) copy-start(f32[16,256]{1,0:T(8,128)} %momentum_ref.1) | copy-start | bytes 49156
  16.9 4.7 %copy-start.4 = (f32[16,256]{1,0:T(8,128)S(1)}, f32[16,256]{1,0:T(8,128)}, u32[]{:S(2)}) copy-start(f32[16,256]{1,0:T(8,128)} %param.12) | copy-start | bytes 49156
  18.8 33.7 %copy-start.6 = (s32[16]{0:T(128)S(1)}, s32[16]{0:T(128)}, u32[]{:S(2)}) copy-start(s32[16]{0:T(128)} %param.11) | copy-start | bytes 196
  21.6 8.0 %collective-permute-start.20 = (f32[16,256]{1,0:T(8,128)S(1)}, f32[16,256]{1,0:T(8,128)S(1)}, u32[]{:S(2)}, u32[]{:S(2)}) collective-permute-start(f32[16,256]{1,0:T(8,128)S(1)} %multiply_subtract_fusion), channel_id=1, source_target_pairs={{0,3},{1,2},{2,1},{3,0},{4,7},{5,6},{6,5},{7,4},{8,11},{9,10},{10,... | collective-permute-start | bytes 49160 | tf_op jit(solution)/shard_map/ppermute | solution.py:195
  26.0 3.8 %collective-permute-start.21 = (f32[16,256]{1,0:T(8,128)S(1)}, f32[16,256]{1,0:T(8,128)S(1)}, u32[]{:S(2)}, u32[]{:S(2)}) collective-permute-start(f32[16,256]{1,0:T(8,128)S(1)} %multiply_subtract_fusion), channel_id=1, source_target_pairs={{0,2},{1,3},{2,0},{3,1},{4,6},{5,7},{6,4},{7,5},{8,10},{9,11},{10,... | collective-permute-start | bytes 49160 | tf_op jit(solution)/shard_map/ppermute | solution.py:195
  26.0 3.8 %collective-permute-start.22 = (f32[16,256]{1,0:T(8,128)S(1)}, f32[16,256]{1,0:T(8,128)S(1)}, u32[]{:S(2)}, u32[]{:S(2)}) collective-permute-start(f32[16,256]{1,0:T(8,128)S(1)} %multiply_subtract_fusion), channel_id=1, source_target_pairs={{0,1},{1,0},{2,3},{3,2},{4,5},{5,4},{6,7},{7,6},{8,9},{9,8},{10,11... | collective-permute-start | bytes 49160 | tf_op jit(solution)/shard_map/ppermute | solution.py:195
  26.4 8.5 %collective-permute-start.2 = (f32[4,72,128]{2,1,0:T(8,128)}, f32[4,72,128]{2,1,0:T(8,128)S(1)}, u32[]{:S(2)}, u32[]{:S(2)}) collective-permute-start(f32[4,72,128]{2,1,0:T(8,128)} %get-tuple-element.27), channel_id=1, source_target_pairs={{0,192},{16,208},{32,224},{48,240},{64,128},{80,144},{96,160},{112... | collective-permute-start | bytes 442376 | tf_op jit(solution)/shard_map/ppermute | solution.py:195
  29.0 6.0 %collective-permute-start.1 = (f32[4,72,128]{2,1,0:T(8,128)}, f32[4,72,128]{2,1,0:T(8,128)S(1)}, u32[]{:S(2)}, u32[]{:S(2)}) collective-permute-start(f32[4,72,128]{2,1,0:T(8,128)} %get-tuple-element.26), channel_id=1, source_target_pairs={{0,128},{16,144},{32,160},{48,176},{64,192},{80,208},{96,224},{112... | collective-permute-start | bytes 442376 | tf_op jit(solution)/shard_map/ppermute | solution.py:195
  29.5 5.6 %collective-permute-start = (f32[4,72,128]{2,1,0:T(8,128)}, f32[4,72,128]{2,1,0:T(8,128)}, u32[]{:S(2)}, u32[]{:S(2)}) collective-permute-start(f32[4,72,128]{2,1,0:T(8,128)} %get-tuple-element.25), channel_id=1, source_target_pairs={{0,64},{16,80},{32,96},{48,112},{64,0},{80,16},{96,32},{112,48},{1... | collective-permute-start | bytes 442376 | tf_op jit(solution)/shard_map/ppermute | solution.py:195
  36.1 5.4 %collective-permute-start.5 = (f32[72,128]{1,0:T(8,128)S(1)}, f32[72,128]{1,0:T(8,128)S(1)}, u32[]{:S(2)}, u32[]{:S(2)}) collective-permute-start(f32[72,128]{1,0:T(8,128)S(1)} %get-tuple-element.44), channel_id=1, source_target_pairs={{0,48},{16,32},{32,16},{48,0},{64,112},{80,96},{96,80},{112,64},{1... | collective-permute-start | bytes 110600 | tf_op jit(solution)/shard_map/ppermute | solution.py:195
  38.4 3.0 %collective-permute-start.3 = (f32[72,128]{1,0:T(8,128)S(1)}, f32[72,128]{1,0:T(8,128)S(1)}, u32[]{:S(2)}, u32[]{:S(2)}) collective-permute-start(f32[72,128]{1,0:T(8,128)S(1)} %get-tuple-element.45), channel_id=1, source_target_pairs={{0,16},{16,0},{32,48},{48,32},{64,80},{80,64},{96,112},{112,96},{1... | collective-permute-start | bytes 110600 | tf_op jit(solution)/shard_map/ppermute | solution.py:195
  38.4 4.3 %collective-permute-start.4 = (f32[72,128]{1,0:T(8,128)S(1)}, f32[72,128]{1,0:T(8,128)S(1)}, u32[]{:S(2)}, u32[]{:S(2)}) collective-permute-start(f32[72,128]{1,0:T(8,128)S(1)} %get-tuple-element.43), channel_id=1, source_target_pairs={{0,32},{16,48},{32,0},{48,16},{64,96},{80,112},{96,64},{112,80},{1... | collective-permute-start | bytes 110600 | tf_op jit(solution)/shard_map/ppermute | solution.py:195
  43.6 10.7 %collective-permute-start.6 = (f32[72,128]{1,0:T(8,128)S(1)}, f32[72,128]{1,0:T(8,128)S(1)}, u32[]{:S(2)}, u32[]{:S(2)}) collective-permute-start(f32[72,128]{1,0:T(8,128)S(1)} %fusion.10), channel_id=1, source_target_pairs={{0,4},{4,0},{8,12},{12,8},{1,5},{5,1},{9,13},{13,9},{2,6},{6,2},{1... | collective-permute-start | bytes 110600 | tf_op jit(solution)/shard_map/ppermute | solution.py:195
  48.9 8.6 %collective-permute-start.17 = (f32[64,256]{1,0:T(8,128)S(1)}, f32[64,256]{1,0:T(8,128)S(1)}, u32[]{:S(2)}, u32[]{:S(2)}) collective-permute-start(f32[64,256]{1,0:T(8,128)S(1)} %reduce_sum.19), channel_id=1, source_target_pairs={{0,1},{1,0},{2,3},{3,2},{4,5},{5,4},{6,7},{7,6},{8,9},{9,8},{10,11... | collective-permute-start | bytes 196616 | tf_op jit(solution)/shard_map/ppermute | solution.py:195
  50.1 7.8 %collective-permute-start.18 = (f32[64,256]{1,0:T(8,128)S(1)}, f32[64,256]{1,0:T(8,128)S(1)}, u32[]{:S(2)}, u32[]{:S(2)}) collective-permute-start(f32[64,256]{1,0:T(8,128)S(1)} %reduce_sum.19), channel_id=1, source_target_pairs={{0,2},{1,3},{2,0},{3,1},{4,6},{5,7},{6,4},{7,5},{8,10},{9,11},{10,... | collective-permute-start | bytes 196616 | tf_op jit(solution)/shard_map/ppermute | solution.py:195
  52.4 5.5 %collective-permute-start.19 = (f32[64,256]{1,0:T(8,128)S(1)}, f32[64,256]{1,0:T(8,128)S(1)}, u32[]{:S(2)}, u32[]{:S(2)}) collective-permute-start(f32[64,256]{1,0:T(8,128)S(1)} %reduce_sum.19), channel_id=1, source_target_pairs={{0,3},{1,2},{2,1},{3,0},{4,7},{5,6},{6,5},{7,4},{8,11},{9,10},{10,... | collective-permute-start | bytes 196616 | tf_op jit(solution)/shard_map/ppermute | solution.py:195
  54.2 16.8 %copy-start.2 = (f32[72,128]{1,0:T(8,128)S(1)}, f32[72,128]{1,0:T(8,128)}, u32[]{:S(2)}) copy-start(f32[72,128]{1,0:T(8,128)} %fold_one.1) | copy-start | bytes 110596
  54.2 9.6 %collective-permute-start.9 = (f32[72,128]{1,0:T(8,128)S(1)}, f32[72,128]{1,0:T(8,128)S(1)}, u32[]{:S(2)}, u32[]{:S(2)}) collective-permute-start(f32[72,128]{1,0:T(8,128)S(1)} %add.147), channel_id=1, source_target_pairs={{0,3},{1,2},{2,1},{3,0},{4,7},{5,6},{6,5},{7,4},{8,11},{9,10},{10,... | collective-permute-start | bytes 110600 | tf_op jit(solution)/shard_map/ppermute | solution.py:195
  57.5 6.4 %collective-permute-start.8 = (f32[72,128]{1,0:T(8,128)S(1)}, f32[72,128]{1,0:T(8,128)S(1)}, u32[]{:S(2)}, u32[]{:S(2)}) collective-permute-start(f32[72,128]{1,0:T(8,128)S(1)} %add.147), channel_id=1, source_target_pairs={{0,2},{1,3},{2,0},{3,1},{4,6},{5,7},{6,4},{7,5},{8,10},{9,11},{10,... | collective-permute-start | bytes 110600 | tf_op jit(solution)/shard_map/ppermute | solution.py:195
  57.5 6.4 %collective-permute-start.7 = (f32[72,128]{1,0:T(8,128)S(1)}, f32[72,128]{1,0:T(8,128)S(1)}, u32[]{:S(2)}, u32[]{:S(2)}) collective-permute-start(f32[72,128]{1,0:T(8,128)S(1)} %add.147), channel_id=1, source_target_pairs={{0,1},{1,0},{2,3},{3,2},{4,5},{5,4},{6,7},{7,6},{8,9},{9,8},{10,11... | collective-permute-start | bytes 110600 | tf_op jit(solution)/shard_map/ppermute | solution.py:195
  59.0 32.9 %all-to-all-start.1 = ((f32[16,64,256]{2,1,0:T(8,128)}), f32[16,64,256]{2,1,0:T(8,128)S(1)}, u32[]{:S(2)}, u32[]{:S(2)}) async-start(f32[16,64,256]{2,1,0:T(8,128)} %broadcast_in_dim.12), calls=%async_computation.1 | async-start | bytes 2097152 | tf_op jit(solution)/shard_map/all_to_all | solution.py:204
  63.9 7.2 %collective-permute-start.10 = (f32[72,128]{1,0:T(8,128)S(1)}, f32[72,128]{1,0:T(8,128)S(1)}, u32[]{:S(2)}, u32[]{:S(2)}) collective-permute-start(f32[72,128]{1,0:T(8,128)S(1)} %add_add_fusion.1), channel_id=1, source_target_pairs={{0,8},{4,12},{8,0},{12,4},{1,9},{5,13},{9,1},{13,5},{2,10},{6,14},... | collective-permute-start | bytes 110600 | tf_op jit(solution)/shard_map/ppermute | solution.py:195
  71.1 9.3 %collective-permute-start.13 = (f32[72,128]{1,0:T(8,128)S(1)}, f32[72,128]{1,0:T(8,128)S(1)}, u32[]{:S(2)}, u32[]{:S(2)}) collective-permute-start(f32[72,128]{1,0:T(8,128)S(1)} %multiply_add_fusion), channel_id=1, source_target_pairs={{0,48},{16,32},{32,16},{48,0},{64,112},{80,96},{96,80},{112,64},{1... | collective-permute-start | bytes 110600 | tf_op jit(solution)/shard_map/ppermute | solution.py:195
  73.7 9.0 %collective-permute-start.12 = (f32[72,128]{1,0:T(8,128)S(1)}, f32[72,128]{1,0:T(8,128)S(1)}, u32[]{:S(2)}, u32[]{:S(2)}) collective-permute-start(f32[72,128]{1,0:T(8,128)S(1)} %multiply_add_fusion), channel_id=1, source_target_pairs={{0,32},{16,48},{32,0},{48,16},{64,96},{80,112},{96,64},{112,80},{1... | collective-permute-start | bytes 110600 | tf_op jit(solution)/shard_map/ppermute | solution.py:195
  74.3 9.1 %collective-permute-start.11 = (f32[72,128]{1,0:T(8,128)S(1)}, f32[72,128]{1,0:T(8,128)S(1)}, u32[]{:S(2)}, u32[]{:S(2)}) collective-permute-start(f32[72,128]{1,0:T(8,128)S(1)} %multiply_add_fusion), channel_id=1, source_target_pairs={{0,16},{16,0},{32,48},{48,32},{64,80},{80,64},{96,112},{112,96},{1... | collective-permute-start | bytes 110600 | tf_op jit(solution)/shard_map/ppermute | solution.py:195
  83.4 4.9 %collective-permute-start.14 = (f32[4,72,128]{2,1,0:T(8,128)S(1)}, f32[4,72,128]{2,1,0:T(8,128)S(1)}, u32[]{:S(2)}, u32[]{:S(2)}) collective-permute-start(f32[4,72,128]{2,1,0:T(8,128)S(1)} %pad_maximum_fusion.refs_1_), channel_id=1, source_target_pairs={{0,64},{16,80},{32,96},{48,112},{64,0},{80,16},{96,32},{112,48},{1... | collective-permute-start | bytes 442376 | tf_op jit(solution)/shard_map/ppermute | solution.py:195
  83.5 7.7 %collective-permute-start.15 = (f32[4,72,128]{2,1,0:T(8,128)S(1)}, f32[4,72,128]{2,1,0:T(8,128)}, u32[]{:S(2)}, u32[]{:S(2)}) collective-permute-start(f32[4,72,128]{2,1,0:T(8,128)S(1)} %pad_maximum_fusion.refs_1_), channel_id=1, source_target_pairs={{0,128},{16,144},{32,160},{48,176},{64,192},{80,208},{96,224},{112... | collective-permute-start | bytes 442376 | tf_op jit(solution)/shard_map/ppermute | solution.py:195
  85.1 6.8 %collective-permute-start.16 = (f32[4,72,128]{2,1,0:T(8,128)S(1)}, f32[4,72,128]{2,1,0:T(8,128)}, u32[]{:S(2)}, u32[]{:S(2)}) collective-permute-start(f32[4,72,128]{2,1,0:T(8,128)S(1)} %pad_maximum_fusion.refs_1_), channel_id=1, source_target_pairs={{0,192},{16,208},{32,224},{48,240},{64,128},{80,144},{96,160},{112... | collective-permute-start | bytes 442376 | tf_op jit(solution)/shard_map/ppermute | solution.py:195
  100.8 1.0 copy-start.1
  101.7 4.7 %collective-permute-start.23 = (f32[1,128]{1,0:T(1,128)S(1)}, f32[1,128]{1,0:T(1,128)S(1)}, u32[]{:S(2)}, u32[]{:S(2)}) collective-permute-start(f32[1,128]{1,0:T(1,128)S(1)} %get-tuple-element.37), channel_id=1, source_target_pairs={{0,4},{4,0},{8,12},{12,8},{1,5},{5,1},{9,13},{13,9},{2,6},{6,2},{1... | collective-permute-start | bytes 1544 | tf_op jit(solution)/shard_map/ppermute | solution.py:195
  106.4 6.5 %collective-permute-start.24 = (f32[1,128]{1,0:T(1,128)S(1)}, f32[1,128]{1,0:T(1,128)S(1)}, u32[]{:S(2)}, u32[]{:S(2)}) collective-permute-start(f32[1,128]{1,0:T(1,128)S(1)} %add.156), channel_id=1, source_target_pairs={{0,8},{4,12},{8,0},{12,4},{1,9},{5,13},{9,1},{13,5},{2,10},{6,14},... | collective-permute-start | bytes 1544 | tf_op jit(solution)/shard_map/ppermute | solution.py:195
Sparse Core Ops, SparseCore 0:
  30.6 57.4 all-gather.1

commit v7 on v6

--- a/solution.py
+++ b/solution.py
@@ -231,11 +231,11 @@
         side,
     )
     parts = [along_x[0]] + [swap(along_x[k], "shards", k * side) for k in range(1, side)]
-    along_y = [sum(part[j] for part in parts) for j in range(side)]
-    own_stats = along_y[0] + sum(swap(along_y[j], "shards", j) for j in range(1, side))
-    own_stats = own_stats + swap(own_stats, "tensor", 1)
-
-    weights, momentum_then, old_then = after((weights, momentum, old_factors), along_x[0])
+
+    grad_in, weights, momentum_then, old_then = after(
+        (grad_in, weights, momentum, old_factors), along_x[0]
+    )
+    old_block = fold_one(lax.dynamic_slice_in_dim(old_then, shard, 1, 0))
     base_parts = exchange(weights - (step_rate * momentum_rate) * momentum_then, "replica")
     base_rows = []
     for place in range(replica_count):
@@ -244,13 +244,18 @@
             rows = jnp.where(replica ^ flip == place, base_parts[flip], rows)
         base_rows.append(rows)
     base = lax.all_gather(jnp.concatenate(base_rows, axis=0), "shards", axis=0, tiled=True)
-    old_block = fold_one(lax.dynamic_slice_in_dim(old_then, shard, 1, 0))
-
-    grad_parts_in = exchange(jnp.sum(after(grad_in, along_x[0]), axis=0), "replica")
-    own_grad = sum(after(grad_parts_in, own_stats))
+    grad_rows = jnp.sum(grad_in, axis=0)
+    row_parts = exchange(grad_rows, "replica")
+
+    parts = after(parts, (grad_rows, old_block))
+    along_y = [sum(part[j] for part in parts) for j in range(side)]
+    own_stats = along_y[0] + sum(swap(along_y[j], "shards", j) for j in range(1, side))
+    own_stats = own_stats + swap(own_stats, "tensor", 1)
+
+    own_grad = sum(after(row_parts, own_stats))
     gradient = spread(own_grad, "shards").reshape(row_count, col_count)
 
-    own_stats = sum(exchange(after(own_stats, old_block), "replica"))
+    own_stats = sum(exchange(own_stats, "replica"))
     own_stats = own_stats + swap(own_stats, "tensor", 2)
     blended = decay_rate * old_block + ((1.0 - decay_rate) / sample_count) * own_stats
     row_of_y = jnp.stack([blended] + [swap(blended, "shards", j) for j in range(1, side)])

time: 124 us -> 125 us (level)
  starting transfers between devices: 59.7 us -> 56.5 us
  waiting for transfers between devices: 22.5 us -> 25 us
  other arithmetic: 4.09 us -> 5.55 us
    all_to_all x1, waiting for transfers between devices: 0.01 us -> 4.94 us  [body(): lax.all_to_all(partial_grad.reshape(shard_count, piece_rows, col_count),...]
    ppermute x25, waiting for transfers between devices: 22.5 us -> 20.1 us  [swap(): return lax.ppermute(value, axis, [(i, i ^ flip) for i in range(size)])]
    ppermute x25, starting transfers between devices: 47.1 us -> 44.9 us  [swap(): return lax.ppermute(value, axis, [(i, i ^ flip) for i in range(size)])]
  transfers between devices with their start and end apart: 28 -> 28, of which waited for: 13 -> 9; matrix products, arithmetic and copies ran while one was open for 8% -> 8% of each run, Pallas kernels for 10% -> 10%
where the time goes in v7:
time: 125 us; the launch traced here: 124 us
  starting transfers between devices  56.5 us (45%)
  waiting for transfers between devices  25 us (20%)
  Pallas kernels  15.3 us (12%)
  between operations  14.2 us (11%)
  other arithmetic  5.55 us (4%)
  matrix products  3.77 us (3%)
  local copies, waits for them, and re-layouts  3.54 us (3%)
    ppermute x25, starting transfers between devices, swap(): return lax.ppermute(value, axis, [(i, i ^ flip) for i in range(size)])  44.9 us
    ppermute x25, waiting for transfers between devices, swap(): return lax.ppermute(value, axis, [(i, i ^ flip) for i in range(size)])  20.1 us
    pallas_call x1, Pallas kernels, update(): pl.pallas_call(lambda *refs: update_kernel(side, *refs), in_specs=[pl.Blo...  8.84 us
    all_to_all x1, starting transfers between devices, body(): lax.all_to_all(partial_grad.reshape(shard_count, piece_rows, col_count),...  7.73 us
    all_to_all x1, waiting for transfers between devices, body(): lax.all_to_all(partial_grad.reshape(shard_count, piece_rows, col_count),...  4.94 us
    all_to_all x1, starting transfers between devices, spread(): return lax.all_to_all(copies, axis, 0, 0)  3.79 us
    dot_general x2, matrix products, sample_stats(): jnp.einsum('tnb,tnc->nbc', blocks, blocks, preferred_element_type=jnp.flo...  3.77 us
    pallas_call x1, Pallas kernels, finish(): pl.pallas_call(finish_kernel, in_specs=[pl.BlockSpec(memory_space=pltpu.S...  2.78 us
  transfers between devices with their start and end apart: 28, of which 9 were waited for; matrix products, arithmetic and copies ran while one was open for 8% of the time, Pallas kernels for 10%

profile of v7, /device:TPU:1, one launch (start us, length us, event | category | flops | bytes accessed | tf_op | source)
XLA Modules:
  0.0 123.9 jit_solution(6203703953803759661)
XLA Ops:
  7.2 7.7 %all-to-all-start = ((f32[16,64,256]{2,1,0:T(8,128)}), f32[16,64,256]{2,1,0:T(8,128)S(1)}, u32[]{:S(2)}, u32[]{:S(2)}) async-start(f32[16,64,256]{2,1,0:T(8,128)} %bitcast.33), calls=%async_computation | async-start | bytes 2097152 | tf_op jit(solution)/shard_map/all_to_all | solution.py:223
  15.0 0.6 pad_add_fusion.1.place_ref
  15.6 1.8 %fusion.3.left_ref = f32[8,128,128]{2,1,0:T(8,128)} fusion(bf16[1024,1024]{1,0:T(8,128)(2,1)S(1)} %copy-done), kind=kOutput, calls=%fused_computation.3 | convolution fusion | flops 268435456 | bytes 2621440 | tf_op jit(solution)/shard_map/tnb,tnc->nbc/dot_general | solution.py:23
  17.4 1.9 %fusion.right_ref = f32[8,128,128]{2,1,0:T(8,128)} fusion(bf16[1024,1024]{1,0:T(8,128)(2,1)S(1)} %copy-done.5), kind=kOutput, calls=%fused_computation | convolution fusion | flops 268435456 | bytes 2621440 | tf_op jit(solution)/shard_map/tnb,tnc->nbc/dot_general | solution.py:23
  19.4 2.2 %fold.1 = (f32[4,72,128]{2,1,0:T(8,128)}, f32[4,72,128]{2,1,0:T(8,128)}, f32[4,72,128]{2,1,0:T(8,128)}, f32[4,72,128]{2,1,0:T(8,128)}) custom-call(s32[2]{0:T(128)} %pad_add_fusion.1.place_ref, f32[8,128,128]{2,1,0:T(8,128)} %fusion.3.left_ref, f32[8,128,128]{2,1,0:T(8,128)} %fusion.right_ref), custom_call_target="tpu_custom_call" | custom-call | tf_op jit(solution)/shard_map/fold/pallas_call | solution.py:54
  21.5 1.4 %collective-permute-start = (f32[4,72,128]{2,1,0:T(8,128)}, f32[4,72,128]{2,1,0:T(8,128)S(1)}, u32[]{:S(2)}, u32[]{:S(2)}) collective-permute-start(f32[4,72,128]{2,1,0:T(8,128)} %get-tuple-element.28), channel_id=1, source_target_pairs={{0,64},{16,80},{32,96},{48,112},{64,0},{80,16},{96,32},{112,48},{1... | collective-permute-start | bytes 442376 | tf_op jit(solution)/shard_map/ppermute | solution.py:195
  22.9 2.4 %collective-permute-start.1 = (f32[4,72,128]{2,1,0:T(8,128)}, f32[4,72,128]{2,1,0:T(8,128)S(1)}, u32[]{:S(2)}, u32[]{:S(2)}) collective-permute-start(f32[4,72,128]{2,1,0:T(8,128)} %get-tuple-element.29), channel_id=1, source_target_pairs={{0,128},{16,144},{32,160},{48,176},{64,192},{80,208},{96,224},{112... | collective-permute-start | bytes 442376 | tf_op jit(solution)/shard_map/ppermute | solution.py:195
  25.4 4.9 %all-to-all-done = f32[16,64,256]{2,1,0:T(8,128)S(1)} async-done(((f32[16,64,256]{2,1,0:T(8,128)}), f32[16,64,256]{2,1,0:T(8,128)S(1)}, u32[]{:S(2)}, u32[]{:S(2)}) %all-to-all-start) | async-done | bytes 1048608 | tf_op jit(solution)/shard_map/all_to_all | solution.py:223
  30.3 4.4 %collective-permute-start.20 = (f32[16,256]{1,0:T(8,128)S(1)}, f32[16,256]{1,0:T(8,128)S(1)}, u32[]{:S(2)}, u32[]{:S(2)}) collective-permute-start(f32[16,256]{1,0:T(8,128)S(1)} %multiply_subtract_fusion), channel_id=1, source_target_pairs={{0,3},{1,2},{2,1},{3,0},{4,7},{5,6},{6,5},{7,4},{8,11},{9,10},{10,... | collective-permute-start | bytes 49160 | tf_op jit(solution)/shard_map/ppermute | solution.py:195
  34.8 0.4 collective-permute-start.22
  35.2 1.5 %constant_dynamic-slice_fusion.block_ref = f32[1,128,128]{2,1,0:T(8,128)} fusion(f32[16,128,128]{2,1,0:T(8,128)} %param.10, s32[]{:T(128)S(6)} %select_n.95), kind=kLoop, calls=%fused_computation.29 | loop fusion | bytes 131076 | tf_op jit(solution)/shard_map/dynamic_slice | solution.py:238
  36.6 1.5 %fold_one.1 = f32[72,128]{1,0:T(8,128)} custom-call(f32[1,128,128]{2,1,0:T(8,128)} %constant_dynamic-slice_fusion.block_ref), custom_call_target="tpu_custom_call" | custom-call | tf_op jit(solution)/shard_map/fold_one/pallas_call | solution.py:75
  38.3 0.7 select_select_fusion.3
  39.0 0.6 pad_maximum_fusion.1
  39.7 0.9 add_bitcast_fusion.1
  40.6 1.0 collective-permute-start.5
  41.6 2.9 %collective-permute-start.4 = (f32[72,128]{1,0:T(8,128)S(1)}, f32[72,128]{1,0:T(8,128)S(1)}, u32[]{:S(2)}, u32[]{:S(2)}) collective-permute-start(f32[72,128]{1,0:T(8,128)S(1)} %get-tuple-element.49), channel_id=1, source_target_pairs={{0,32},{16,48},{32,0},{48,16},{64,96},{80,112},{96,64},{112,80},{1... | collective-permute-start | bytes 110600 | tf_op jit(solution)/shard_map/ppermute | solution.py:195
  44.5 1.1 collective-permute-start.17
  45.6 2.4 %collective-permute-start.18 = (f32[64,256]{1,0:T(8,128)S(1)}, f32[64,256]{1,0:T(8,128)S(1)}, u32[]{:S(2)}, u32[]{:S(2)}) collective-permute-start(f32[64,256]{1,0:T(8,128)S(1)} %reduce_sum.19), channel_id=1, source_target_pairs={{0,2},{1,3},{2,0},{3,1},{4,6},{5,7},{6,4},{7,5},{8,10},{9,11},{10,... | collective-permute-start | bytes 196616 | tf_op jit(solution)/shard_map/ppermute | solution.py:195
  48.0 0.1 collective-permute-start.19
  48.1 0.8 bitcast_add_fusion
  48.9 6.1 %collective-permute-start.6 = (f32[72,128]{1,0:T(8,128)S(1)}, f32[72,128]{1,0:T(8,128)S(1)}, u32[]{:S(2)}, u32[]{:S(2)}) collective-permute-start(f32[72,128]{1,0:T(8,128)S(1)} %bitcast_add_fusion), channel_id=1, source_target_pairs={{0,4},{4,0},{8,12},{12,8},{1,5},{5,1},{9,13},{13,9},{2,6},{6,2},{1... | collective-permute-start | bytes 110600 | tf_op jit(solution)/shard_map/ppermute | solution.py:195
  55.0 0.9 convert_reduce_fusion
  55.9 2.7 %collective-permute-start.9 = (f32[72,128]{1,0:T(8,128)S(1)}, f32[72,128]{1,0:T(8,128)S(1)}, u32[]{:S(2)}, u32[]{:S(2)}) collective-permute-start(f32[72,128]{1,0:T(8,128)S(1)} %add.147), channel_id=1, source_target_pairs={{0,3},{1,2},{2,1},{3,0},{4,7},{5,6},{6,5},{7,4},{8,11},{9,10},{10,... | collective-permute-start | bytes 110600 | tf_op jit(solution)/shard_map/ppermute | solution.py:195
  58.6 1.0 collective-permute-start.7
  59.6 1.1 broadcast_in_dim.12
  60.6 3.8 %all-to-all-start.1 = ((f32[16,64,256]{2,1,0:T(8,128)}), f32[16,64,256]{2,1,0:T(8,128)S(1)}, u32[]{:S(2)}, u32[]{:S(2)}) async-start(f32[16,64,256]{2,1,0:T(8,128)} %broadcast_in_dim.12), calls=%async_computation.1 | async-start | bytes 2097152 | tf_op jit(solution)/shard_map/all_to_all | solution.py:204
  64.5 5.2 %collective-permute-start.10 = (f32[72,128]{1,0:T(8,128)S(1)}, f32[72,128]{1,0:T(8,128)S(1)}, u32[]{:S(2)}, u32[]{:S(2)}) collective-permute-start(f32[72,128]{1,0:T(8,128)S(1)} %add_add_fusion.1), channel_id=1, source_target_pairs={{0,8},{4,12},{8,0},{12,4},{1,9},{5,13},{9,1},{13,5},{2,10},{6,14},... | collective-permute-start | bytes 110600 | tf_op jit(solution)/shard_map/ppermute | solution.py:195
  69.7 1.5 %collective-permute-done.10 = f32[72,128]{1,0:T(8,128)S(1)} collective-permute-done((f32[72,128]{1,0:T(8,128)S(1)}, f32[72,128]{1,0:T(8,128)S(1)}, u32[]{:S(2)}, u32[]{:S(2)}) %collective-permute-start.10) | collective-permute-done | bytes 36896 | tf_op jit(solution)/shard_map/ppermute | solution.py:195
  71.3 2.7 %collective-permute-start.13 = (f32[72,128]{1,0:T(8,128)S(1)}, f32[72,128]{1,0:T(8,128)S(1)}, u32[]{:S(2)}, u32[]{:S(2)}) collective-permute-start(f32[72,128]{1,0:T(8,128)S(1)} %multiply_add_fusion), channel_id=1, source_target_pairs={{0,48},{16,32},{32,16},{48,0},{64,112},{80,96},{96,80},{112,64},{1... | collective-permute-start | bytes 110600 | tf_op jit(solution)/shard_map/ppermute | solution.py:195
  74.0 0.6 collective-permute-start.12
  74.5 0.1 collective-permute-start.11
  74.6 6.7 %collective-permute-done.13 = f32[72,128]{1,0:T(8,128)S(1)} collective-permute-done((f32[72,128]{1,0:T(8,128)S(1)}, f32[72,128]{1,0:T(8,128)S(1)}, u32[]{:S(2)}, u32[]{:S(2)}) %collective-permute-start.13) | collective-permute-done | bytes 36896 | tf_op jit(solution)/shard_map/ppermute | solution.py:195
  81.4 2.4 %collective-permute-done.12 = f32[72,128]{1,0:T(8,128)S(1)} collective-permute-done((f32[72,128]{1,0:T(8,128)S(1)}, f32[72,128]{1,0:T(8,128)S(1)}, u32[]{:S(2)}, u32[]{:S(2)}) %collective-permute-start.12) | collective-permute-done | bytes 36896 | tf_op jit(solution)/shard_map/ppermute | solution.py:195
  83.9 0.6 collective-permute-start.15
  84.5 3.2 %collective-permute-start.16 = (f32[4,72,128]{2,1,0:T(8,128)S(1)}, f32[4,72,128]{2,1,0:T(8,128)}, u32[]{:S(2)}, u32[]{:S(2)}) collective-permute-start(f32[4,72,128]{2,1,0:T(8,128)S(1)} %pad_maximum_fusion.refs_1_), channel_id=1, source_target_pairs={{0,192},{16,208},{32,224},{48,240},{64,128},{80,144},{96,160},{112... | collective-permute-start | bytes 442376 | tf_op jit(solution)/shard_map/ppermute | solution.py:195
  87.7 0.2 fusion.7
  88.0 2.2 %collective-permute-done.14.refs_2_ = f32[4,72,128]{2,1,0:T(8,128)S(1)} collective-permute-done((f32[4,72,128]{2,1,0:T(8,128)S(1)}, f32[4,72,128]{2,1,0:T(8,128)S(1)}, u32[]{:S(2)}, u32[]{:S(2)}) %collective-permute-start.14) | collective-permute-done | bytes 147488 | tf_op jit(solution)/shard_map/ppermute | solution.py:195
  90.2 3.2 %collective-permute-done.15.refs_3_ = f32[4,72,128]{2,1,0:T(8,128)} collective-permute-done((f32[4,72,128]{2,1,0:T(8,128)S(1)}, f32[4,72,128]{2,1,0:T(8,128)}, u32[]{:S(2)}, u32[]{:S(2)}) %collective-permute-start.15) | collective-permute-done | bytes 147488 | tf_op jit(solution)/shard_map/ppermute | solution.py:195
  93.4 2.0 %collective-permute-done.16.refs_4_ = f32[4,72,128]{2,1,0:T(8,128)} collective-permute-done((f32[4,72,128]{2,1,0:T(8,128)S(1)}, f32[4,72,128]{2,1,0:T(8,128)}, u32[]{:S(2)}, u32[]{:S(2)}) %collective-permute-start.16) | collective-permute-done | bytes 147488 | tf_op jit(solution)/shard_map/ppermute | solution.py:195
  95.4 8.8 %update.1 = (f32[1024,256]{1,0:T(8,128)S(1)}, f32[2,128,128]{2,1,0:T(8,128)}, f32[1,128]{1,0:T(1,128)S(1)}) custom-call(s32[5]{0:T(128)S(1)} %pad_add_fusion.refs_0_, f32[4,72,128]{2,1,0:T(8,128)S(1)} %pad_maximum_fusion.refs_1_, f32[4,72,128]{2,1,0:T(8,128)S(1)} %collective-permute-done.14.refs_2_, f32[4,72,128]{2,1,0:T(8,128)} %collective-permute-done.15.refs_3_, ...), custom_call_target="tpu_custom_call" | custom-call | tf_op jit(solution)/shard_map/update/pallas_call | solution.py:153
  104.2 1.0 copy-done.1
  105.2 1.4 %collective-permute-start.23 = (f32[1,128]{1,0:T(1,128)S(1)}, f32[1,128]{1,0:T(1,128)S(1)}, u32[]{:S(2)}, u32[]{:S(2)}) collective-permute-start(f32[1,128]{1,0:T(1,128)S(1)} %get-tuple-element.43), channel_id=1, source_target_pairs={{0,4},{4,0},{8,12},{12,8},{1,5},{5,1},{9,13},{13,9},{2,6},{6,2},{1... | collective-permute-start | bytes 1544 | tf_op jit(solution)/shard_map/ppermute | solution.py:195
  106.6 0.8 collective-permute-done.23
  107.4 5.1 %collective-permute-start.24 = (f32[1,128]{1,0:T(1,128)S(1)}, f32[1,128]{1,0:T(1,128)S(1)}, u32[]{:S(2)}, u32[]{:S(2)}) collective-permute-start(f32[1,128]{1,0:T(1,128)S(1)} %add.156), channel_id=1, source_target_pairs={{0,8},{4,12},{8,0},{12,4},{1,9},{5,13},{9,1},{13,5},{2,10},{6,14},... | collective-permute-start | bytes 1544 | tf_op jit(solution)/shard_map/ppermute | solution.py:195
  112.6 1.2 collective-permute-done.24
  113.7 0.6 add.157.align_ref
  114.3 2.8 %finish.1 = (f32[1024,256]{1,0:T(8,128)}, f32[16,256]{1,0:T(8,128)}) custom-call(s32[1]{0:T(128)} %bitcast.row_ref, f32[1,128]{1,0:T(1,128)} %add.157.align_ref, f32[16,256]{1,0:T(8,128)} %momentum_ref.1, f32[1024,256]{1,0:T(8,128)} %copy-done.1, f32[1024,256]{1,0:T(8,128)} %all-gather.2.cloned.1.call-done.base_ref), custom_call_target="tpu_custom_call" | custom-call | tf_op jit(solution)/shard_map/finish/pallas_call | solution.py:177
  (50 shorter events, 0.6 us)
Async XLA Ops:
  7.2 8.4 %copy-start = (bf16[1024,1024]{1,0:T(8,128)(2,1)S(1)}, bf16[1024,1024]{1,0:T(8,128)(2,1)}, u32[]{:S(2)}) copy-start(bf16[1024,1024]{1,0:T(8,128)(2,1)} %param.7) | copy-start | bytes 6291460
  7.2 23.1 %all-to-all-start = ((f32[16,64,256]{2,1,0:T(8,128)}), f32[16,64,256]{2,1,0:T(8,128)S(1)}, u32[]{:S(2)}, u32[]{:S(2)}) async-start(f32[16,64,256]{2,1,0:T(8,128)} %bitcast.33), calls=%async_computation | async-start | bytes 2097152 | tf_op jit(solution)/shard_map/all_to_all | solution.py:223
  14.9 90.3 %all-gather.2.cloned.1.call-start = ((), (), s32[]{:S(2)}) async-start(), calls=%async_computation.2 | async-start | bytes 1114112 | tf_op jit(solution)/shard_map/all_gather | solution.py:246
  15.0 2.5 %copy-start.5 = (bf16[1024,1024]{1,0:T(8,128)(2,1)S(1)}, bf16[1024,1024]{1,0:T(8,128)(2,1)}, u32[]{:S(2)}) copy-start(bf16[1024,1024]{1,0:T(8,128)(2,1)} %param.8) | copy-start | bytes 6291460
  17.4 12.9 %copy-start.3 = (f32[16,256]{1,0:T(8,128)S(1)}, f32[16,256]{1,0:T(8,128)}, u32[]{:S(2)}) copy-start(f32[16,256]{1,0:T(8,128)} %momentum_ref.1) | copy-start | bytes 49156
  17.4 12.9 %copy-start.4 = (f32[16,256]{1,0:T(8,128)S(1)}, f32[16,256]{1,0:T(8,128)}, u32[]{:S(2)}) copy-start(f32[16,256]{1,0:T(8,128)} %param.12) | copy-start | bytes 49156
  21.5 13.2 %collective-permute-start = (f32[4,72,128]{2,1,0:T(8,128)}, f32[4,72,128]{2,1,0:T(8,128)S(1)}, u32[]{:S(2)}, u32[]{:S(2)}) collective-permute-start(f32[4,72,128]{2,1,0:T(8,128)} %get-tuple-element.28), channel_id=1, source_target_pairs={{0,64},{16,80},{32,96},{48,112},{64,0},{80,16},{96,32},{112,48},{1... | collective-permute-start | bytes 442376 | tf_op jit(solution)/shard_map/ppermute | solution.py:195
  22.9 15.3 %collective-permute-start.1 = (f32[4,72,128]{2,1,0:T(8,128)}, f32[4,72,128]{2,1,0:T(8,128)S(1)}, u32[]{:S(2)}, u32[]{:S(2)}) collective-permute-start(f32[4,72,128]{2,1,0:T(8,128)} %get-tuple-element.29), channel_id=1, source_target_pairs={{0,128},{16,144},{32,160},{48,176},{64,192},{80,208},{96,224},{112... | collective-permute-start | bytes 442376 | tf_op jit(solution)/shard_map/ppermute | solution.py:195
  25.3 12.9 %collective-permute-start.2 = (f32[4,72,128]{2,1,0:T(8,128)}, f32[4,72,128]{2,1,0:T(8,128)}, u32[]{:S(2)}, u32[]{:S(2)}) collective-permute-start(f32[4,72,128]{2,1,0:T(8,128)} %get-tuple-element.30), channel_id=1, source_target_pairs={{0,192},{16,208},{32,224},{48,240},{64,128},{80,144},{96,160},{112... | collective-permute-start | bytes 442376 | tf_op jit(solution)/shard_map/ppermute | solution.py:195
  30.3 7.9 %collective-permute-start.20 = (f32[16,256]{1,0:T(8,128)S(1)}, f32[16,256]{1,0:T(8,128)S(1)}, u32[]{:S(2)}, u32[]{:S(2)}) collective-permute-start(f32[16,256]{1,0:T(8,128)S(1)} %multiply_subtract_fusion), channel_id=1, source_target_pairs={{0,3},{1,2},{2,1},{3,0},{4,7},{5,6},{6,5},{7,4},{8,11},{9,10},{10,... | collective-permute-start | bytes 49160 | tf_op jit(solution)/shard_map/ppermute | solution.py:195
  34.8 3.5 %collective-permute-start.21 = (f32[16,256]{1,0:T(8,128)S(1)}, f32[16,256]{1,0:T(8,128)S(1)}, u32[]{:S(2)}, u32[]{:S(2)}) collective-permute-start(f32[16,256]{1,0:T(8,128)S(1)} %multiply_subtract_fusion), channel_id=1, source_target_pairs={{0,2},{1,3},{2,0},{3,1},{4,6},{5,7},{6,4},{7,5},{8,10},{9,11},{10,... | collective-permute-start | bytes 49160 | tf_op jit(solution)/shard_map/ppermute | solution.py:195
  34.8 3.5 %collective-permute-start.22 = (f32[16,256]{1,0:T(8,128)S(1)}, f32[16,256]{1,0:T(8,128)}, u32[]{:S(2)}, u32[]{:S(2)}) collective-permute-start(f32[16,256]{1,0:T(8,128)S(1)} %multiply_subtract_fusion), channel_id=1, source_target_pairs={{0,1},{1,0},{2,3},{3,2},{4,5},{5,4},{6,7},{7,6},{8,9},{9,8},{10,11... | collective-permute-start | bytes 49160 | tf_op jit(solution)/shard_map/ppermute | solution.py:195
  40.5 29.2 %copy-start.6 = (s32[16]{0:T(128)S(1)}, s32[16]{0:T(128)}, u32[]{:S(2)}) copy-start(s32[16]{0:T(128)} %param.11) | copy-start | bytes 196
  40.6 30.7 %copy-start.2 = (f32[72,128]{1,0:T(8,128)S(1)}, f32[72,128]{1,0:T(8,128)}, u32[]{:S(2)}) copy-start(f32[72,128]{1,0:T(8,128)} %fold_one.1) | copy-start | bytes 110596
  40.6 7.4 %collective-permute-start.5 = (f32[72,128]{1,0:T(8,128)S(1)}, f32[72,128]{1,0:T(8,128)S(1)}, u32[]{:S(2)}, u32[]{:S(2)}) collective-permute-start(f32[72,128]{1,0:T(8,128)S(1)} %get-tuple-element.50), channel_id=1, source_target_pairs={{0,48},{16,32},{32,16},{48,0},{64,112},{80,96},{96,80},{112,64},{1... | collective-permute-start | bytes 110600 | tf_op jit(solution)/shard_map/ppermute | solution.py:195
  41.6 6.5 %collective-permute-start.3 = (f32[72,128]{1,0:T(8,128)S(1)}, f32[72,128]{1,0:T(8,128)S(1)}, u32[]{:S(2)}, u32[]{:S(2)}) collective-permute-start(f32[72,128]{1,0:T(8,128)S(1)} %get-tuple-element.51), channel_id=1, source_target_pairs={{0,16},{16,0},{32,48},{48,32},{64,80},{80,64},{96,112},{112,96},{1... | collective-permute-start | bytes 110600 | tf_op jit(solution)/shard_map/ppermute | solution.py:195
  41.6 6.5 %collective-permute-start.4 = (f32[72,128]{1,0:T(8,128)S(1)}, f32[72,128]{1,0:T(8,128)S(1)}, u32[]{:S(2)}, u32[]{:S(2)}) collective-permute-start(f32[72,128]{1,0:T(8,128)S(1)} %get-tuple-element.49), channel_id=1, source_target_pairs={{0,32},{16,48},{32,0},{48,16},{64,96},{80,112},{96,64},{112,80},{1... | collective-permute-start | bytes 110600 | tf_op jit(solution)/shard_map/ppermute | solution.py:195
  44.5 14.1 %collective-permute-start.17 = (f32[64,256]{1,0:T(8,128)S(1)}, f32[64,256]{1,0:T(8,128)S(1)}, u32[]{:S(2)}, u32[]{:S(2)}) collective-permute-start(f32[64,256]{1,0:T(8,128)S(1)} %reduce_sum.19), channel_id=1, source_target_pairs={{0,1},{1,0},{2,3},{3,2},{4,5},{5,4},{6,7},{7,6},{8,9},{9,8},{10,11... | collective-permute-start | bytes 196616 | tf_op jit(solution)/shard_map/ppermute | solution.py:195
  45.6 13.9 %collective-permute-start.18 = (f32[64,256]{1,0:T(8,128)S(1)}, f32[64,256]{1,0:T(8,128)S(1)}, u32[]{:S(2)}, u32[]{:S(2)}) collective-permute-start(f32[64,256]{1,0:T(8,128)S(1)} %reduce_sum.19), channel_id=1, source_target_pairs={{0,2},{1,3},{2,0},{3,1},{4,6},{5,7},{6,4},{7,5},{8,10},{9,11},{10,... | collective-permute-start | bytes 196616 | tf_op jit(solution)/shard_map/ppermute | solution.py:195
  48.0 11.6 %collective-permute-start.19 = (f32[64,256]{1,0:T(8,128)S(1)}, f32[64,256]{1,0:T(8,128)S(1)}, u32[]{:S(2)}, u32[]{:S(2)}) collective-permute-start(f32[64,256]{1,0:T(8,128)S(1)} %reduce_sum.19), channel_id=1, source_target_pairs={{0,3},{1,2},{2,1},{3,0},{4,7},{5,6},{6,5},{7,4},{8,11},{9,10},{10,... | collective-permute-start | bytes 196616 | tf_op jit(solution)/shard_map/ppermute | solution.py:195
  48.9 7.0 %collective-permute-start.6 = (f32[72,128]{1,0:T(8,128)S(1)}, f32[72,128]{1,0:T(8,128)S(1)}, u32[]{:S(2)}, u32[]{:S(2)}) collective-permute-start(f32[72,128]{1,0:T(8,128)S(1)} %bitcast_add_fusion), channel_id=1, source_target_pairs={{0,4},{4,0},{8,12},{12,8},{1,5},{5,1},{9,13},{13,9},{2,6},{6,2},{1... | collective-permute-start | bytes 110600 | tf_op jit(solution)/shard_map/ppermute | solution.py:195
  55.9 8.5 %collective-permute-start.9 = (f32[72,128]{1,0:T(8,128)S(1)}, f32[72,128]{1,0:T(8,128)S(1)}, u32[]{:S(2)}, u32[]{:S(2)}) collective-permute-start(f32[72,128]{1,0:T(8,128)S(1)} %add.147), channel_id=1, source_target_pairs={{0,3},{1,2},{2,1},{3,0},{4,7},{5,6},{6,5},{7,4},{8,11},{9,10},{10,... | collective-permute-start | bytes 110600 | tf_op jit(solution)/shard_map/ppermute | solution.py:195
  58.6 5.9 %collective-permute-start.8 = (f32[72,128]{1,0:T(8,128)S(1)}, f32[72,128]{1,0:T(8,128)S(1)}, u32[]{:S(2)}, u32[]{:S(2)}) collective-permute-start(f32[72,128]{1,0:T(8,128)S(1)} %add.147), channel_id=1, source_target_pairs={{0,2},{1,3},{2,0},{3,1},{4,6},{5,7},{6,4},{7,5},{8,10},{9,11},{10,... | collective-permute-start | bytes 110600 | tf_op jit(solution)/shard_map/ppermute | solution.py:195
  58.6 5.9 %collective-permute-start.7 = (f32[72,128]{1,0:T(8,128)S(1)}, f32[72,128]{1,0:T(8,128)S(1)}, u32[]{:S(2)}, u32[]{:S(2)}) collective-permute-start(f32[72,128]{1,0:T(8,128)S(1)} %add.147), channel_id=1, source_target_pairs={{0,1},{1,0},{2,3},{3,2},{4,5},{5,4},{6,7},{7,6},{8,9},{9,8},{10,11... | collective-permute-start | bytes 110600 | tf_op jit(solution)/shard_map/ppermute | solution.py:195
  60.6 34.8 %all-to-all-start.1 = ((f32[16,64,256]{2,1,0:T(8,128)}), f32[16,64,256]{2,1,0:T(8,128)S(1)}, u32[]{:S(2)}, u32[]{:S(2)}) async-start(f32[16,64,256]{2,1,0:T(8,128)} %broadcast_in_dim.12), calls=%async_computation.1 | async-start | bytes 2097152 | tf_op jit(solution)/shard_map/all_to_all | solution.py:204
  64.5 6.8 %collective-permute-start.10 = (f32[72,128]{1,0:T(8,128)S(1)}, f32[72,128]{1,0:T(8,128)S(1)}, u32[]{:S(2)}, u32[]{:S(2)}) collective-permute-start(f32[72,128]{1,0:T(8,128)S(1)} %add_add_fusion.1), channel_id=1, source_target_pairs={{0,8},{4,12},{8,0},{12,4},{1,9},{5,13},{9,1},{13,5},{2,10},{6,14},... | collective-permute-start | bytes 110600 | tf_op jit(solution)/shard_map/ppermute | solution.py:195
  71.3 10.1 %collective-permute-start.13 = (f32[72,128]{1,0:T(8,128)S(1)}, f32[72,128]{1,0:T(8,128)S(1)}, u32[]{:S(2)}, u32[]{:S(2)}) collective-permute-start(f32[72,128]{1,0:T(8,128)S(1)} %multiply_add_fusion), channel_id=1, source_target_pairs={{0,48},{16,32},{32,16},{48,0},{64,112},{80,96},{96,80},{112,64},{1... | collective-permute-start | bytes 110600 | tf_op jit(solution)/shard_map/ppermute | solution.py:195
  74.0 9.8 %collective-permute-start.12 = (f32[72,128]{1,0:T(8,128)S(1)}, f32[72,128]{1,0:T(8,128)S(1)}, u32[]{:S(2)}, u32[]{:S(2)}) collective-permute-start(f32[72,128]{1,0:T(8,128)S(1)} %multiply_add_fusion), channel_id=1, source_target_pairs={{0,32},{16,48},{32,0},{48,16},{64,96},{80,112},{96,64},{112,80},{1... | collective-permute-start | bytes 110600 | tf_op jit(solution)/shard_map/ppermute | solution.py:195
  74.5 9.2 %collective-permute-start.11 = (f32[72,128]{1,0:T(8,128)S(1)}, f32[72,128]{1,0:T(8,128)S(1)}, u32[]{:S(2)}, u32[]{:S(2)}) collective-permute-start(f32[72,128]{1,0:T(8,128)S(1)} %multiply_add_fusion), channel_id=1, source_target_pairs={{0,16},{16,0},{32,48},{48,32},{64,80},{80,64},{96,112},{112,96},{1... | collective-permute-start | bytes 110600 | tf_op jit(solution)/shard_map/ppermute | solution.py:195
  83.8 6.4 %collective-permute-start.14 = (f32[4,72,128]{2,1,0:T(8,128)S(1)}, f32[4,72,128]{2,1,0:T(8,128)S(1)}, u32[]{:S(2)}, u32[]{:S(2)}) collective-permute-start(f32[4,72,128]{2,1,0:T(8,128)S(1)} %pad_maximum_fusion.refs_1_), channel_id=1, source_target_pairs={{0,64},{16,80},{32,96},{48,112},{64,0},{80,16},{96,32},{112,48},{1... | collective-permute-start | bytes 442376 | tf_op jit(solution)/shard_map/ppermute | solution.py:195
  83.9 9.5 %collective-permute-start.15 = (f32[4,72,128]{2,1,0:T(8,128)S(1)}, f32[4,72,128]{2,1,0:T(8,128)}, u32[]{:S(2)}, u32[]{:S(2)}) collective-permute-start(f32[4,72,128]{2,1,0:T(8,128)S(1)} %pad_maximum_fusion.refs_1_), channel_id=1, source_target_pairs={{0,128},{16,144},{32,160},{48,176},{64,192},{80,208},{96,224},{112... | collective-permute-start | bytes 442376 | tf_op jit(solution)/shard_map/ppermute | solution.py:195
  84.5 10.9 %collective-permute-start.16 = (f32[4,72,128]{2,1,0:T(8,128)S(1)}, f32[4,72,128]{2,1,0:T(8,128)}, u32[]{:S(2)}, u32[]{:S(2)}) collective-permute-start(f32[4,72,128]{2,1,0:T(8,128)S(1)} %pad_maximum_fusion.refs_1_), channel_id=1, source_target_pairs={{0,192},{16,208},{32,224},{48,240},{64,128},{80,144},{96,160},{112... | collective-permute-start | bytes 442376 | tf_op jit(solution)/shard_map/ppermute | solution.py:195
  104.2 1.0 copy-start.1
  105.2 2.2 %collective-permute-start.23 = (f32[1,128]{1,0:T(1,128)S(1)}, f32[1,128]{1,0:T(1,128)S(1)}, u32[]{:S(2)}, u32[]{:S(2)}) collective-permute-start(f32[1,128]{1,0:T(1,128)S(1)} %get-tuple-element.43), channel_id=1, source_target_pairs={{0,4},{4,0},{8,12},{12,8},{1,5},{5,1},{9,13},{13,9},{2,6},{6,2},{1... | collective-permute-start | bytes 1544 | tf_op jit(solution)/shard_map/ppermute | solution.py:195
  107.4 6.3 %collective-permute-start.24 = (f32[1,128]{1,0:T(1,128)S(1)}, f32[1,128]{1,0:T(1,128)S(1)}, u32[]{:S(2)}, u32[]{:S(2)}) collective-permute-start(f32[1,128]{1,0:T(1,128)S(1)} %add.156), channel_id=1, source_target_pairs={{0,8},{4,12},{8,0},{12,4},{1,9},{5,13},{9,1},{13,5},{2,10},{6,14},... | collective-permute-start | bytes 1544 | tf_op jit(solution)/shard_map/ppermute | solution.py:195
Sparse Core Ops, SparseCore 0:
  39.8 50.6 all-gather.1

commit v8 on v7

--- a/solution.py
+++ b/solution.py
@@ -34,33 +34,24 @@
     return triangle, jnp.broadcast_to(diagonal, (rows - half, size))
 
 
-def fold_kernel(place_ref, left_ref, right_ref, *folded_refs):
+def fold_kernel(left_ref, right_ref, folded_ref):
     left_count, size, _ = left_ref.shape
-    side = len(folded_refs)
-    rows = folded_refs[0].shape[1]
-    for k in range(side):
-        for j in range(side):
-            n = (place_ref[0] ^ k) * side + (place_ref[1] ^ j)
-            at = n % left_count
-            triangle, diagonal = fold_block(
-                jnp.where(n < left_count, left_ref[at], right_ref[at]), rows
-            )
-            folded_refs[k][j, : size // 2, :] = triangle
-            folded_refs[k][j, size // 2 :, :] = diagonal
-
-
-def fold(places, left_stats, right_stats, side):
-    size = left_stats.shape[1]
+    for n in range(folded_ref.shape[0]):
+        block = left_ref[n] if n < left_count else right_ref[n - left_count]
+        triangle, diagonal = fold_block(block, folded_ref.shape[1])
+        folded_ref[n, : size // 2, :] = triangle
+        folded_ref[n, size // 2 :, :] = diagonal
+
+
+def fold(left_stats, right_stats):
+    count, size, _ = left_stats.shape
     return pl.pallas_call(
         fold_kernel,
-        in_specs=[
-            pl.BlockSpec(memory_space=pltpu.SMEM),
-            pl.BlockSpec(memory_space=pltpu.VMEM),
-            pl.BlockSpec(memory_space=pltpu.VMEM),
-        ],
-        out_shape=[jax.ShapeDtypeStruct((side, size // 2 + 8, size), jnp.float32)] * side,
+        out_shape=jax.ShapeDtypeStruct(
+            (count + right_stats.shape[0], size // 2 + 8, size), jnp.float32
+        ),
         name="fold",
-    )(places, left_stats, right_stats)
+    )(left_stats, right_stats)
 
 
 def fold_one_kernel(block_ref, folded_ref):
@@ -97,27 +88,21 @@
     return jnp.concatenate([top, bottom], axis=0)
 
 
-def update_kernel(side, place_ref, *refs):
-    folded_refs = refs[:side]
-    grad_ref, precond_ref, owned_ref, align_ref, blended_ref = refs[side:]
-    size = blended_ref.shape[2]
-    half = blended_ref.shape[1] - 8
+def update_kernel(place_ref, folded_ref, grad_ref, precond_ref, owned_ref, align_ref):
+    size = folded_ref.shape[2]
+    half = size // 2
     right_count = grad_ref.shape[1] // size
     left_count = grad_ref.shape[0] // size
-    for k in range(side):
-        for j in range(side):
-            n = (place_ref[0] ^ k) * side + (place_ref[1] ^ j)
-            blended_ref[n] = folded_refs[k][j]
 
     def load(block):
-        return unfold(blended_ref[block, :half, :], blended_ref[block, half : half + 1, :])
+        return unfold(folded_ref[block, :half, :], folded_ref[block, half : half + 1, :])
 
     on_diagonal = lax.broadcasted_iota(jnp.int32, (size, size), 0) == lax.broadcasted_iota(
         jnp.int32, (size, size), 1
     )
     unit = jnp.where(on_diagonal, 1.0, 0.0)
     powers, bounds, inverses = [], [], []
-    for block in list(range(left_count)) + [place_ref[2] + n for n in range(right_count)]:
+    for block in list(range(left_count)) + [place_ref[0] + n for n in range(right_count)]:
         mixed = load(block)
         trace = jnp.sum(jnp.where(on_diagonal, mixed, 0.0), keepdims=True)
         damped = mixed + jnp.where(on_diagonal, damping * trace / size + damp_shift, 0.0)
@@ -143,26 +128,28 @@
     align_ref[...] = jnp.broadcast_to(jnp.sum(total, keepdims=True), align_ref.shape)
 
     for place in range(owned_ref.shape[0]):
-        block = place_ref[3 + place]
+        block = place_ref[1 + place]
         value = load(jnp.maximum(block, 0))
         owned_ref[place] = jnp.where(block >= 0, value, jnp.zeros_like(value))
 
 
 def update(places, folded, gradient, capacity):
-    side, rows, size = folded[0].shape
-    return pl.pallas_call(
-        lambda *refs: update_kernel(side, *refs),
-        in_specs=[pl.BlockSpec(memory_space=pltpu.SMEM)]
-        + [pl.BlockSpec(memory_space=pltpu.VMEM)] * (side + 1),
+    size = folded.shape[2]
+    return pl.pallas_call(
+        update_kernel,
+        in_specs=[
+            pl.BlockSpec(memory_space=pltpu.SMEM),
+            pl.BlockSpec(memory_space=pltpu.VMEM),
+            pl.BlockSpec(memory_space=pltpu.VMEM),
+        ],
         out_shape=(
             jax.ShapeDtypeStruct(gradient.shape, jnp.float32),
             jax.ShapeDtypeStruct((capacity, size, size), jnp.float32),
             jax.ShapeDtypeStruct((1, size), jnp.float32),
         ),
-        scratch_shapes=[pltpu.VMEM((side * side, rows, size), jnp.float32)],
         compiler_params=pltpu.CompilerParams(vmem_limit_bytes=40 * 1024 * 1024),
         name="update",
-    )(places, *folded, gradient)
+    )(places, folded, gradient)
 
 
 def finish_kernel(row_ref, align_ref, momentum_ref, precond_ref, base_ref, weights_ref, next_ref):
@@ -222,44 +209,29 @@
 
     grad_in = lax.all_to_all(partial_grad.reshape(shard_count, piece_rows, col_count), "shards", 0, 0)
 
-    side = 4
-    coords = jnp.stack([shard // side, shard % side]).astype(jnp.int32)
-    along_x = fold(
-        coords,
-        sample_stats(activations, block_size),
-        sample_stats(grads_out, block_size),
-        side,
-    )
-    parts = [along_x[0]] + [swap(along_x[k], "shards", k * side) for k in range(1, side)]
-
-    grad_in, weights, momentum_then, old_then = after(
-        (grad_in, weights, momentum, old_factors), along_x[0]
-    )
-    old_block = fold_one(lax.dynamic_slice_in_dim(old_then, shard, 1, 0))
-    base_parts = exchange(weights - (step_rate * momentum_rate) * momentum_then, "replica")
-    base_rows = []
-    for place in range(replica_count):
-        rows = base_parts[0]
-        for flip in range(1, replica_count):
-            rows = jnp.where(replica ^ flip == place, base_parts[flip], rows)
-        base_rows.append(rows)
-    base = lax.all_gather(jnp.concatenate(base_rows, axis=0), "shards", axis=0, tiled=True)
+    folded = fold(sample_stats(activations, block_size), sample_stats(grads_out, block_size))
+    folded, grad_in = lax.optimization_barrier((folded, grad_in))
+    stats_in = lax.all_to_all(folded, "shards", 0, 0)
+
+    base = weights - (step_rate * momentum_rate) * momentum
+    base_rows = lax.dynamic_update_slice_in_dim(
+        jnp.zeros((piece_rows, col_count), jnp.float32), base, replica * own_rows, 0
+    )
     grad_rows = jnp.sum(grad_in, axis=0)
-    row_parts = exchange(grad_rows, "replica")
-
-    parts = after(parts, (grad_rows, old_block))
-    along_y = [sum(part[j] for part in parts) for j in range(side)]
-    own_stats = along_y[0] + sum(swap(along_y[j], "shards", j) for j in range(1, side))
+    rows = sum(exchange(jnp.concatenate([grad_rows, base_rows], axis=0), "replica"))
+    base = lax.all_gather(rows[piece_rows:], "shards", axis=0, tiled=True)
+
+    old_block = fold_one(lax.dynamic_slice_in_dim(after(old_factors, rows), shard, 1, 0))
+    own_stats = jnp.sum(stats_in, axis=0)
+    own_stats, own_grad, old_block = lax.optimization_barrier(
+        (own_stats, rows[:piece_rows], old_block)
+    )
+    gradient = spread(own_grad, "shards").reshape(row_count, col_count)
     own_stats = own_stats + swap(own_stats, "tensor", 1)
-
-    own_grad = sum(after(row_parts, own_stats))
-    gradient = spread(own_grad, "shards").reshape(row_count, col_count)
-
     own_stats = sum(exchange(own_stats, "replica"))
     own_stats = own_stats + swap(own_stats, "tensor", 2)
     blended = decay_rate * old_block + ((1.0 - decay_rate) / sample_count) * own_stats
-    row_of_y = jnp.stack([blended] + [swap(blended, "shards", j) for j in range(1, side)])
-    folded = [row_of_y] + [swap(row_of_y, "shards", k * side) for k in range(1, side)]
+    folded = spread(after(blended, gradient), "shards")
 
     positions = jnp.arange(block_count, dtype=jnp.int32)
     earlier = (block_owner[:, None] == block_owner[None, :]) & (
@@ -269,7 +241,7 @@
     own_slots = shard * capacity + jnp.arange(capacity, dtype=jnp.int32)
     holds = jnp.max(jnp.where(slots[None, :] == own_slots[:, None], positions[None, :], -1), axis=1)
     right_first = left_count + lax.axis_index("tensor") * right_count
-    places = jnp.concatenate([coords, right_first.reshape(1).astype(jnp.int32), holds])
+    places = jnp.concatenate([right_first.reshape(1).astype(jnp.int32), holds])
     precond, owned_blocks, align = update(places, folded, gradient, capacity)
     align, base = lax.optimization_barrier((align, base))
     align = align + swap(align, "tensor", 1)

time: 125 us -> 125 us (level)
  waiting for transfers between devices: 25 us -> 35.8 us
  starting transfers between devices: 56.5 us -> 49 us
  other arithmetic: 5.55 us -> 1.14 us
  local copies, waits for them, and re-layouts: 3.54 us -> 5.05 us
    ppermute x25 -> x10, starting transfers between devices: 44.9 us -> 27 us  [swap(): return lax.ppermute(value, axis, [(i, i ^ flip) for i in range(size)])]
    all_to_all x1 -> x2, waiting for transfers between devices: 0.01 us -> 9.13 us  [spread(): return lax.all_to_all(copies, axis, 0, 0)]
    all_to_all x1 -> x2, starting transfers between devices: 3.79 us -> 10.3 us  [spread(): return lax.all_to_all(copies, axis, 0, 0)]
    ppermute x25 -> x10, waiting for transfers between devices: 20.1 us -> 14.8 us  [swap(): return lax.ppermute(value, axis, [(i, i ^ flip) for i in range(size)])]
    all_to_all x1, waiting for transfers between devices: 4.94 us -> 9.41 us  [body(): lax.all_to_all(partial_grad.reshape(shard_count, piece_rows, col_count),...]
    all_to_all x0 -> x1, starting transfers between devices: none -> 3.97 us  [body(): stats_in = lax.all_to_all(folded, 'shards', 0, 0)]
    all_to_all x0 -> x1, waiting for transfers between devices: none -> 2.5 us  [body(): stats_in = lax.all_to_all(folded, 'shards', 0, 0)]
    add x3 -> x1, other arithmetic: 1.72 us -> 0.03 us  [body(): sum(exchange(jnp.concatenate([grad_rows, base_rows], axis=0), 'replica'))]
  transfers between devices with their start and end apart: 28 -> 15, of which waited for: 9 -> 10; matrix products, arithmetic and copies ran while one was open for 8% -> 7% of each run, Pallas kernels for 10% -> 10%
where the time goes in v8:
time: 125 us; the launch traced here: 124 us
  starting transfers between devices  49 us (39%)
  waiting for transfers between devices  35.8 us (29%)
  Pallas kernels  15.4 us (12%)
  between operations  14.2 us (11%)
  local copies, waits for them, and re-layouts  5.05 us (4%)
  matrix products  3.81 us (3%)
    ppermute x10, starting transfers between devices, swap(): return lax.ppermute(value, axis, [(i, i ^ flip) for i in range(size)])  27 us
    ppermute x10, waiting for transfers between devices, swap(): return lax.ppermute(value, axis, [(i, i ^ flip) for i in range(size)])  14.8 us
    all_to_all x2, starting transfers between devices, spread(): return lax.all_to_all(copies, axis, 0, 0)  10.3 us
    all_to_all x1, waiting for transfers between devices, body(): lax.all_to_all(partial_grad.reshape(shard_count, piece_rows, col_count),...  9.41 us
    all_to_all x2, waiting for transfers between devices, spread(): return lax.all_to_all(copies, axis, 0, 0)  9.13 us
    pallas_call x1, Pallas kernels, update(): pl.pallas_call(update_kernel, in_specs=[pl.BlockSpec(memory_space=pltpu.S...  8.88 us
    all_to_all x1, starting transfers between devices, body(): lax.all_to_all(partial_grad.reshape(shard_count, piece_rows, col_count),...  7.73 us
    all_to_all x1, starting transfers between devices, body(): stats_in = lax.all_to_all(folded, 'shards', 0, 0)  3.97 us
  transfers between devices with their start and end apart: 15, of which 10 were waited for; matrix products, arithmetic and copies ran while one was open for 7% of the time, Pallas kernels for 10%

profile of v8, /device:TPU:1, one launch (start us, length us, event | category | flops | bytes accessed | tf_op | source)
XLA Modules:
  0.0 124.5 jit_solution(1464575583569362647)
XLA Ops:
  7.2 0.0 copy-start
  7.2 7.7 %all-to-all-start = ((f32[16,64,256]{2,1,0:T(8,128)}), f32[16,64,256]{2,1,0:T(8,128)S(1)}, u32[]{:S(2)}, u32[]{:S(2)}) async-start(f32[16,64,256]{2,1,0:T(8,128)} %bitcast.19), calls=%async_computation | async-start | bytes 2097152 | tf_op jit(solution)/shard_map/all_to_all | solution.py:210
  14.9 0.0 copy-start.5
  14.9 1.9 %fusion.right_ref = f32[8,128,128]{2,1,0:T(8,128)} fusion(bf16[1024,1024]{1,0:T(8,128)(2,1)S(1)} %copy-done), kind=kOutput, calls=%fused_computation | convolution fusion | flops 268435456 | bytes 2621440 | tf_op jit(solution)/shard_map/tnb,tnc->nbc/dot_general | solution.py:23
  16.8 1.9 %fusion.3.left_ref = f32[8,128,128]{2,1,0:T(8,128)} fusion(bf16[1024,1024]{1,0:T(8,128)(2,1)S(1)} %copy-done.5), kind=kOutput, calls=%fused_computation.3 | convolution fusion | flops 268435456 | bytes 2621440 | tf_op jit(solution)/shard_map/tnb,tnc->nbc/dot_general | solution.py:23
  18.8 2.2 %fold.1 = f32[16,72,128]{2,1,0:T(8,128)} custom-call(f32[8,128,128]{2,1,0:T(8,128)} %fusion.3.left_ref, f32[8,128,128]{2,1,0:T(8,128)} %fusion.right_ref), custom_call_target="tpu_custom_call" | custom-call | tf_op jit(solution)/shard_map/fold/pallas_call | solution.py:48
  21.0 9.4 %all-to-all-done = f32[16,64,256]{2,1,0:T(8,128)S(1)} async-done(((f32[16,64,256]{2,1,0:T(8,128)}), f32[16,64,256]{2,1,0:T(8,128)S(1)}, u32[]{:S(2)}, u32[]{:S(2)}) %all-to-all-start) | async-done | bytes 1048608 | tf_op jit(solution)/shard_map/all_to_all | solution.py:210
  30.4 0.1 reduce_sum.29
  30.5 1.7 %collective-permute-start = (f32[128,256]{1,0:T(8,128)S(1)}, f32[128,256]{1,0:T(8,128)S(1)}, u32[]{:S(2)}, u32[]{:S(2)}) collective-permute-start(f32[128,256]{1,0:T(8,128)S(1)} %pad_maximum_fusion), channel_id=1, source_target_pairs={{0,1},{1,0},{2,3},{3,2},{4,5},{5,4},{6,7},{7,6},{8,9},{9,8},{10,11... | collective-permute-start | bytes 393224 | tf_op jit(solution)/shard_map/ppermute | solution.py:182
  32.2 3.0 %collective-permute-start.1 = (f32[128,256]{1,0:T(8,128)S(1)}, f32[128,256]{1,0:T(8,128)S(1)}, u32[]{:S(2)}, u32[]{:S(2)}) collective-permute-start(f32[128,256]{1,0:T(8,128)S(1)} %pad_maximum_fusion), channel_id=1, source_target_pairs={{0,2},{1,3},{2,0},{3,1},{4,6},{5,7},{6,4},{7,5},{8,10},{9,11},{10,... | collective-permute-start | bytes 393224 | tf_op jit(solution)/shard_map/ppermute | solution.py:182
  35.2 0.0 collective-permute-start.2
  35.2 4.0 %all-to-all-start.1 = ((f32[16,72,128]{2,1,0:T(8,128)}), f32[16,72,128]{2,1,0:T(8,128)S(1)}, u32[]{:S(2)}, u32[]{:S(2)}) async-start(f32[16,72,128]{2,1,0:T(8,128)} %fold.1), calls=%async_computation.1 | async-start | bytes 1179648 | tf_op jit(solution)/shard_map/all_to_all | solution.py:214
  39.2 0.0 all-gather.2.cloned.1.call-start
  39.3 0.0 collective-permute-done
  39.3 0.0 collective-permute-done.1
  39.3 3.1 %collective-permute-done.2 = f32[128,256]{1,0:T(8,128)S(1)} collective-permute-done((f32[128,256]{1,0:T(8,128)S(1)}, f32[128,256]{1,0:T(8,128)S(1)}, u32[]{:S(2)}, u32[]{:S(2)}) %collective-permute-start.2) | collective-permute-done | bytes 131104 | tf_op jit(solution)/shard_map/ppermute | solution.py:182
  42.4 0.6 fusion.8
  43.0 0.0 all-gather.2.cloned.1.call-update
  43.0 1.5 %constant_dynamic-slice_fusion.block_ref = f32[1,128,128]{2,1,0:T(8,128)} fusion(f32[16,128,128]{2,1,0:T(8,128)} %param.10, s32[]{:T(128)S(6)} %select_n.12), kind=kLoop, calls=%fused_computation.18 | loop fusion | bytes 131076 | tf_op jit(solution)/shard_map/dynamic_slice | solution.py:224
  44.5 1.5 %fold_one.1 = f32[72,128]{1,0:T(8,128)} custom-call(f32[1,128,128]{2,1,0:T(8,128)} %constant_dynamic-slice_fusion.block_ref), custom_call_target="tpu_custom_call" | custom-call | tf_op jit(solution)/shard_map/fold_one/pallas_call | solution.py:66
  46.1 2.5 %all-to-all-done.1 = f32[16,72,128]{2,1,0:T(8,128)S(1)} async-done(((f32[16,72,128]{2,1,0:T(8,128)}), f32[16,72,128]{2,1,0:T(8,128)S(1)}, u32[]{:S(2)}, u32[]{:S(2)}) %all-to-all-start.1) | async-done | bytes 589856 | tf_op jit(solution)/shard_map/all_to_all | solution.py:214
  48.6 1.1 broadcast_in_dim.17
  49.7 3.7 %all-to-all-start.2 = ((f32[16,64,256]{2,1,0:T(8,128)}), f32[16,64,256]{2,1,0:T(8,128)S(1)}, u32[]{:S(2)}, u32[]{:S(2)}) async-start(f32[16,64,256]{2,1,0:T(8,128)} %broadcast_in_dim.17), calls=%async_computation.2 | async-start | bytes 2097152 | tf_op jit(solution)/shard_map/all_to_all | solution.py:191
  53.3 4.4 %collective-permute-start.3 = (f32[72,128]{1,0:T(8,128)S(1)}, f32[72,128]{1,0:T(8,128)S(1)}, u32[]{:S(2)}, u32[]{:S(2)}) collective-permute-start(f32[72,128]{1,0:T(8,128)S(1)} %reduce_sum.28), channel_id=1, source_target_pairs={{0,4},{4,0},{8,12},{12,8},{1,5},{5,1},{9,13},{13,9},{2,6},{6,2},{1... | collective-permute-start | bytes 110600 | tf_op jit(solution)/shard_map/ppermute | solution.py:182
  57.8 0.9 collective-permute-done.3
  58.7 0.3 collective-permute-start.4
  59.0 3.5 %collective-permute-start.5 = (f32[72,128]{1,0:T(8,128)S(1)}, f32[72,128]{1,0:T(8,128)S(1)}, u32[]{:S(2)}, u32[]{:S(2)}) collective-permute-start(f32[72,128]{1,0:T(8,128)S(1)} %add.64), channel_id=1, source_target_pairs={{0,2},{1,3},{2,0},{3,1},{4,6},{5,7},{6,4},{7,5},{8,10},{9,11},{10,... | collective-permute-start | bytes 110600 | tf_op jit(solution)/shard_map/ppermute | solution.py:182
  62.5 0.0 collective-permute-start.6
  62.5 0.0 collective-permute-done.4
  62.5 2.1 %collective-permute-done.5 = f32[72,128]{1,0:T(8,128)S(1)} collective-permute-done((f32[72,128]{1,0:T(8,128)S(1)}, f32[72,128]{1,0:T(8,128)S(1)}, u32[]{:S(2)}, u32[]{:S(2)}) %collective-permute-start.5) | collective-permute-done | bytes 36896 | tf_op jit(solution)/shard_map/ppermute | solution.py:182
  64.6 2.8 %collective-permute-done.6 = f32[72,128]{1,0:T(8,128)S(1)} collective-permute-done((f32[72,128]{1,0:T(8,128)S(1)}, f32[72,128]{1,0:T(8,128)S(1)}, u32[]{:S(2)}, u32[]{:S(2)}) %collective-permute-start.6) | collective-permute-done | bytes 36896 | tf_op jit(solution)/shard_map/ppermute | solution.py:182
  67.4 4.3 %collective-permute-start.7 = (f32[72,128]{1,0:T(8,128)S(1)}, f32[72,128]{1,0:T(8,128)S(1)}, u32[]{:S(2)}, u32[]{:S(2)}) collective-permute-start(f32[72,128]{1,0:T(8,128)S(1)} %add_add_fusion.1), channel_id=1, source_target_pairs={{0,8},{4,12},{8,0},{12,4},{1,9},{5,13},{9,1},{13,5},{2,10},{6,14},... | collective-permute-start | bytes 110600 | tf_op jit(solution)/shard_map/ppermute | solution.py:182
  71.7 0.2 convert_reduce_fusion
  71.9 2.3 %collective-permute-done.7 = f32[72,128]{1,0:T(8,128)S(1)} collective-permute-done((f32[72,128]{1,0:T(8,128)S(1)}, f32[72,128]{1,0:T(8,128)S(1)}, u32[]{:S(2)}, u32[]{:S(2)}) %collective-permute-start.7) | collective-permute-done | bytes 36896 | tf_op jit(solution)/shard_map/ppermute | solution.py:182
  74.2 0.0 all-to-all-done.2
  74.2 0.9 broadcast_in_dim.18
  75.1 6.7 %all-to-all-start.3 = ((f32[16,72,128]{2,1,0:T(8,128)}), f32[16,72,128]{2,1,0:T(8,128)}, u32[]{:S(2)}, u32[]{:S(2)}) async-start(f32[16,72,128]{2,1,0:T(8,128)} %broadcast_in_dim.18), calls=%async_computation.3 | async-start | bytes 1179648 | tf_op jit(solution)/shard_map/all_to_all | solution.py:191
  81.8 0.2 fusion.7
  82.0 0.1 pad_add_fusion.place_ref
  82.0 9.1 %all-to-all-done.3.folded_ref = f32[16,72,128]{2,1,0:T(8,128)} async-done(((f32[16,72,128]{2,1,0:T(8,128)}), f32[16,72,128]{2,1,0:T(8,128)}, u32[]{:S(2)}, u32[]{:S(2)}) %all-to-all-start.3) | async-done | bytes 589856 | tf_op jit(solution)/shard_map/all_to_all | solution.py:191
  91.2 8.9 %update.1 = (f32[1024,256]{1,0:T(8,128)S(1)}, f32[2,128,128]{2,1,0:T(8,128)}, f32[1,128]{1,0:T(1,128)S(1)}) custom-call(s32[3]{0:T(128)S(1)} %pad_add_fusion.place_ref, f32[16,72,128]{2,1,0:T(8,128)} %all-to-all-done.3.folded_ref, f32[1024,256]{1,0:T(8,128)S(1)} %bitcast.18), custom_call_target="tpu_custom_call" | custom-call | tf_op jit(solution)/shard_map/update/pallas_call | solution.py:138
  100.1 1.0 copy-done.1
  101.0 6.2 %collective-permute-start.8 = (f32[1,128]{1,0:T(1,128)S(1)}, f32[1,128]{1,0:T(1,128)S(1)}, u32[]{:S(2)}, u32[]{:S(2)}) collective-permute-start(f32[1,128]{1,0:T(1,128)S(1)} %get-tuple-element.25), channel_id=1, source_target_pairs={{0,4},{4,0},{8,12},{12,8},{1,5},{5,1},{9,13},{13,9},{2,6},{6,2},{1... | collective-permute-start | bytes 1544 | tf_op jit(solution)/shard_map/ppermute | solution.py:182
  107.2 0.8 collective-permute-done.8
  108.0 3.5 %collective-permute-start.9 = (f32[1,128]{1,0:T(1,128)S(1)}, f32[1,128]{1,0:T(1,128)S(1)}, u32[]{:S(2)}, u32[]{:S(2)}) collective-permute-start(f32[1,128]{1,0:T(1,128)S(1)} %add.70), channel_id=1, source_target_pairs={{0,8},{4,12},{8,0},{12,4},{1,9},{5,13},{9,1},{13,5},{2,10},{6,14},... | collective-permute-start | bytes 1544 | tf_op jit(solution)/shard_map/ppermute | solution.py:182
  111.6 2.8 %collective-permute-done.9 = f32[1,128]{1,0:T(1,128)S(1)} collective-permute-done((f32[1,128]{1,0:T(1,128)S(1)}, f32[1,128]{1,0:T(1,128)S(1)}, u32[]{:S(2)}, u32[]{:S(2)}) %collective-permute-start.9) | collective-permute-done | bytes 544 | tf_op jit(solution)/shard_map/ppermute | solution.py:182
  114.3 0.5 add.71.align_ref
  114.8 2.8 %finish.1 = (f32[1024,256]{1,0:T(8,128)}, f32[16,256]{1,0:T(8,128)}) custom-call(s32[1]{0:T(128)} %bitcast.row_ref, f32[1,128]{1,0:T(1,128)} %add.71.align_ref, f32[16,256]{1,0:T(8,128)} %momentum_ref.1, f32[1024,256]{1,0:T(8,128)} %copy-done.1, f32[1024,256]{1,0:T(8,128)} %all-gather.2.cloned.1.call-done.base_ref), custom_call_target="tpu_custom_call" | custom-call | tf_op jit(solution)/shard_map/finish/pallas_call | solution.py:164
  (23 shorter events, 0.2 us)
Async XLA Ops:
  7.2 7.8 %copy-start = (bf16[1024,1024]{1,0:T(8,128)(2,1)S(1)}, bf16[1024,1024]{1,0:T(8,128)(2,1)}, u32[]{:S(2)}) copy-start(bf16[1024,1024]{1,0:T(8,128)(2,1)} %param.8) | copy-start | bytes 6291460
  7.2 23.2 %all-to-all-start = ((f32[16,64,256]{2,1,0:T(8,128)}), f32[16,64,256]{2,1,0:T(8,128)S(1)}, u32[]{:S(2)}, u32[]{:S(2)}) async-start(f32[16,64,256]{2,1,0:T(8,128)} %bitcast.19), calls=%async_computation | async-start | bytes 2097152 | tf_op jit(solution)/shard_map/all_to_all | solution.py:210
  14.9 1.9 %copy-start.5 = (bf16[1024,1024]{1,0:T(8,128)(2,1)S(1)}, bf16[1024,1024]{1,0:T(8,128)(2,1)}, u32[]{:S(2)}) copy-start(bf16[1024,1024]{1,0:T(8,128)(2,1)} %param.7) | copy-start | bytes 6291460
  16.8 4.2 %copy-start.3 = (f32[16,256]{1,0:T(8,128)S(1)}, f32[16,256]{1,0:T(8,128)}, u32[]{:S(2)}) copy-start(f32[16,256]{1,0:T(8,128)} %momentum_ref.1) | copy-start | bytes 49156
  16.8 4.2 %copy-start.4 = (f32[16,256]{1,0:T(8,128)S(1)}, f32[16,256]{1,0:T(8,128)}, u32[]{:S(2)}) copy-start(f32[16,256]{1,0:T(8,128)} %param.12) | copy-start | bytes 49156
  30.5 8.7 %collective-permute-start = (f32[128,256]{1,0:T(8,128)S(1)}, f32[128,256]{1,0:T(8,128)S(1)}, u32[]{:S(2)}, u32[]{:S(2)}) collective-permute-start(f32[128,256]{1,0:T(8,128)S(1)} %pad_maximum_fusion), channel_id=1, source_target_pairs={{0,1},{1,0},{2,3},{3,2},{4,5},{5,4},{6,7},{7,6},{8,9},{9,8},{10,11... | collective-permute-start | bytes 393224 | tf_op jit(solution)/shard_map/ppermute | solution.py:182
  32.2 7.0 %collective-permute-start.1 = (f32[128,256]{1,0:T(8,128)S(1)}, f32[128,256]{1,0:T(8,128)S(1)}, u32[]{:S(2)}, u32[]{:S(2)}) collective-permute-start(f32[128,256]{1,0:T(8,128)S(1)} %pad_maximum_fusion), channel_id=1, source_target_pairs={{0,2},{1,3},{2,0},{3,1},{4,6},{5,7},{6,4},{7,5},{8,10},{9,11},{10,... | collective-permute-start | bytes 393224 | tf_op jit(solution)/shard_map/ppermute | solution.py:182
  35.2 7.1 %collective-permute-start.2 = (f32[128,256]{1,0:T(8,128)S(1)}, f32[128,256]{1,0:T(8,128)S(1)}, u32[]{:S(2)}, u32[]{:S(2)}) collective-permute-start(f32[128,256]{1,0:T(8,128)S(1)} %pad_maximum_fusion), channel_id=1, source_target_pairs={{0,3},{1,2},{2,1},{3,0},{4,7},{5,6},{6,5},{7,4},{8,11},{9,10},{10,... | collective-permute-start | bytes 393224 | tf_op jit(solution)/shard_map/ppermute | solution.py:182
  35.2 13.3 %all-to-all-start.1 = ((f32[16,72,128]{2,1,0:T(8,128)}), f32[16,72,128]{2,1,0:T(8,128)S(1)}, u32[]{:S(2)}, u32[]{:S(2)}) async-start(f32[16,72,128]{2,1,0:T(8,128)} %fold.1), calls=%async_computation.1 | async-start | bytes 1179648 | tf_op jit(solution)/shard_map/all_to_all | solution.py:214
  39.2 61.8 %all-gather.2.cloned.1.call-start = ((), (), s32[]{:S(2)}) async-start(), calls=%async_computation.4 | async-start | bytes 1114112 | tf_op jit(solution)/shard_map/all_gather | solution.py:222
  44.5 27.2 %copy-start.6 = (s32[16]{0:T(128)S(1)}, s32[16]{0:T(128)}, u32[]{:S(2)}) copy-start(s32[16]{0:T(128)} %param.11) | copy-start | bytes 196
  46.1 28.1 %copy-start.2 = (f32[72,128]{1,0:T(8,128)S(1)}, f32[72,128]{1,0:T(8,128)}, u32[]{:S(2)}) copy-start(f32[72,128]{1,0:T(8,128)} %fold_one.1) | copy-start | bytes 110596
  49.7 24.5 %all-to-all-start.2 = ((f32[16,64,256]{2,1,0:T(8,128)}), f32[16,64,256]{2,1,0:T(8,128)S(1)}, u32[]{:S(2)}, u32[]{:S(2)}) async-start(f32[16,64,256]{2,1,0:T(8,128)} %broadcast_in_dim.17), calls=%async_computation.2 | async-start | bytes 2097152 | tf_op jit(solution)/shard_map/all_to_all | solution.py:191
  53.3 5.3 %collective-permute-start.3 = (f32[72,128]{1,0:T(8,128)S(1)}, f32[72,128]{1,0:T(8,128)S(1)}, u32[]{:S(2)}, u32[]{:S(2)}) collective-permute-start(f32[72,128]{1,0:T(8,128)S(1)} %reduce_sum.28), channel_id=1, source_target_pairs={{0,4},{4,0},{8,12},{12,8},{1,5},{5,1},{9,13},{13,9},{2,6},{6,2},{1... | collective-permute-start | bytes 110600 | tf_op jit(solution)/shard_map/ppermute | solution.py:182
  58.7 3.8 %collective-permute-start.4 = (f32[72,128]{1,0:T(8,128)S(1)}, f32[72,128]{1,0:T(8,128)S(1)}, u32[]{:S(2)}, u32[]{:S(2)}) collective-permute-start(f32[72,128]{1,0:T(8,128)S(1)} %add.64), channel_id=1, source_target_pairs={{0,1},{1,0},{2,3},{3,2},{4,5},{5,4},{6,7},{7,6},{8,9},{9,8},{10,11... | collective-permute-start | bytes 110600 | tf_op jit(solution)/shard_map/ppermute | solution.py:182
  59.0 5.6 %collective-permute-start.5 = (f32[72,128]{1,0:T(8,128)S(1)}, f32[72,128]{1,0:T(8,128)S(1)}, u32[]{:S(2)}, u32[]{:S(2)}) collective-permute-start(f32[72,128]{1,0:T(8,128)S(1)} %add.64), channel_id=1, source_target_pairs={{0,2},{1,3},{2,0},{3,1},{4,6},{5,7},{6,4},{7,5},{8,10},{9,11},{10,... | collective-permute-start | bytes 110600 | tf_op jit(solution)/shard_map/ppermute | solution.py:182
  62.5 4.9 %collective-permute-start.6 = (f32[72,128]{1,0:T(8,128)S(1)}, f32[72,128]{1,0:T(8,128)S(1)}, u32[]{:S(2)}, u32[]{:S(2)}) collective-permute-start(f32[72,128]{1,0:T(8,128)S(1)} %add.64), channel_id=1, source_target_pairs={{0,3},{1,2},{2,1},{3,0},{4,7},{5,6},{6,5},{7,4},{8,11},{9,10},{10,... | collective-permute-start | bytes 110600 | tf_op jit(solution)/shard_map/ppermute | solution.py:182
  67.4 6.8 %collective-permute-start.7 = (f32[72,128]{1,0:T(8,128)S(1)}, f32[72,128]{1,0:T(8,128)S(1)}, u32[]{:S(2)}, u32[]{:S(2)}) collective-permute-start(f32[72,128]{1,0:T(8,128)S(1)} %add_add_fusion.1), channel_id=1, source_target_pairs={{0,8},{4,12},{8,0},{12,4},{1,9},{5,13},{9,1},{13,5},{2,10},{6,14},... | collective-permute-start | bytes 110600 | tf_op jit(solution)/shard_map/ppermute | solution.py:182
  75.1 16.1 %all-to-all-start.3 = ((f32[16,72,128]{2,1,0:T(8,128)}), f32[16,72,128]{2,1,0:T(8,128)}, u32[]{:S(2)}, u32[]{:S(2)}) async-start(f32[16,72,128]{2,1,0:T(8,128)} %broadcast_in_dim.18), calls=%async_computation.3 | async-start | bytes 1179648 | tf_op jit(solution)/shard_map/all_to_all | solution.py:191
  100.1 1.0 copy-start.1
  101.0 7.0 %collective-permute-start.8 = (f32[1,128]{1,0:T(1,128)S(1)}, f32[1,128]{1,0:T(1,128)S(1)}, u32[]{:S(2)}, u32[]{:S(2)}) collective-permute-start(f32[1,128]{1,0:T(1,128)S(1)} %get-tuple-element.25), channel_id=1, source_target_pairs={{0,4},{4,0},{8,12},{12,8},{1,5},{5,1},{9,13},{13,9},{2,6},{6,2},{1... | collective-permute-start | bytes 1544 | tf_op jit(solution)/shard_map/ppermute | solution.py:182
  108.0 6.3 %collective-permute-start.9 = (f32[1,128]{1,0:T(1,128)S(1)}, f32[1,128]{1,0:T(1,128)S(1)}, u32[]{:S(2)}, u32[]{:S(2)}) collective-permute-start(f32[1,128]{1,0:T(1,128)S(1)} %add.70), channel_id=1, source_target_pairs={{0,8},{4,12},{8,0},{12,4},{1,9},{5,13},{9,1},{13,5},{2,10},{6,14},... | collective-permute-start | bytes 1544 | tf_op jit(solution)/shard_map/ppermute | solution.py:182
Sparse Core Ops, SparseCore 0:
  43.2 57.1 all-gather.1

commit v9 on v8

--- a/solution.py
+++ b/solution.py
@@ -88,11 +88,11 @@
     return jnp.concatenate([top, bottom], axis=0)
 
 
-def update_kernel(place_ref, folded_ref, grad_ref, precond_ref, owned_ref, align_ref):
-    size = folded_ref.shape[2]
+def inverse_kernel(place_ref, folded_ref, inverse_ref, owned_ref):
+    needed, size, _ = inverse_ref.shape
     half = size // 2
-    right_count = grad_ref.shape[1] // size
-    left_count = grad_ref.shape[0] // size
+    right_count = needed - folded_ref.shape[0] // 2
+    left_count = needed - right_count
 
     def load(block):
         return unfold(folded_ref[block, :half, :], folded_ref[block, half : half + 1, :])
@@ -114,18 +114,8 @@
     for step in range(NS_STEPS - 1):
         powers = [dot(power, power) for power in powers]
         inverses = [x + dot(x, power) for x, power in zip(inverses, powers)]
-    inverses = [x / bound for x, bound in zip(inverses, bounds)]
-
-    total = jnp.zeros((size, size), jnp.float32)
-    for a in range(left_count):
-        rows = slice(a * size, (a + 1) * size)
-        left_part = dot(inverses[a], grad_ref[rows, :])
-        for c in range(right_count):
-            cols = slice(c * size, (c + 1) * size)
-            value = dot(left_part[:, cols], inverses[left_count + c])
-            precond_ref[rows, cols] = value
-            total = total + value * grad_ref[rows, cols]
-    align_ref[...] = jnp.broadcast_to(jnp.sum(total, keepdims=True), align_ref.shape)
+    for n, (x, bound) in enumerate(zip(inverses, bounds)):
+        inverse_ref[n] = x / bound
 
     for place in range(owned_ref.shape[0]):
         block = place_ref[1 + place]
@@ -133,23 +123,47 @@
         owned_ref[place] = jnp.where(block >= 0, value, jnp.zeros_like(value))
 
 
-def update(places, folded, gradient, capacity):
+def invert_needed(places, folded, needed, capacity):
     size = folded.shape[2]
     return pl.pallas_call(
-        update_kernel,
+        inverse_kernel,
         in_specs=[
             pl.BlockSpec(memory_space=pltpu.SMEM),
             pl.BlockSpec(memory_space=pltpu.VMEM),
-            pl.BlockSpec(memory_space=pltpu.VMEM),
         ],
         out_shape=(
+            jax.ShapeDtypeStruct((needed, size, size), jnp.float32),
+            jax.ShapeDtypeStruct((capacity, size, size), jnp.float32),
+        ),
+        name="inverse",
+    )(places, folded)
+
+
+def precondition_kernel(inverse_ref, grad_ref, precond_ref, align_ref):
+    size = inverse_ref.shape[1]
+    left_count = grad_ref.shape[0] // size
+    right_count = grad_ref.shape[1] // size
+    total = jnp.zeros((size, size), jnp.float32)
+    for a in range(left_count):
+        rows = slice(a * size, (a + 1) * size)
+        left_part = dot(inverse_ref[a], grad_ref[rows, :])
+        for c in range(right_count):
+            cols = slice(c * size, (c + 1) * size)
+            value = dot(left_part[:, cols], inverse_ref[left_count + c])
+            precond_ref[rows, cols] = value
+            total = total + value * grad_ref[rows, cols]
+    align_ref[...] = jnp.broadcast_to(jnp.sum(total, keepdims=True), align_ref.shape)
+
+
+def precondition(inverses, gradient):
+    return pl.pallas_call(
+        precondition_kernel,
+        out_shape=(
             jax.ShapeDtypeStruct(gradient.shape, jnp.float32),
-            jax.ShapeDtypeStruct((capacity, size, size), jnp.float32),
-            jax.ShapeDtypeStruct((1, size), jnp.float32),
-        ),
-        compiler_params=pltpu.CompilerParams(vmem_limit_bytes=40 * 1024 * 1024),
-        name="update",
-    )(places, folded, gradient)
+            jax.ShapeDtypeStruct((1, inverses.shape[2]), jnp.float32),
+        ),
+        name="precondition",
+    )(inverses, gradient)
 
 
 def finish_kernel(row_ref, align_ref, momentum_ref, precond_ref, base_ref, weights_ref, next_ref):
@@ -207,31 +221,34 @@
     shard = lax.axis_index("shards")
     replica = lax.axis_index("replica")
 
-    grad_in = lax.all_to_all(partial_grad.reshape(shard_count, piece_rows, col_count), "shards", 0, 0)
-
     folded = fold(sample_stats(activations, block_size), sample_stats(grads_out, block_size))
-    folded, grad_in = lax.optimization_barrier((folded, grad_in))
     stats_in = lax.all_to_all(folded, "shards", 0, 0)
 
-    base = weights - (step_rate * momentum_rate) * momentum
-    base_rows = lax.dynamic_update_slice_in_dim(
-        jnp.zeros((piece_rows, col_count), jnp.float32), base, replica * own_rows, 0
-    )
-    grad_rows = jnp.sum(grad_in, axis=0)
-    rows = sum(exchange(jnp.concatenate([grad_rows, base_rows], axis=0), "replica"))
-    base = lax.all_gather(rows[piece_rows:], "shards", axis=0, tiled=True)
-
-    old_block = fold_one(lax.dynamic_slice_in_dim(after(old_factors, rows), shard, 1, 0))
-    own_stats = jnp.sum(stats_in, axis=0)
-    own_stats, own_grad, old_block = lax.optimization_barrier(
-        (own_stats, rows[:piece_rows], old_block)
-    )
-    gradient = spread(own_grad, "shards").reshape(row_count, col_count)
+    weights, momentum_then, old_then = after((weights, momentum, old_factors), folded)
+    base_parts = exchange(weights - (step_rate * momentum_rate) * momentum_then, "replica")
+    base_rows = []
+    for place in range(replica_count):
+        rows = base_parts[0]
+        for flip in range(1, replica_count):
+            rows = jnp.where(replica ^ flip == place, base_parts[flip], rows)
+        base_rows.append(rows)
+    base_rows = jnp.concatenate(base_rows, axis=0)
+    old_block = fold_one(lax.dynamic_slice_in_dim(old_then, shard, 1, 0))
+    base = lax.all_gather(base_rows, "shards", axis=0, tiled=True)
+
+    own_stats = after(jnp.sum(stats_in, axis=0), (base_rows, old_block))
+    grad_in = lax.all_to_all(
+        after(partial_grad, own_stats).reshape(shard_count, piece_rows, col_count), "shards", 0, 0
+    )
     own_stats = own_stats + swap(own_stats, "tensor", 1)
     own_stats = sum(exchange(own_stats, "replica"))
     own_stats = own_stats + swap(own_stats, "tensor", 2)
     blended = decay_rate * old_block + ((1.0 - decay_rate) / sample_count) * own_stats
-    folded = spread(after(blended, gradient), "shards")
+    blended, grad_in = lax.optimization_barrier((blended, grad_in))
+    folded = spread(blended, "shards")
+    own_grad = sum(exchange(jnp.sum(grad_in, axis=0), "replica"))
+    folded, own_grad = lax.optimization_barrier((folded, own_grad))
+    gradient = spread(own_grad, "shards").reshape(row_count, col_count)
 
     positions = jnp.arange(block_count, dtype=jnp.int32)
     earlier = (block_owner[:, None] == block_owner[None, :]) & (
@@ -242,7 +259,8 @@
     holds = jnp.max(jnp.where(slots[None, :] == own_slots[:, None], positions[None, :], -1), axis=1)
     right_first = left_count + lax.axis_index("tensor") * right_count
     places = jnp.concatenate([right_first.reshape(1).astype(jnp.int32), holds])
-    precond, owned_blocks, align = update(places, folded, gradient, capacity)
+    inverses, owned_blocks = invert_needed(places, folded, left_count + right_count, capacity)
+    precond, align = precondition(inverses, gradient)
     align, base = lax.optimization_barrier((align, base))
     align = align + swap(align, "tensor", 1)
     align = align + swap(align, "tensor", 2)

time: 125 us -> 123 us (0.984)
  waiting for transfers between devices: 35.8 us -> 27.8 us
  Pallas kernels: 15.4 us -> 18.4 us
  other arithmetic: 1.14 us -> 3.07 us
    all_to_all x1, waiting for transfers between devices: 9.41 us -> 0.01 us  [body(): lax.all_to_all(after(partial_grad, own_stats).reshape(shard_count, piece_...]
    all_gather x1, waiting for transfers between devices: 0.01 us -> 5.38 us  [body(): base = lax.all_gather(base_rows, 'shards', axis=0, tiled=True)]
    all_to_all x1, starting transfers between devices: 3.97 us -> 7.58 us  [body(): stats_in = lax.all_to_all(folded, 'shards', 0, 0)]
    all_to_all x2, waiting for transfers between devices: 9.13 us -> 5.77 us  [spread(): return lax.all_to_all(copies, axis, 0, 0)]
    all_to_all x1, starting transfers between devices: 7.73 us -> 4.56 us  [body(): lax.all_to_all(after(partial_grad, own_stats).reshape(shard_count, piece_...]
    pallas_call x1 -> x2, Pallas kernels: 8.88 us -> 11.8 us  [the longest x1 7.25 us: invert_needed(): pl.pallas_call(inverse_kernel, in_specs=[pl.BlockSpec(memory_space=pltpu....]
    unnamed x14, local copies, waits for them, and re-layouts: 1.01 us -> 2.57 us
    ppermute x10 -> x13, starting transfers between devices: 27 us -> 25.9 us  [swap(): return lax.ppermute(value, axis, [(i, i ^ flip) for i in range(size)])]
  transfers between devices with their start and end apart: 15 -> 18, of which waited for: 10 -> 13; matrix products, arithmetic and copies ran while one was open for 7% -> 4% of each run, Pallas kernels for 10% -> 11%
where the time goes in v9:
time: 123 us
  starting transfers between devices  49.5 us (40%)
  waiting for transfers between devices  27.8 us (23%)
  Pallas kernels  18.4 us (15%)
  between operations  14.2 us (12%)
  local copies, waits for them, and re-layouts  5.97 us (5%)
  matrix products  3.78 us (3%)
  other arithmetic  3.07 us (2%)
    ppermute x13, starting transfers between devices, swap(): return lax.ppermute(value, axis, [(i, i ^ flip) for i in range(size)])  25.9 us
    ppermute x13, waiting for transfers between devices, swap(): return lax.ppermute(value, axis, [(i, i ^ flip) for i in range(size)])  14.5 us
    all_to_all x2, starting transfers between devices, spread(): return lax.all_to_all(copies, axis, 0, 0)  11.4 us
    all_to_all x1, starting transfers between devices, body(): stats_in = lax.all_to_all(folded, 'shards', 0, 0)  7.58 us
    pallas_call x1, Pallas kernels, invert_needed(): pl.pallas_call(inverse_kernel, in_specs=[pl.BlockSpec(memory_space=pltpu....  7.25 us
    all_to_all x2, waiting for transfers between devices, spread(): return lax.all_to_all(copies, axis, 0, 0)  5.77 us
    all_gather x1, waiting for transfers between devices, body(): base = lax.all_gather(base_rows, 'shards', axis=0, tiled=True)  5.38 us
    all_to_all x1, starting transfers between devices, body(): lax.all_to_all(after(partial_grad, own_stats).reshape(shard_count, piece_...  4.56 us
  transfers between devices with their start and end apart: 18, of which 13 were waited for; matrix products, arithmetic and copies ran while one was open for 4% of the time, Pallas kernels for 11%

profile of v9, /device:TPU:1, one launch (start us, length us, event | category | flops | bytes accessed | tf_op | source)
XLA Modules:
  0.0 122.7 jit_solution(1424108426727849693)
XLA Ops:
  7.2 1.6 %copy-done = bf16[1024,1024]{1,0:T(8,128)(2,1)S(1)} copy-done((bf16[1024,1024]{1,0:T(8,128)(2,1)S(1)}, bf16[1024,1024]{1,0:T(8,128)(2,1)}, u32[]{:S(2)}) %copy-start) | copy-done | bytes 2097176
  8.8 1.8 %fusion.right_ref = f32[8,128,128]{2,1,0:T(8,128)} fusion(bf16[1024,1024]{1,0:T(8,128)(2,1)S(1)} %copy-done), kind=kOutput, calls=%fused_computation | convolution fusion | flops 268435456 | bytes 2621440 | tf_op jit(solution)/shard_map/tnb,tnc->nbc/dot_general | solution.py:23
  10.6 1.9 %fusion.3.left_ref = f32[8,128,128]{2,1,0:T(8,128)} fusion(bf16[1024,1024]{1,0:T(8,128)(2,1)S(1)} %copy-done.5), kind=kOutput, calls=%fused_computation.3 | convolution fusion | flops 268435456 | bytes 2621440 | tf_op jit(solution)/shard_map/tnb,tnc->nbc/dot_general | solution.py:23
  12.5 2.2 %fold.1 = f32[16,72,128]{2,1,0:T(8,128)} custom-call(f32[8,128,128]{2,1,0:T(8,128)} %fusion.3.left_ref, f32[8,128,128]{2,1,0:T(8,128)} %fusion.right_ref), custom_call_target="tpu_custom_call" | custom-call | tf_op jit(solution)/shard_map/fold/pallas_call | solution.py:48
  14.8 7.6 %all-to-all-start = ((f32[16,72,128]{2,1,0:T(8,128)}), f32[16,72,128]{2,1,0:T(8,128)S(1)}, u32[]{:S(2)}, u32[]{:S(2)}) async-start(f32[16,72,128]{2,1,0:T(8,128)} %fold.1), calls=%async_computation | async-start | bytes 1179648 | tf_op jit(solution)/shard_map/all_to_all | solution.py:225
  22.4 4.4 %collective-permute-start = (f32[16,256]{1,0:T(8,128)S(1)}, f32[16,256]{1,0:T(8,128)S(1)}, u32[]{:S(2)}, u32[]{:S(2)}) collective-permute-start(f32[16,256]{1,0:T(8,128)S(1)} %multiply_subtract_fusion), channel_id=1, source_target_pairs={{0,3},{1,2},{2,1},{3,0},{4,7},{5,6},{6,5},{7,4},{8,11},{9,10},{10,... | collective-permute-start | bytes 49160 | tf_op jit(solution)/shard_map/ppermute | solution.py:196
  26.8 0.4 collective-permute-start.2
  27.2 1.5 %constant_dynamic-slice_fusion.block_ref = f32[1,128,128]{2,1,0:T(8,128)} fusion(f32[16,128,128]{2,1,0:T(8,128)} %param.10, s32[]{:T(128)S(6)} %select_n.82), kind=kLoop, calls=%fused_computation.23 | loop fusion | bytes 131076 | tf_op jit(solution)/shard_map/dynamic_slice | solution.py:236
  28.7 1.5 %fold_one.1 = f32[72,128]{1,0:T(8,128)} custom-call(f32[1,128,128]{2,1,0:T(8,128)} %constant_dynamic-slice_fusion.block_ref), custom_call_target="tpu_custom_call" | custom-call | tf_op jit(solution)/shard_map/fold_one/pallas_call | solution.py:66
  30.2 0.4 collective-permute-done.1
  30.6 0.6 pad_maximum_fusion
  31.3 2.1 %all-to-all-done = f32[16,72,128]{2,1,0:T(8,128)S(1)} async-done(((f32[16,72,128]{2,1,0:T(8,128)}), f32[16,72,128]{2,1,0:T(8,128)S(1)}, u32[]{:S(2)}, u32[]{:S(2)}) %all-to-all-start) | async-done | bytes 589856 | tf_op jit(solution)/shard_map/all_to_all | solution.py:225
  33.4 4.6 %all-to-all-start.1 = ((f32[16,64,256]{2,1,0:T(8,128)}), f32[16,64,256]{2,1,0:T(8,128)S(1)}, u32[]{:S(2)}, u32[]{:S(2)}) async-start(f32[16,64,256]{2,1,0:T(8,128)} %bitcast.20), calls=%async_computation.1 | async-start | bytes 2097152 | tf_op jit(solution)/shard_map/all_to_all | solution.py:240
  38.0 0.0 all-gather.2.cloned.1.call-start
  38.0 2.7 %collective-permute-start.3 = (f32[72,128]{1,0:T(8,128)S(1)}, f32[72,128]{1,0:T(8,128)S(1)}, u32[]{:S(2)}, u32[]{:S(2)}) collective-permute-start(f32[72,128]{1,0:T(8,128)S(1)} %reduce_sum.28), channel_id=1, source_target_pairs={{0,4},{4,0},{8,12},{12,8},{1,5},{5,1},{9,13},{13,9},{2,6},{6,2},{1... | collective-permute-start | bytes 110600 | tf_op jit(solution)/shard_map/ppermute | solution.py:196
  40.8 0.9 collective-permute-done.3
  41.6 0.1 collective-permute-start.4
  41.8 2.9 %collective-permute-start.5 = (f32[72,128]{1,0:T(8,128)S(1)}, f32[72,128]{1,0:T(8,128)S(1)}, u32[]{:S(2)}, u32[]{:S(2)}) collective-permute-start(f32[72,128]{1,0:T(8,128)S(1)} %add.57), channel_id=1, source_target_pairs={{0,2},{1,3},{2,0},{3,1},{4,6},{5,7},{6,4},{7,5},{8,10},{9,11},{10,... | collective-permute-start | bytes 110600 | tf_op jit(solution)/shard_map/ppermute | solution.py:196
  44.7 0.5 collective-permute-start.6
  45.2 1.1 collective-permute-done.5
  46.4 3.3 %collective-permute-done.6 = f32[72,128]{1,0:T(8,128)S(1)} collective-permute-done((f32[72,128]{1,0:T(8,128)S(1)}, f32[72,128]{1,0:T(8,128)S(1)}, u32[]{:S(2)}, u32[]{:S(2)}) %collective-permute-start.6) | collective-permute-done | bytes 36896 | tf_op jit(solution)/shard_map/ppermute | solution.py:196
  49.6 4.3 %collective-permute-start.7 = (f32[72,128]{1,0:T(8,128)S(1)}, f32[72,128]{1,0:T(8,128)S(1)}, u32[]{:S(2)}, u32[]{:S(2)}) collective-permute-start(f32[72,128]{1,0:T(8,128)S(1)} %add_add_fusion.1), channel_id=1, source_target_pairs={{0,8},{4,12},{8,0},{12,4},{1,9},{5,13},{9,1},{13,5},{2,10},{6,14},... | collective-permute-start | bytes 110600 | tf_op jit(solution)/shard_map/ppermute | solution.py:196
  53.9 2.6 %collective-permute-done.7 = f32[72,128]{1,0:T(8,128)S(1)} collective-permute-done((f32[72,128]{1,0:T(8,128)S(1)}, f32[72,128]{1,0:T(8,128)S(1)}, u32[]{:S(2)}, u32[]{:S(2)}) %collective-permute-start.7) | collective-permute-done | bytes 36896 | tf_op jit(solution)/shard_map/ppermute | solution.py:196
  56.6 0.9 broadcast_in_dim.14
  57.4 6.7 %all-to-all-start.2 = ((f32[16,72,128]{2,1,0:T(8,128)}), f32[16,72,128]{2,1,0:T(8,128)}, u32[]{:S(2)}, u32[]{:S(2)}) async-start(f32[16,72,128]{2,1,0:T(8,128)} %broadcast_in_dim.14), calls=%async_computation.2 | async-start | bytes 1179648 | tf_op jit(solution)/shard_map/all_to_all | solution.py:205
  64.1 0.1 reduce_sum.29
  64.2 0.8 collective-permute-start.10
  65.0 2.8 %collective-permute-start.9 = (f32[64,256]{1,0:T(8,128)S(1)}, f32[64,256]{1,0:T(8,128)S(1)}, u32[]{:S(2)}, u32[]{:S(2)}) collective-permute-start(f32[64,256]{1,0:T(8,128)S(1)} %reduce_sum.29), channel_id=1, source_target_pairs={{0,2},{1,3},{2,0},{3,1},{4,6},{5,7},{6,4},{7,5},{8,10},{9,11},{10,... | collective-permute-start | bytes 196616 | tf_op jit(solution)/shard_map/ppermute | solution.py:196
  67.8 1.6 %collective-permute-done.10 = f32[64,256]{1,0:T(8,128)S(1)} collective-permute-done((f32[64,256]{1,0:T(8,128)S(1)}, f32[64,256]{1,0:T(8,128)S(1)}, u32[]{:S(2)}, u32[]{:S(2)}) %collective-permute-start.10) | collective-permute-done | bytes 65568 | tf_op jit(solution)/shard_map/ppermute | solution.py:196
  69.4 1.9 %collective-permute-done.9 = f32[64,256]{1,0:T(8,128)S(1)} collective-permute-done((f32[64,256]{1,0:T(8,128)S(1)}, f32[64,256]{1,0:T(8,128)S(1)}, u32[]{:S(2)}, u32[]{:S(2)}) %collective-permute-start.9) | collective-permute-done | bytes 65568 | tf_op jit(solution)/shard_map/ppermute | solution.py:196
  71.3 2.2 %all-to-all-done.2.folded_ref = f32[16,72,128]{2,1,0:T(8,128)} async-done(((f32[16,72,128]{2,1,0:T(8,128)}), f32[16,72,128]{2,1,0:T(8,128)}, u32[]{:S(2)}, u32[]{:S(2)}) %all-to-all-start.2) | async-done | bytes 589856 | tf_op jit(solution)/shard_map/all_to_all | solution.py:205
  73.5 1.1 broadcast_in_dim.15
  74.6 4.8 %all-to-all-start.3 = ((f32[16,64,256]{2,1,0:T(8,128)}), f32[16,64,256]{2,1,0:T(8,128)S(1)}, u32[]{:S(2)}, u32[]{:S(2)}) async-start(f32[16,64,256]{2,1,0:T(8,128)} %broadcast_in_dim.15), calls=%async_computation.3 | async-start | bytes 2097152 | tf_op jit(solution)/shard_map/all_to_all | solution.py:205
  79.4 0.2 convert_reduce_fusion
  79.6 0.2 fusion.7
  79.7 0.7 pad_add_fusion.place_ref
  80.4 7.3 %inverse.1 = (f32[10,128,128]{2,1,0:T(8,128)}, f32[2,128,128]{2,1,0:T(8,128)}) custom-call(s32[3]{0:T(128)} %pad_add_fusion.place_ref, f32[16,72,128]{2,1,0:T(8,128)} %all-to-all-done.2.folded_ref), custom_call_target="tpu_custom_call" | custom-call | tf_op jit(solution)/shard_map/inverse/pallas_call | solution.py:128
  87.7 3.6 %all-to-all-done.3 = f32[16,64,256]{2,1,0:T(8,128)S(1)} async-done(((f32[16,64,256]{2,1,0:T(8,128)}), f32[16,64,256]{2,1,0:T(8,128)S(1)}, u32[]{:S(2)}, u32[]{:S(2)}) %all-to-all-start.3) | async-done | bytes 1048608 | tf_op jit(solution)/shard_map/all_to_all | solution.py:205
  91.2 1.0 copy-done.1
  92.2 4.6 %precondition.1 = (f32[1024,256]{1,0:T(8,128)}, f32[1,128]{1,0:T(1,128)}) custom-call(f32[10,128,128]{2,1,0:T(8,128)} %get-tuple-element.28.inverse_ref, f32[1024,256]{1,0:T(8,128)} %bitcast.19), custom_call_target="tpu_custom_call" | custom-call | tf_op jit(solution)/shard_map/precondition/pallas_call | solution.py:159
  96.7 5.4 %all-gather.2.cloned.1.call-done.base_ref = f32[1024,256]{1,0:T(8,128)} async-done(((f32[64,256]{1,0:T(8,128)}), f32[1024,256]{1,0:T(8,128)}) %all-gather.2.cloned.1.call-update) | async-done | bytes 1048592 | tf_op jit(solution)/shard_map/all_gather | solution.py:237
  102.1 2.4 %collective-permute-start.11 = (f32[1,128]{1,0:T(1,128)}, f32[1,128]{1,0:T(1,128)S(1)}, u32[]{:S(2)}, u32[]{:S(2)}) collective-permute-start(f32[1,128]{1,0:T(1,128)} %get-tuple-element.31), channel_id=1, source_target_pairs={{0,4},{4,0},{8,12},{12,8},{1,5},{5,1},{9,13},{13,9},{2,6},{6,2},{1... | collective-permute-start | bytes 1544 | tf_op jit(solution)/shard_map/ppermute | solution.py:196
  104.5 1.0 collective-permute-done.11
  105.5 0.7 add.66
  106.1 4.4 %collective-permute-start.12 = (f32[1,128]{1,0:T(1,128)S(1)}, f32[1,128]{1,0:T(1,128)S(1)}, u32[]{:S(2)}, u32[]{:S(2)}) collective-permute-start(f32[1,128]{1,0:T(1,128)S(1)} %add.66), channel_id=1, source_target_pairs={{0,8},{4,12},{8,0},{12,4},{1,9},{5,13},{9,1},{13,5},{2,10},{6,14},... | collective-permute-start | bytes 1544 | tf_op jit(solution)/shard_map/ppermute | solution.py:196
  110.6 1.9 %collective-permute-done.12 = f32[1,128]{1,0:T(1,128)S(1)} collective-permute-done((f32[1,128]{1,0:T(1,128)S(1)}, f32[1,128]{1,0:T(1,128)S(1)}, u32[]{:S(2)}, u32[]{:S(2)}) %collective-permute-start.12) | collective-permute-done | bytes 544 | tf_op jit(solution)/shard_map/ppermute | solution.py:196
  112.4 0.6 add.67.align_ref
  113.0 2.8 %finish.1 = (f32[1024,256]{1,0:T(8,128)}, f32[16,256]{1,0:T(8,128)}) custom-call(s32[1]{0:T(128)} %bitcast.row_ref, f32[1,128]{1,0:T(1,128)} %add.67.align_ref, f32[16,256]{1,0:T(8,128)} %momentum_ref.1, f32[1024,256]{1,0:T(8,128)} %get-tuple-element.32.precond_ref, f32[1024,256]{1,0:T(8,128)} %all-gather.2.cloned.1.call-done.base_ref), custom_call_target="tpu_custom_call" | custom-call | tf_op jit(solution)/shard_map/finish/pallas_call | solution.py:178
  (29 shorter events, 0.2 us)
Async XLA Ops:
  7.2 1.6 %copy-start = (bf16[1024,1024]{1,0:T(8,128)(2,1)S(1)}, bf16[1024,1024]{1,0:T(8,128)(2,1)}, u32[]{:S(2)}) copy-start(bf16[1024,1024]{1,0:T(8,128)(2,1)} %param.8) | copy-start | bytes 6291460
  7.2 3.4 %copy-start.5 = (bf16[1024,1024]{1,0:T(8,128)(2,1)S(1)}, bf16[1024,1024]{1,0:T(8,128)(2,1)}, u32[]{:S(2)}) copy-start(bf16[1024,1024]{1,0:T(8,128)(2,1)} %param.7) | copy-start | bytes 6291460
  12.5 9.8 %copy-start.3 = (f32[16,256]{1,0:T(8,128)S(1)}, f32[16,256]{1,0:T(8,128)}, u32[]{:S(2)}) copy-start(f32[16,256]{1,0:T(8,128)} %momentum_ref.1) | copy-start | bytes 49156
  12.5 9.8 %copy-start.4 = (f32[16,256]{1,0:T(8,128)S(1)}, f32[16,256]{1,0:T(8,128)}, u32[]{:S(2)}) copy-start(f32[16,256]{1,0:T(8,128)} %param.12) | copy-start | bytes 49156
  14.8 18.6 %all-to-all-start = ((f32[16,72,128]{2,1,0:T(8,128)}), f32[16,72,128]{2,1,0:T(8,128)S(1)}, u32[]{:S(2)}, u32[]{:S(2)}) async-start(f32[16,72,128]{2,1,0:T(8,128)} %fold.1), calls=%async_computation | async-start | bytes 1179648 | tf_op jit(solution)/shard_map/all_to_all | solution.py:225
  22.4 7.8 %collective-permute-start = (f32[16,256]{1,0:T(8,128)S(1)}, f32[16,256]{1,0:T(8,128)S(1)}, u32[]{:S(2)}, u32[]{:S(2)}) collective-permute-start(f32[16,256]{1,0:T(8,128)S(1)} %multiply_subtract_fusion), channel_id=1, source_target_pairs={{0,3},{1,2},{2,1},{3,0},{4,7},{5,6},{6,5},{7,4},{8,11},{9,10},{10,... | collective-permute-start | bytes 49160 | tf_op jit(solution)/shard_map/ppermute | solution.py:196
  26.8 3.8 %collective-permute-start.1 = (f32[16,256]{1,0:T(8,128)S(1)}, f32[16,256]{1,0:T(8,128)S(1)}, u32[]{:S(2)}, u32[]{:S(2)}) collective-permute-start(f32[16,256]{1,0:T(8,128)S(1)} %multiply_subtract_fusion), channel_id=1, source_target_pairs={{0,2},{1,3},{2,0},{3,1},{4,6},{5,7},{6,4},{7,5},{8,10},{9,11},{10,... | collective-permute-start | bytes 49160 | tf_op jit(solution)/shard_map/ppermute | solution.py:196
  26.8 3.8 %collective-permute-start.2 = (f32[16,256]{1,0:T(8,128)S(1)}, f32[16,256]{1,0:T(8,128)S(1)}, u32[]{:S(2)}, u32[]{:S(2)}) collective-permute-start(f32[16,256]{1,0:T(8,128)S(1)} %multiply_subtract_fusion), channel_id=1, source_target_pairs={{0,1},{1,0},{2,3},{3,2},{4,5},{5,4},{6,7},{7,6},{8,9},{9,8},{10,11... | collective-permute-start | bytes 49160 | tf_op jit(solution)/shard_map/ppermute | solution.py:196
  30.2 26.3 %copy-start.2 = (f32[72,128]{1,0:T(8,128)S(1)}, f32[72,128]{1,0:T(8,128)}, u32[]{:S(2)}) copy-start(f32[72,128]{1,0:T(8,128)} %fold_one.1) | copy-start | bytes 110596
  33.4 23.1 %all-to-all-start.1 = ((f32[16,64,256]{2,1,0:T(8,128)}), f32[16,64,256]{2,1,0:T(8,128)S(1)}, u32[]{:S(2)}, u32[]{:S(2)}) async-start(f32[16,64,256]{2,1,0:T(8,128)} %bitcast.20), calls=%async_computation.1 | async-start | bytes 2097152 | tf_op jit(solution)/shard_map/all_to_all | solution.py:240
  38.0 64.1 %all-gather.2.cloned.1.call-start = ((), (), s32[]{:S(2)}) async-start(), calls=%async_computation.4 | async-start | bytes 1114112 | tf_op jit(solution)/shard_map/all_gather | solution.py:237
  38.0 3.6 %collective-permute-start.3 = (f32[72,128]{1,0:T(8,128)S(1)}, f32[72,128]{1,0:T(8,128)S(1)}, u32[]{:S(2)}, u32[]{:S(2)}) collective-permute-start(f32[72,128]{1,0:T(8,128)S(1)} %reduce_sum.28), channel_id=1, source_target_pairs={{0,4},{4,0},{8,12},{12,8},{1,5},{5,1},{9,13},{13,9},{2,6},{6,2},{1... | collective-permute-start | bytes 110600 | tf_op jit(solution)/shard_map/ppermute | solution.py:196
  41.6 3.6 %collective-permute-start.4 = (f32[72,128]{1,0:T(8,128)S(1)}, f32[72,128]{1,0:T(8,128)S(1)}, u32[]{:S(2)}, u32[]{:S(2)}) collective-permute-start(f32[72,128]{1,0:T(8,128)S(1)} %add.57), channel_id=1, source_target_pairs={{0,1},{1,0},{2,3},{3,2},{4,5},{5,4},{6,7},{7,6},{8,9},{9,8},{10,11... | collective-permute-start | bytes 110600 | tf_op jit(solution)/shard_map/ppermute | solution.py:196
  41.8 4.6 %collective-permute-start.5 = (f32[72,128]{1,0:T(8,128)S(1)}, f32[72,128]{1,0:T(8,128)S(1)}, u32[]{:S(2)}, u32[]{:S(2)}) collective-permute-start(f32[72,128]{1,0:T(8,128)S(1)} %add.57), channel_id=1, source_target_pairs={{0,2},{1,3},{2,0},{3,1},{4,6},{5,7},{6,4},{7,5},{8,10},{9,11},{10,... | collective-permute-start | bytes 110600 | tf_op jit(solution)/shard_map/ppermute | solution.py:196
  44.7 4.9 %collective-permute-start.6 = (f32[72,128]{1,0:T(8,128)S(1)}, f32[72,128]{1,0:T(8,128)S(1)}, u32[]{:S(2)}, u32[]{:S(2)}) collective-permute-start(f32[72,128]{1,0:T(8,128)S(1)} %add.57), channel_id=1, source_target_pairs={{0,3},{1,2},{2,1},{3,0},{4,7},{5,6},{6,5},{7,4},{8,11},{9,10},{10,... | collective-permute-start | bytes 110600 | tf_op jit(solution)/shard_map/ppermute | solution.py:196
  49.6 6.9 %collective-permute-start.7 = (f32[72,128]{1,0:T(8,128)S(1)}, f32[72,128]{1,0:T(8,128)S(1)}, u32[]{:S(2)}, u32[]{:S(2)}) collective-permute-start(f32[72,128]{1,0:T(8,128)S(1)} %add_add_fusion.1), channel_id=1, source_target_pairs={{0,8},{4,12},{8,0},{12,4},{1,9},{5,13},{9,1},{13,5},{2,10},{6,14},... | collective-permute-start | bytes 110600 | tf_op jit(solution)/shard_map/ppermute | solution.py:196
  57.4 16.1 %all-to-all-start.2 = ((f32[16,72,128]{2,1,0:T(8,128)}), f32[16,72,128]{2,1,0:T(8,128)}, u32[]{:S(2)}, u32[]{:S(2)}) async-start(f32[16,72,128]{2,1,0:T(8,128)} %broadcast_in_dim.14), calls=%async_computation.2 | async-start | bytes 1179648 | tf_op jit(solution)/shard_map/all_to_all | solution.py:205
  64.1 15.2 %copy-start.6 = (s32[16]{0:T(128)S(1)}, s32[16]{0:T(128)}, u32[]{:S(2)}) copy-start(s32[16]{0:T(128)} %param.11) | copy-start | bytes 196
  64.2 5.2 %collective-permute-start.10 = (f32[64,256]{1,0:T(8,128)S(1)}, f32[64,256]{1,0:T(8,128)S(1)}, u32[]{:S(2)}, u32[]{:S(2)}) collective-permute-start(f32[64,256]{1,0:T(8,128)S(1)} %reduce_sum.29), channel_id=1, source_target_pairs={{0,3},{1,2},{2,1},{3,0},{4,7},{5,6},{6,5},{7,4},{8,11},{9,10},{10,... | collective-permute-start | bytes 196616 | tf_op jit(solution)/shard_map/ppermute | solution.py:196
  65.0 4.4 %collective-permute-start.8 = (f32[64,256]{1,0:T(8,128)S(1)}, f32[64,256]{1,0:T(8,128)S(1)}, u32[]{:S(2)}, u32[]{:S(2)}) collective-permute-start(f32[64,256]{1,0:T(8,128)S(1)} %reduce_sum.29), channel_id=1, source_target_pairs={{0,1},{1,0},{2,3},{3,2},{4,5},{5,4},{6,7},{7,6},{8,9},{9,8},{10,11... | collective-permute-start | bytes 196616 | tf_op jit(solution)/shard_map/ppermute | solution.py:196
  65.0 6.3 %collective-permute-start.9 = (f32[64,256]{1,0:T(8,128)S(1)}, f32[64,256]{1,0:T(8,128)S(1)}, u32[]{:S(2)}, u32[]{:S(2)}) collective-permute-start(f32[64,256]{1,0:T(8,128)S(1)} %reduce_sum.29), channel_id=1, source_target_pairs={{0,2},{1,3},{2,0},{3,1},{4,6},{5,7},{6,4},{7,5},{8,10},{9,11},{10,... | collective-permute-start | bytes 196616 | tf_op jit(solution)/shard_map/ppermute | solution.py:196
  74.6 16.6 %all-to-all-start.3 = ((f32[16,64,256]{2,1,0:T(8,128)}), f32[16,64,256]{2,1,0:T(8,128)S(1)}, u32[]{:S(2)}, u32[]{:S(2)}) async-start(f32[16,64,256]{2,1,0:T(8,128)} %broadcast_in_dim.15), calls=%async_computation.3 | async-start | bytes 2097152 | tf_op jit(solution)/shard_map/all_to_all | solution.py:205
  91.2 1.0 copy-start.1
  102.1 3.4 %collective-permute-start.11 = (f32[1,128]{1,0:T(1,128)}, f32[1,128]{1,0:T(1,128)S(1)}, u32[]{:S(2)}, u32[]{:S(2)}) collective-permute-start(f32[1,128]{1,0:T(1,128)} %get-tuple-element.31), channel_id=1, source_target_pairs={{0,4},{4,0},{8,12},{12,8},{1,5},{5,1},{9,13},{13,9},{2,6},{6,2},{1... | collective-permute-start | bytes 1544 | tf_op jit(solution)/shard_map/ppermute | solution.py:196
  106.1 6.3 %collective-permute-start.12 = (f32[1,128]{1,0:T(1,128)S(1)}, f32[1,128]{1,0:T(1,128)S(1)}, u32[]{:S(2)}, u32[]{:S(2)}) collective-permute-start(f32[1,128]{1,0:T(1,128)S(1)} %add.66), channel_id=1, source_target_pairs={{0,8},{4,12},{8,0},{12,4},{1,9},{5,13},{9,1},{13,5},{2,10},{6,14},... | collective-permute-start | bytes 1544 | tf_op jit(solution)/shard_map/ppermute | solution.py:196
Sparse Core Ops, SparseCore 0:
  45.3 56.7 all-gather.1

commit v10 on v9

--- a/solution.py
+++ b/solution.py
@@ -234,7 +234,6 @@
         base_rows.append(rows)
     base_rows = jnp.concatenate(base_rows, axis=0)
     old_block = fold_one(lax.dynamic_slice_in_dim(old_then, shard, 1, 0))
-    base = lax.all_gather(base_rows, "shards", axis=0, tiled=True)
 
     own_stats = after(jnp.sum(stats_in, axis=0), (base_rows, old_block))
     grad_in = lax.all_to_all(
@@ -260,8 +259,14 @@
     right_first = left_count + lax.axis_index("tensor") * right_count
     places = jnp.concatenate([right_first.reshape(1).astype(jnp.int32), holds])
     inverses, owned_blocks = invert_needed(places, folded, left_count + right_count, capacity)
+    base_copies = jnp.broadcast_to(
+        after(base_rows, inverses)[None], (shard_count,) + base_rows.shape
+    )
+    inverses, gradient = lax.optimization_barrier((inverses, gradient))
+    base = lax.all_to_all(after(base_copies, gradient), "shards", 0, 0).reshape(
+        row_count, col_count
+    )
     precond, align = precondition(inverses, gradient)
-    align, base = lax.optimization_barrier((align, base))
     align = align + swap(align, "tensor", 1)
     align = align + swap(align, "tensor", 2)
     first_row = (shard * replica_count + replica) * own_rows

time: 123 us -> 113 us (0.919); the launches traced: 123 us -> 111 us
  between operations: 14.2 us -> 0.82 us
  starting transfers between devices: 49.5 us -> 57.6 us
  waiting for transfers between devices: 27.8 us -> 21.8 us
    all_gather x1 -> x0, waiting for transfers between devices: 5.38 us -> none  [body(): base = lax.all_gather(base_rows, 'shards', axis=0, tiled=True)]
    ppermute x13, starting transfers between devices: 25.9 us -> 30.7 us  [swap(): return lax.ppermute(value, axis, [(i, i ^ flip) for i in range(size)])]
    all_to_all x0 -> x1, starting transfers between devices: none -> 4.34 us  [body(): lax.all_to_all(after(base_copies, gradient), 'shards', 0, 0)]
    ppermute x13, waiting for transfers between devices: 14.5 us -> 12.8 us  [swap(): return lax.ppermute(value, axis, [(i, i ^ flip) for i in range(size)])]
    broadcast_in_dim x0 -> x1, local copies, waits for them, and re-layouts: none -> 1.24 us  [body(): jnp.broadcast_to(after(base_rows, inverses)[None], (shard_count,) + base_...]
  transfers between devices with their start and end apart: 18 -> 18, of which waited for: 13 -> 12; matrix products, arithmetic and copies ran while one was open for 4% -> 3% of each run, Pallas kernels for 11% -> 12%
where the time goes in v10:
time: 113 us; the launch traced here: 111 us
  starting transfers between devices  57.6 us (51%)
  waiting for transfers between devices  21.8 us (19%)
  Pallas kernels  18.3 us (16%)
  local copies, waits for them, and re-layouts  6.25 us (6%)
  matrix products  3.79 us (3%)
  other arithmetic  2.33 us (2%)
    ppermute x13, starting transfers between devices, swap(): return lax.ppermute(value, axis, [(i, i ^ flip) for i in range(size)])  30.7 us
    ppermute x13, waiting for transfers between devices, swap(): return lax.ppermute(value, axis, [(i, i ^ flip) for i in range(size)])  12.8 us
    all_to_all x2, starting transfers between devices, spread(): return lax.all_to_all(copies, axis, 0, 0)  11 us
    all_to_all x1, starting transfers between devices, body(): stats_in = lax.all_to_all(folded, 'shards', 0, 0)  7.58 us
    pallas_call x1, Pallas kernels, invert_needed(): pl.pallas_call(inverse_kernel, in_specs=[pl.BlockSpec(memory_space=pltpu....  7.25 us
    all_to_all x2, waiting for transfers between devices, spread(): return lax.all_to_all(copies, axis, 0, 0)  6.27 us
    pallas_call x1, Pallas kernels, precondition(): pl.pallas_call(precondition_kernel, out_shape=(jax.ShapeDtypeStruct(gradi...  4.54 us
    all_to_all x1, starting transfers between devices, body(): lax.all_to_all(after(base_copies, gradient), 'shards', 0, 0)  4.34 us
  transfers between devices with their start and end apart: 18, of which 12 were waited for; matrix products, arithmetic and copies ran while one was open for 3% of the time, Pallas kernels for 12%

profile of v10, /device:TPU:1, one launch (start us, length us, event | category | flops | bytes accessed | tf_op | source)
XLA Modules:
  0.0 110.9 jit_solution(12998371435986982180)
XLA Ops:
  0.6 0.0 copy-start
  0.7 1.6 %copy-done = bf16[1024,1024]{1,0:T(8,128)(2,1)S(1)} copy-done((bf16[1024,1024]{1,0:T(8,128)(2,1)S(1)}, bf16[1024,1024]{1,0:T(8,128)(2,1)}, u32[]{:S(2)}) %copy-start) | copy-done | bytes 2097176
  2.2 1.9 %fusion.3.left_ref = f32[8,128,128]{2,1,0:T(8,128)} fusion(bf16[1024,1024]{1,0:T(8,128)(2,1)S(1)} %copy-done), kind=kOutput, calls=%fused_computation.3 | convolution fusion | flops 268435456 | bytes 2621440 | tf_op jit(solution)/shard_map/tnb,tnc->nbc/dot_general | solution.py:23
  4.1 1.9 %fusion.right_ref = f32[8,128,128]{2,1,0:T(8,128)} fusion(bf16[1024,1024]{1,0:T(8,128)(2,1)S(1)} %copy-done.5), kind=kOutput, calls=%fused_computation | convolution fusion | flops 268435456 | bytes 2621440 | tf_op jit(solution)/shard_map/tnb,tnc->nbc/dot_general | solution.py:23
  6.0 2.2 %fold.1 = f32[16,72,128]{2,1,0:T(8,128)} custom-call(f32[8,128,128]{2,1,0:T(8,128)} %fusion.3.left_ref, f32[8,128,128]{2,1,0:T(8,128)} %fusion.right_ref), custom_call_target="tpu_custom_call" | custom-call | tf_op jit(solution)/shard_map/fold/pallas_call | solution.py:48
  8.3 7.6 %all-to-all-start = ((f32[16,72,128]{2,1,0:T(8,128)}), f32[16,72,128]{2,1,0:T(8,128)S(1)}, u32[]{:S(2)}, u32[]{:S(2)}) async-start(f32[16,72,128]{2,1,0:T(8,128)} %fold.1), calls=%async_computation | async-start | bytes 1179648 | tf_op jit(solution)/shard_map/all_to_all | solution.py:225
  15.9 4.4 %collective-permute-start = (f32[16,256]{1,0:T(8,128)S(1)}, f32[16,256]{1,0:T(8,128)S(1)}, u32[]{:S(2)}, u32[]{:S(2)}) collective-permute-start(f32[16,256]{1,0:T(8,128)S(1)} %multiply_subtract_fusion), channel_id=1, source_target_pairs={{0,3},{1,2},{2,1},{3,0},{4,7},{5,6},{6,5},{7,4},{8,11},{9,10},{10,... | collective-permute-start | bytes 49160 | tf_op jit(solution)/shard_map/ppermute | solution.py:196
  20.3 0.4 collective-permute-start.2
  20.7 1.5 %constant_dynamic-slice_fusion.block_ref = f32[1,128,128]{2,1,0:T(8,128)} fusion(f32[16,128,128]{2,1,0:T(8,128)} %param.10, s32[]{:T(128)S(6)} %select_n.82), kind=kLoop, calls=%fused_computation.23 | loop fusion | bytes 131076 | tf_op jit(solution)/shard_map/dynamic_slice | solution.py:236
  22.2 1.5 %fold_one.1 = f32[72,128]{1,0:T(8,128)} custom-call(f32[1,128,128]{2,1,0:T(8,128)} %constant_dynamic-slice_fusion.block_ref), custom_call_target="tpu_custom_call" | custom-call | tf_op jit(solution)/shard_map/fold_one/pallas_call | solution.py:66
  23.7 0.4 collective-permute-done.1
  24.1 2.7 %all-to-all-done = f32[16,72,128]{2,1,0:T(8,128)S(1)} async-done(((f32[16,72,128]{2,1,0:T(8,128)}), f32[16,72,128]{2,1,0:T(8,128)S(1)}, u32[]{:S(2)}, u32[]{:S(2)}) %all-to-all-start) | async-done | bytes 589856 | tf_op jit(solution)/shard_map/all_to_all | solution.py:225
  26.9 4.0 %all-to-all-start.1 = ((f32[16,64,256]{2,1,0:T(8,128)}), f32[16,64,256]{2,1,0:T(8,128)S(1)}, u32[]{:S(2)}, u32[]{:S(2)}) async-start(f32[16,64,256]{2,1,0:T(8,128)} %bitcast.21), calls=%async_computation.1 | async-start | bytes 2097152 | tf_op jit(solution)/shard_map/all_to_all | solution.py:239
  30.9 2.7 %collective-permute-start.3 = (f32[72,128]{1,0:T(8,128)S(1)}, f32[72,128]{1,0:T(8,128)S(1)}, u32[]{:S(2)}, u32[]{:S(2)}) collective-permute-start(f32[72,128]{1,0:T(8,128)S(1)} %reduce_sum.28), channel_id=1, source_target_pairs={{0,4},{4,0},{8,12},{12,8},{1,5},{5,1},{9,13},{13,9},{2,6},{6,2},{1... | collective-permute-start | bytes 110600 | tf_op jit(solution)/shard_map/ppermute | solution.py:196
  33.6 0.9 collective-permute-done.3
  34.5 3.4 %collective-permute-start.6 = (f32[72,128]{1,0:T(8,128)S(1)}, f32[72,128]{1,0:T(8,128)S(1)}, u32[]{:S(2)}, u32[]{:S(2)}) collective-permute-start(f32[72,128]{1,0:T(8,128)S(1)} %add.57), channel_id=1, source_target_pairs={{0,3},{1,2},{2,1},{3,0},{4,7},{5,6},{6,5},{7,4},{8,11},{9,10},{10,... | collective-permute-start | bytes 110600 | tf_op jit(solution)/shard_map/ppermute | solution.py:196
  37.9 0.4 collective-permute-start.4
  38.2 1.3 %collective-permute-done.6 = f32[72,128]{1,0:T(8,128)S(1)} collective-permute-done((f32[72,128]{1,0:T(8,128)S(1)}, f32[72,128]{1,0:T(8,128)S(1)}, u32[]{:S(2)}, u32[]{:S(2)}) %collective-permute-start.6) | collective-permute-done | bytes 36896 | tf_op jit(solution)/shard_map/ppermute | solution.py:196
  39.5 2.5 %collective-permute-done.5 = f32[72,128]{1,0:T(8,128)S(1)} collective-permute-done((f32[72,128]{1,0:T(8,128)S(1)}, f32[72,128]{1,0:T(8,128)S(1)}, u32[]{:S(2)}, u32[]{:S(2)}) %collective-permute-start.5) | collective-permute-done | bytes 36896 | tf_op jit(solution)/shard_map/ppermute | solution.py:196
  42.0 5.1 %collective-permute-start.7 = (f32[72,128]{1,0:T(8,128)S(1)}, f32[72,128]{1,0:T(8,128)S(1)}, u32[]{:S(2)}, u32[]{:S(2)}) collective-permute-start(f32[72,128]{1,0:T(8,128)S(1)} %add_add_fusion.1), channel_id=1, source_target_pairs={{0,8},{4,12},{8,0},{12,4},{1,9},{5,13},{9,1},{13,5},{2,10},{6,14},... | collective-permute-start | bytes 110600 | tf_op jit(solution)/shard_map/ppermute | solution.py:196
  47.1 1.7 %collective-permute-done.7 = f32[72,128]{1,0:T(8,128)S(1)} collective-permute-done((f32[72,128]{1,0:T(8,128)S(1)}, f32[72,128]{1,0:T(8,128)S(1)}, u32[]{:S(2)}, u32[]{:S(2)}) %collective-permute-start.7) | collective-permute-done | bytes 36896 | tf_op jit(solution)/shard_map/ppermute | solution.py:196
  48.8 0.9 broadcast_in_dim.16
  49.7 6.9 %all-to-all-start.2 = ((f32[16,72,128]{2,1,0:T(8,128)}), f32[16,72,128]{2,1,0:T(8,128)}, u32[]{:S(2)}, u32[]{:S(2)}) async-start(f32[16,72,128]{2,1,0:T(8,128)} %broadcast_in_dim.16), calls=%async_computation.2 | async-start | bytes 1179648 | tf_op jit(solution)/shard_map/all_to_all | solution.py:205
  56.6 0.0 copy-start.6
  56.6 0.1 reduce_sum.29
  56.7 1.4 %collective-permute-start.10 = (f32[64,256]{1,0:T(8,128)S(1)}, f32[64,256]{1,0:T(8,128)S(1)}, u32[]{:S(2)}, u32[]{:S(2)}) collective-permute-start(f32[64,256]{1,0:T(8,128)S(1)} %reduce_sum.29), channel_id=1, source_target_pairs={{0,3},{1,2},{2,1},{3,0},{4,7},{5,6},{6,5},{7,4},{8,11},{9,10},{10,... | collective-permute-start | bytes 196616 | tf_op jit(solution)/shard_map/ppermute | solution.py:196
  58.1 0.1 collective-permute-start.9
  58.2 2.1 %collective-permute-start.8 = (f32[64,256]{1,0:T(8,128)S(1)}, f32[64,256]{1,0:T(8,128)S(1)}, u32[]{:S(2)}, u32[]{:S(2)}) collective-permute-start(f32[64,256]{1,0:T(8,128)S(1)} %reduce_sum.29), channel_id=1, source_target_pairs={{0,1},{1,0},{2,3},{3,2},{4,5},{5,4},{6,7},{7,6},{8,9},{9,8},{10,11... | collective-permute-start | bytes 196616 | tf_op jit(solution)/shard_map/ppermute | solution.py:196
  60.3 1.4 %collective-permute-done.10 = f32[64,256]{1,0:T(8,128)S(1)} collective-permute-done((f32[64,256]{1,0:T(8,128)S(1)}, f32[64,256]{1,0:T(8,128)S(1)}, u32[]{:S(2)}, u32[]{:S(2)}) %collective-permute-start.10) | collective-permute-done | bytes 65568 | tf_op jit(solution)/shard_map/ppermute | solution.py:196
  61.8 2.3 %collective-permute-done.9 = f32[64,256]{1,0:T(8,128)S(1)} collective-permute-done((f32[64,256]{1,0:T(8,128)S(1)}, f32[64,256]{1,0:T(8,128)S(1)}, u32[]{:S(2)}, u32[]{:S(2)}) %collective-permute-start.9) | collective-permute-done | bytes 65568 | tf_op jit(solution)/shard_map/ppermute | solution.py:196
  64.1 2.2 %all-to-all-done.2.folded_ref = f32[16,72,128]{2,1,0:T(8,128)} async-done(((f32[16,72,128]{2,1,0:T(8,128)}), f32[16,72,128]{2,1,0:T(8,128)}, u32[]{:S(2)}, u32[]{:S(2)}) %all-to-all-start.2) | async-done | bytes 589856 | tf_op jit(solution)/shard_map/all_to_all | solution.py:205
  66.3 1.1 broadcast_in_dim.17
  67.4 4.1 %all-to-all-start.3 = ((f32[16,64,256]{2,1,0:T(8,128)}), f32[16,64,256]{2,1,0:T(8,128)S(1)}, u32[]{:S(2)}, u32[]{:S(2)}) async-start(f32[16,64,256]{2,1,0:T(8,128)} %broadcast_in_dim.17), calls=%async_computation.3 | async-start | bytes 2097152 | tf_op jit(solution)/shard_map/all_to_all | solution.py:205
  71.5 0.2 convert_reduce_fusion
  71.7 0.2 fusion.7
  71.9 0.6 pad_add_fusion.place_ref
  72.5 7.2 %inverse.1 = (f32[10,128,128]{2,1,0:T(8,128)}, f32[2,128,128]{2,1,0:T(8,128)}) custom-call(s32[3]{0:T(128)} %pad_add_fusion.place_ref, f32[16,72,128]{2,1,0:T(8,128)} %all-to-all-done.2.folded_ref), custom_call_target="tpu_custom_call" | custom-call | tf_op jit(solution)/shard_map/inverse/pallas_call | solution.py:128
  79.7 4.0 %all-to-all-done.3 = f32[16,64,256]{2,1,0:T(8,128)S(1)} async-done(((f32[16,64,256]{2,1,0:T(8,128)}), f32[16,64,256]{2,1,0:T(8,128)S(1)}, u32[]{:S(2)}, u32[]{:S(2)}) %all-to-all-start.3) | async-done | bytes 1048608 | tf_op jit(solution)/shard_map/all_to_all | solution.py:205
  83.8 1.2 %broadcast_in_dim.18 = f32[16,64,256]{2,1,0:T(8,128)} broadcast(f32[64,256]{1,0:T(8,128)S(1)} %pad_maximum_fusion), dimensions={1,2} | broadcast | bytes 1114112 | tf_op jit(solution)/shard_map/broadcast_in_dim | solution.py:262
  85.0 4.3 %all-to-all-start.4 = ((f32[16,64,256]{2,1,0:T(8,128)}), f32[16,64,256]{2,1,0:T(8,128)}, u32[]{:S(2)}, u32[]{:S(2)}) async-start(f32[16,64,256]{2,1,0:T(8,128)} %broadcast_in_dim.18), calls=%async_computation.4 | async-start | bytes 2097152 | tf_op jit(solution)/shard_map/all_to_all | solution.py:266
  89.4 4.5 %precondition.1 = (f32[1024,256]{1,0:T(8,128)}, f32[1,128]{1,0:T(1,128)}) custom-call(f32[10,128,128]{2,1,0:T(8,128)} %get-tuple-element.32.inverse_ref, f32[1024,256]{1,0:T(8,128)} %bitcast.20), custom_call_target="tpu_custom_call" | custom-call | tf_op jit(solution)/shard_map/precondition/pallas_call | solution.py:159
  93.9 5.7 %collective-permute-start.11 = (f32[1,128]{1,0:T(1,128)}, f32[1,128]{1,0:T(1,128)S(1)}, u32[]{:S(2)}, u32[]{:S(2)}) collective-permute-start(f32[1,128]{1,0:T(1,128)} %get-tuple-element.34), channel_id=1, source_target_pairs={{0,4},{4,0},{8,12},{12,8},{1,5},{5,1},{9,13},{13,9},{2,6},{6,2},{1... | collective-permute-start | bytes 1544 | tf_op jit(solution)/shard_map/ppermute | solution.py:196
  99.7 1.0 collective-permute-done.11
  100.6 0.7 add.66
  101.3 4.9 %collective-permute-start.12 = (f32[1,128]{1,0:T(1,128)S(1)}, f32[1,128]{1,0:T(1,128)S(1)}, u32[]{:S(2)}, u32[]{:S(2)}) collective-permute-start(f32[1,128]{1,0:T(1,128)S(1)} %add.66), channel_id=1, source_target_pairs={{0,8},{4,12},{8,0},{12,4},{1,9},{5,13},{9,1},{13,5},{2,10},{6,14},... | collective-permute-start | bytes 1544 | tf_op jit(solution)/shard_map/ppermute | solution.py:196
  106.2 1.4 %collective-permute-done.12 = f32[1,128]{1,0:T(1,128)S(1)} collective-permute-done((f32[1,128]{1,0:T(1,128)S(1)}, f32[1,128]{1,0:T(1,128)S(1)}, u32[]{:S(2)}, u32[]{:S(2)}) %collective-permute-start.12) | collective-permute-done | bytes 544 | tf_op jit(solution)/shard_map/ppermute | solution.py:196
  107.6 0.5 add.67.align_ref
  108.1 2.8 %finish.1 = (f32[1024,256]{1,0:T(8,128)}, f32[16,256]{1,0:T(8,128)}) custom-call(s32[1]{0:T(128)} %bitcast.row_ref, f32[1,128]{1,0:T(1,128)} %add.67.align_ref, f32[16,256]{1,0:T(8,128)} %momentum_ref.1, f32[1024,256]{1,0:T(8,128)} %get-tuple-element.35.precond_ref, f32[1024,256]{1,0:T(8,128)} %bitcast.5.base_ref), custom_call_target="tpu_custom_call" | custom-call | tf_op jit(solution)/shard_map/finish/pallas_call | solution.py:178
  (29 shorter events, 0.2 us)
Async XLA Ops:
  0.6 1.6 %copy-start = (bf16[1024,1024]{1,0:T(8,128)(2,1)S(1)}, bf16[1024,1024]{1,0:T(8,128)(2,1)}, u32[]{:S(2)}) copy-start(bf16[1024,1024]{1,0:T(8,128)(2,1)} %param.7) | copy-start | bytes 6291460
  0.6 3.4 %copy-start.5 = (bf16[1024,1024]{1,0:T(8,128)(2,1)S(1)}, bf16[1024,1024]{1,0:T(8,128)(2,1)}, u32[]{:S(2)}) copy-start(bf16[1024,1024]{1,0:T(8,128)(2,1)} %param.8) | copy-start | bytes 6291460
  6.0 9.8 %copy-start.3 = (f32[16,256]{1,0:T(8,128)S(1)}, f32[16,256]{1,0:T(8,128)}, u32[]{:S(2)}) copy-start(f32[16,256]{1,0:T(8,128)} %momentum_ref.1) | copy-start | bytes 49156
  6.0 9.8 %copy-start.4 = (f32[16,256]{1,0:T(8,128)S(1)}, f32[16,256]{1,0:T(8,128)}, u32[]{:S(2)}) copy-start(f32[16,256]{1,0:T(8,128)} %param.12) | copy-start | bytes 49156
  8.3 18.6 %all-to-all-start = ((f32[16,72,128]{2,1,0:T(8,128)}), f32[16,72,128]{2,1,0:T(8,128)S(1)}, u32[]{:S(2)}, u32[]{:S(2)}) async-start(f32[16,72,128]{2,1,0:T(8,128)} %fold.1), calls=%async_computation | async-start | bytes 1179648 | tf_op jit(solution)/shard_map/all_to_all | solution.py:225
  15.9 7.8 %collective-permute-start = (f32[16,256]{1,0:T(8,128)S(1)}, f32[16,256]{1,0:T(8,128)S(1)}, u32[]{:S(2)}, u32[]{:S(2)}) collective-permute-start(f32[16,256]{1,0:T(8,128)S(1)} %multiply_subtract_fusion), channel_id=1, source_target_pairs={{0,3},{1,2},{2,1},{3,0},{4,7},{5,6},{6,5},{7,4},{8,11},{9,10},{10,... | collective-permute-start | bytes 49160 | tf_op jit(solution)/shard_map/ppermute | solution.py:196
  20.3 3.8 %collective-permute-start.1 = (f32[16,256]{1,0:T(8,128)S(1)}, f32[16,256]{1,0:T(8,128)S(1)}, u32[]{:S(2)}, u32[]{:S(2)}) collective-permute-start(f32[16,256]{1,0:T(8,128)S(1)} %multiply_subtract_fusion), channel_id=1, source_target_pairs={{0,2},{1,3},{2,0},{3,1},{4,6},{5,7},{6,4},{7,5},{8,10},{9,11},{10,... | collective-permute-start | bytes 49160 | tf_op jit(solution)/shard_map/ppermute | solution.py:196
  20.3 3.8 %collective-permute-start.2 = (f32[16,256]{1,0:T(8,128)S(1)}, f32[16,256]{1,0:T(8,128)S(1)}, u32[]{:S(2)}, u32[]{:S(2)}) collective-permute-start(f32[16,256]{1,0:T(8,128)S(1)} %multiply_subtract_fusion), channel_id=1, source_target_pairs={{0,1},{1,0},{2,3},{3,2},{4,5},{5,4},{6,7},{7,6},{8,9},{9,8},{10,11... | collective-permute-start | bytes 49160 | tf_op jit(solution)/shard_map/ppermute | solution.py:196
  23.7 25.1 %copy-start.2 = (f32[72,128]{1,0:T(8,128)S(1)}, f32[72,128]{1,0:T(8,128)}, u32[]{:S(2)}) copy-start(f32[72,128]{1,0:T(8,128)} %fold_one.1) | copy-start | bytes 110596
  26.9 21.9 %all-to-all-start.1 = ((f32[16,64,256]{2,1,0:T(8,128)}), f32[16,64,256]{2,1,0:T(8,128)S(1)}, u32[]{:S(2)}, u32[]{:S(2)}) async-start(f32[16,64,256]{2,1,0:T(8,128)} %bitcast.21), calls=%async_computation.1 | async-start | bytes 2097152 | tf_op jit(solution)/shard_map/all_to_all | solution.py:239
  30.9 3.6 %collective-permute-start.3 = (f32[72,128]{1,0:T(8,128)S(1)}, f32[72,128]{1,0:T(8,128)S(1)}, u32[]{:S(2)}, u32[]{:S(2)}) collective-permute-start(f32[72,128]{1,0:T(8,128)S(1)} %reduce_sum.28), channel_id=1, source_target_pairs={{0,4},{4,0},{8,12},{12,8},{1,5},{5,1},{9,13},{13,9},{2,6},{6,2},{1... | collective-permute-start | bytes 110600 | tf_op jit(solution)/shard_map/ppermute | solution.py:196
  34.5 5.0 %collective-permute-start.6 = (f32[72,128]{1,0:T(8,128)S(1)}, f32[72,128]{1,0:T(8,128)S(1)}, u32[]{:S(2)}, u32[]{:S(2)}) collective-permute-start(f32[72,128]{1,0:T(8,128)S(1)} %add.57), channel_id=1, source_target_pairs={{0,3},{1,2},{2,1},{3,0},{4,7},{5,6},{6,5},{7,4},{8,11},{9,10},{10,... | collective-permute-start | bytes 110600 | tf_op jit(solution)/shard_map/ppermute | solution.py:196
  37.9 4.1 %collective-permute-start.5 = (f32[72,128]{1,0:T(8,128)S(1)}, f32[72,128]{1,0:T(8,128)S(1)}, u32[]{:S(2)}, u32[]{:S(2)}) collective-permute-start(f32[72,128]{1,0:T(8,128)S(1)} %add.57), channel_id=1, source_target_pairs={{0,2},{1,3},{2,0},{3,1},{4,6},{5,7},{6,4},{7,5},{8,10},{9,11},{10,... | collective-permute-start | bytes 110600 | tf_op jit(solution)/shard_map/ppermute | solution.py:196
  37.9 4.1 %collective-permute-start.4 = (f32[72,128]{1,0:T(8,128)S(1)}, f32[72,128]{1,0:T(8,128)S(1)}, u32[]{:S(2)}, u32[]{:S(2)}) collective-permute-start(f32[72,128]{1,0:T(8,128)S(1)} %add.57), channel_id=1, source_target_pairs={{0,1},{1,0},{2,3},{3,2},{4,5},{5,4},{6,7},{7,6},{8,9},{9,8},{10,11... | collective-permute-start | bytes 110600 | tf_op jit(solution)/shard_map/ppermute | solution.py:196
  42.0 6.8 %collective-permute-start.7 = (f32[72,128]{1,0:T(8,128)S(1)}, f32[72,128]{1,0:T(8,128)S(1)}, u32[]{:S(2)}, u32[]{:S(2)}) collective-permute-start(f32[72,128]{1,0:T(8,128)S(1)} %add_add_fusion.1), channel_id=1, source_target_pairs={{0,8},{4,12},{8,0},{12,4},{1,9},{5,13},{9,1},{13,5},{2,10},{6,14},... | collective-permute-start | bytes 110600 | tf_op jit(solution)/shard_map/ppermute | solution.py:196
  49.7 16.6 %all-to-all-start.2 = ((f32[16,72,128]{2,1,0:T(8,128)}), f32[16,72,128]{2,1,0:T(8,128)}, u32[]{:S(2)}, u32[]{:S(2)}) async-start(f32[16,72,128]{2,1,0:T(8,128)} %broadcast_in_dim.16), calls=%async_computation.2 | async-start | bytes 1179648 | tf_op jit(solution)/shard_map/all_to_all | solution.py:205
  56.6 14.9 %copy-start.6 = (s32[16]{0:T(128)S(1)}, s32[16]{0:T(128)}, u32[]{:S(2)}) copy-start(s32[16]{0:T(128)} %param.11) | copy-start | bytes 196
  56.7 5.1 %collective-permute-start.10 = (f32[64,256]{1,0:T(8,128)S(1)}, f32[64,256]{1,0:T(8,128)S(1)}, u32[]{:S(2)}, u32[]{:S(2)}) collective-permute-start(f32[64,256]{1,0:T(8,128)S(1)} %reduce_sum.29), channel_id=1, source_target_pairs={{0,3},{1,2},{2,1},{3,0},{4,7},{5,6},{6,5},{7,4},{8,11},{9,10},{10,... | collective-permute-start | bytes 196616 | tf_op jit(solution)/shard_map/ppermute | solution.py:196
  58.1 5.9 %collective-permute-start.9 = (f32[64,256]{1,0:T(8,128)S(1)}, f32[64,256]{1,0:T(8,128)S(1)}, u32[]{:S(2)}, u32[]{:S(2)}) collective-permute-start(f32[64,256]{1,0:T(8,128)S(1)} %reduce_sum.29), channel_id=1, source_target_pairs={{0,2},{1,3},{2,0},{3,1},{4,6},{5,7},{6,4},{7,5},{8,10},{9,11},{10,... | collective-permute-start | bytes 196616 | tf_op jit(solution)/shard_map/ppermute | solution.py:196
  58.2 5.9 %collective-permute-start.8 = (f32[64,256]{1,0:T(8,128)S(1)}, f32[64,256]{1,0:T(8,128)S(1)}, u32[]{:S(2)}, u32[]{:S(2)}) collective-permute-start(f32[64,256]{1,0:T(8,128)S(1)} %reduce_sum.29), channel_id=1, source_target_pairs={{0,1},{1,0},{2,3},{3,2},{4,5},{5,4},{6,7},{7,6},{8,9},{9,8},{10,11... | collective-permute-start | bytes 196616 | tf_op jit(solution)/shard_map/ppermute | solution.py:196
  67.4 16.4 %all-to-all-start.3 = ((f32[16,64,256]{2,1,0:T(8,128)}), f32[16,64,256]{2,1,0:T(8,128)S(1)}, u32[]{:S(2)}, u32[]{:S(2)}) async-start(f32[16,64,256]{2,1,0:T(8,128)} %broadcast_in_dim.17), calls=%async_computation.3 | async-start | bytes 2097152 | tf_op jit(solution)/shard_map/all_to_all | solution.py:205
  83.8 5.6 %copy-start.1 = (f32[16,64,256]{2,1,0:T(8,128)}, f32[16,64,256]{2,1,0:T(8,128)S(1)}, u32[]{:S(2)}) copy-start(f32[16,64,256]{2,1,0:T(8,128)S(1)} %all-to-all-done.3) | copy-start | bytes 3145732
  85.0 23.1 %all-to-all-start.4 = ((f32[16,64,256]{2,1,0:T(8,128)}), f32[16,64,256]{2,1,0:T(8,128)}, u32[]{:S(2)}, u32[]{:S(2)}) async-start(f32[16,64,256]{2,1,0:T(8,128)} %broadcast_in_dim.18), calls=%async_computation.4 | async-start | bytes 2097152 | tf_op jit(solution)/shard_map/all_to_all | solution.py:266
  93.9 6.7 %collective-permute-start.11 = (f32[1,128]{1,0:T(1,128)}, f32[1,128]{1,0:T(1,128)S(1)}, u32[]{:S(2)}, u32[]{:S(2)}) collective-permute-start(f32[1,128]{1,0:T(1,128)} %get-tuple-element.34), channel_id=1, source_target_pairs={{0,4},{4,0},{8,12},{12,8},{1,5},{5,1},{9,13},{13,9},{2,6},{6,2},{1... | collective-permute-start | bytes 1544 | tf_op jit(solution)/shard_map/ppermute | solution.py:196
  101.3 6.4 %collective-permute-start.12 = (f32[1,128]{1,0:T(1,128)S(1)}, f32[1,128]{1,0:T(1,128)S(1)}, u32[]{:S(2)}, u32[]{:S(2)}) collective-permute-start(f32[1,128]{1,0:T(1,128)S(1)} %add.66), channel_id=1, source_target_pairs={{0,8},{4,12},{8,0},{12,4},{1,9},{5,13},{9,1},{13,5},{2,10},{6,14},... | collective-permute-start | bytes 1544 | tf_op jit(solution)/shard_map/ppermute | solution.py:196

commit v11 on v10

--- a/solution.py
+++ b/solution.py
@@ -166,25 +166,43 @@
     )(inverses, gradient)
 
 
-def finish_kernel(row_ref, align_ref, momentum_ref, precond_ref, base_ref, weights_ref, next_ref):
-    scale = jnp.minimum(1.0, clip_norm / jnp.sqrt(align_ref[0:1, 0:1]))
-    rows = next_ref.shape[0]
-    own = precond_ref[pl.ds(pl.multiple_of(row_ref[0], rows), rows), :]
-    next_ref[...] = momentum_rate * momentum_ref[...] + scale * own
+def finish_kernel(
+    row_ref, align_ref, other_ref, momentum_ref, precond_ref, base_ref, weights_ref, next_ref
+):
+    total = align_ref[0:1, 0:1] + other_ref[0:1, 0:1]
+    scale = jnp.minimum(1.0, clip_norm / jnp.sqrt(total))
+    own_rows = next_ref.shape[0]
+    first = row_ref[0] - pl.program_id(0) * precond_ref.shape[0]
     weights_ref[...] = base_ref[...] - (step_rate * scale) * precond_ref[...]
 
-
-def finish(first_row, align, momentum, precond, base):
+    @pl.when((first >= 0) & (first < precond_ref.shape[0]))
+    def _():
+        own = precond_ref[pl.ds(pl.multiple_of(first, own_rows), own_rows), :]
+        next_ref[...] = momentum_rate * momentum_ref[...] + scale * own
+
+
+def finish(first_row, align, other, momentum, precond, base, steps=4):
+    rows, cols = base.shape
+    whole = lambda value: pl.BlockSpec(value.shape, lambda i: (0, 0))
+    part = pl.BlockSpec((rows // steps, cols), lambda i: (i, 0))
     return pl.pallas_call(
         finish_kernel,
-        in_specs=[pl.BlockSpec(memory_space=pltpu.SMEM)]
-        + [pl.BlockSpec(memory_space=pltpu.VMEM)] * 4,
+        grid=(steps,),
+        in_specs=[
+            pl.BlockSpec(memory_space=pltpu.SMEM),
+            whole(align),
+            whole(other),
+            whole(momentum),
+            part,
+            part,
+        ],
+        out_specs=(part, whole(momentum)),
         out_shape=(
             jax.ShapeDtypeStruct(base.shape, jnp.float32),
             jax.ShapeDtypeStruct(momentum.shape, jnp.float32),
         ),
         name="finish",
-    )(first_row.reshape(1).astype(jnp.int32), align, momentum, precond, base)
+    )(first_row.reshape(1).astype(jnp.int32), align, other, momentum, precond, base)
 
 
 def after(value, first):
@@ -258,19 +276,22 @@
     holds = jnp.max(jnp.where(slots[None, :] == own_slots[:, None], positions[None, :], -1), axis=1)
     right_first = left_count + lax.axis_index("tensor") * right_count
     places = jnp.concatenate([right_first.reshape(1).astype(jnp.int32), holds])
+    places = after(places, folded)
+    base_copies = jnp.broadcast_to(
+        after(base_rows, places)[None], (shard_count,) + base_rows.shape
+    )
+    places = after(places, base_copies)
     inverses, owned_blocks = invert_needed(places, folded, left_count + right_count, capacity)
-    base_copies = jnp.broadcast_to(
-        after(base_rows, inverses)[None], (shard_count,) + base_rows.shape
-    )
     inverses, gradient = lax.optimization_barrier((inverses, gradient))
     base = lax.all_to_all(after(base_copies, gradient), "shards", 0, 0).reshape(
         row_count, col_count
     )
     precond, align = precondition(inverses, gradient)
     align = align + swap(align, "tensor", 1)
-    align = align + swap(align, "tensor", 2)
     first_row = (shard * replica_count + replica) * own_rows
-    weights_next, momentum_next = finish(first_row, align, momentum, precond, base)
+    weights_next, momentum_next = finish(
+        first_row, align, swap(align, "tensor", 2), momentum, precond, base
+    )
     return (weights_next, momentum_next, owned_blocks)
 
 

time: 113 us -> 113 us (level)
  local copies, waits for them, and re-layouts: 6.25 us -> 8.08 us
  waiting for transfers between devices: 21.8 us -> 20.5 us
    unnamed x14 -> x20, local copies, waits for them, and re-layouts: 1.6 us -> 3.57 us
    all_to_all x1, waiting for transfers between devices: 2.72 us -> 1.54 us  [body(): stats_in = lax.all_to_all(folded, 'shards', 0, 0)]
  transfers between devices with their start and end apart: 18 -> 18, of which waited for: 12 -> 12; matrix products, arithmetic and copies ran while one was open for 3% -> 4% of each run, Pallas kernels for 12% -> 12%
where the time goes in v11:
time: 113 us; the launch traced here: 112 us
  starting transfers between devices  57.3 us (51%)
  waiting for transfers between devices  20.5 us (18%)
  Pallas kernels  19.3 us (17%)
  local copies, waits for them, and re-layouts  8.08 us (7%)
  matrix products  3.79 us (3%)
  other arithmetic  1.88 us (2%)
    ppermute x13, starting transfers between devices, swap(): return lax.ppermute(value, axis, [(i, i ^ flip) for i in range(size)])  30.1 us
    ppermute x13, waiting for transfers between devices, swap(): return lax.ppermute(value, axis, [(i, i ^ flip) for i in range(size)])  13.5 us
    all_to_all x2, starting transfers between devices, spread(): return lax.all_to_all(copies, axis, 0, 0)  10.6 us
    all_to_all x1, starting transfers between devices, body(): stats_in = lax.all_to_all(folded, 'shards', 0, 0)  7.58 us
    pallas_call x1, Pallas kernels, invert_needed(): pl.pallas_call(inverse_kernel, in_specs=[pl.BlockSpec(memory_space=pltpu....  7.24 us
    all_to_all x2, waiting for transfers between devices, spread(): return lax.all_to_all(copies, axis, 0, 0)  5.4 us
    all_to_all x1, starting transfers between devices, body(): lax.all_to_all(after(partial_grad, own_stats).reshape(shard_count, piece_...  4.87 us
    pallas_call x1, Pallas kernels, precondition(): pl.pallas_call(precondition_kernel, out_shape=(jax.ShapeDtypeStruct(gradi...  4.53 us
  transfers between devices with their start and end apart: 18, of which 12 were waited for; matrix products, arithmetic and copies ran while one was open for 4% of the time, Pallas kernels for 12%

profile of v11, /device:TPU:1, one launch (start us, length us, event | category | flops | bytes accessed | tf_op | source)
XLA Modules:
  0.0 111.6 jit_solution(10244506250214821511)
XLA Ops:
  0.6 0.0 copy-start
  0.7 1.6 %copy-done = bf16[1024,1024]{1,0:T(8,128)(2,1)S(1)} copy-done((bf16[1024,1024]{1,0:T(8,128)(2,1)S(1)}, bf16[1024,1024]{1,0:T(8,128)(2,1)}, u32[]{:S(2)}) %copy-start) | copy-done | bytes 2097176
  2.2 1.9 %fusion.3.left_ref = f32[8,128,128]{2,1,0:T(8,128)} fusion(bf16[1024,1024]{1,0:T(8,128)(2,1)S(1)} %copy-done), kind=kOutput, calls=%fused_computation.3 | convolution fusion | flops 268435456 | bytes 2621440 | tf_op jit(solution)/shard_map/tnb,tnc->nbc/dot_general | solution.py:23
  4.1 1.9 %fusion.right_ref = f32[8,128,128]{2,1,0:T(8,128)} fusion(bf16[1024,1024]{1,0:T(8,128)(2,1)S(1)} %copy-done.8), kind=kOutput, calls=%fused_computation | convolution fusion | flops 268435456 | bytes 2621440 | tf_op jit(solution)/shard_map/tnb,tnc->nbc/dot_general | solution.py:23
  6.0 2.2 %fold.1 = f32[16,72,128]{2,1,0:T(8,128)} custom-call(f32[8,128,128]{2,1,0:T(8,128)} %fusion.3.left_ref, f32[8,128,128]{2,1,0:T(8,128)} %fusion.right_ref), custom_call_target="tpu_custom_call" | custom-call | tf_op jit(solution)/shard_map/fold/pallas_call | solution.py:48
  8.3 7.6 %all-to-all-start = ((f32[16,72,128]{2,1,0:T(8,128)}), f32[16,72,128]{2,1,0:T(8,128)S(1)}, u32[]{:S(2)}, u32[]{:S(2)}) async-start(f32[16,72,128]{2,1,0:T(8,128)} %fold.1), calls=%async_computation | async-start | bytes 1179648 | tf_op jit(solution)/shard_map/all_to_all | solution.py:243
  15.9 1.7 %collective-permute-start.2 = (f32[16,256]{1,0:T(8,128)S(1)}, f32[16,256]{1,0:T(8,128)S(1)}, u32[]{:S(2)}, u32[]{:S(2)}) collective-permute-start(f32[16,256]{1,0:T(8,128)S(1)} %multiply_subtract_fusion), channel_id=1, source_target_pairs={{0,1},{1,0},{2,3},{3,2},{4,5},{5,4},{6,7},{7,6},{8,9},{9,8},{10,11... | collective-permute-start | bytes 49160 | tf_op jit(solution)/shard_map/ppermute | solution.py:214
  17.6 3.0 %collective-permute-start.1 = (f32[16,256]{1,0:T(8,128)S(1)}, f32[16,256]{1,0:T(8,128)S(1)}, u32[]{:S(2)}, u32[]{:S(2)}) collective-permute-start(f32[16,256]{1,0:T(8,128)S(1)} %multiply_subtract_fusion), channel_id=1, source_target_pairs={{0,2},{1,3},{2,0},{3,1},{4,6},{5,7},{6,4},{7,5},{8,10},{9,11},{10,... | collective-permute-start | bytes 49160 | tf_op jit(solution)/shard_map/ppermute | solution.py:214
  20.6 1.5 %constant_dynamic-slice_fusion.block_ref = f32[1,128,128]{2,1,0:T(8,128)} fusion(f32[16,128,128]{2,1,0:T(8,128)} %param.10, s32[]{:T(128)S(6)} %select_n.82), kind=kLoop, calls=%fused_computation.23 | loop fusion | bytes 131076 | tf_op jit(solution)/shard_map/dynamic_slice | solution.py:254
  22.1 1.5 %fold_one.1 = f32[72,128]{1,0:T(8,128)} custom-call(f32[1,128,128]{2,1,0:T(8,128)} %constant_dynamic-slice_fusion.block_ref), custom_call_target="tpu_custom_call" | custom-call | tf_op jit(solution)/shard_map/fold_one/pallas_call | solution.py:66
  23.6 1.7 %collective-permute-done = f32[16,256]{1,0:T(8,128)S(1)} collective-permute-done((f32[16,256]{1,0:T(8,128)S(1)}, f32[16,256]{1,0:T(8,128)S(1)}, u32[]{:S(2)}, u32[]{:S(2)}) %collective-permute-start) | collective-permute-done | bytes 16416 | tf_op jit(solution)/shard_map/ppermute | solution.py:214
  25.3 1.5 %all-to-all-done = f32[16,72,128]{2,1,0:T(8,128)S(1)} async-done(((f32[16,72,128]{2,1,0:T(8,128)}), f32[16,72,128]{2,1,0:T(8,128)S(1)}, u32[]{:S(2)}, u32[]{:S(2)}) %all-to-all-start) | async-done | bytes 589856 | tf_op jit(solution)/shard_map/all_to_all | solution.py:243
  26.9 4.9 %all-to-all-start.1 = ((f32[16,64,256]{2,1,0:T(8,128)}), f32[16,64,256]{2,1,0:T(8,128)S(1)}, u32[]{:S(2)}, u32[]{:S(2)}) async-start(f32[16,64,256]{2,1,0:T(8,128)} %bitcast.22), calls=%async_computation.1 | async-start | bytes 2097152 | tf_op jit(solution)/shard_map/all_to_all | solution.py:257
  31.8 3.3 %collective-permute-start.3 = (f32[72,128]{1,0:T(8,128)S(1)}, f32[72,128]{1,0:T(8,128)S(1)}, u32[]{:S(2)}, u32[]{:S(2)}) collective-permute-start(f32[72,128]{1,0:T(8,128)S(1)} %reduce_sum.28), channel_id=1, source_target_pairs={{0,4},{4,0},{8,12},{12,8},{1,5},{5,1},{9,13},{13,9},{2,6},{6,2},{1... | collective-permute-start | bytes 110600 | tf_op jit(solution)/shard_map/ppermute | solution.py:214
  35.1 0.9 collective-permute-done.3
  35.9 1.9 %collective-permute-start.6 = (f32[72,128]{1,0:T(8,128)S(1)}, f32[72,128]{1,0:T(8,128)S(1)}, u32[]{:S(2)}, u32[]{:S(2)}) collective-permute-start(f32[72,128]{1,0:T(8,128)S(1)} %add.54), channel_id=1, source_target_pairs={{0,3},{1,2},{2,1},{3,0},{4,7},{5,6},{6,5},{7,4},{8,11},{9,10},{10,... | collective-permute-start | bytes 110600 | tf_op jit(solution)/shard_map/ppermute | solution.py:214
  37.9 1.6 %collective-permute-start.4 = (f32[72,128]{1,0:T(8,128)S(1)}, f32[72,128]{1,0:T(8,128)S(1)}, u32[]{:S(2)}, u32[]{:S(2)}) collective-permute-start(f32[72,128]{1,0:T(8,128)S(1)} %add.54), channel_id=1, source_target_pairs={{0,1},{1,0},{2,3},{3,2},{4,5},{5,4},{6,7},{7,6},{8,9},{9,8},{10,11... | collective-permute-start | bytes 110600 | tf_op jit(solution)/shard_map/ppermute | solution.py:214
  39.5 1.4 %collective-permute-done.6 = f32[72,128]{1,0:T(8,128)S(1)} collective-permute-done((f32[72,128]{1,0:T(8,128)S(1)}, f32[72,128]{1,0:T(8,128)S(1)}, u32[]{:S(2)}, u32[]{:S(2)}) %collective-permute-start.6) | collective-permute-done | bytes 36896 | tf_op jit(solution)/shard_map/ppermute | solution.py:214
  40.8 1.6 %collective-permute-done.5 = f32[72,128]{1,0:T(8,128)S(1)} collective-permute-done((f32[72,128]{1,0:T(8,128)S(1)}, f32[72,128]{1,0:T(8,128)S(1)}, u32[]{:S(2)}, u32[]{:S(2)}) %collective-permute-start.5) | collective-permute-done | bytes 36896 | tf_op jit(solution)/shard_map/ppermute | solution.py:214
  42.5 4.7 %collective-permute-start.7 = (f32[72,128]{1,0:T(8,128)S(1)}, f32[72,128]{1,0:T(8,128)S(1)}, u32[]{:S(2)}, u32[]{:S(2)}) collective-permute-start(f32[72,128]{1,0:T(8,128)S(1)} %add_add_fusion.1), channel_id=1, source_target_pairs={{0,8},{4,12},{8,0},{12,4},{1,9},{5,13},{9,1},{13,5},{2,10},{6,14},... | collective-permute-start | bytes 110600 | tf_op jit(solution)/shard_map/ppermute | solution.py:214
  47.1 2.3 %collective-permute-done.7 = f32[72,128]{1,0:T(8,128)S(1)} collective-permute-done((f32[72,128]{1,0:T(8,128)S(1)}, f32[72,128]{1,0:T(8,128)S(1)}, u32[]{:S(2)}, u32[]{:S(2)}) %collective-permute-start.7) | collective-permute-done | bytes 36896 | tf_op jit(solution)/shard_map/ppermute | solution.py:214
  49.5 0.9 broadcast_in_dim.16
  50.3 6.7 %all-to-all-start.2 = ((f32[16,72,128]{2,1,0:T(8,128)}), f32[16,72,128]{2,1,0:T(8,128)}, u32[]{:S(2)}, u32[]{:S(2)}) async-start(f32[16,72,128]{2,1,0:T(8,128)} %broadcast_in_dim.16), calls=%async_computation.2 | async-start | bytes 1179648 | tf_op jit(solution)/shard_map/all_to_all | solution.py:223
  57.1 0.1 reduce_sum.29
  57.1 2.3 %collective-permute-start.10 = (f32[64,256]{1,0:T(8,128)S(1)}, f32[64,256]{1,0:T(8,128)S(1)}, u32[]{:S(2)}, u32[]{:S(2)}) collective-permute-start(f32[64,256]{1,0:T(8,128)S(1)} %reduce_sum.29), channel_id=1, source_target_pairs={{0,3},{1,2},{2,1},{3,0},{4,7},{5,6},{6,5},{7,4},{8,11},{9,10},{10,... | collective-permute-start | bytes 196616 | tf_op jit(solution)/shard_map/ppermute | solution.py:214
  59.4 1.3 %collective-permute-start.8 = (f32[64,256]{1,0:T(8,128)S(1)}, f32[64,256]{1,0:T(8,128)S(1)}, u32[]{:S(2)}, u32[]{:S(2)}) collective-permute-start(f32[64,256]{1,0:T(8,128)S(1)} %reduce_sum.29), channel_id=1, source_target_pairs={{0,1},{1,0},{2,3},{3,2},{4,5},{5,4},{6,7},{7,6},{8,9},{9,8},{10,11... | collective-permute-start | bytes 196616 | tf_op jit(solution)/shard_map/ppermute | solution.py:214
  60.8 1.4 %collective-permute-done.10 = f32[64,256]{1,0:T(8,128)S(1)} collective-permute-done((f32[64,256]{1,0:T(8,128)S(1)}, f32[64,256]{1,0:T(8,128)S(1)}, u32[]{:S(2)}, u32[]{:S(2)}) %collective-permute-start.10) | collective-permute-done | bytes 65568 | tf_op jit(solution)/shard_map/ppermute | solution.py:214
  62.2 1.9 %collective-permute-done.9 = f32[64,256]{1,0:T(8,128)S(1)} collective-permute-done((f32[64,256]{1,0:T(8,128)S(1)}, f32[64,256]{1,0:T(8,128)S(1)}, u32[]{:S(2)}, u32[]{:S(2)}) %collective-permute-start.9) | collective-permute-done | bytes 65568 | tf_op jit(solution)/shard_map/ppermute | solution.py:214
  64.1 2.8 %all-to-all-done.2.folded_ref = f32[16,72,128]{2,1,0:T(8,128)} async-done(((f32[16,72,128]{2,1,0:T(8,128)}), f32[16,72,128]{2,1,0:T(8,128)}, u32[]{:S(2)}, u32[]{:S(2)}) %all-to-all-start.2) | async-done | bytes 589856 | tf_op jit(solution)/shard_map/all_to_all | solution.py:223
  66.9 1.1 broadcast_in_dim.18
  67.9 3.9 %all-to-all-start.3 = ((f32[16,64,256]{2,1,0:T(8,128)}), f32[16,64,256]{2,1,0:T(8,128)S(1)}, u32[]{:S(2)}, u32[]{:S(2)}) async-start(f32[16,64,256]{2,1,0:T(8,128)} %broadcast_in_dim.18), calls=%async_computation.3 | async-start | bytes 2097152 | tf_op jit(solution)/shard_map/all_to_all | solution.py:223
  71.8 0.2 convert_reduce_fusion
  72.0 0.2 fusion.7
  72.2 0.7 pad_add_fusion.place_ref
  72.9 1.1 broadcast_in_dim.17
  74.0 7.2 %inverse.1 = (f32[10,128,128]{2,1,0:T(8,128)}, f32[2,128,128]{2,1,0:T(8,128)}) custom-call(s32[3]{0:T(128)} %pad_add_fusion.place_ref, f32[16,72,128]{2,1,0:T(8,128)} %all-to-all-done.2.folded_ref), custom_call_target="tpu_custom_call" | custom-call | tf_op jit(solution)/shard_map/inverse/pallas_call | solution.py:128
  81.2 2.6 %all-to-all-done.3 = f32[16,64,256]{2,1,0:T(8,128)S(1)} async-done(((f32[16,64,256]{2,1,0:T(8,128)}), f32[16,64,256]{2,1,0:T(8,128)S(1)}, u32[]{:S(2)}, u32[]{:S(2)}) %all-to-all-start.3) | async-done | bytes 1048608 | tf_op jit(solution)/shard_map/all_to_all | solution.py:223
  83.8 1.0 copy-done.2
  84.8 4.1 %all-to-all-start.4 = ((f32[16,64,256]{2,1,0:T(8,128)}), f32[16,64,256]{2,1,0:T(8,128)S(1)}, u32[]{:S(2)}, u32[]{:S(2)}) async-start(f32[16,64,256]{2,1,0:T(8,128)} %broadcast_in_dim.17), calls=%async_computation.4 | async-start | bytes 2097152 | tf_op jit(solution)/shard_map/all_to_all | solution.py:286
  88.9 4.5 %precondition.1 = (f32[1024,256]{1,0:T(8,128)}, f32[1,128]{1,0:T(1,128)}) custom-call(f32[10,128,128]{2,1,0:T(8,128)} %get-tuple-element.37.inverse_ref, f32[1024,256]{1,0:T(8,128)} %bitcast.21), custom_call_target="tpu_custom_call" | custom-call | tf_op jit(solution)/shard_map/precondition/pallas_call | solution.py:159
  93.4 5.4 %collective-permute-start.11 = (f32[1,128]{1,0:T(1,128)}, f32[1,128]{1,0:T(1,128)S(1)}, u32[]{:S(2)}, u32[]{:S(2)}) collective-permute-start(f32[1,128]{1,0:T(1,128)} %get-tuple-element.39), channel_id=1, source_target_pairs={{0,4},{4,0},{8,12},{12,8},{1,5},{5,1},{9,13},{13,9},{2,6},{6,2},{1... | collective-permute-start | bytes 1544 | tf_op jit(solution)/shard_map/ppermute | solution.py:214
  98.9 1.0 collective-permute-done.11
  99.8 0.7 add.63.align_ref
  100.5 4.8 %collective-permute-start.12 = (f32[1,128]{1,0:T(1,128)S(1)}, f32[1,128]{1,0:T(1,128)S(1)}, u32[]{:S(2)}, u32[]{:S(2)}) collective-permute-start(f32[1,128]{1,0:T(1,128)S(1)} %add.63.align_ref), channel_id=1, source_target_pairs={{0,8},{4,12},{8,0},{12,4},{1,9},{5,13},{9,1},{13,5},{2,10},{6,14},... | collective-permute-start | bytes 1544 | tf_op jit(solution)/shard_map/ppermute | solution.py:214
  105.3 1.5 %collective-permute-done.12.other_ref = f32[1,128]{1,0:T(1,128)S(1)} collective-permute-done((f32[1,128]{1,0:T(1,128)S(1)}, f32[1,128]{1,0:T(1,128)S(1)}, u32[]{:S(2)}, u32[]{:S(2)}) %collective-permute-start.12) | collective-permute-done | bytes 544 | tf_op jit(solution)/shard_map/ppermute | solution.py:214
  106.8 0.5 copy-done.7
  107.4 0.5 copy-done.1
  107.8 3.8 %finish.1 = (f32[1024,256]{1,0:T(8,128)}, f32[16,256]{1,0:T(8,128)}) custom-call(s32[1]{0:T(128)} %bitcast.row_ref, f32[1,128]{1,0:T(1,128)} %copy-done.6, f32[1,128]{1,0:T(1,128)} %copy-done.7, f32[16,256]{1,0:T(8,128)} %momentum_ref.1, f32[1024,256]{1,0:T(8,128)} %get-tuple-element.40.precond_ref, f32[1024,256]{1,0:T(8,128)} %bitcast.20), custom_call_target="tpu_custom_call" | custom-call | tf_op jit(solution)/shard_map/finish/pallas_call | solution.py:188
  (34 shorter events, 0.2 us)
Async XLA Ops:
  0.6 1.6 %copy-start = (bf16[1024,1024]{1,0:T(8,128)(2,1)S(1)}, bf16[1024,1024]{1,0:T(8,128)(2,1)}, u32[]{:S(2)}) copy-start(bf16[1024,1024]{1,0:T(8,128)(2,1)} %param.7) | copy-start | bytes 6291460
  0.6 3.4 %copy-start.8 = (bf16[1024,1024]{1,0:T(8,128)(2,1)S(1)}, bf16[1024,1024]{1,0:T(8,128)(2,1)}, u32[]{:S(2)}) copy-start(bf16[1024,1024]{1,0:T(8,128)(2,1)} %param.8) | copy-start | bytes 6291460
  6.0 9.8 %copy-start.4 = (f32[16,256]{1,0:T(8,128)S(1)}, f32[16,256]{1,0:T(8,128)}, u32[]{:S(2)}) copy-start(f32[16,256]{1,0:T(8,128)} %momentum_ref.1) | copy-start | bytes 49156
  6.0 9.8 %copy-start.5 = (f32[16,256]{1,0:T(8,128)S(1)}, f32[16,256]{1,0:T(8,128)}, u32[]{:S(2)}) copy-start(f32[16,256]{1,0:T(8,128)} %param.12) | copy-start | bytes 49156
  8.3 18.6 %all-to-all-start = ((f32[16,72,128]{2,1,0:T(8,128)}), f32[16,72,128]{2,1,0:T(8,128)S(1)}, u32[]{:S(2)}, u32[]{:S(2)}) async-start(f32[16,72,128]{2,1,0:T(8,128)} %fold.1), calls=%async_computation | async-start | bytes 1179648 | tf_op jit(solution)/shard_map/all_to_all | solution.py:243
  15.9 7.7 %collective-permute-start.2 = (f32[16,256]{1,0:T(8,128)S(1)}, f32[16,256]{1,0:T(8,128)S(1)}, u32[]{:S(2)}, u32[]{:S(2)}) collective-permute-start(f32[16,256]{1,0:T(8,128)S(1)} %multiply_subtract_fusion), channel_id=1, source_target_pairs={{0,1},{1,0},{2,3},{3,2},{4,5},{5,4},{6,7},{7,6},{8,9},{9,8},{10,11... | collective-permute-start | bytes 49160 | tf_op jit(solution)/shard_map/ppermute | solution.py:214
  17.6 6.0 %collective-permute-start.1 = (f32[16,256]{1,0:T(8,128)S(1)}, f32[16,256]{1,0:T(8,128)S(1)}, u32[]{:S(2)}, u32[]{:S(2)}) collective-permute-start(f32[16,256]{1,0:T(8,128)S(1)} %multiply_subtract_fusion), channel_id=1, source_target_pairs={{0,2},{1,3},{2,0},{3,1},{4,6},{5,7},{6,4},{7,5},{8,10},{9,11},{10,... | collective-permute-start | bytes 49160 | tf_op jit(solution)/shard_map/ppermute | solution.py:214
  20.6 4.7 %collective-permute-start = (f32[16,256]{1,0:T(8,128)S(1)}, f32[16,256]{1,0:T(8,128)S(1)}, u32[]{:S(2)}, u32[]{:S(2)}) collective-permute-start(f32[16,256]{1,0:T(8,128)S(1)} %multiply_subtract_fusion), channel_id=1, source_target_pairs={{0,3},{1,2},{2,1},{3,0},{4,7},{5,6},{6,5},{7,4},{8,11},{9,10},{10,... | collective-permute-start | bytes 49160 | tf_op jit(solution)/shard_map/ppermute | solution.py:214
  23.6 25.8 %copy-start.3 = (f32[72,128]{1,0:T(8,128)S(1)}, f32[72,128]{1,0:T(8,128)}, u32[]{:S(2)}) copy-start(f32[72,128]{1,0:T(8,128)} %fold_one.1) | copy-start | bytes 110596
  26.9 22.6 %all-to-all-start.1 = ((f32[16,64,256]{2,1,0:T(8,128)}), f32[16,64,256]{2,1,0:T(8,128)S(1)}, u32[]{:S(2)}, u32[]{:S(2)}) async-start(f32[16,64,256]{2,1,0:T(8,128)} %bitcast.22), calls=%async_computation.1 | async-start | bytes 2097152 | tf_op jit(solution)/shard_map/all_to_all | solution.py:257
  31.8 4.2 %collective-permute-start.3 = (f32[72,128]{1,0:T(8,128)S(1)}, f32[72,128]{1,0:T(8,128)S(1)}, u32[]{:S(2)}, u32[]{:S(2)}) collective-permute-start(f32[72,128]{1,0:T(8,128)S(1)} %reduce_sum.28), channel_id=1, source_target_pairs={{0,4},{4,0},{8,12},{12,8},{1,5},{5,1},{9,13},{13,9},{2,6},{6,2},{1... | collective-permute-start | bytes 110600 | tf_op jit(solution)/shard_map/ppermute | solution.py:214
  35.9 4.9 %collective-permute-start.6 = (f32[72,128]{1,0:T(8,128)S(1)}, f32[72,128]{1,0:T(8,128)S(1)}, u32[]{:S(2)}, u32[]{:S(2)}) collective-permute-start(f32[72,128]{1,0:T(8,128)S(1)} %add.54), channel_id=1, source_target_pairs={{0,3},{1,2},{2,1},{3,0},{4,7},{5,6},{6,5},{7,4},{8,11},{9,10},{10,... | collective-permute-start | bytes 110600 | tf_op jit(solution)/shard_map/ppermute | solution.py:214
  37.9 4.6 %collective-permute-start.5 = (f32[72,128]{1,0:T(8,128)S(1)}, f32[72,128]{1,0:T(8,128)S(1)}, u32[]{:S(2)}, u32[]{:S(2)}) collective-permute-start(f32[72,128]{1,0:T(8,128)S(1)} %add.54), channel_id=1, source_target_pairs={{0,2},{1,3},{2,0},{3,1},{4,6},{5,7},{6,4},{7,5},{8,10},{9,11},{10,... | collective-permute-start | bytes 110600 | tf_op jit(solution)/shard_map/ppermute | solution.py:214
  37.9 4.6 %collective-permute-start.4 = (f32[72,128]{1,0:T(8,128)S(1)}, f32[72,128]{1,0:T(8,128)S(1)}, u32[]{:S(2)}, u32[]{:S(2)}) collective-permute-start(f32[72,128]{1,0:T(8,128)S(1)} %add.54), channel_id=1, source_target_pairs={{0,1},{1,0},{2,3},{3,2},{4,5},{5,4},{6,7},{7,6},{8,9},{9,8},{10,11... | collective-permute-start | bytes 110600 | tf_op jit(solution)/shard_map/ppermute | solution.py:214
  42.5 7.0 %collective-permute-start.7 = (f32[72,128]{1,0:T(8,128)S(1)}, f32[72,128]{1,0:T(8,128)S(1)}, u32[]{:S(2)}, u32[]{:S(2)}) collective-permute-start(f32[72,128]{1,0:T(8,128)S(1)} %add_add_fusion.1), channel_id=1, source_target_pairs={{0,8},{4,12},{8,0},{12,4},{1,9},{5,13},{9,1},{13,5},{2,10},{6,14},... | collective-permute-start | bytes 110600 | tf_op jit(solution)/shard_map/ppermute | solution.py:214
  50.3 16.5 %all-to-all-start.2 = ((f32[16,72,128]{2,1,0:T(8,128)}), f32[16,72,128]{2,1,0:T(8,128)}, u32[]{:S(2)}, u32[]{:S(2)}) async-start(f32[16,72,128]{2,1,0:T(8,128)} %broadcast_in_dim.16), calls=%async_computation.2 | async-start | bytes 1179648 | tf_op jit(solution)/shard_map/all_to_all | solution.py:223
  57.0 14.8 %copy-start.9 = (s32[16]{0:T(128)S(1)}, s32[16]{0:T(128)}, u32[]{:S(2)}) copy-start(s32[16]{0:T(128)} %param.11) | copy-start | bytes 196
  57.1 5.0 %collective-permute-start.10 = (f32[64,256]{1,0:T(8,128)S(1)}, f32[64,256]{1,0:T(8,128)S(1)}, u32[]{:S(2)}, u32[]{:S(2)}) collective-permute-start(f32[64,256]{1,0:T(8,128)S(1)} %reduce_sum.29), channel_id=1, source_target_pairs={{0,3},{1,2},{2,1},{3,0},{4,7},{5,6},{6,5},{7,4},{8,11},{9,10},{10,... | collective-permute-start | bytes 196616 | tf_op jit(solution)/shard_map/ppermute | solution.py:214
  59.4 4.6 %collective-permute-start.9 = (f32[64,256]{1,0:T(8,128)S(1)}, f32[64,256]{1,0:T(8,128)S(1)}, u32[]{:S(2)}, u32[]{:S(2)}) collective-permute-start(f32[64,256]{1,0:T(8,128)S(1)} %reduce_sum.29), channel_id=1, source_target_pairs={{0,2},{1,3},{2,0},{3,1},{4,6},{5,7},{6,4},{7,5},{8,10},{9,11},{10,... | collective-permute-start | bytes 196616 | tf_op jit(solution)/shard_map/ppermute | solution.py:214
  59.4 4.6 %collective-permute-start.8 = (f32[64,256]{1,0:T(8,128)S(1)}, f32[64,256]{1,0:T(8,128)S(1)}, u32[]{:S(2)}, u32[]{:S(2)}) collective-permute-start(f32[64,256]{1,0:T(8,128)S(1)} %reduce_sum.29), channel_id=1, source_target_pairs={{0,1},{1,0},{2,3},{3,2},{4,5},{5,4},{6,7},{7,6},{8,9},{9,8},{10,11... | collective-permute-start | bytes 196616 | tf_op jit(solution)/shard_map/ppermute | solution.py:214
  67.9 15.9 %all-to-all-start.3 = ((f32[16,64,256]{2,1,0:T(8,128)}), f32[16,64,256]{2,1,0:T(8,128)S(1)}, u32[]{:S(2)}, u32[]{:S(2)}) async-start(f32[16,64,256]{2,1,0:T(8,128)} %broadcast_in_dim.18), calls=%async_computation.3 | async-start | bytes 2097152 | tf_op jit(solution)/shard_map/all_to_all | solution.py:223
  83.8 1.0 copy-start.2
  84.8 22.0 %all-to-all-start.4 = ((f32[16,64,256]{2,1,0:T(8,128)}), f32[16,64,256]{2,1,0:T(8,128)S(1)}, u32[]{:S(2)}, u32[]{:S(2)}) async-start(f32[16,64,256]{2,1,0:T(8,128)} %broadcast_in_dim.17), calls=%async_computation.4 | async-start | bytes 2097152 | tf_op jit(solution)/shard_map/all_to_all | solution.py:286
  93.4 6.4 %collective-permute-start.11 = (f32[1,128]{1,0:T(1,128)}, f32[1,128]{1,0:T(1,128)S(1)}, u32[]{:S(2)}, u32[]{:S(2)}) collective-permute-start(f32[1,128]{1,0:T(1,128)} %get-tuple-element.39), channel_id=1, source_target_pairs={{0,4},{4,0},{8,12},{12,8},{1,5},{5,1},{9,13},{13,9},{2,6},{6,2},{1... | collective-permute-start | bytes 1544 | tf_op jit(solution)/shard_map/ppermute | solution.py:214
  100.5 6.3 %copy-start.6 = (f32[1,128]{1,0:T(1,128)}, f32[1,128]{1,0:T(1,128)S(1)}, u32[]{:S(2)}) copy-start(f32[1,128]{1,0:T(1,128)S(1)} %add.63.align_ref) | copy-start | bytes 1540
  100.5 6.3 %collective-permute-start.12 = (f32[1,128]{1,0:T(1,128)S(1)}, f32[1,128]{1,0:T(1,128)S(1)}, u32[]{:S(2)}, u32[]{:S(2)}) collective-permute-start(f32[1,128]{1,0:T(1,128)S(1)} %add.63.align_ref), channel_id=1, source_target_pairs={{0,8},{4,12},{8,0},{12,4},{1,9},{5,13},{9,1},{13,5},{2,10},{6,14},... | collective-permute-start | bytes 1544 | tf_op jit(solution)/shard_map/ppermute | solution.py:214
  106.8 0.5 copy-start.7
  106.8 1.0 copy-start.1

commit v12 on v11

--- a/solution.py
+++ b/solution.py
@@ -171,32 +171,17 @@
 ):
     total = align_ref[0:1, 0:1] + other_ref[0:1, 0:1]
     scale = jnp.minimum(1.0, clip_norm / jnp.sqrt(total))
-    own_rows = next_ref.shape[0]
-    first = row_ref[0] - pl.program_id(0) * precond_ref.shape[0]
+    rows = next_ref.shape[0]
+    own = precond_ref[pl.ds(pl.multiple_of(row_ref[0], rows), rows), :]
+    next_ref[...] = momentum_rate * momentum_ref[...] + scale * own
     weights_ref[...] = base_ref[...] - (step_rate * scale) * precond_ref[...]
 
-    @pl.when((first >= 0) & (first < precond_ref.shape[0]))
-    def _():
-        own = precond_ref[pl.ds(pl.multiple_of(first, own_rows), own_rows), :]
-        next_ref[...] = momentum_rate * momentum_ref[...] + scale * own
-
-
-def finish(first_row, align, other, momentum, precond, base, steps=4):
-    rows, cols = base.shape
-    whole = lambda value: pl.BlockSpec(value.shape, lambda i: (0, 0))
-    part = pl.BlockSpec((rows // steps, cols), lambda i: (i, 0))
+
+def finish(first_row, align, other, momentum, precond, base):
     return pl.pallas_call(
         finish_kernel,
-        grid=(steps,),
-        in_specs=[
-            pl.BlockSpec(memory_space=pltpu.SMEM),
-            whole(align),
-            whole(other),
-            whole(momentum),
-            part,
-            part,
-        ],
-        out_specs=(part, whole(momentum)),
+        in_specs=[pl.BlockSpec(memory_space=pltpu.SMEM)]
+        + [pl.BlockSpec(memory_space=pltpu.VMEM)] * 5,
         out_shape=(
             jax.ShapeDtypeStruct(base.shape, jnp.float32),
             jax.ShapeDtypeStruct(momentum.shape, jnp.float32),

time: 113 us -> 112 us (level)
  no operation moved by 1% of the time
where the time goes in v12:
time: 112 us; the launch traced here: 111 us
  starting transfers between devices  57.3 us (51%)
  waiting for transfers between devices  20.5 us (18%)
  Pallas kernels  18.3 us (16%)
  local copies, waits for them, and re-layouts  8.08 us (7%)
  matrix products  3.79 us (3%)
  other arithmetic  1.88 us (2%)
    ppermute x13, starting transfers between devices, swap(): return lax.ppermute(value, axis, [(i, i ^ flip) for i in range(size)])  30.1 us
    ppermute x13, waiting for transfers between devices, swap(): return lax.ppermute(value, axis, [(i, i ^ flip) for i in range(size)])  13.5 us
    all_to_all x2, starting transfers between devices, spread(): return lax.all_to_all(copies, axis, 0, 0)  10.6 us
    all_to_all x1, starting transfers between devices, body(): stats_in = lax.all_to_all(folded, 'shards', 0, 0)  7.58 us
    pallas_call x1, Pallas kernels, invert_needed(): pl.pallas_call(inverse_kernel, in_specs=[pl.BlockSpec(memory_space=pltpu....  7.24 us
    all_to_all x2, waiting for transfers between devices, spread(): return lax.all_to_all(copies, axis, 0, 0)  5.4 us
    all_to_all x1, starting transfers between devices, body(): lax.all_to_all(after(partial_grad, own_stats).reshape(shard_count, piece_...  4.87 us
    pallas_call x1, Pallas kernels, precondition(): pl.pallas_call(precondition_kernel, out_shape=(jax.ShapeDtypeStruct(gradi...  4.53 us
  transfers between devices with their start and end apart: 18, of which 12 were waited for; matrix products, arithmetic and copies ran while one was open for 4% of the time, Pallas kernels for 12%

profile of v12, /device:TPU:1, one launch (start us, length us, event | category | flops | bytes accessed | tf_op | source)
XLA Modules:
  0.0 110.6 jit_solution(16889051285763097690)
XLA Ops:
  0.6 0.0 copy-start
  0.7 1.6 %copy-done = bf16[1024,1024]{1,0:T(8,128)(2,1)S(1)} copy-done((bf16[1024,1024]{1,0:T(8,128)(2,1)S(1)}, bf16[1024,1024]{1,0:T(8,128)(2,1)}, u32[]{:S(2)}) %copy-start) | copy-done | bytes 2097176
  2.2 1.9 %fusion.3.left_ref = f32[8,128,128]{2,1,0:T(8,128)} fusion(bf16[1024,1024]{1,0:T(8,128)(2,1)S(1)} %copy-done), kind=kOutput, calls=%fused_computation.3 | convolution fusion | flops 268435456 | bytes 2621440 | tf_op jit(solution)/shard_map/tnb,tnc->nbc/dot_general | solution.py:23
  4.1 1.9 %fusion.right_ref = f32[8,128,128]{2,1,0:T(8,128)} fusion(bf16[1024,1024]{1,0:T(8,128)(2,1)S(1)} %copy-done.8), kind=kOutput, calls=%fused_computation | convolution fusion | flops 268435456 | bytes 2621440 | tf_op jit(solution)/shard_map/tnb,tnc->nbc/dot_general | solution.py:23
  6.0 2.2 %fold.1 = f32[16,72,128]{2,1,0:T(8,128)} custom-call(f32[8,128,128]{2,1,0:T(8,128)} %fusion.3.left_ref, f32[8,128,128]{2,1,0:T(8,128)} %fusion.right_ref), custom_call_target="tpu_custom_call" | custom-call | tf_op jit(solution)/shard_map/fold/pallas_call | solution.py:48
  8.3 7.6 %all-to-all-start = ((f32[16,72,128]{2,1,0:T(8,128)}), f32[16,72,128]{2,1,0:T(8,128)S(1)}, u32[]{:S(2)}, u32[]{:S(2)}) async-start(f32[16,72,128]{2,1,0:T(8,128)} %fold.1), calls=%async_computation | async-start | bytes 1179648 | tf_op jit(solution)/shard_map/all_to_all | solution.py:228
  15.9 1.7 %collective-permute-start.2 = (f32[16,256]{1,0:T(8,128)S(1)}, f32[16,256]{1,0:T(8,128)S(1)}, u32[]{:S(2)}, u32[]{:S(2)}) collective-permute-start(f32[16,256]{1,0:T(8,128)S(1)} %multiply_subtract_fusion), channel_id=1, source_target_pairs={{0,1},{1,0},{2,3},{3,2},{4,5},{5,4},{6,7},{7,6},{8,9},{9,8},{10,11... | collective-permute-start | bytes 49160 | tf_op jit(solution)/shard_map/ppermute | solution.py:199
  17.6 3.0 %collective-permute-start.1 = (f32[16,256]{1,0:T(8,128)S(1)}, f32[16,256]{1,0:T(8,128)S(1)}, u32[]{:S(2)}, u32[]{:S(2)}) collective-permute-start(f32[16,256]{1,0:T(8,128)S(1)} %multiply_subtract_fusion), channel_id=1, source_target_pairs={{0,2},{1,3},{2,0},{3,1},{4,6},{5,7},{6,4},{7,5},{8,10},{9,11},{10,... | collective-permute-start | bytes 49160 | tf_op jit(solution)/shard_map/ppermute | solution.py:199
  20.6 1.5 %constant_dynamic-slice_fusion.block_ref = f32[1,128,128]{2,1,0:T(8,128)} fusion(f32[16,128,128]{2,1,0:T(8,128)} %param.10, s32[]{:T(128)S(6)} %select_n.82), kind=kLoop, calls=%fused_computation.23 | loop fusion | bytes 131076 | tf_op jit(solution)/shard_map/dynamic_slice | solution.py:239
  22.1 1.5 %fold_one.1 = f32[72,128]{1,0:T(8,128)} custom-call(f32[1,128,128]{2,1,0:T(8,128)} %constant_dynamic-slice_fusion.block_ref), custom_call_target="tpu_custom_call" | custom-call | tf_op jit(solution)/shard_map/fold_one/pallas_call | solution.py:66
  23.6 1.7 %collective-permute-done = f32[16,256]{1,0:T(8,128)S(1)} collective-permute-done((f32[16,256]{1,0:T(8,128)S(1)}, f32[16,256]{1,0:T(8,128)S(1)}, u32[]{:S(2)}, u32[]{:S(2)}) %collective-permute-start) | collective-permute-done | bytes 16416 | tf_op jit(solution)/shard_map/ppermute | solution.py:199
  25.3 1.5 %all-to-all-done = f32[16,72,128]{2,1,0:T(8,128)S(1)} async-done(((f32[16,72,128]{2,1,0:T(8,128)}), f32[16,72,128]{2,1,0:T(8,128)S(1)}, u32[]{:S(2)}, u32[]{:S(2)}) %all-to-all-start) | async-done | bytes 589856 | tf_op jit(solution)/shard_map/all_to_all | solution.py:228
  26.9 4.9 %all-to-all-start.1 = ((f32[16,64,256]{2,1,0:T(8,128)}), f32[16,64,256]{2,1,0:T(8,128)S(1)}, u32[]{:S(2)}, u32[]{:S(2)}) async-start(f32[16,64,256]{2,1,0:T(8,128)} %bitcast.22), calls=%async_computation.1 | async-start | bytes 2097152 | tf_op jit(solution)/shard_map/all_to_all | solution.py:242
  31.8 3.3 %collective-permute-start.3 = (f32[72,128]{1,0:T(8,128)S(1)}, f32[72,128]{1,0:T(8,128)S(1)}, u32[]{:S(2)}, u32[]{:S(2)}) collective-permute-start(f32[72,128]{1,0:T(8,128)S(1)} %reduce_sum.28), channel_id=1, source_target_pairs={{0,4},{4,0},{8,12},{12,8},{1,5},{5,1},{9,13},{13,9},{2,6},{6,2},{1... | collective-permute-start | bytes 110600 | tf_op jit(solution)/shard_map/ppermute | solution.py:199
  35.1 0.9 collective-permute-done.3
  35.9 1.9 %collective-permute-start.6 = (f32[72,128]{1,0:T(8,128)S(1)}, f32[72,128]{1,0:T(8,128)S(1)}, u32[]{:S(2)}, u32[]{:S(2)}) collective-permute-start(f32[72,128]{1,0:T(8,128)S(1)} %add.54), channel_id=1, source_target_pairs={{0,3},{1,2},{2,1},{3,0},{4,7},{5,6},{6,5},{7,4},{8,11},{9,10},{10,... | collective-permute-start | bytes 110600 | tf_op jit(solution)/shard_map/ppermute | solution.py:199
  37.9 1.6 %collective-permute-start.4 = (f32[72,128]{1,0:T(8,128)S(1)}, f32[72,128]{1,0:T(8,128)S(1)}, u32[]{:S(2)}, u32[]{:S(2)}) collective-permute-start(f32[72,128]{1,0:T(8,128)S(1)} %add.54), channel_id=1, source_target_pairs={{0,1},{1,0},{2,3},{3,2},{4,5},{5,4},{6,7},{7,6},{8,9},{9,8},{10,11... | collective-permute-start | bytes 110600 | tf_op jit(solution)/shard_map/ppermute | solution.py:199
  39.5 1.4 %collective-permute-done.6 = f32[72,128]{1,0:T(8,128)S(1)} collective-permute-done((f32[72,128]{1,0:T(8,128)S(1)}, f32[72,128]{1,0:T(8,128)S(1)}, u32[]{:S(2)}, u32[]{:S(2)}) %collective-permute-start.6) | collective-permute-done | bytes 36896 | tf_op jit(solution)/shard_map/ppermute | solution.py:199
  40.8 1.6 %collective-permute-done.5 = f32[72,128]{1,0:T(8,128)S(1)} collective-permute-done((f32[72,128]{1,0:T(8,128)S(1)}, f32[72,128]{1,0:T(8,128)S(1)}, u32[]{:S(2)}, u32[]{:S(2)}) %collective-permute-start.5) | collective-permute-done | bytes 36896 | tf_op jit(solution)/shard_map/ppermute | solution.py:199
  42.5 4.7 %collective-permute-start.7 = (f32[72,128]{1,0:T(8,128)S(1)}, f32[72,128]{1,0:T(8,128)S(1)}, u32[]{:S(2)}, u32[]{:S(2)}) collective-permute-start(f32[72,128]{1,0:T(8,128)S(1)} %add_add_fusion.1), channel_id=1, source_target_pairs={{0,8},{4,12},{8,0},{12,4},{1,9},{5,13},{9,1},{13,5},{2,10},{6,14},... | collective-permute-start | bytes 110600 | tf_op jit(solution)/shard_map/ppermute | solution.py:199
  47.1 2.3 %collective-permute-done.7 = f32[72,128]{1,0:T(8,128)S(1)} collective-permute-done((f32[72,128]{1,0:T(8,128)S(1)}, f32[72,128]{1,0:T(8,128)S(1)}, u32[]{:S(2)}, u32[]{:S(2)}) %collective-permute-start.7) | collective-permute-done | bytes 36896 | tf_op jit(solution)/shard_map/ppermute | solution.py:199
  49.5 0.9 broadcast_in_dim.16
  50.3 6.7 %all-to-all-start.2 = ((f32[16,72,128]{2,1,0:T(8,128)}), f32[16,72,128]{2,1,0:T(8,128)}, u32[]{:S(2)}, u32[]{:S(2)}) async-start(f32[16,72,128]{2,1,0:T(8,128)} %broadcast_in_dim.16), calls=%async_computation.2 | async-start | bytes 1179648 | tf_op jit(solution)/shard_map/all_to_all | solution.py:208
  57.1 0.1 reduce_sum.29
  57.1 2.3 %collective-permute-start.10 = (f32[64,256]{1,0:T(8,128)S(1)}, f32[64,256]{1,0:T(8,128)S(1)}, u32[]{:S(2)}, u32[]{:S(2)}) collective-permute-start(f32[64,256]{1,0:T(8,128)S(1)} %reduce_sum.29), channel_id=1, source_target_pairs={{0,3},{1,2},{2,1},{3,0},{4,7},{5,6},{6,5},{7,4},{8,11},{9,10},{10,... | collective-permute-start | bytes 196616 | tf_op jit(solution)/shard_map/ppermute | solution.py:199
  59.4 1.3 %collective-permute-start.8 = (f32[64,256]{1,0:T(8,128)S(1)}, f32[64,256]{1,0:T(8,128)S(1)}, u32[]{:S(2)}, u32[]{:S(2)}) collective-permute-start(f32[64,256]{1,0:T(8,128)S(1)} %reduce_sum.29), channel_id=1, source_target_pairs={{0,1},{1,0},{2,3},{3,2},{4,5},{5,4},{6,7},{7,6},{8,9},{9,8},{10,11... | collective-permute-start | bytes 196616 | tf_op jit(solution)/shard_map/ppermute | solution.py:199
  60.8 1.4 %collective-permute-done.10 = f32[64,256]{1,0:T(8,128)S(1)} collective-permute-done((f32[64,256]{1,0:T(8,128)S(1)}, f32[64,256]{1,0:T(8,128)S(1)}, u32[]{:S(2)}, u32[]{:S(2)}) %collective-permute-start.10) | collective-permute-done | bytes 65568 | tf_op jit(solution)/shard_map/ppermute | solution.py:199
  62.2 1.9 %collective-permute-done.9 = f32[64,256]{1,0:T(8,128)S(1)} collective-permute-done((f32[64,256]{1,0:T(8,128)S(1)}, f32[64,256]{1,0:T(8,128)S(1)}, u32[]{:S(2)}, u32[]{:S(2)}) %collective-permute-start.9) | collective-permute-done | bytes 65568 | tf_op jit(solution)/shard_map/ppermute | solution.py:199
  64.1 2.8 %all-to-all-done.2.folded_ref = f32[16,72,128]{2,1,0:T(8,128)} async-done(((f32[16,72,128]{2,1,0:T(8,128)}), f32[16,72,128]{2,1,0:T(8,128)}, u32[]{:S(2)}, u32[]{:S(2)}) %all-to-all-start.2) | async-done | bytes 589856 | tf_op jit(solution)/shard_map/all_to_all | solution.py:208
  66.9 1.1 broadcast_in_dim.18
  67.9 3.9 %all-to-all-start.3 = ((f32[16,64,256]{2,1,0:T(8,128)}), f32[16,64,256]{2,1,0:T(8,128)S(1)}, u32[]{:S(2)}, u32[]{:S(2)}) async-start(f32[16,64,256]{2,1,0:T(8,128)} %broadcast_in_dim.18), calls=%async_computation.3 | async-start | bytes 2097152 | tf_op jit(solution)/shard_map/all_to_all | solution.py:208
  71.8 0.2 convert_reduce_fusion
  72.0 0.2 fusion.7
  72.2 0.7 pad_add_fusion.place_ref
  72.9 1.1 broadcast_in_dim.17
  74.0 7.2 %inverse.1 = (f32[10,128,128]{2,1,0:T(8,128)}, f32[2,128,128]{2,1,0:T(8,128)}) custom-call(s32[3]{0:T(128)} %pad_add_fusion.place_ref, f32[16,72,128]{2,1,0:T(8,128)} %all-to-all-done.2.folded_ref), custom_call_target="tpu_custom_call" | custom-call | tf_op jit(solution)/shard_map/inverse/pallas_call | solution.py:128
  81.2 2.6 %all-to-all-done.3 = f32[16,64,256]{2,1,0:T(8,128)S(1)} async-done(((f32[16,64,256]{2,1,0:T(8,128)}), f32[16,64,256]{2,1,0:T(8,128)S(1)}, u32[]{:S(2)}, u32[]{:S(2)}) %all-to-all-start.3) | async-done | bytes 1048608 | tf_op jit(solution)/shard_map/all_to_all | solution.py:208
  83.8 1.0 copy-done.2
  84.8 4.1 %all-to-all-start.4 = ((f32[16,64,256]{2,1,0:T(8,128)}), f32[16,64,256]{2,1,0:T(8,128)S(1)}, u32[]{:S(2)}, u32[]{:S(2)}) async-start(f32[16,64,256]{2,1,0:T(8,128)} %broadcast_in_dim.17), calls=%async_computation.4 | async-start | bytes 2097152 | tf_op jit(solution)/shard_map/all_to_all | solution.py:271
  88.9 4.5 %precondition.1 = (f32[1024,256]{1,0:T(8,128)}, f32[1,128]{1,0:T(1,128)}) custom-call(f32[10,128,128]{2,1,0:T(8,128)} %get-tuple-element.37.inverse_ref, f32[1024,256]{1,0:T(8,128)} %bitcast.21), custom_call_target="tpu_custom_call" | custom-call | tf_op jit(solution)/shard_map/precondition/pallas_call | solution.py:159
  93.4 5.4 %collective-permute-start.11 = (f32[1,128]{1,0:T(1,128)}, f32[1,128]{1,0:T(1,128)S(1)}, u32[]{:S(2)}, u32[]{:S(2)}) collective-permute-start(f32[1,128]{1,0:T(1,128)} %get-tuple-element.39), channel_id=1, source_target_pairs={{0,4},{4,0},{8,12},{12,8},{1,5},{5,1},{9,13},{13,9},{2,6},{6,2},{1... | collective-permute-start | bytes 1544 | tf_op jit(solution)/shard_map/ppermute | solution.py:199
  98.9 1.0 collective-permute-done.11
  99.8 0.7 add.63.align_ref
  100.5 4.8 %collective-permute-start.12 = (f32[1,128]{1,0:T(1,128)S(1)}, f32[1,128]{1,0:T(1,128)S(1)}, u32[]{:S(2)}, u32[]{:S(2)}) collective-permute-start(f32[1,128]{1,0:T(1,128)S(1)} %add.63.align_ref), channel_id=1, source_target_pairs={{0,8},{4,12},{8,0},{12,4},{1,9},{5,13},{9,1},{13,5},{2,10},{6,14},... | collective-permute-start | bytes 1544 | tf_op jit(solution)/shard_map/ppermute | solution.py:199
  105.3 1.5 %collective-permute-done.12.other_ref = f32[1,128]{1,0:T(1,128)S(1)} collective-permute-done((f32[1,128]{1,0:T(1,128)S(1)}, f32[1,128]{1,0:T(1,128)S(1)}, u32[]{:S(2)}, u32[]{:S(2)}) %collective-permute-start.12) | collective-permute-done | bytes 544 | tf_op jit(solution)/shard_map/ppermute | solution.py:199
  106.8 0.5 copy-done.7
  107.4 0.5 copy-done.1
  107.8 2.8 %finish.1 = (f32[1024,256]{1,0:T(8,128)}, f32[16,256]{1,0:T(8,128)}) custom-call(s32[1]{0:T(128)} %bitcast.row_ref, f32[1,128]{1,0:T(1,128)} %copy-done.6, f32[1,128]{1,0:T(1,128)} %copy-done.7, f32[16,256]{1,0:T(8,128)} %momentum_ref.1, f32[1024,256]{1,0:T(8,128)} %get-tuple-element.40.precond_ref, f32[1024,256]{1,0:T(8,128)} %bitcast.20), custom_call_target="tpu_custom_call" | custom-call | tf_op jit(solution)/shard_map/finish/pallas_call | solution.py:181
  (34 shorter events, 0.2 us)
Async XLA Ops:
  0.6 1.6 %copy-start = (bf16[1024,1024]{1,0:T(8,128)(2,1)S(1)}, bf16[1024,1024]{1,0:T(8,128)(2,1)}, u32[]{:S(2)}) copy-start(bf16[1024,1024]{1,0:T(8,128)(2,1)} %param.7) | copy-start | bytes 6291460
  0.6 3.4 %copy-start.8 = (bf16[1024,1024]{1,0:T(8,128)(2,1)S(1)}, bf16[1024,1024]{1,0:T(8,128)(2,1)}, u32[]{:S(2)}) copy-start(bf16[1024,1024]{1,0:T(8,128)(2,1)} %param.8) | copy-start | bytes 6291460
  6.0 9.8 %copy-start.4 = (f32[16,256]{1,0:T(8,128)S(1)}, f32[16,256]{1,0:T(8,128)}, u32[]{:S(2)}) copy-start(f32[16,256]{1,0:T(8,128)} %momentum_ref.1) | copy-start | bytes 49156
  6.0 9.8 %copy-start.5 = (f32[16,256]{1,0:T(8,128)S(1)}, f32[16,256]{1,0:T(8,128)}, u32[]{:S(2)}) copy-start(f32[16,256]{1,0:T(8,128)} %param.12) | copy-start | bytes 49156
  8.3 18.6 %all-to-all-start = ((f32[16,72,128]{2,1,0:T(8,128)}), f32[16,72,128]{2,1,0:T(8,128)S(1)}, u32[]{:S(2)}, u32[]{:S(2)}) async-start(f32[16,72,128]{2,1,0:T(8,128)} %fold.1), calls=%async_computation | async-start | bytes 1179648 | tf_op jit(solution)/shard_map/all_to_all | solution.py:228
  15.9 7.7 %collective-permute-start.2 = (f32[16,256]{1,0:T(8,128)S(1)}, f32[16,256]{1,0:T(8,128)S(1)}, u32[]{:S(2)}, u32[]{:S(2)}) collective-permute-start(f32[16,256]{1,0:T(8,128)S(1)} %multiply_subtract_fusion), channel_id=1, source_target_pairs={{0,1},{1,0},{2,3},{3,2},{4,5},{5,4},{6,7},{7,6},{8,9},{9,8},{10,11... | collective-permute-start | bytes 49160 | tf_op jit(solution)/shard_map/ppermute | solution.py:199
  17.6 6.0 %collective-permute-start.1 = (f32[16,256]{1,0:T(8,128)S(1)}, f32[16,256]{1,0:T(8,128)S(1)}, u32[]{:S(2)}, u32[]{:S(2)}) collective-permute-start(f32[16,256]{1,0:T(8,128)S(1)} %multiply_subtract_fusion), channel_id=1, source_target_pairs={{0,2},{1,3},{2,0},{3,1},{4,6},{5,7},{6,4},{7,5},{8,10},{9,11},{10,... | collective-permute-start | bytes 49160 | tf_op jit(solution)/shard_map/ppermute | solution.py:199
  20.6 4.7 %collective-permute-start = (f32[16,256]{1,0:T(8,128)S(1)}, f32[16,256]{1,0:T(8,128)S(1)}, u32[]{:S(2)}, u32[]{:S(2)}) collective-permute-start(f32[16,256]{1,0:T(8,128)S(1)} %multiply_subtract_fusion), channel_id=1, source_target_pairs={{0,3},{1,2},{2,1},{3,0},{4,7},{5,6},{6,5},{7,4},{8,11},{9,10},{10,... | collective-permute-start | bytes 49160 | tf_op jit(solution)/shard_map/ppermute | solution.py:199
  23.6 25.8 %copy-start.3 = (f32[72,128]{1,0:T(8,128)S(1)}, f32[72,128]{1,0:T(8,128)}, u32[]{:S(2)}) copy-start(f32[72,128]{1,0:T(8,128)} %fold_one.1) | copy-start | bytes 110596
  26.9 22.6 %all-to-all-start.1 = ((f32[16,64,256]{2,1,0:T(8,128)}), f32[16,64,256]{2,1,0:T(8,128)S(1)}, u32[]{:S(2)}, u32[]{:S(2)}) async-start(f32[16,64,256]{2,1,0:T(8,128)} %bitcast.22), calls=%async_computation.1 | async-start | bytes 2097152 | tf_op jit(solution)/shard_map/all_to_all | solution.py:242
  31.8 4.2 %collective-permute-start.3 = (f32[72,128]{1,0:T(8,128)S(1)}, f32[72,128]{1,0:T(8,128)S(1)}, u32[]{:S(2)}, u32[]{:S(2)}) collective-permute-start(f32[72,128]{1,0:T(8,128)S(1)} %reduce_sum.28), channel_id=1, source_target_pairs={{0,4},{4,0},{8,12},{12,8},{1,5},{5,1},{9,13},{13,9},{2,6},{6,2},{1... | collective-permute-start | bytes 110600 | tf_op jit(solution)/shard_map/ppermute | solution.py:199
  35.9 4.9 %collective-permute-start.6 = (f32[72,128]{1,0:T(8,128)S(1)}, f32[72,128]{1,0:T(8,128)S(1)}, u32[]{:S(2)}, u32[]{:S(2)}) collective-permute-start(f32[72,128]{1,0:T(8,128)S(1)} %add.54), channel_id=1, source_target_pairs={{0,3},{1,2},{2,1},{3,0},{4,7},{5,6},{6,5},{7,4},{8,11},{9,10},{10,... | collective-permute-start | bytes 110600 | tf_op jit(solution)/shard_map/ppermute | solution.py:199
  37.9 4.6 %collective-permute-start.5 = (f32[72,128]{1,0:T(8,128)S(1)}, f32[72,128]{1,0:T(8,128)S(1)}, u32[]{:S(2)}, u32[]{:S(2)}) collective-permute-start(f32[72,128]{1,0:T(8,128)S(1)} %add.54), channel_id=1, source_target_pairs={{0,2},{1,3},{2,0},{3,1},{4,6},{5,7},{6,4},{7,5},{8,10},{9,11},{10,... | collective-permute-start | bytes 110600 | tf_op jit(solution)/shard_map/ppermute | solution.py:199
  37.9 4.6 %collective-permute-start.4 = (f32[72,128]{1,0:T(8,128)S(1)}, f32[72,128]{1,0:T(8,128)S(1)}, u32[]{:S(2)}, u32[]{:S(2)}) collective-permute-start(f32[72,128]{1,0:T(8,128)S(1)} %add.54), channel_id=1, source_target_pairs={{0,1},{1,0},{2,3},{3,2},{4,5},{5,4},{6,7},{7,6},{8,9},{9,8},{10,11... | collective-permute-start | bytes 110600 | tf_op jit(solution)/shard_map/ppermute | solution.py:199
  42.5 7.0 %collective-permute-start.7 = (f32[72,128]{1,0:T(8,128)S(1)}, f32[72,128]{1,0:T(8,128)S(1)}, u32[]{:S(2)}, u32[]{:S(2)}) collective-permute-start(f32[72,128]{1,0:T(8,128)S(1)} %add_add_fusion.1), channel_id=1, source_target_pairs={{0,8},{4,12},{8,0},{12,4},{1,9},{5,13},{9,1},{13,5},{2,10},{6,14},... | collective-permute-start | bytes 110600 | tf_op jit(solution)/shard_map/ppermute | solution.py:199
  50.3 16.5 %all-to-all-start.2 = ((f32[16,72,128]{2,1,0:T(8,128)}), f32[16,72,128]{2,1,0:T(8,128)}, u32[]{:S(2)}, u32[]{:S(2)}) async-start(f32[16,72,128]{2,1,0:T(8,128)} %broadcast_in_dim.16), calls=%async_computation.2 | async-start | bytes 1179648 | tf_op jit(solution)/shard_map/all_to_all | solution.py:208
  57.0 14.8 %copy-start.9 = (s32[16]{0:T(128)S(1)}, s32[16]{0:T(128)}, u32[]{:S(2)}) copy-start(s32[16]{0:T(128)} %param.11) | copy-start | bytes 196
  57.1 5.0 %collective-permute-start.10 = (f32[64,256]{1,0:T(8,128)S(1)}, f32[64,256]{1,0:T(8,128)S(1)}, u32[]{:S(2)}, u32[]{:S(2)}) collective-permute-start(f32[64,256]{1,0:T(8,128)S(1)} %reduce_sum.29), channel_id=1, source_target_pairs={{0,3},{1,2},{2,1},{3,0},{4,7},{5,6},{6,5},{7,4},{8,11},{9,10},{10,... | collective-permute-start | bytes 196616 | tf_op jit(solution)/shard_map/ppermute | solution.py:199
  59.4 4.6 %collective-permute-start.9 = (f32[64,256]{1,0:T(8,128)S(1)}, f32[64,256]{1,0:T(8,128)S(1)}, u32[]{:S(2)}, u32[]{:S(2)}) collective-permute-start(f32[64,256]{1,0:T(8,128)S(1)} %reduce_sum.29), channel_id=1, source_target_pairs={{0,2},{1,3},{2,0},{3,1},{4,6},{5,7},{6,4},{7,5},{8,10},{9,11},{10,... | collective-permute-start | bytes 196616 | tf_op jit(solution)/shard_map/ppermute | solution.py:199
  59.4 4.6 %collective-permute-start.8 = (f32[64,256]{1,0:T(8,128)S(1)}, f32[64,256]{1,0:T(8,128)S(1)}, u32[]{:S(2)}, u32[]{:S(2)}) collective-permute-start(f32[64,256]{1,0:T(8,128)S(1)} %reduce_sum.29), channel_id=1, source_target_pairs={{0,1},{1,0},{2,3},{3,2},{4,5},{5,4},{6,7},{7,6},{8,9},{9,8},{10,11... | collective-permute-start | bytes 196616 | tf_op jit(solution)/shard_map/ppermute | solution.py:199
  67.9 15.9 %all-to-all-start.3 = ((f32[16,64,256]{2,1,0:T(8,128)}), f32[16,64,256]{2,1,0:T(8,128)S(1)}, u32[]{:S(2)}, u32[]{:S(2)}) async-start(f32[16,64,256]{2,1,0:T(8,128)} %broadcast_in_dim.18), calls=%async_computation.3 | async-start | bytes 2097152 | tf_op jit(solution)/shard_map/all_to_all | solution.py:208
  83.8 1.0 copy-start.2
  84.8 22.0 %all-to-all-start.4 = ((f32[16,64,256]{2,1,0:T(8,128)}), f32[16,64,256]{2,1,0:T(8,128)S(1)}, u32[]{:S(2)}, u32[]{:S(2)}) async-start(f32[16,64,256]{2,1,0:T(8,128)} %broadcast_in_dim.17), calls=%async_computation.4 | async-start | bytes 2097152 | tf_op jit(solution)/shard_map/all_to_all | solution.py:271
  93.4 6.4 %collective-permute-start.11 = (f32[1,128]{1,0:T(1,128)}, f32[1,128]{1,0:T(1,128)S(1)}, u32[]{:S(2)}, u32[]{:S(2)}) collective-permute-start(f32[1,128]{1,0:T(1,128)} %get-tuple-element.39), channel_id=1, source_target_pairs={{0,4},{4,0},{8,12},{12,8},{1,5},{5,1},{9,13},{13,9},{2,6},{6,2},{1... | collective-permute-start | bytes 1544 | tf_op jit(solution)/shard_map/ppermute | solution.py:199
  100.5 6.3 %copy-start.6 = (f32[1,128]{1,0:T(1,128)}, f32[1,128]{1,0:T(1,128)S(1)}, u32[]{:S(2)}) copy-start(f32[1,128]{1,0:T(1,128)S(1)} %add.63.align_ref) | copy-start | bytes 1540
  100.5 6.3 %collective-permute-start.12 = (f32[1,128]{1,0:T(1,128)S(1)}, f32[1,128]{1,0:T(1,128)S(1)}, u32[]{:S(2)}, u32[]{:S(2)}) collective-permute-start(f32[1,128]{1,0:T(1,128)S(1)} %add.63.align_ref), channel_id=1, source_target_pairs={{0,8},{4,12},{8,0},{12,4},{1,9},{5,13},{9,1},{13,5},{2,10},{6,14},... | collective-permute-start | bytes 1544 | tf_op jit(solution)/shard_map/ppermute | solution.py:199
  106.8 0.5 copy-start.7
  106.8 1.0 copy-start.1
